TPU v7x, 512 devices: a whole 4x4x16 slice. The times are simulated.
512 devices in a mesh: row: 16 (over z), col: 16 (over y, x_lo, core), depth: 2 (over x_hi).
Axes of the slice: x: 4 (x_hi: 2, x_lo: 2; x = x_hi * 2 + x_lo), y: 4, z: 16, core: 2. Of those that a mesh axis runs over, the one named last changes fastest.
Arguments:
- amplitudes: float32 [3072, 11520], P('row', ('col', 'depth')), may hold values from -6 to 6
- integrals: float32 [11520, 5760], P(('row', 'depth'), 'col'), may hold values from -0.0546875 to 0.0546875
Outputs:
- ladder: float32 [3072, 5760], P(('row', 'depth'), 'col')
All inputs are finite; a program needn't handle non-finite values.
Results may differ from a plain program's by a relative error of at most 0.00007.
Values sent between devices are 32-bit elements; how exact they have to be, the bound alone decides.
No kernel may reach another device: no remote copies, remote signals or barrier semaphores. Data moves between devices by JAX's collectives and lax.ppermute only.
A program may use at most 64 MiB of HBM per device.

v0:
```python
import jax
import jax.numpy as jnp
from jax import lax
from jax.sharding import PartitionSpec as P


def local(amplitudes, integrals):
    slab = lax.all_gather(integrals, "row", axis=0, tiled=True)
    total = jnp.dot(
        lax.all_gather(amplitudes, "col", axis=1, tiled=True),
        slab,
        precision=lax.Precision.HIGHEST,
        preferred_element_type=jnp.float32,
    )
    return lax.psum_scatter(0.5 * total, "depth", scatter_dimension=0, tiled=True)


def solution(mesh):
    placed = (P("row", ("col", "depth")), P(("row", "depth"), "col"))
    return jax.shard_map(
        local, mesh=mesh, in_specs=placed, out_specs=P(("row", "depth"), "col"), check_vma=False
    )
```

profile of v0, /device:TPU:6, one launch (start us, length us, event | category | flops | bytes accessed | tf_op | source)
XLA Modules:
  0.0 211.4 jit_solution(3228303676502207377)
XLA Ops:
  6.5 0.0 all-gather.6.cloned.1.call-start
  6.5 0.7 all-gather.6.cloned.1.call-update
  7.3 0.0 all-gather.4.cloned.1.call-start
  7.3 0.7 all-gather.4.cloned.1.call-update
  8.0 0.0 reduce-scatter.2.cloned.1.call-start
  8.1 51.6 %all-gather.6.cloned.1.call-done = f32[16,360,192]{1,2,0:T(8,128)} async-done(((f32[1,360,192]{1,2,0:T(8,128)}), f32[16,360,192]{1,2,0:T(8,128)}) %all-gather.6.cloned.1.call-update) | async-done | bytes 4423696 | tf_op jit(solution)/shard_map/all_gather | solution.py:10
  59.6 7.2 %copy.4 = f32[16,360,192]{1,0,2:T(8,128)} copy(f32[16,360,192]{1,2,0:T(8,128)} %all-gather.6.cloned.1.call-done) | data formatting | bytes 8847360 | tf_op jit(solution)/shard_map/all_gather | solution.py:10
  66.8 5.9 %reshape.1 = f32[5760,192]{0,1:T(8,128)} reshape(f32[16,360,192]{1,0,2:T(8,128)} %copy.4) | data formatting | bytes 8847360
  72.7 100.1 %all-gather.4.cloned.1.call-done = f32[5760,360]{1,0:T(8,128)} async-done(((f32[360,360]{1,0:T(8,128)}), f32[5760,360]{1,0:T(8,128)}) %all-gather.4.cloned.1.call-update) | async-done | bytes 8294416 | tf_op jit(solution)/shard_map/all_gather | solution.py:8
  172.7 11.8 %convolution_multiply_fusion = f32[192,360]{1,0:T(8,128)} fusion(f32[5760,192]{0,1:T(8,128)} %reshape.1, f32[5760,360]{1,0:T(8,128)} %all-gather.4.cloned.1.call-done), kind=kOutput, calls=%fused_computation | convolution fusion | flops 4777643520 | bytes 12994560 | tf_op jit(solution)/shard_map/dot_general | solution.py:9
  184.5 0.0 reduce-scatter.2.cloned.1.call-update
  184.6 20.3 %reduce-scatter.2.cloned.1.call-done = f32[96,360]{1,0:T(8,128)} async-done(((f32[192,360]{1,0:T(8,128)}), f32[96,360]{1,0:T(8,128)}) %reduce-scatter.2.cloned.1.call-update) | async-done | bytes 138256 | tf_op jit(solution)/shard_map/reduce_scatter | solution.py:15
Async XLA Ops:
  6.5 53.1 %all-gather.6.cloned.1.call-start = ((), (), s32[]{:S(2)}) async-start(), calls=%async_computation.3 | async-start | bytes 5013504 | tf_op jit(solution)/shard_map/all_gather | solution.py:10
  7.3 165.5 %all-gather.4.cloned.1.call-start = ((), (), s32[]{:S(2)}) async-start(), calls=%async_computation.1 | async-start | bytes 9400320 | tf_op jit(solution)/shard_map/all_gather | solution.py:8
  8.0 196.8 %reduce-scatter.2.cloned.1.call-start = ((), (), s32[]{:S(2)}) async-start(), calls=%async_computation.2 | async-start | bytes 442368 | tf_op jit(solution)/shard_map/reduce_scatter | solution.py:15
Sparse Core Ops, SparseCore 0:
  9.5 50.0 all-gather.5
  61.7 110.9 all-gather.3
  184.7 20.1 reduce-scatter.1
where the time goes:
time: 214 us; the launch traced here: 211 us
  waiting for transfers between devices  173 us (81%)
  local copies, waits for them, and re-layouts  13.1 us (6%)
  between operations  13.1 us (6%)
  matrix products  11.8 us (6%)
    all_gather x1, waiting for transfers between devices, local(): slab = lax.all_gather(integrals, 'row', axis=0, tiled=True)  100 us
    all_gather x1, waiting for transfers between devices, local(): lax.all_gather(amplitudes, 'col', axis=1, tiled=True)  51.6 us
    reduce_scatter x1, waiting for transfers between devices, local(): lax.psum_scatter(0.5 * total, 'depth', scatter_dimension=0, tiled=True)  20.3 us
    dot_general x1, matrix products, local(): jnp.dot(lax.all_gather(amplitudes, 'col', axis=1, tiled=True), slab, prec...  11.8 us
    all_gather x1, local copies, waits for them, and re-layouts, local(): lax.all_gather(amplitudes, 'col', axis=1, tiled=True)  7.19 us
    unnamed x1, local copies, waits for them, and re-layouts  5.87 us
  transfers between devices with their start and end apart: 3, of which 3 were waited for; matrix products, arithmetic and copies ran while one was open for 6% of the time, Pallas kernels for 0%

commit v1 on v0

v1 whole, which is shorter than its diff:
```python
import jax
import jax.numpy as jnp
from jax import lax
from jax.sharding import PartitionSpec as P


def local(amplitudes, integrals):
    n = lax.axis_size("row")
    me = lax.axis_index("row")
    d = lax.axis_index("depth")
    kb = integrals.shape[0]
    rows = amplitudes.shape[0]
    half = rows // 2

    strip = lax.all_gather(amplitudes, "col", axis=1, tiled=True)

    def product(block, owner):
        cols = lax.dynamic_slice_in_dim(strip, owner * kb, kb, axis=1)
        return jnp.dot(cols, block, precision=lax.Precision.HIGHEST,
                       preferred_element_type=jnp.float32)

    fwd = [(i, (i + 1) % n) for i in range(n)]
    bwd = [(i, (i - 1) % n) for i in range(n)]
    total = product(integrals, me)
    ahead = integrals
    behind = integrals
    for step in range(1, n // 2 + 1):
        ahead = lax.ppermute(ahead, "row", fwd)
        total = total + product(ahead, (me - step) % n)
        if step < n - n // 2:
            behind = lax.ppermute(behind, "row", bwd)
            total = total + product(behind, (me + step) % n)

    mine = lax.dynamic_slice_in_dim(total, d * half, half, axis=0)
    other = lax.dynamic_slice_in_dim(total, (1 - d) * half, half, axis=0)
    other = lax.ppermute(other, "depth", [(0, 1), (1, 0)])
    return 0.5 * (mine + other)


def solution(mesh):
    placed = (P("row", ("col", "depth")), P(("row", "depth"), "col"))
    return jax.shard_map(
        local, mesh=mesh, in_specs=placed, out_specs=P(("row", "depth"), "col"), check_vma=False
    )
```

time: 214 us -> 174 us (0.81)
  waiting for transfers between devices: 173 us -> 62.1 us
  starting transfers between devices: 0.08 us -> 60.8 us
  matrix products: 11.8 us -> 21.8 us
    all_gather x2 -> x1, waiting for transfers between devices: 152 us -> 0.02 us  [local(): strip = lax.all_gather(amplitudes, 'col', axis=1, tiled=True)]
    ppermute x0 -> x16, waiting for transfers between devices: none -> 61.4 us  [the longest x8 56.2 us: local(): ahead = lax.ppermute(ahead, 'row', fwd)]
    ppermute x0 -> x16, starting transfers between devices: none -> 60.8 us  [the longest x7 40.3 us: local(): behind = lax.ppermute(behind, 'row', bwd)]
    reduce_scatter x1 -> x0, waiting for transfers between devices: 20.3 us -> none  [local(): lax.psum_scatter(0.5 * total, 'depth', scatter_dimension=0, tiled=True)]
    dot_general x1 -> x16, matrix products: 11.8 us -> 21.8 us  [product(): jnp.dot(cols, block, precision=lax.Precision.HIGHEST, preferred_element_t...]
    unnamed x1 -> x17, local copies, waits for them, and re-layouts: 5.87 us -> 5.87 us
  transfers between devices with their start and end apart: 3 -> 17, of which waited for: 3 -> 8; matrix products, arithmetic and copies ran while one was open for 6% -> 19% of each run, Pallas kernels for 0% -> 0%
where the time goes in v1:
time: 174 us; the launch traced here: 173 us
  waiting for transfers between devices  62.1 us (36%)
  starting transfers between devices  60.8 us (35%)
  matrix products  21.8 us (13%)
  between operations  14.1 us (8%)
  local copies, waits for them, and re-layouts  13.2 us (8%)
    ppermute x8, waiting for transfers between devices, local(): ahead = lax.ppermute(ahead, 'row', fwd)  56.2 us
    ppermute x7, starting transfers between devices, local(): behind = lax.ppermute(behind, 'row', bwd)  40.3 us
    dot_general x16, matrix products, product(): jnp.dot(cols, block, precision=lax.Precision.HIGHEST, preferred_element_t...  21.8 us
    ppermute x8, starting transfers between devices, local(): ahead = lax.ppermute(ahead, 'row', fwd)  17.2 us
    all_gather x1, local copies, waits for them, and re-layouts, local(): strip = lax.all_gather(amplitudes, 'col', axis=1, tiled=True)  7.27 us
    unnamed x17, local copies, waits for them, and re-layouts  5.87 us
    ppermute x1, waiting for transfers between devices, local(): other = lax.ppermute(other, 'depth', [(0, 1), (1, 0)])  5.22 us
  transfers between devices with their start and end apart: 17, of which 8 were waited for; matrix products, arithmetic and copies ran while one was open for 19% of the time, Pallas kernels for 0%

profile of v1, /device:TPU:6, one launch (start us, length us, event | category | flops | bytes accessed | tf_op | source)
XLA Modules:
  0.0 172.7 jit_solution(15975501756322274946)
XLA Ops:
  7.3 3.8 %collective-permute-start = (f32[360,360]{1,0:T(8,128)}, f32[360,360]{1,0:T(8,128)S(1)}, u32[]{:S(2)}, u32[]{:S(2)}) collective-permute-start(f32[360,360]{1,0:T(8,128)} %param.3), channel_id=1, source_target_pairs={{0,32},{32,64},{64,96},{96,128},{128,160},{160,192},{192,224},{224... | collective-permute-start | bytes 1555208 | tf_op jit(solution)/shard_map/ppermute | solution.py:28
  11.1 9.5 %collective-permute-start.1 = (f32[360,360]{1,0:T(8,128)}, f32[360,360]{1,0:T(8,128)S(1)}, u32[]{:S(2)}, u32[]{:S(2)}) collective-permute-start(f32[360,360]{1,0:T(8,128)} %param.3), channel_id=1, source_target_pairs={{0,480},{32,0},{64,32},{96,64},{128,96},{160,128},{192,160},{224,1... | collective-permute-start | bytes 1555208 | tf_op jit(solution)/shard_map/ppermute | solution.py:31
  20.6 10.8 %collective-permute-done = f32[360,360]{1,0:T(8,128)S(1)} collective-permute-done((f32[360,360]{1,0:T(8,128)}, f32[360,360]{1,0:T(8,128)S(1)}, u32[]{:S(2)}, u32[]{:S(2)}) %collective-permute-start) | collective-permute-done | bytes 518432 | tf_op jit(solution)/shard_map/ppermute | solution.py:28
  31.4 1.9 %collective-permute-start.2 = (f32[360,360]{1,0:T(8,128)S(1)}, f32[360,360]{1,0:T(8,128)S(1)}, u32[]{:S(2)}, u32[]{:S(2)}) collective-permute-start(f32[360,360]{1,0:T(8,128)S(1)} %collective-permute-done), channel_id=1, source_target_pairs={{0,32},{32,64},{64,96},{96,128},{128,160},{160,192},{192,224},{224... | collective-permute-start | bytes 1555208 | tf_op jit(solution)/shard_map/ppermute | solution.py:28
  33.3 5.1 %collective-permute-start.3 = (f32[360,360]{1,0:T(8,128)S(1)}, f32[360,360]{1,0:T(8,128)S(1)}, u32[]{:S(2)}, u32[]{:S(2)}) collective-permute-start(f32[360,360]{1,0:T(8,128)S(1)} %collective-permute-done.1), channel_id=1, source_target_pairs={{0,480},{32,0},{64,32},{96,64},{128,96},{160,128},{192,160},{224,1... | collective-permute-start | bytes 1555208 | tf_op jit(solution)/shard_map/ppermute | solution.py:31
  38.5 9.7 %collective-permute-done.2 = f32[360,360]{1,0:T(8,128)S(1)} collective-permute-done((f32[360,360]{1,0:T(8,128)S(1)}, f32[360,360]{1,0:T(8,128)S(1)}, u32[]{:S(2)}, u32[]{:S(2)}) %collective-permute-start.2) | collective-permute-done | bytes 518432 | tf_op jit(solution)/shard_map/ppermute | solution.py:28
  48.2 1.9 %collective-permute-start.4 = (f32[360,360]{1,0:T(8,128)S(1)}, f32[360,360]{1,0:T(8,128)S(1)}, u32[]{:S(2)}, u32[]{:S(2)}) collective-permute-start(f32[360,360]{1,0:T(8,128)S(1)} %collective-permute-done.2), channel_id=1, source_target_pairs={{0,32},{32,64},{64,96},{96,128},{128,160},{160,192},{192,224},{224... | collective-permute-start | bytes 1555208 | tf_op jit(solution)/shard_map/ppermute | solution.py:28
  50.2 5.1 %collective-permute-start.5 = (f32[360,360]{1,0:T(8,128)S(1)}, f32[360,360]{1,0:T(8,128)S(1)}, u32[]{:S(2)}, u32[]{:S(2)}) collective-permute-start(f32[360,360]{1,0:T(8,128)S(1)} %collective-permute-done.3), channel_id=1, source_target_pairs={{0,480},{32,0},{64,32},{96,64},{128,96},{160,128},{192,160},{224,1... | collective-permute-start | bytes 1555208 | tf_op jit(solution)/shard_map/ppermute | solution.py:31
  55.3 8.8 %collective-permute-done.4 = f32[360,360]{1,0:T(8,128)S(1)} collective-permute-done((f32[360,360]{1,0:T(8,128)S(1)}, f32[360,360]{1,0:T(8,128)S(1)}, u32[]{:S(2)}, u32[]{:S(2)}) %collective-permute-start.4) | collective-permute-done | bytes 518432 | tf_op jit(solution)/shard_map/ppermute | solution.py:28
  64.1 1.9 %collective-permute-start.6 = (f32[360,360]{1,0:T(8,128)S(1)}, f32[360,360]{1,0:T(8,128)S(1)}, u32[]{:S(2)}, u32[]{:S(2)}) collective-permute-start(f32[360,360]{1,0:T(8,128)S(1)} %collective-permute-done.4), channel_id=1, source_target_pairs={{0,32},{32,64},{64,96},{96,128},{128,160},{160,192},{192,224},{224... | collective-permute-start | bytes 1555208 | tf_op jit(solution)/shard_map/ppermute | solution.py:28
  66.1 5.1 %collective-permute-start.7 = (f32[360,360]{1,0:T(8,128)S(1)}, f32[360,360]{1,0:T(8,128)S(1)}, u32[]{:S(2)}, u32[]{:S(2)}) collective-permute-start(f32[360,360]{1,0:T(8,128)S(1)} %collective-permute-done.5), channel_id=1, source_target_pairs={{0,480},{32,0},{64,32},{96,64},{128,96},{160,128},{192,160},{224,1... | collective-permute-start | bytes 1555208 | tf_op jit(solution)/shard_map/ppermute | solution.py:31
  71.2 7.9 %collective-permute-done.6 = f32[360,360]{1,0:T(8,128)S(1)} collective-permute-done((f32[360,360]{1,0:T(8,128)S(1)}, f32[360,360]{1,0:T(8,128)S(1)}, u32[]{:S(2)}, u32[]{:S(2)}) %collective-permute-start.6) | collective-permute-done | bytes 518432 | tf_op jit(solution)/shard_map/ppermute | solution.py:28
  79.1 1.9 %collective-permute-start.8 = (f32[360,360]{1,0:T(8,128)S(1)}, f32[360,360]{1,0:T(8,128)S(1)}, u32[]{:S(2)}, u32[]{:S(2)}) collective-permute-start(f32[360,360]{1,0:T(8,128)S(1)} %collective-permute-done.6), channel_id=1, source_target_pairs={{0,32},{32,64},{64,96},{96,128},{128,160},{160,192},{192,224},{224... | collective-permute-start | bytes 1555208 | tf_op jit(solution)/shard_map/ppermute | solution.py:28
  81.0 5.1 %collective-permute-start.9 = (f32[360,360]{1,0:T(8,128)S(1)}, f32[360,360]{1,0:T(8,128)}, u32[]{:S(2)}, u32[]{:S(2)}) collective-permute-start(f32[360,360]{1,0:T(8,128)S(1)} %collective-permute-done.7), channel_id=1, source_target_pairs={{0,480},{32,0},{64,32},{96,64},{128,96},{160,128},{192,160},{224,1... | collective-permute-start | bytes 1555208 | tf_op jit(solution)/shard_map/ppermute | solution.py:31
  86.2 7.0 %collective-permute-done.8 = f32[360,360]{1,0:T(8,128)S(1)} collective-permute-done((f32[360,360]{1,0:T(8,128)S(1)}, f32[360,360]{1,0:T(8,128)S(1)}, u32[]{:S(2)}, u32[]{:S(2)}) %collective-permute-start.8) | collective-permute-done | bytes 518432 | tf_op jit(solution)/shard_map/ppermute | solution.py:28
  93.1 1.9 %collective-permute-start.10 = (f32[360,360]{1,0:T(8,128)S(1)}, f32[360,360]{1,0:T(8,128)S(1)}, u32[]{:S(2)}, u32[]{:S(2)}) collective-permute-start(f32[360,360]{1,0:T(8,128)S(1)} %collective-permute-done.8), channel_id=1, source_target_pairs={{0,32},{32,64},{64,96},{96,128},{128,160},{160,192},{192,224},{224... | collective-permute-start | bytes 1555208 | tf_op jit(solution)/shard_map/ppermute | solution.py:28
  95.1 5.1 %collective-permute-start.11 = (f32[360,360]{1,0:T(8,128)}, f32[360,360]{1,0:T(8,128)}, u32[]{:S(2)}, u32[]{:S(2)}) collective-permute-start(f32[360,360]{1,0:T(8,128)} %collective-permute-done.9), channel_id=1, source_target_pairs={{0,480},{32,0},{64,32},{96,64},{128,96},{160,128},{192,160},{224,1... | collective-permute-start | bytes 1555208 | tf_op jit(solution)/shard_map/ppermute | solution.py:31
  100.2 6.1 %collective-permute-done.10 = f32[360,360]{1,0:T(8,128)S(1)} collective-permute-done((f32[360,360]{1,0:T(8,128)S(1)}, f32[360,360]{1,0:T(8,128)S(1)}, u32[]{:S(2)}, u32[]{:S(2)}) %collective-permute-start.10) | collective-permute-done | bytes 518432 | tf_op jit(solution)/shard_map/ppermute | solution.py:28
  106.3 1.9 %collective-permute-start.12 = (f32[360,360]{1,0:T(8,128)S(1)}, f32[360,360]{1,0:T(8,128)S(1)}, u32[]{:S(2)}, u32[]{:S(2)}) collective-permute-start(f32[360,360]{1,0:T(8,128)S(1)} %collective-permute-done.10), channel_id=1, source_target_pairs={{0,32},{32,64},{64,96},{96,128},{128,160},{160,192},{192,224},{224... | collective-permute-start | bytes 1555208 | tf_op jit(solution)/shard_map/ppermute | solution.py:28
  108.5 5.1 %collective-permute-start.13 = (f32[360,360]{1,0:T(8,128)}, f32[360,360]{1,0:T(8,128)}, u32[]{:S(2)}, u32[]{:S(2)}) collective-permute-start(f32[360,360]{1,0:T(8,128)} %collective-permute-done.11), channel_id=1, source_target_pairs={{0,480},{32,0},{64,32},{96,64},{128,96},{160,128},{192,160},{224,1... | collective-permute-start | bytes 1555208 | tf_op jit(solution)/shard_map/ppermute | solution.py:31
  113.6 5.9 %collective-permute-done.12 = f32[360,360]{1,0:T(8,128)S(1)} collective-permute-done((f32[360,360]{1,0:T(8,128)S(1)}, f32[360,360]{1,0:T(8,128)S(1)}, u32[]{:S(2)}, u32[]{:S(2)}) %collective-permute-start.12) | collective-permute-done | bytes 518432 | tf_op jit(solution)/shard_map/ppermute | solution.py:28
  119.6 1.9 %collective-permute-start.14 = (f32[360,360]{1,0:T(8,128)S(1)}, f32[360,360]{1,0:T(8,128)}, u32[]{:S(2)}, u32[]{:S(2)}) collective-permute-start(f32[360,360]{1,0:T(8,128)S(1)} %collective-permute-done.12), channel_id=1, source_target_pairs={{0,32},{32,64},{64,96},{96,128},{128,160},{160,192},{192,224},{224... | collective-permute-start | bytes 1555208 | tf_op jit(solution)/shard_map/ppermute | solution.py:28
  121.5 7.3 %copy.4 = f32[16,360,192]{1,0,2:T(8,128)} copy(f32[16,360,192]{1,2,0:T(8,128)} %all-gather.3.cloned.1.call-done) | data formatting | bytes 8847360 | tf_op jit(solution)/shard_map/all_gather | solution.py:15
  128.8 5.8 %reshape.1 = f32[5760,192]{0,1:T(8,128)} reshape(f32[16,360,192]{1,0,2:T(8,128)} %copy.4) | data formatting | bytes 8847360
  134.6 2.1 %fusion.27 = f32[192,360]{1,0:T(8,128)S(1)} fusion(f32[360,360]{1,0:T(8,128)} %param.3, f32[5760,192]{0,1:T(8,128)} %reshape.1, s32[]{:T(128)S(6)} %select_n.117), kind=kOutput, calls=%fused_computation.36 | convolution fusion | flops 298598400 | bytes 1124356 | tf_op jit(solution)/shard_map/dot_general | solution.py:19
  136.8 2.0 %fusion.22 = f32[192,360]{1,0:T(8,128)S(1)} fusion(f32[360,360]{1,0:T(8,128)} %copy-done.5, f32[5760,192]{0,1:T(8,128)} %reshape.1, s32[]{:T(128)S(6)} %select_n.125), kind=kOutput, calls=%fused_computation.31 | convolution fusion | flops 298598400 | bytes 1124356 | tf_op jit(solution)/shard_map/dot_general | solution.py:19
  138.7 2.0 %fusion.19 = f32[192,360]{1,0:T(8,128)S(1)} fusion(f32[360,360]{1,0:T(8,128)} %copy-done.6, f32[5760,192]{0,1:T(8,128)} %reshape.1, s32[]{:T(128)S(6)} %select_n.129), kind=kOutput, calls=%fused_computation.28 | convolution fusion | flops 298598400 | bytes 1124356 | tf_op jit(solution)/shard_map/dot_general | solution.py:19
  140.7 2.0 %fusion.16 = f32[192,360]{1,0:T(8,128)S(1)} fusion(f32[360,360]{1,0:T(8,128)} %copy-done.7, f32[5760,192]{0,1:T(8,128)} %reshape.1, s32[]{:T(128)S(6)} %select_n.133), kind=kOutput, calls=%fused_computation.25 | convolution fusion | flops 298598400 | bytes 1124356 | tf_op jit(solution)/shard_map/dot_general | solution.py:19
  148.0 1.8 %fusion.7 = f32[192,360]{1,0:T(8,128)S(1)} fusion(f32[360,360]{1,0:T(8,128)} %collective-permute-done.13, f32[5760,192]{0,1:T(8,128)S(1)} %copy-done, s32[]{:T(128)S(6)} %select_n.145), kind=kOutput, calls=%fused_computation.16 | convolution fusion | flops 298598400 | bytes 1089796 | tf_op jit(solution)/shard_map/dot_general | solution.py:19
  154.7 1.8 %convolution_add_fusion = f32[192,360]{1,0:T(8,128)S(1)} fusion(f32[192,360]{1,0:T(8,128)S(1)} %fusion.5, f32[360,360]{1,0:T(8,128)} %collective-permute-done.14, f32[5760,192]{0,1:T(8,128)S(1)} %copy-done, s32[]{:T(128)S(6)} %select_n.147), kind=kOutput, calls=%fused_computation | convolution fusion | flops 298667520 | bytes 1384708 | tf_op jit(solution)/shard_map/dot_general | solution.py:19
  156.6 3.3 %collective-permute-start.15 = (f32[96,360]{1,0:T(8,128)S(1)}, f32[96,360]{1,0:T(8,128)S(1)}, u32[]{:S(2)}, u32[]{:S(2)}) collective-permute-start(f32[96,360]{1,0:T(8,128)S(1)} %constant_dynamic-slice_fusion), channel_id=1, source_target_pairs={{0,1},{1,0},{2,3},{3,2},{4,5},{5,4},{6,7},{7,6},{8,9},{9,8},{10,11... | collective-permute-start | bytes 414728 | tf_op jit(solution)/shard_map/ppermute | solution.py:36
  159.9 5.2 %collective-permute-done.15 = f32[96,360]{1,0:T(8,128)S(1)} collective-permute-done((f32[96,360]{1,0:T(8,128)S(1)}, f32[96,360]{1,0:T(8,128)S(1)}, u32[]{:S(2)}, u32[]{:S(2)}) %collective-permute-start.15) | collective-permute-done | bytes 138272 | tf_op jit(solution)/shard_map/ppermute | solution.py:36
  (39 shorter events, 11.6 us)
Async XLA Ops:
  6.5 115.0 %all-gather.3.cloned.1.call-start = ((), (), s32[]{:S(2)}) async-start(), calls=%async_computation | async-start | bytes 5013504 | tf_op jit(solution)/shard_map/all_gather | solution.py:15
  7.3 24.1 %collective-permute-start = (f32[360,360]{1,0:T(8,128)}, f32[360,360]{1,0:T(8,128)S(1)}, u32[]{:S(2)}, u32[]{:S(2)}) collective-permute-start(f32[360,360]{1,0:T(8,128)} %param.3), channel_id=1, source_target_pairs={{0,32},{32,64},{64,96},{96,128},{128,160},{160,192},{192,224},{224... | collective-permute-start | bytes 1555208 | tf_op jit(solution)/shard_map/ppermute | solution.py:28
  11.1 22.2 %collective-permute-start.1 = (f32[360,360]{1,0:T(8,128)}, f32[360,360]{1,0:T(8,128)S(1)}, u32[]{:S(2)}, u32[]{:S(2)}) collective-permute-start(f32[360,360]{1,0:T(8,128)} %param.3), channel_id=1, source_target_pairs={{0,480},{32,0},{64,32},{96,64},{128,96},{160,128},{192,160},{224,1... | collective-permute-start | bytes 1555208 | tf_op jit(solution)/shard_map/ppermute | solution.py:31
  31.4 7.1 %copy-start.1 = (f32[360,360]{1,0:T(8,128)}, f32[360,360]{1,0:T(8,128)S(1)}, u32[]{:S(2)}) copy-start(f32[360,360]{1,0:T(8,128)S(1)} %collective-permute-done) | copy-start | bytes 1555204
  31.4 16.8 %collective-permute-start.2 = (f32[360,360]{1,0:T(8,128)S(1)}, f32[360,360]{1,0:T(8,128)S(1)}, u32[]{:S(2)}, u32[]{:S(2)}) collective-permute-start(f32[360,360]{1,0:T(8,128)S(1)} %collective-permute-done), channel_id=1, source_target_pairs={{0,32},{32,64},{64,96},{96,128},{128,160},{160,192},{192,224},{224... | collective-permute-start | bytes 1555208 | tf_op jit(solution)/shard_map/ppermute | solution.py:28
  33.3 22.0 %copy-start.3 = (f32[360,360]{1,0:T(8,128)}, f32[360,360]{1,0:T(8,128)S(1)}, u32[]{:S(2)}) copy-start(f32[360,360]{1,0:T(8,128)S(1)} %collective-permute-done.1) | copy-start | bytes 1555204
  33.3 16.8 %collective-permute-start.3 = (f32[360,360]{1,0:T(8,128)S(1)}, f32[360,360]{1,0:T(8,128)S(1)}, u32[]{:S(2)}, u32[]{:S(2)}) collective-permute-start(f32[360,360]{1,0:T(8,128)S(1)} %collective-permute-done.1), channel_id=1, source_target_pairs={{0,480},{32,0},{64,32},{96,64},{128,96},{160,128},{192,160},{224,1... | collective-permute-start | bytes 1555208 | tf_op jit(solution)/shard_map/ppermute | solution.py:31
  48.2 15.9 %collective-permute-start.4 = (f32[360,360]{1,0:T(8,128)S(1)}, f32[360,360]{1,0:T(8,128)S(1)}, u32[]{:S(2)}, u32[]{:S(2)}) collective-permute-start(f32[360,360]{1,0:T(8,128)S(1)} %collective-permute-done.2), channel_id=1, source_target_pairs={{0,32},{32,64},{64,96},{96,128},{128,160},{160,192},{192,224},{224... | collective-permute-start | bytes 1555208 | tf_op jit(solution)/shard_map/ppermute | solution.py:28
  50.1 21.0 %copy-start.5 = (f32[360,360]{1,0:T(8,128)}, f32[360,360]{1,0:T(8,128)S(1)}, u32[]{:S(2)}) copy-start(f32[360,360]{1,0:T(8,128)S(1)} %collective-permute-done.3) | copy-start | bytes 1555204
  50.2 15.9 %collective-permute-start.5 = (f32[360,360]{1,0:T(8,128)S(1)}, f32[360,360]{1,0:T(8,128)S(1)}, u32[]{:S(2)}, u32[]{:S(2)}) collective-permute-start(f32[360,360]{1,0:T(8,128)S(1)} %collective-permute-done.3), channel_id=1, source_target_pairs={{0,480},{32,0},{64,32},{96,64},{128,96},{160,128},{192,160},{224,1... | collective-permute-start | bytes 1555208 | tf_op jit(solution)/shard_map/ppermute | solution.py:31
  64.1 15.0 %collective-permute-start.6 = (f32[360,360]{1,0:T(8,128)S(1)}, f32[360,360]{1,0:T(8,128)S(1)}, u32[]{:S(2)}, u32[]{:S(2)}) collective-permute-start(f32[360,360]{1,0:T(8,128)S(1)} %collective-permute-done.4), channel_id=1, source_target_pairs={{0,32},{32,64},{64,96},{96,128},{128,160},{160,192},{192,224},{224... | collective-permute-start | bytes 1555208 | tf_op jit(solution)/shard_map/ppermute | solution.py:28
  66.0 20.1 %copy-start.6 = (f32[360,360]{1,0:T(8,128)}, f32[360,360]{1,0:T(8,128)S(1)}, u32[]{:S(2)}) copy-start(f32[360,360]{1,0:T(8,128)S(1)} %collective-permute-done.5) | copy-start | bytes 1555204
  66.1 15.0 %collective-permute-start.7 = (f32[360,360]{1,0:T(8,128)S(1)}, f32[360,360]{1,0:T(8,128)S(1)}, u32[]{:S(2)}, u32[]{:S(2)}) collective-permute-start(f32[360,360]{1,0:T(8,128)S(1)} %collective-permute-done.5), channel_id=1, source_target_pairs={{0,480},{32,0},{64,32},{96,64},{128,96},{160,128},{192,160},{224,1... | collective-permute-start | bytes 1555208 | tf_op jit(solution)/shard_map/ppermute | solution.py:31
  79.1 14.1 %collective-permute-start.8 = (f32[360,360]{1,0:T(8,128)S(1)}, f32[360,360]{1,0:T(8,128)S(1)}, u32[]{:S(2)}, u32[]{:S(2)}) collective-permute-start(f32[360,360]{1,0:T(8,128)S(1)} %collective-permute-done.6), channel_id=1, source_target_pairs={{0,32},{32,64},{64,96},{96,128},{128,160},{160,192},{192,224},{224... | collective-permute-start | bytes 1555208 | tf_op jit(solution)/shard_map/ppermute | solution.py:28
  81.0 19.2 %copy-start.7 = (f32[360,360]{1,0:T(8,128)}, f32[360,360]{1,0:T(8,128)S(1)}, u32[]{:S(2)}) copy-start(f32[360,360]{1,0:T(8,128)S(1)} %collective-permute-done.7) | copy-start | bytes 1555204
  81.0 14.0 %collective-permute-start.9 = (f32[360,360]{1,0:T(8,128)S(1)}, f32[360,360]{1,0:T(8,128)}, u32[]{:S(2)}, u32[]{:S(2)}) collective-permute-start(f32[360,360]{1,0:T(8,128)S(1)} %collective-permute-done.7), channel_id=1, source_target_pairs={{0,480},{32,0},{64,32},{96,64},{128,96},{160,128},{192,160},{224,1... | collective-permute-start | bytes 1555208 | tf_op jit(solution)/shard_map/ppermute | solution.py:31
  93.1 13.1 %collective-permute-start.10 = (f32[360,360]{1,0:T(8,128)S(1)}, f32[360,360]{1,0:T(8,128)S(1)}, u32[]{:S(2)}, u32[]{:S(2)}) collective-permute-start(f32[360,360]{1,0:T(8,128)S(1)} %collective-permute-done.8), channel_id=1, source_target_pairs={{0,32},{32,64},{64,96},{96,128},{128,160},{160,192},{192,224},{224... | collective-permute-start | bytes 1555208 | tf_op jit(solution)/shard_map/ppermute | solution.py:28
  95.1 13.4 %collective-permute-start.11 = (f32[360,360]{1,0:T(8,128)}, f32[360,360]{1,0:T(8,128)}, u32[]{:S(2)}, u32[]{:S(2)}) collective-permute-start(f32[360,360]{1,0:T(8,128)} %collective-permute-done.9), channel_id=1, source_target_pairs={{0,480},{32,0},{64,32},{96,64},{128,96},{160,128},{192,160},{224,1... | collective-permute-start | bytes 1555208 | tf_op jit(solution)/shard_map/ppermute | solution.py:31
  106.3 13.3 %collective-permute-start.12 = (f32[360,360]{1,0:T(8,128)S(1)}, f32[360,360]{1,0:T(8,128)S(1)}, u32[]{:S(2)}, u32[]{:S(2)}) collective-permute-start(f32[360,360]{1,0:T(8,128)S(1)} %collective-permute-done.10), channel_id=1, source_target_pairs={{0,32},{32,64},{64,96},{96,128},{128,160},{160,192},{192,224},{224... | collective-permute-start | bytes 1555208 | tf_op jit(solution)/shard_map/ppermute | solution.py:28
  108.5 39.5 %collective-permute-start.13 = (f32[360,360]{1,0:T(8,128)}, f32[360,360]{1,0:T(8,128)}, u32[]{:S(2)}, u32[]{:S(2)}) collective-permute-start(f32[360,360]{1,0:T(8,128)} %collective-permute-done.11), channel_id=1, source_target_pairs={{0,480},{32,0},{64,32},{96,64},{128,96},{160,128},{192,160},{224,1... | collective-permute-start | bytes 1555208 | tf_op jit(solution)/shard_map/ppermute | solution.py:31
  119.6 35.1 %collective-permute-start.14 = (f32[360,360]{1,0:T(8,128)S(1)}, f32[360,360]{1,0:T(8,128)}, u32[]{:S(2)}, u32[]{:S(2)}) collective-permute-start(f32[360,360]{1,0:T(8,128)S(1)} %collective-permute-done.12), channel_id=1, source_target_pairs={{0,32},{32,64},{64,96},{96,128},{128,160},{160,192},{192,224},{224... | collective-permute-start | bytes 1555208 | tf_op jit(solution)/shard_map/ppermute | solution.py:28
  134.6 8.0 %copy-start = (f32[5760,192]{0,1:T(8,128)S(1)}, f32[5760,192]{0,1:T(8,128)}, u32[]{:S(2)}) copy-start(f32[5760,192]{0,1:T(8,128)} %reshape.1) | copy-start | bytes 13271044
  134.6 11.8 %copy-start.2 = (f32[360,360]{1,0:T(8,128)S(1)}, f32[360,360]{1,0:T(8,128)}, u32[]{:S(2)}) copy-start(f32[360,360]{1,0:T(8,128)} %copy-done.1) | copy-start | bytes 1555204
  134.6 12.6 %copy-start.4 = (f32[360,360]{1,0:T(8,128)S(1)}, f32[360,360]{1,0:T(8,128)}, u32[]{:S(2)}) copy-start(f32[360,360]{1,0:T(8,128)} %copy-done.3) | copy-start | bytes 1555204
  156.6 8.5 %collective-permute-start.15 = (f32[96,360]{1,0:T(8,128)S(1)}, f32[96,360]{1,0:T(8,128)S(1)}, u32[]{:S(2)}, u32[]{:S(2)}) collective-permute-start(f32[96,360]{1,0:T(8,128)S(1)} %constant_dynamic-slice_fusion), channel_id=1, source_target_pairs={{0,1},{1,0},{2,3},{3,2},{4,5},{5,4},{6,7},{7,6},{8,9},{9,8},{10,11... | collective-permute-start | bytes 414728 | tf_op jit(solution)/shard_map/ppermute | solution.py:36
Sparse Core Ops, SparseCore 0:
  9.5 50.0 all-gather.2

commit v2 on v1

--- a/solution.py
+++ b/solution.py
@@ -2,6 +2,10 @@
 import jax.numpy as jnp
 from jax import lax
 from jax.sharding import PartitionSpec as P
+
+
+FIRST_DOT_STEP = 4
+DOTS_PER_STEP = 5
 
 
 def local(amplitudes, integrals):
@@ -12,24 +16,36 @@
     rows = amplitudes.shape[0]
     half = rows // 2
 
-    strip = lax.all_gather(amplitudes, "col", axis=1, tiled=True)
+    strip = lax.all_gather(amplitudes, "col", axis=0, tiled=False)
 
     def product(block, owner):
-        cols = lax.dynamic_slice_in_dim(strip, owner * kb, kb, axis=1)
+        cols = lax.dynamic_index_in_dim(strip, owner, axis=0, keepdims=False)
         return jnp.dot(cols, block, precision=lax.Precision.HIGHEST,
                        preferred_element_type=jnp.float32)
 
     fwd = [(i, (i + 1) % n) for i in range(n)]
     bwd = [(i, (i - 1) % n) for i in range(n)]
-    total = product(integrals, me)
+    total = None
+    pending = [(integrals, me)]
     ahead = integrals
     behind = integrals
     for step in range(1, n // 2 + 1):
+        arrived = []
         ahead = lax.ppermute(ahead, "row", fwd)
-        total = total + product(ahead, (me - step) % n)
+        arrived.append((ahead, (me - step) % n))
         if step < n - n // 2:
             behind = lax.ppermute(behind, "row", bwd)
-            total = total + product(behind, (me + step) % n)
+            arrived.append((behind, (me + step) % n))
+        if step >= FIRST_DOT_STEP:
+            for block, owner in pending[:DOTS_PER_STEP]:
+                part = product(block, owner)
+                total = part if total is None else total + part
+            pending = pending[DOTS_PER_STEP:]
+            total, ahead, behind = lax.optimization_barrier((total, ahead, behind))
+        pending = pending + arrived
+    for block, owner in pending:
+        part = product(block, owner)
+        total = part if total is None else total + part
 
     mine = lax.dynamic_slice_in_dim(total, d * half, half, axis=0)
     other = lax.dynamic_slice_in_dim(total, (1 - d) * half, half, axis=0)

time: 174 us -> 159 us (0.914)
  local copies, waits for them, and re-layouts: 13.2 us -> 0.02 us
  waiting for transfers between devices: 62.1 us -> 51.4 us
  matrix products: 21.8 us -> 28.3 us
  starting transfers between devices: 60.8 us -> 63.1 us
    ppermute x8, waiting for transfers between devices: 56.2 us -> 14.9 us  [local(): ahead = lax.ppermute(ahead, 'row', fwd)]
    ppermute x7, waiting for transfers between devices: 0.02 us -> 30.5 us  [local(): behind = lax.ppermute(behind, 'row', bwd)]
    all_gather x1 -> x0, local copies, waits for them, and re-layouts: 7.27 us -> none  [local(): strip = lax.all_gather(amplitudes, 'col', axis=1, tiled=True)]
    dot_general x16, matrix products: 21.8 us -> 28.3 us  [product(): jnp.dot(cols, block, precision=lax.Precision.HIGHEST, preferred_element_t...]
    unnamed x17 -> x2, local copies, waits for them, and re-layouts: 5.87 us -> 0.01 us
    ppermute x7, starting transfers between devices: 40.3 us -> 44.5 us  [local(): behind = lax.ppermute(behind, 'row', bwd)]
    ppermute x8, starting transfers between devices: 17.2 us -> 15.3 us  [local(): ahead = lax.ppermute(ahead, 'row', fwd)]
  transfers between devices with their start and end apart: 17 -> 17, of which waited for: 8 -> 11; matrix products, arithmetic and copies ran while one was open for 19% -> 17% of each run, Pallas kernels for 0% -> 0%
where the time goes in v2:
time: 159 us; the launch traced here: 158 us
  starting transfers between devices  63.1 us (40%)
  waiting for transfers between devices  51.4 us (32%)
  matrix products  28.3 us (18%)
  between operations  14 us (9%)
    ppermute x7, starting transfers between devices, local(): behind = lax.ppermute(behind, 'row', bwd)  44.5 us
    ppermute x7, waiting for transfers between devices, local(): behind = lax.ppermute(behind, 'row', bwd)  30.5 us
    dot_general x16, matrix products, product(): jnp.dot(cols, block, precision=lax.Precision.HIGHEST, preferred_element_t...  28.3 us
    ppermute x8, starting transfers between devices, local(): ahead = lax.ppermute(ahead, 'row', fwd)  15.3 us
    ppermute x8, waiting for transfers between devices, local(): ahead = lax.ppermute(ahead, 'row', fwd)  14.9 us
    ppermute x1, waiting for transfers between devices, local(): other = lax.ppermute(other, 'depth', [(0, 1), (1, 0)])  5.22 us
    ppermute x1, starting transfers between devices, local(): other = lax.ppermute(other, 'depth', [(0, 1), (1, 0)])  3.31 us
  transfers between devices with their start and end apart: 17, of which 11 were waited for; matrix products, arithmetic and copies ran while one was open for 17% of the time, Pallas kernels for 0%

profile of v2, /device:TPU:6, one launch (start us, length us, event | category | flops | bytes accessed | tf_op | source)
XLA Modules:
  0.0 157.5 jit_solution(5826651398681277199)
XLA Ops:
  7.3 11.4 %collective-permute-start.1 = (f32[360,360]{1,0:T(8,128)}, f32[360,360]{1,0:T(8,128)S(1)}, u32[]{:S(2)}, u32[]{:S(2)}) collective-permute-start(f32[360,360]{1,0:T(8,128)} %param.3), channel_id=1, source_target_pairs={{0,480},{32,0},{64,32},{96,64},{128,96},{160,128},{192,160},{224,1... | collective-permute-start | bytes 1555208 | tf_op jit(solution)/shard_map/ppermute | solution.py:37
  18.7 1.9 %collective-permute-start = (f32[360,360]{1,0:T(8,128)}, f32[360,360]{1,0:T(8,128)S(1)}, u32[]{:S(2)}, u32[]{:S(2)}) collective-permute-start(f32[360,360]{1,0:T(8,128)} %param.3), channel_id=1, source_target_pairs={{0,32},{32,64},{64,96},{96,128},{128,160},{160,192},{192,224},{224... | collective-permute-start | bytes 1555208 | tf_op jit(solution)/shard_map/ppermute | solution.py:34
  20.6 10.2 %collective-permute-done.1 = f32[360,360]{1,0:T(8,128)S(1)} collective-permute-done((f32[360,360]{1,0:T(8,128)}, f32[360,360]{1,0:T(8,128)S(1)}, u32[]{:S(2)}, u32[]{:S(2)}) %collective-permute-start.1) | collective-permute-done | bytes 518432 | tf_op jit(solution)/shard_map/ppermute | solution.py:37
  30.8 5.5 %collective-permute-start.3 = (f32[360,360]{1,0:T(8,128)S(1)}, f32[360,360]{1,0:T(8,128)S(1)}, u32[]{:S(2)}, u32[]{:S(2)}) collective-permute-start(f32[360,360]{1,0:T(8,128)S(1)} %collective-permute-done.1), channel_id=1, source_target_pairs={{0,480},{32,0},{64,32},{96,64},{128,96},{160,128},{192,160},{224,1... | collective-permute-start | bytes 1555208 | tf_op jit(solution)/shard_map/ppermute | solution.py:37
  36.3 1.9 %collective-permute-start.2 = (f32[360,360]{1,0:T(8,128)S(1)}, f32[360,360]{1,0:T(8,128)S(1)}, u32[]{:S(2)}, u32[]{:S(2)}) collective-permute-start(f32[360,360]{1,0:T(8,128)S(1)} %collective-permute-done), channel_id=1, source_target_pairs={{0,32},{32,64},{64,96},{96,128},{128,160},{160,192},{192,224},{224... | collective-permute-start | bytes 1555208 | tf_op jit(solution)/shard_map/ppermute | solution.py:34
  38.2 9.0 %collective-permute-done.3 = f32[360,360]{1,0:T(8,128)S(1)} collective-permute-done((f32[360,360]{1,0:T(8,128)S(1)}, f32[360,360]{1,0:T(8,128)S(1)}, u32[]{:S(2)}, u32[]{:S(2)}) %collective-permute-start.3) | collective-permute-done | bytes 518432 | tf_op jit(solution)/shard_map/ppermute | solution.py:37
  47.2 5.6 %collective-permute-start.6 = (f32[360,360]{1,0:T(8,128)S(1)}, f32[360,360]{1,0:T(8,128)S(1)}, u32[]{:S(2)}, u32[]{:S(2)}) collective-permute-start(f32[360,360]{1,0:T(8,128)S(1)} %collective-permute-done.3), channel_id=1, source_target_pairs={{0,480},{32,0},{64,32},{96,64},{128,96},{160,128},{192,160},{224,1... | collective-permute-start | bytes 1555208 | tf_op jit(solution)/shard_map/ppermute | solution.py:37
  52.8 1.9 %collective-permute-start.4 = (f32[360,360]{1,0:T(8,128)S(1)}, f32[360,360]{1,0:T(8,128)S(1)}, u32[]{:S(2)}, u32[]{:S(2)}) collective-permute-start(f32[360,360]{1,0:T(8,128)S(1)} %collective-permute-done.2), channel_id=1, source_target_pairs={{0,32},{32,64},{64,96},{96,128},{128,160},{160,192},{192,224},{224... | collective-permute-start | bytes 1555208 | tf_op jit(solution)/shard_map/ppermute | solution.py:34
  54.8 7.9 %collective-permute-done.6 = f32[360,360]{1,0:T(8,128)S(1)} collective-permute-done((f32[360,360]{1,0:T(8,128)S(1)}, f32[360,360]{1,0:T(8,128)S(1)}, u32[]{:S(2)}, u32[]{:S(2)}) %collective-permute-start.6) | collective-permute-done | bytes 518432 | tf_op jit(solution)/shard_map/ppermute | solution.py:37
  62.7 5.6 %collective-permute-start.7 = (f32[360,360]{1,0:T(8,128)S(1)}, f32[360,360]{1,0:T(8,128)}, u32[]{:S(2)}, u32[]{:S(2)}) collective-permute-start(f32[360,360]{1,0:T(8,128)S(1)} %collective-permute-done.6), channel_id=1, source_target_pairs={{0,480},{32,0},{64,32},{96,64},{128,96},{160,128},{192,160},{224,1... | collective-permute-start | bytes 1555208 | tf_op jit(solution)/shard_map/ppermute | solution.py:37
  68.3 1.9 %collective-permute-start.5 = (f32[360,360]{1,0:T(8,128)S(1)}, f32[360,360]{1,0:T(8,128)S(1)}, u32[]{:S(2)}, u32[]{:S(2)}) collective-permute-start(f32[360,360]{1,0:T(8,128)S(1)} %collective-permute-done.4), channel_id=1, source_target_pairs={{0,32},{32,64},{64,96},{96,128},{128,160},{160,192},{192,224},{224... | collective-permute-start | bytes 1555208 | tf_op jit(solution)/shard_map/ppermute | solution.py:34
  70.3 1.9 %fusion.28 = f32[192,360]{1,0:T(8,128)S(1)} fusion(f32[360,360]{1,0:T(8,128)} %param.3, f32[16,192,360]{2,1,0:T(8,128)} %bitcast.71, s32[]{:T(128)S(6)} %select_n.118), kind=kOutput, calls=%fused_computation.32 | convolution fusion | flops 298598400 | bytes 1124356 | tf_op jit(solution)/shard_map/dot_general | solution.py:23
  73.9 1.9 %fusion.23 = f32[192,360]{1,0:T(8,128)S(1)} fusion(f32[360,360]{1,0:T(8,128)} %copy-done, f32[16,192,360]{2,1,0:T(8,128)} %bitcast.73, s32[]{:T(128)S(6)} %select_n.126), kind=kOutput, calls=%fused_computation.27 | convolution fusion | flops 298598400 | bytes 1124356 | tf_op jit(solution)/shard_map/dot_general | solution.py:23
  79.3 3.4 %collective-permute-done.5 = f32[360,360]{1,0:T(8,128)S(1)} collective-permute-done((f32[360,360]{1,0:T(8,128)S(1)}, f32[360,360]{1,0:T(8,128)S(1)}, u32[]{:S(2)}, u32[]{:S(2)}) %collective-permute-start.5) | collective-permute-done | bytes 518432 | tf_op jit(solution)/shard_map/ppermute | solution.py:34
  82.7 1.9 %collective-permute-start.8 = (f32[360,360]{1,0:T(8,128)S(1)}, f32[360,360]{1,0:T(8,128)}, u32[]{:S(2)}, u32[]{:S(2)}) collective-permute-start(f32[360,360]{1,0:T(8,128)S(1)} %collective-permute-done.5), channel_id=1, source_target_pairs={{0,32},{32,64},{64,96},{96,128},{128,160},{160,192},{192,224},{224... | collective-permute-start | bytes 1555208 | tf_op jit(solution)/shard_map/ppermute | solution.py:34
  84.7 5.1 %collective-permute-start.9 = (f32[360,360]{1,0:T(8,128)}, f32[360,360]{1,0:T(8,128)S(1)}, u32[]{:S(2)}, u32[]{:S(2)}) collective-permute-start(f32[360,360]{1,0:T(8,128)} %collective-permute-done.7), channel_id=1, source_target_pairs={{0,480},{32,0},{64,32},{96,64},{128,96},{160,128},{192,160},{224,1... | collective-permute-start | bytes 1555208 | tf_op jit(solution)/shard_map/ppermute | solution.py:37
  91.5 1.9 %fusion.16 = f32[192,360]{1,0:T(8,128)S(1)} fusion(f32[360,360]{1,0:T(8,128)} %collective-permute-done.7, f32[16,192,360]{2,1,0:T(8,128)} %bitcast.77, s32[]{:T(128)S(6)} %select_n.134), kind=kOutput, calls=%fused_computation.20 | convolution fusion | flops 298598400 | bytes 1124356 | tf_op jit(solution)/shard_map/dot_general | solution.py:23
  95.2 1.7 %fusion.1 = f32[192,360]{1,0:T(8,128)S(1)} fusion(f32[192,360]{1,0:T(8,128)S(1)} %fusion.16, f32[360,360]{1,0:T(8,128)S(1)} %collective-permute-done.5, f32[16,192,360]{2,1,0:T(8,128)} %bitcast.79, s32[]{:T(128)S(6)} %select_n.132, f32[192,360]{1,0:T(8,128)S(1)} %fusion.19, f32[192,360]{1,0:T(8,128)S(1)} %fusion, f32[192,360]{1,0:T(8,128)S(1)} %fusion.21), kind=kOutput, calls=%fused_computation.5 | convolution fusion | flops 298874880 | bytes 2195716 | tf_op jit(solution)/shard_map/dot_general | solution.py:23
  97.7 1.9 %collective-permute-start.10 = (f32[360,360]{1,0:T(8,128)}, f32[360,360]{1,0:T(8,128)S(1)}, u32[]{:S(2)}, u32[]{:S(2)}) collective-permute-start(f32[360,360]{1,0:T(8,128)} %collective-permute-done.8), channel_id=1, source_target_pairs={{0,32},{32,64},{64,96},{96,128},{128,160},{160,192},{192,224},{224... | collective-permute-start | bytes 1555208 | tf_op jit(solution)/shard_map/ppermute | solution.py:34
  99.6 5.5 %collective-permute-start.11 = (f32[360,360]{1,0:T(8,128)S(1)}, f32[360,360]{1,0:T(8,128)S(1)}, u32[]{:S(2)}, u32[]{:S(2)}) collective-permute-start(f32[360,360]{1,0:T(8,128)S(1)} %collective-permute-done.9), channel_id=1, source_target_pairs={{0,480},{32,0},{64,32},{96,64},{128,96},{160,128},{192,160},{224,1... | collective-permute-start | bytes 1555208 | tf_op jit(solution)/shard_map/ppermute | solution.py:37
  105.1 1.9 %fusion.14 = f32[192,360]{1,0:T(8,128)S(1)} fusion(f32[360,360]{1,0:T(8,128)} %collective-permute-done.8, f32[16,192,360]{2,1,0:T(8,128)} %bitcast.80, s32[]{:T(128)S(6)} %select_n.136), kind=kOutput, calls=%fused_computation.18 | convolution fusion | flops 298598400 | bytes 1124356 | tf_op jit(solution)/shard_map/dot_general | solution.py:23
  107.0 1.7 %add_add_fusion.2 = f32[192,360]{1,0:T(8,128)S(1)} fusion(f32[192,360]{1,0:T(8,128)S(1)} %fusion.1, f32[192,360]{1,0:T(8,128)S(1)} %fusion.14, f32[360,360]{1,0:T(8,128)S(1)} %collective-permute-done.9, f32[16,192,360]{2,1,0:T(8,128)} %bitcast.81, s32[]{:T(128)S(6)} %select_n.138), kind=kOutput, calls=%fused_computation.42 | convolution fusion | flops 298736640 | bytes 1642756 | tf_op jit(solution)/shard_map/dot_general | solution.py:23
  108.8 2.1 %collective-permute-done.10 = f32[360,360]{1,0:T(8,128)S(1)} collective-permute-done((f32[360,360]{1,0:T(8,128)}, f32[360,360]{1,0:T(8,128)S(1)}, u32[]{:S(2)}, u32[]{:S(2)}) %collective-permute-start.10) | collective-permute-done | bytes 518432 | tf_op jit(solution)/shard_map/ppermute | solution.py:34
  112.1 1.9 %collective-permute-start.12 = (f32[360,360]{1,0:T(8,128)S(1)}, f32[360,360]{1,0:T(8,128)S(1)}, u32[]{:S(2)}, u32[]{:S(2)}) collective-permute-start(f32[360,360]{1,0:T(8,128)S(1)} %collective-permute-done.10), channel_id=1, source_target_pairs={{0,32},{32,64},{64,96},{96,128},{128,160},{160,192},{192,224},{224... | collective-permute-start | bytes 1555208 | tf_op jit(solution)/shard_map/ppermute | solution.py:34
  114.0 5.8 %collective-permute-start.13 = (f32[360,360]{1,0:T(8,128)S(1)}, f32[360,360]{1,0:T(8,128)S(1)}, u32[]{:S(2)}, u32[]{:S(2)}) collective-permute-start(f32[360,360]{1,0:T(8,128)S(1)} %collective-permute-done.11), channel_id=1, source_target_pairs={{0,480},{32,0},{64,32},{96,64},{128,96},{160,128},{192,160},{224,1... | collective-permute-start | bytes 1555208 | tf_op jit(solution)/shard_map/ppermute | solution.py:37
  121.6 1.7 %add_add_fusion.1 = f32[192,360]{1,0:T(8,128)S(1)} fusion(f32[192,360]{1,0:T(8,128)S(1)} %add_add_fusion.2, f32[192,360]{1,0:T(8,128)S(1)} %fusion.10, f32[360,360]{1,0:T(8,128)S(1)} %collective-permute-done.11, f32[16,192,360]{2,1,0:T(8,128)} %bitcast.83, s32[]{:T(128)S(6)} %select_n.142), kind=kOutput, calls=%fused_computation.39 | convolution fusion | flops 298736640 | bytes 1642756 | tf_op jit(solution)/shard_map/dot_general | solution.py:23
  123.3 1.8 %collective-permute-done.12 = f32[360,360]{1,0:T(8,128)S(1)} collective-permute-done((f32[360,360]{1,0:T(8,128)S(1)}, f32[360,360]{1,0:T(8,128)S(1)}, u32[]{:S(2)}, u32[]{:S(2)}) %collective-permute-start.12) | collective-permute-done | bytes 518432 | tf_op jit(solution)/shard_map/ppermute | solution.py:34
  126.6 1.9 %collective-permute-start.14 = (f32[360,360]{1,0:T(8,128)S(1)}, f32[360,360]{1,0:T(8,128)S(1)}, u32[]{:S(2)}, u32[]{:S(2)}) collective-permute-start(f32[360,360]{1,0:T(8,128)S(1)} %collective-permute-done.12), channel_id=1, source_target_pairs={{0,32},{32,64},{64,96},{96,128},{128,160},{160,192},{192,224},{224... | collective-permute-start | bytes 1555208 | tf_op jit(solution)/shard_map/ppermute | solution.py:34
  130.3 1.7 %add_add_fusion = f32[192,360]{1,0:T(8,128)S(1)} fusion(f32[192,360]{1,0:T(8,128)S(1)} %add_add_fusion.1, f32[192,360]{1,0:T(8,128)S(1)} %fusion.6, f32[360,360]{1,0:T(8,128)S(1)} %collective-permute-done.13, f32[16,192,360]{2,1,0:T(8,128)} %bitcast.85, s32[]{:T(128)S(6)} %select_n.146), kind=kOutput, calls=%fused_computation.36 | convolution fusion | flops 298736640 | bytes 1642756 | tf_op jit(solution)/shard_map/dot_general | solution.py:23
  132.0 7.6 %collective-permute-done.14 = f32[360,360]{1,0:T(8,128)S(1)} collective-permute-done((f32[360,360]{1,0:T(8,128)S(1)}, f32[360,360]{1,0:T(8,128)S(1)}, u32[]{:S(2)}, u32[]{:S(2)}) %collective-permute-start.14) | collective-permute-done | bytes 518432 | tf_op jit(solution)/shard_map/ppermute | solution.py:34
  141.4 3.3 %collective-permute-start.15 = (f32[96,360]{1,0:T(8,128)S(1)}, f32[96,360]{1,0:T(8,128)S(1)}, u32[]{:S(2)}, u32[]{:S(2)}) collective-permute-start(f32[96,360]{1,0:T(8,128)S(1)} %constant_dynamic-slice_fusion), channel_id=1, source_target_pairs={{0,1},{1,0},{2,3},{3,2},{4,5},{5,4},{6,7},{7,6},{8,9},{9,8},{10,11... | collective-permute-start | bytes 414728 | tf_op jit(solution)/shard_map/ppermute | solution.py:52
  144.8 5.2 %collective-permute-done.15 = f32[96,360]{1,0:T(8,128)S(1)} collective-permute-done((f32[96,360]{1,0:T(8,128)S(1)}, f32[96,360]{1,0:T(8,128)S(1)}, u32[]{:S(2)}, u32[]{:S(2)}) %collective-permute-start.15) | collective-permute-done | bytes 138272 | tf_op jit(solution)/shard_map/ppermute | solution.py:52
  (24 shorter events, 18.7 us)
Async XLA Ops:
  6.5 63.8 %all-gather.3.cloned.1.call-start = ((), (), s32[]{:S(2)}) async-start(), calls=%async_computation | async-start | bytes 5013504 | tf_op jit(solution)/shard_map/all_gather | solution.py:19
  7.3 23.5 %collective-permute-start.1 = (f32[360,360]{1,0:T(8,128)}, f32[360,360]{1,0:T(8,128)S(1)}, u32[]{:S(2)}, u32[]{:S(2)}) collective-permute-start(f32[360,360]{1,0:T(8,128)} %param.3), channel_id=1, source_target_pairs={{0,480},{32,0},{64,32},{96,64},{128,96},{160,128},{192,160},{224,1... | collective-permute-start | bytes 1555208 | tf_op jit(solution)/shard_map/ppermute | solution.py:37
  18.7 17.6 %collective-permute-start = (f32[360,360]{1,0:T(8,128)}, f32[360,360]{1,0:T(8,128)S(1)}, u32[]{:S(2)}, u32[]{:S(2)}) collective-permute-start(f32[360,360]{1,0:T(8,128)} %param.3), channel_id=1, source_target_pairs={{0,32},{32,64},{64,96},{96,128},{128,160},{160,192},{192,224},{224... | collective-permute-start | bytes 1555208 | tf_op jit(solution)/shard_map/ppermute | solution.py:34
  30.8 16.4 %collective-permute-start.3 = (f32[360,360]{1,0:T(8,128)S(1)}, f32[360,360]{1,0:T(8,128)S(1)}, u32[]{:S(2)}, u32[]{:S(2)}) collective-permute-start(f32[360,360]{1,0:T(8,128)S(1)} %collective-permute-done.1), channel_id=1, source_target_pairs={{0,480},{32,0},{64,32},{96,64},{128,96},{160,128},{192,160},{224,1... | collective-permute-start | bytes 1555208 | tf_op jit(solution)/shard_map/ppermute | solution.py:37
  36.3 16.5 %collective-permute-start.2 = (f32[360,360]{1,0:T(8,128)S(1)}, f32[360,360]{1,0:T(8,128)S(1)}, u32[]{:S(2)}, u32[]{:S(2)}) collective-permute-start(f32[360,360]{1,0:T(8,128)S(1)} %collective-permute-done), channel_id=1, source_target_pairs={{0,32},{32,64},{64,96},{96,128},{128,160},{160,192},{192,224},{224... | collective-permute-start | bytes 1555208 | tf_op jit(solution)/shard_map/ppermute | solution.py:34
  47.2 21.2 %copy-start = (f32[360,360]{1,0:T(8,128)}, f32[360,360]{1,0:T(8,128)S(1)}, u32[]{:S(2)}) copy-start(f32[360,360]{1,0:T(8,128)S(1)} %collective-permute-done.3) | copy-start | bytes 1555204
  47.2 15.6 %collective-permute-start.6 = (f32[360,360]{1,0:T(8,128)S(1)}, f32[360,360]{1,0:T(8,128)S(1)}, u32[]{:S(2)}, u32[]{:S(2)}) collective-permute-start(f32[360,360]{1,0:T(8,128)S(1)} %collective-permute-done.3), channel_id=1, source_target_pairs={{0,480},{32,0},{64,32},{96,64},{128,96},{160,128},{192,160},{224,1... | collective-permute-start | bytes 1555208 | tf_op jit(solution)/shard_map/ppermute | solution.py:37
  52.8 15.6 %collective-permute-start.4 = (f32[360,360]{1,0:T(8,128)S(1)}, f32[360,360]{1,0:T(8,128)S(1)}, u32[]{:S(2)}, u32[]{:S(2)}) collective-permute-start(f32[360,360]{1,0:T(8,128)S(1)} %collective-permute-done.2), channel_id=1, source_target_pairs={{0,32},{32,64},{64,96},{96,128},{128,160},{160,192},{192,224},{224... | collective-permute-start | bytes 1555208 | tf_op jit(solution)/shard_map/ppermute | solution.py:34
  62.7 16.6 %collective-permute-start.7 = (f32[360,360]{1,0:T(8,128)S(1)}, f32[360,360]{1,0:T(8,128)}, u32[]{:S(2)}, u32[]{:S(2)}) collective-permute-start(f32[360,360]{1,0:T(8,128)S(1)} %collective-permute-done.6), channel_id=1, source_target_pairs={{0,480},{32,0},{64,32},{96,64},{128,96},{160,128},{192,160},{224,1... | collective-permute-start | bytes 1555208 | tf_op jit(solution)/shard_map/ppermute | solution.py:37
  68.3 14.4 %collective-permute-start.5 = (f32[360,360]{1,0:T(8,128)S(1)}, f32[360,360]{1,0:T(8,128)S(1)}, u32[]{:S(2)}, u32[]{:S(2)}) collective-permute-start(f32[360,360]{1,0:T(8,128)S(1)} %collective-permute-done.4), channel_id=1, source_target_pairs={{0,32},{32,64},{64,96},{96,128},{128,160},{160,192},{192,224},{224... | collective-permute-start | bytes 1555208 | tf_op jit(solution)/shard_map/ppermute | solution.py:34
  82.7 14.2 %collective-permute-start.8 = (f32[360,360]{1,0:T(8,128)S(1)}, f32[360,360]{1,0:T(8,128)}, u32[]{:S(2)}, u32[]{:S(2)}) collective-permute-start(f32[360,360]{1,0:T(8,128)S(1)} %collective-permute-done.5), channel_id=1, source_target_pairs={{0,32},{32,64},{64,96},{96,128},{128,160},{160,192},{192,224},{224... | collective-permute-start | bytes 1555208 | tf_op jit(solution)/shard_map/ppermute | solution.py:34
  84.7 13.0 %collective-permute-start.9 = (f32[360,360]{1,0:T(8,128)}, f32[360,360]{1,0:T(8,128)S(1)}, u32[]{:S(2)}, u32[]{:S(2)}) collective-permute-start(f32[360,360]{1,0:T(8,128)} %collective-permute-done.7), channel_id=1, source_target_pairs={{0,480},{32,0},{64,32},{96,64},{128,96},{160,128},{192,160},{224,1... | collective-permute-start | bytes 1555208 | tf_op jit(solution)/shard_map/ppermute | solution.py:37
  97.7 13.2 %collective-permute-start.10 = (f32[360,360]{1,0:T(8,128)}, f32[360,360]{1,0:T(8,128)S(1)}, u32[]{:S(2)}, u32[]{:S(2)}) collective-permute-start(f32[360,360]{1,0:T(8,128)} %collective-permute-done.8), channel_id=1, source_target_pairs={{0,32},{32,64},{64,96},{96,128},{128,160},{160,192},{192,224},{224... | collective-permute-start | bytes 1555208 | tf_op jit(solution)/shard_map/ppermute | solution.py:34
  99.6 12.5 %collective-permute-start.11 = (f32[360,360]{1,0:T(8,128)S(1)}, f32[360,360]{1,0:T(8,128)S(1)}, u32[]{:S(2)}, u32[]{:S(2)}) collective-permute-start(f32[360,360]{1,0:T(8,128)S(1)} %collective-permute-done.9), channel_id=1, source_target_pairs={{0,480},{32,0},{64,32},{96,64},{128,96},{160,128},{192,160},{224,1... | collective-permute-start | bytes 1555208 | tf_op jit(solution)/shard_map/ppermute | solution.py:37
  112.1 13.0 %collective-permute-start.12 = (f32[360,360]{1,0:T(8,128)S(1)}, f32[360,360]{1,0:T(8,128)S(1)}, u32[]{:S(2)}, u32[]{:S(2)}) collective-permute-start(f32[360,360]{1,0:T(8,128)S(1)} %collective-permute-done.10), channel_id=1, source_target_pairs={{0,32},{32,64},{64,96},{96,128},{128,160},{160,192},{192,224},{224... | collective-permute-start | bytes 1555208 | tf_op jit(solution)/shard_map/ppermute | solution.py:34
  114.0 12.6 %collective-permute-start.13 = (f32[360,360]{1,0:T(8,128)S(1)}, f32[360,360]{1,0:T(8,128)S(1)}, u32[]{:S(2)}, u32[]{:S(2)}) collective-permute-start(f32[360,360]{1,0:T(8,128)S(1)} %collective-permute-done.11), channel_id=1, source_target_pairs={{0,480},{32,0},{64,32},{96,64},{128,96},{160,128},{192,160},{224,1... | collective-permute-start | bytes 1555208 | tf_op jit(solution)/shard_map/ppermute | solution.py:37
  126.6 13.0 %collective-permute-start.14 = (f32[360,360]{1,0:T(8,128)S(1)}, f32[360,360]{1,0:T(8,128)S(1)}, u32[]{:S(2)}, u32[]{:S(2)}) collective-permute-start(f32[360,360]{1,0:T(8,128)S(1)} %collective-permute-done.12), channel_id=1, source_target_pairs={{0,32},{32,64},{64,96},{96,128},{128,160},{160,192},{192,224},{224... | collective-permute-start | bytes 1555208 | tf_op jit(solution)/shard_map/ppermute | solution.py:34
  141.4 8.5 %collective-permute-start.15 = (f32[96,360]{1,0:T(8,128)S(1)}, f32[96,360]{1,0:T(8,128)S(1)}, u32[]{:S(2)}, u32[]{:S(2)}) collective-permute-start(f32[96,360]{1,0:T(8,128)S(1)} %constant_dynamic-slice_fusion), channel_id=1, source_target_pairs={{0,1},{1,0},{2,3},{3,2},{4,5},{5,4},{6,7},{7,6},{8,9},{9,8},{10,11... | collective-permute-start | bytes 414728 | tf_op jit(solution)/shard_map/ppermute | solution.py:52
Sparse Core Ops, SparseCore 0:
  9.5 50.0 all-gather.2

commit v3 on v0

v3 whole, which is shorter than its diff:
```python
import jax
import jax.numpy as jnp
from jax import lax
from jax.sharding import PartitionSpec as P


def local(amplitudes, integrals):
    n = lax.axis_size("row")
    swap = [(i * n + c, c * n + i) for i in range(n) for c in range(n)]
    moved = lax.ppermute(amplitudes, ("row", "col"), swap)
    strip = lax.all_gather(moved, "col", axis=0, tiled=True)
    partial = jnp.dot(strip, integrals, precision=lax.Precision.HIGHEST,
                      preferred_element_type=jnp.float32)
    total = lax.psum_scatter(partial, ("row", "depth"), scatter_dimension=0, tiled=True)
    return 0.5 * total


def solution(mesh):
    placed = (P("row", ("col", "depth")), P(("row", "depth"), "col"))
    return jax.shard_map(
        local, mesh=mesh, in_specs=placed, out_specs=P(("row", "depth"), "col"), check_vma=False
    )
```

time: 214 us -> 830 us (3.88)
  waiting for transfers between devices: 173 us -> 795 us
  local copies, waits for them, and re-layouts: 13.1 us -> 0.73 us
    reduce_scatter x1, waiting for transfers between devices: 20.3 us -> 698 us  [local(): lax.psum_scatter(partial, ('row', 'depth'), scatter_dimension=0, tiled=True)]
    all_gather x2 -> x1, waiting for transfers between devices: 152 us -> 49 us  [local(): strip = lax.all_gather(moved, 'col', axis=0, tiled=True)]
    ppermute x0 -> x1, waiting for transfers between devices: none -> 47.4 us  [local(): moved = lax.ppermute(amplitudes, ('row', 'col'), swap)]
  transfers between devices with their start and end apart: 3 -> 3, of which waited for: 3 -> 3; matrix products, arithmetic and copies ran while one was open for 6% -> 0% of each run, Pallas kernels for 0% -> 0%
where the time goes in v3:
time: 830 us; the launch traced here: 828 us
  waiting for transfers between devices  795 us (96%)
  between operations  13.4 us (2%)
  matrix products  12.2 us (1%)
    reduce_scatter x1, waiting for transfers between devices, local(): lax.psum_scatter(partial, ('row', 'depth'), scatter_dimension=0, tiled=True)  698 us
    all_gather x1, waiting for transfers between devices, local(): strip = lax.all_gather(moved, 'col', axis=0, tiled=True)  49 us
    ppermute x1, waiting for transfers between devices, local(): moved = lax.ppermute(amplitudes, ('row', 'col'), swap)  47.4 us
  transfers between devices with their start and end apart: 3, of which 3 were waited for; matrix products, arithmetic and copies ran while one was open for 0% of the time, Pallas kernels for 0%

profile of v3, /device:TPU:6, one launch (start us, length us, event | category | flops | bytes accessed | tf_op | source)
XLA Modules:
  0.0 828.5 jit_solution(16946107439396596906)
XLA Ops:
  6.5 0.0 copy-start
  6.5 0.0 all-gather.2.cloned.1.call-start
  6.5 5.6 collective-permute-start
  12.1 47.4 %collective-permute-done = f32[192,360]{1,0:T(8,128)S(1)} collective-permute-done((f32[192,360]{1,0:T(8,128)}, f32[192,360]{1,0:T(8,128)S(1)}, u32[]{:S(2)}, u32[]{:S(2)}) %collective-permute-start) | collective-permute-done | bytes 276512 | tf_op jit(solution)/shard_map/ppermute | solution.py:10
  59.5 0.0 copy-start.1
  59.5 0.7 copy-done.1
  60.3 0.0 all-gather.2.cloned.1.call-update
  60.3 0.0 reduce-scatter.2.cloned.1.call-start
  60.3 49.0 %all-gather.2.cloned.1.call-done = f32[3072,360]{1,0:T(8,128)} async-done(((f32[192,360]{1,0:T(8,128)}), f32[3072,360]{1,0:T(8,128)}) %all-gather.2.cloned.1.call-update) | async-done | bytes 4423696 | tf_op jit(solution)/shard_map/all_gather | solution.py:11
  109.4 0.0 copy-done
  109.4 12.2 %fusion = f32[3072,360]{1,0:T(8,128)} fusion(f32[3072,360]{1,0:T(8,128)} %all-gather.2.cloned.1.call-done, f32[360,360]{1,0:T(8,128)S(1)} %copy-done), kind=kOutput, calls=%fused_computation.1 | convolution fusion | flops 4777574400 | bytes 9365760 | tf_op jit(solution)/shard_map/dot_general | solution.py:12
  121.5 0.0 reduce-scatter.2.cloned.1.call-update
  121.6 698.5 %reduce-scatter.2.cloned.1.call-done = f32[96,360]{1,0:T(8,128)} async-done(((f32[3072,360]{1,0:T(8,128)}), f32[96,360]{1,0:T(8,128)}) %reduce-scatter.2.cloned.1.call-update) | async-done | bytes 138256 | tf_op jit(solution)/shard_map/reduce_scatter | solution.py:14
  820.1 1.6 broadcast_multiply_fusion
Async XLA Ops:
  6.5 102.9 %copy-start = (f32[360,360]{1,0:T(8,128)S(1)}, f32[360,360]{1,0:T(8,128)}, u32[]{:S(2)}) copy-start(f32[360,360]{1,0:T(8,128)} %param.3) | copy-start | bytes 1555204
  6.5 102.8 %all-gather.2.cloned.1.call-start = ((), (), s32[]{:S(2)}) async-start(), calls=%async_computation.1 | async-start | bytes 5013504 | tf_op jit(solution)/shard_map/all_gather | solution.py:11
  6.5 53.0 %collective-permute-start = (f32[192,360]{1,0:T(8,128)}, f32[192,360]{1,0:T(8,128)S(1)}, u32[]{:S(2)}, u32[]{:S(2)}) collective-permute-start(f32[192,360]{1,0:T(8,128)} %param.2), channel_id=1, source_target_pairs={{0,0},{2,32},{4,64},{6,96},{8,128},{10,160},{12,192},{14,224},{16,... | collective-permute-start | bytes 829448 | tf_op jit(solution)/shard_map/ppermute | solution.py:10
  59.5 0.7 copy-start.1
  60.3 759.8 %reduce-scatter.2.cloned.1.call-start = ((), (), s32[]{:S(2)}) async-start(), calls=%async_computation.2 | async-start | bytes 4866048 | tf_op jit(solution)/shard_map/reduce_scatter | solution.py:14
Sparse Core Ops, SparseCore 0:
  60.4 48.9 all-gather.1
  121.7 698.3 reduce-scatter.1

commit v4 on v2

v4 whole, which is shorter than its diff:
```python
import jax
import jax.numpy as jnp
from jax import lax
from jax.sharding import PartitionSpec as P

FIRST_DOT_STEP = 5
DOTS_PER_STEP = 5


def gather_col(block):
    n = lax.axis_size("col")
    c = lax.axis_index("col")
    core, xlo, y = c % 2, (c // 2) % 2, c // 4
    ny = n // 4
    other = lax.ppermute(block, "col", [(i, i ^ 1) for i in range(n)])
    pair = jnp.where(core == 0, jnp.stack([block, other]), jnp.stack([other, block]))
    far = lax.ppermute(pair, "col", [(i, i ^ 2) for i in range(n)])
    quad = jnp.where(xlo == 0, jnp.concatenate([pair, far]), jnp.concatenate([far, pair]))
    up = [(i, (i + 4) % n) for i in range(n)]
    down = [(i, (i - 4) % n) for i in range(n)]
    below = lax.ppermute(quad, "col", up)
    above = lax.ppermute(quad, "col", down)
    h = quad.shape[1] // 2
    opp_a = lax.ppermute(below[:, :h], "col", up)
    opp_b = lax.ppermute(above[:, h:], "col", down)
    opposite = jnp.concatenate([opp_a, opp_b], axis=1)
    stack = jnp.concatenate([quad, above, opposite, below])

    def place(owner):
        return ((owner // 4 - y) % ny) * 4 + owner % 4

    return stack, place


def local(amplitudes, integrals):
    n = lax.axis_size("row")
    me = lax.axis_index("row")
    d = lax.axis_index("depth")
    kb = integrals.shape[0]
    rows = amplitudes.shape[0]
    half = rows // 2

    strip, place = gather_col(amplitudes)

    def product(block, owner, lo=0, hi=None):
        hi = kb if hi is None else hi
        cols = lax.dynamic_index_in_dim(strip, place(owner), axis=0, keepdims=False)
        return jnp.dot(cols[:, lo:hi], block, precision=lax.Precision.HIGHEST,
                       preferred_element_type=jnp.float32)

    fwd = [(i, (i + 1) % n) for i in range(n)]
    bwd = [(i, (i - 1) % n) for i in range(n)]
    total = None
    pending = [(integrals, me, 0, kb)]
    ahead = integrals
    behind = integrals
    last = n // 2
    for step in range(1, last + 1):
        arrived = []
        if step < last:
            ahead = lax.ppermute(ahead, "row", fwd)
            arrived.append((ahead, (me - step) % n, 0, kb))
            behind = lax.ppermute(behind, "row", bwd)
            arrived.append((behind, (me + step) % n, 0, kb))
        else:
            m = kb // 2
            top = lax.ppermute(ahead[:m], "row", fwd)
            bottom = lax.ppermute(behind[m:], "row", bwd)
            arrived.append((top, (me - step) % n, 0, m))
            arrived.append((bottom, (me - step) % n, m, kb))
            ahead, behind = top, bottom
        if step >= FIRST_DOT_STEP:
            for block, owner, lo, hi in pending[:DOTS_PER_STEP]:
                part = product(block, owner, lo, hi)
                total = part if total is None else total + part
            pending = pending[DOTS_PER_STEP:]
            total, ahead, behind = lax.optimization_barrier((total, ahead, behind))
        pending = pending + arrived
    for block, owner, lo, hi in pending:
        part = product(block, owner, lo, hi)
        total = part if total is None else total + part

    mine = lax.dynamic_slice_in_dim(total, d * half, half, axis=0)
    other = lax.dynamic_slice_in_dim(total, (1 - d) * half, half, axis=0)
    other = lax.ppermute(other, "depth", [(0, 1), (1, 0)])
    return 0.5 * (mine + other)


def solution(mesh):
    placed = (P("row", ("col", "depth")), P(("row", "depth"), "col"))
    return jax.shard_map(
        local, mesh=mesh, in_specs=placed, out_specs=P(("row", "depth"), "col"), check_vma=False
    )
```

time: 159 us -> 157 us (0.987)
  starting transfers between devices: 63.1 us -> 89.5 us
  between operations: 14 us -> 1.5 us
  waiting for transfers between devices: 51.4 us -> 40.5 us
  matrix products: 28.3 us -> 18.8 us
  other arithmetic: 0.72 us -> 3.96 us
  local copies, waits for them, and re-layouts: 0.02 us -> 1.84 us
    ppermute x7, waiting for transfers between devices: 30.5 us -> 2.67 us  [local(): behind = lax.ppermute(behind, 'row', bwd)]
    ppermute x0 -> x8, starting transfers between devices: none -> 26.2 us  [the longest x1 5.6 us: local(): bottom = lax.ppermute(behind[m:], 'row', bwd)]
    ppermute x8 -> x7, waiting for transfers between devices: 14.9 us -> 27.2 us  [local(): ahead = lax.ppermute(ahead, 'row', fwd)]
    dot_general x16 -> x17, matrix products: 28.3 us -> 18.8 us  [product(): jnp.dot(cols[:, lo:hi], block, precision=lax.Precision.HIGHEST, preferred...]
    ppermute x0 -> x8, waiting for transfers between devices: none -> 5.46 us  [the longest x1 1.74 us: gather_col(): other = lax.ppermute(block, 'col', [(i, i ^ 1) for i in range(n)])]
    concatenate x0 -> x1, other arithmetic: none -> 2.1 us  [gather_col(): stack = jnp.concatenate([quad, above, opposite, below])]
    slice x0 -> x4, local copies, waits for them, and re-layouts: none -> 1.77 us  [the longest x1 0.86 us: gather_col(): opp_a = lax.ppermute(below[:, :h], 'col', up)]
    ppermute x8 -> x7, starting transfers between devices: 15.3 us -> 15.3 us  [local(): ahead = lax.ppermute(ahead, 'row', fwd)]
  transfers between devices with their start and end apart: 17 -> 23, of which waited for: 11 -> 12; matrix products, arithmetic and copies ran while one was open for 17% -> 14% of each run, Pallas kernels for 0% -> 0%
where the time goes in v4:
time: 157 us; the launch traced here: 156 us
  starting transfers between devices  89.5 us (57%)
  waiting for transfers between devices  40.5 us (26%)
  matrix products  18.8 us (12%)
  other arithmetic  3.96 us (3%)
  local copies, waits for them, and re-layouts  1.84 us (1%)
    ppermute x7, starting transfers between devices, local(): behind = lax.ppermute(behind, 'row', bwd)  44.6 us
    ppermute x7, waiting for transfers between devices, local(): ahead = lax.ppermute(ahead, 'row', fwd)  27.2 us
    dot_general x17, matrix products, product(): jnp.dot(cols[:, lo:hi], block, precision=lax.Precision.HIGHEST, preferred...  18.8 us
    ppermute x7, starting transfers between devices, local(): ahead = lax.ppermute(ahead, 'row', fwd)  15.3 us
    ppermute x1, starting transfers between devices, local(): bottom = lax.ppermute(behind[m:], 'row', bwd)  5.6 us
    ppermute x1, waiting for transfers between devices, local(): other = lax.ppermute(other, 'depth', [(0, 1), (1, 0)])  5.22 us
    ppermute x1, starting transfers between devices, gather_col(): opp_b = lax.ppermute(above[:, h:], 'col', down)  4.84 us
    ppermute x1, starting transfers between devices, gather_col(): above = lax.ppermute(quad, 'col', down)  3.57 us
  transfers between devices with their start and end apart: 23, of which 12 were waited for; matrix products, arithmetic and copies ran while one was open for 14% of the time, Pallas kernels for 0%

profile of v4, /device:TPU:6, one launch (start us, length us, event | category | flops | bytes accessed | tf_op | source)
XLA Modules:
  0.0 156.1 jit_solution(14795494915384315952)
XLA Ops:
  0.0 1.9 %collective-permute-start = (f32[192,360]{1,0:T(8,128)}, f32[192,360]{1,0:T(8,128)S(1)}, u32[]{:S(2)}, u32[]{:S(2)}) collective-permute-start(f32[192,360]{1,0:T(8,128)} %param.2), channel_id=1, source_target_pairs={{0,2},{2,0},{4,6},{6,4},{8,10},{10,8},{12,14},{14,12},{16,18},{18,... | collective-permute-start | bytes 829448 | tf_op jit(solution)/shard_map/ppermute | solution.py:15
  4.8 2.7 %collective-permute-start.1 = (f32[2,192,360]{2,1,0:T(8,128)S(1)}, f32[2,192,360]{2,1,0:T(8,128)S(1)}, u32[]{:S(2)}, u32[]{:S(2)}) collective-permute-start(f32[2,192,360]{2,1,0:T(8,128)S(1)} %maximum_select_fusion.1), channel_id=1, source_target_pairs={{0,4},{2,6},{4,0},{6,2},{8,12},{10,14},{12,8},{14,10},{16,20},{18,... | collective-permute-start | bytes 1658888 | tf_op jit(solution)/shard_map/ppermute | solution.py:17
  7.5 3.8 %collective-permute-start.6 = (f32[360,360]{1,0:T(8,128)}, f32[360,360]{1,0:T(8,128)}, u32[]{:S(2)}, u32[]{:S(2)}) collective-permute-start(f32[360,360]{1,0:T(8,128)} %param.3), channel_id=1, source_target_pairs={{0,32},{32,64},{64,96},{96,128},{128,160},{160,192},{192,224},{224... | collective-permute-start | bytes 1555208 | tf_op jit(solution)/shard_map/ppermute | solution.py:61
  11.4 9.5 %collective-permute-start.7 = (f32[360,360]{1,0:T(8,128)}, f32[360,360]{1,0:T(8,128)}, u32[]{:S(2)}, u32[]{:S(2)}) collective-permute-start(f32[360,360]{1,0:T(8,128)} %param.3), channel_id=1, source_target_pairs={{0,480},{32,0},{64,32},{96,64},{128,96},{160,128},{192,160},{224,1... | collective-permute-start | bytes 1555208 | tf_op jit(solution)/shard_map/ppermute | solution.py:63
  22.1 3.5 %collective-permute-start.3 = (f32[4,192,360]{2,1,0:T(8,128)S(1)}, f32[4,192,360]{2,1,0:T(8,128)S(1)}, u32[]{:S(2)}, u32[]{:S(2)}) collective-permute-start(f32[4,192,360]{2,1,0:T(8,128)S(1)} %maximum_select_fusion), channel_id=1, source_target_pairs={{0,8},{2,10},{4,12},{6,14},{8,16},{10,18},{12,20},{14,22},{16,24},... | collective-permute-start | bytes 3317768 | tf_op jit(solution)/shard_map/ppermute | solution.py:21
  25.6 3.6 %collective-permute-start.2 = (f32[4,192,360]{2,1,0:T(8,128)S(1)}, f32[4,192,360]{2,1,0:T(8,128)S(1)}, u32[]{:S(2)}, u32[]{:S(2)}) collective-permute-start(f32[4,192,360]{2,1,0:T(8,128)S(1)} %maximum_select_fusion), channel_id=1, source_target_pairs={{0,24},{2,26},{4,28},{6,30},{8,0},{10,2},{12,4},{14,6},{16,8},{18,... | collective-permute-start | bytes 3317768 | tf_op jit(solution)/shard_map/ppermute | solution.py:22
  29.2 2.6 %collective-permute-done.6 = f32[360,360]{1,0:T(8,128)} collective-permute-done((f32[360,360]{1,0:T(8,128)}, f32[360,360]{1,0:T(8,128)}, u32[]{:S(2)}, u32[]{:S(2)}) %collective-permute-start.6) | collective-permute-done | bytes 518432 | tf_op jit(solution)/shard_map/ppermute | solution.py:61
  31.8 1.9 %collective-permute-start.8 = (f32[360,360]{1,0:T(8,128)}, f32[360,360]{1,0:T(8,128)S(1)}, u32[]{:S(2)}, u32[]{:S(2)}) collective-permute-start(f32[360,360]{1,0:T(8,128)} %collective-permute-done.6), channel_id=1, source_target_pairs={{0,32},{32,64},{64,96},{96,128},{128,160},{160,192},{192,224},{224... | collective-permute-start | bytes 1555208 | tf_op jit(solution)/shard_map/ppermute | solution.py:61
  33.7 8.8 %collective-permute-start.9 = (f32[360,360]{1,0:T(8,128)}, f32[360,360]{1,0:T(8,128)S(1)}, u32[]{:S(2)}, u32[]{:S(2)}) collective-permute-start(f32[360,360]{1,0:T(8,128)} %collective-permute-done.7), channel_id=1, source_target_pairs={{0,480},{32,0},{64,32},{96,64},{128,96},{160,128},{192,160},{224,1... | collective-permute-start | bytes 1555208 | tf_op jit(solution)/shard_map/ppermute | solution.py:63
  42.6 9.9 %collective-permute-done.8 = f32[360,360]{1,0:T(8,128)S(1)} collective-permute-done((f32[360,360]{1,0:T(8,128)}, f32[360,360]{1,0:T(8,128)S(1)}, u32[]{:S(2)}, u32[]{:S(2)}) %collective-permute-start.8) | collective-permute-done | bytes 518432 | tf_op jit(solution)/shard_map/ppermute | solution.py:61
  52.4 1.9 %collective-permute-start.10 = (f32[360,360]{1,0:T(8,128)S(1)}, f32[360,360]{1,0:T(8,128)}, u32[]{:S(2)}, u32[]{:S(2)}) collective-permute-start(f32[360,360]{1,0:T(8,128)S(1)} %collective-permute-done.8), channel_id=1, source_target_pairs={{0,32},{32,64},{64,96},{96,128},{128,160},{160,192},{192,224},{224... | collective-permute-start | bytes 1555208 | tf_op jit(solution)/shard_map/ppermute | solution.py:61
  54.4 5.1 %collective-permute-start.13 = (f32[360,360]{1,0:T(8,128)S(1)}, f32[360,360]{1,0:T(8,128)}, u32[]{:S(2)}, u32[]{:S(2)}) collective-permute-start(f32[360,360]{1,0:T(8,128)S(1)} %collective-permute-done.9), channel_id=1, source_target_pairs={{0,480},{32,0},{64,32},{96,64},{128,96},{160,128},{192,160},{224,1... | collective-permute-start | bytes 1555208 | tf_op jit(solution)/shard_map/ppermute | solution.py:63
  60.4 2.2 %collective-permute-start.4 = (f32[4,96,360]{2,1,0:T(8,128)}, f32[4,96,360]{2,1,0:T(8,128)}, u32[]{:S(2)}, u32[]{:S(2)}) collective-permute-start(f32[4,96,360]{2,1,0:T(8,128)} %slice.24), channel_id=1, source_target_pairs={{0,8},{2,10},{4,12},{6,14},{8,16},{10,18},{12,20},{14,22},{16,24},... | collective-permute-start | bytes 1658888 | tf_op jit(solution)/shard_map/ppermute | solution.py:24
  63.5 4.8 %collective-permute-start.5 = (f32[4,96,360]{2,1,0:T(8,128)}, f32[4,96,360]{2,1,0:T(8,128)}, u32[]{:S(2)}, u32[]{:S(2)}) collective-permute-start(f32[4,96,360]{2,1,0:T(8,128)} %slice.25), channel_id=1, source_target_pairs={{0,24},{2,26},{4,28},{6,30},{8,0},{10,2},{12,4},{14,6},{16,8},{18,... | collective-permute-start | bytes 1658888 | tf_op jit(solution)/shard_map/ppermute | solution.py:25
  68.4 1.9 %collective-permute-start.11 = (f32[360,360]{1,0:T(8,128)}, f32[360,360]{1,0:T(8,128)}, u32[]{:S(2)}, u32[]{:S(2)}) collective-permute-start(f32[360,360]{1,0:T(8,128)} %collective-permute-done.10), channel_id=1, source_target_pairs={{0,32},{32,64},{64,96},{96,128},{128,160},{160,192},{192,224},{224... | collective-permute-start | bytes 1555208 | tf_op jit(solution)/shard_map/ppermute | solution.py:61
  70.3 5.1 %collective-permute-start.14 = (f32[360,360]{1,0:T(8,128)}, f32[360,360]{1,0:T(8,128)}, u32[]{:S(2)}, u32[]{:S(2)}) collective-permute-start(f32[360,360]{1,0:T(8,128)} %collective-permute-done.13), channel_id=1, source_target_pairs={{0,480},{32,0},{64,32},{96,64},{128,96},{160,128},{192,160},{224,1... | collective-permute-start | bytes 1555208 | tf_op jit(solution)/shard_map/ppermute | solution.py:63
  76.4 7.4 %collective-permute-done.11 = f32[360,360]{1,0:T(8,128)} collective-permute-done((f32[360,360]{1,0:T(8,128)}, f32[360,360]{1,0:T(8,128)}, u32[]{:S(2)}, u32[]{:S(2)}) %collective-permute-start.11) | collective-permute-done | bytes 518432 | tf_op jit(solution)/shard_map/ppermute | solution.py:61
  83.8 1.9 %collective-permute-start.12 = (f32[360,360]{1,0:T(8,128)}, f32[360,360]{1,0:T(8,128)S(1)}, u32[]{:S(2)}, u32[]{:S(2)}) collective-permute-start(f32[360,360]{1,0:T(8,128)} %collective-permute-done.11), channel_id=1, source_target_pairs={{0,32},{32,64},{64,96},{96,128},{128,160},{160,192},{192,224},{224... | collective-permute-start | bytes 1555208 | tf_op jit(solution)/shard_map/ppermute | solution.py:61
  85.7 5.1 %collective-permute-start.15 = (f32[360,360]{1,0:T(8,128)}, f32[360,360]{1,0:T(8,128)S(1)}, u32[]{:S(2)}, u32[]{:S(2)}) collective-permute-start(f32[360,360]{1,0:T(8,128)} %collective-permute-done.14), channel_id=1, source_target_pairs={{0,480},{32,0},{64,32},{96,64},{128,96},{160,128},{192,160},{224,1... | collective-permute-start | bytes 1555208 | tf_op jit(solution)/shard_map/ppermute | solution.py:63
  90.9 2.1 %pad_maximum_fusion = f32[16,192,360]{2,1,0:T(8,128)S(1)} fusion(f32[4,192,360]{2,1,0:T(8,128)S(1)} %collective-permute-done.3, f32[4,96,360]{2,1,0:T(8,128)} %collective-permute-done.5, f32[4,96,360]{2,1,0:T(8,128)} %collective-permute-done.4, f32[4,192,360]{2,1,0:T(8,128)S(1)} %collective-permute-done.2, f32[4,192,360]{2,1,0:T(8,128)S(1)} %maximum_select_fusion), kind=kLoop, calls=%fused_computation | loop fusion | flops 4423680 | bytes 8847360 | tf_op jit(solution)/shard_map/concatenate | solution.py:27
  93.1 1.9 %fusion.20 = f32[192,360]{1,0:T(8,128)S(1)} fusion(f32[360,360]{1,0:T(8,128)} %collective-permute-done.10, f32[16,192,360]{2,1,0:T(8,128)S(1)} %pad_maximum_fusion, s32[]{:T(128)S(6)} %select_n.369), kind=kOutput, calls=%fused_computation.28 | convolution fusion | flops 298598400 | bytes 1089796 | tf_op jit(solution)/shard_map/dot_general | solution.py:48
  104.6 1.9 %collective-permute-start.16 = (f32[360,360]{1,0:T(8,128)S(1)}, f32[360,360]{1,0:T(8,128)S(1)}, u32[]{:S(2)}, u32[]{:S(2)}) collective-permute-start(f32[360,360]{1,0:T(8,128)S(1)} %collective-permute-done.12), channel_id=1, source_target_pairs={{0,32},{32,64},{64,96},{96,128},{128,160},{160,192},{192,224},{224... | collective-permute-start | bytes 1555208 | tf_op jit(solution)/shard_map/ppermute | solution.py:61
  106.5 5.1 %collective-permute-start.17 = (f32[360,360]{1,0:T(8,128)S(1)}, f32[360,360]{1,0:T(8,128)S(1)}, u32[]{:S(2)}, u32[]{:S(2)}) collective-permute-start(f32[360,360]{1,0:T(8,128)S(1)} %collective-permute-done.15), channel_id=1, source_target_pairs={{0,480},{32,0},{64,32},{96,64},{128,96},{160,128},{192,160},{224,1... | collective-permute-start | bytes 1555208 | tf_op jit(solution)/shard_map/ppermute | solution.py:63
  111.7 1.8 %fusion.2 = f32[192,360]{1,0:T(8,128)S(1)} fusion(f32[192,360]{1,0:T(8,128)S(1)} %fusion.15, f32[360,360]{1,0:T(8,128)} %collective-permute-done.11, f32[16,192,360]{2,1,0:T(8,128)S(1)} %pad_maximum_fusion, s32[]{:T(128)S(6)} %select_n.379, f32[192,360]{1,0:T(8,128)S(1)} %fusion.18, f32[192,360]{1,0:T(8,128)S(1)} %fusion.1, f32[192,360]{1,0:T(8,128)S(1)} %fusion.20), kind=kOutput, calls=%fused_computation.9 | convolution fusion | flops 298874880 | bytes 2269444 | tf_op jit(solution)/shard_map/dot_general | solution.py:48
  114.2 4.0 %collective-permute-done.16 = f32[360,360]{1,0:T(8,128)S(1)} collective-permute-done((f32[360,360]{1,0:T(8,128)S(1)}, f32[360,360]{1,0:T(8,128)S(1)}, u32[]{:S(2)}, u32[]{:S(2)}) %collective-permute-start.16) | collective-permute-done | bytes 518432 | tf_op jit(solution)/shard_map/ppermute | solution.py:61
  119.4 1.9 %collective-permute-start.18 = (f32[360,360]{1,0:T(8,128)S(1)}, f32[360,360]{1,0:T(8,128)S(1)}, u32[]{:S(2)}, u32[]{:S(2)}) collective-permute-start(f32[360,360]{1,0:T(8,128)S(1)} %collective-permute-done.16), channel_id=1, source_target_pairs={{0,32},{32,64},{64,96},{96,128},{128,160},{160,192},{192,224},{224... | collective-permute-start | bytes 1555208 | tf_op jit(solution)/shard_map/ppermute | solution.py:61
  121.4 5.8 %collective-permute-start.19 = (f32[360,360]{1,0:T(8,128)S(1)}, f32[360,360]{1,0:T(8,128)S(1)}, u32[]{:S(2)}, u32[]{:S(2)}) collective-permute-start(f32[360,360]{1,0:T(8,128)S(1)} %collective-permute-done.17), channel_id=1, source_target_pairs={{0,480},{32,0},{64,32},{96,64},{128,96},{160,128},{192,160},{224,1... | collective-permute-start | bytes 1555208 | tf_op jit(solution)/shard_map/ppermute | solution.py:63
  129.4 3.2 %collective-permute-done.18 = f32[360,360]{1,0:T(8,128)S(1)} collective-permute-done((f32[360,360]{1,0:T(8,128)S(1)}, f32[360,360]{1,0:T(8,128)S(1)}, u32[]{:S(2)}, u32[]{:S(2)}) %collective-permute-start.18) | collective-permute-done | bytes 518432 | tf_op jit(solution)/shard_map/ppermute | solution.py:61
  134.2 1.9 %collective-permute-start.20 = (f32[180,360]{1,0:T(8,128)S(1)}, f32[180,360]{1,0:T(8,128)S(1)}, u32[]{:S(2)}, u32[]{:S(2)}) collective-permute-start(f32[180,360]{1,0:T(8,128)S(1)} %slice.20), channel_id=1, source_target_pairs={{0,32},{32,64},{64,96},{96,128},{128,160},{160,192},{192,224},{224... | collective-permute-start | bytes 777608 | tf_op jit(solution)/shard_map/ppermute | solution.py:67
  136.1 5.6 %collective-permute-start.21 = (f32[180,360]{1,0:T(8,128)S(1)}, f32[180,360]{1,0:T(8,128)S(1)}, u32[]{:S(2)}, u32[]{:S(2)}) collective-permute-start(f32[180,360]{1,0:T(8,128)S(1)} %slice.21), channel_id=1, source_target_pairs={{0,480},{32,0},{64,32},{96,64},{128,96},{160,128},{192,160},{224,1... | collective-permute-start | bytes 777608 | tf_op jit(solution)/shard_map/ppermute | solution.py:68
  146.9 3.3 %collective-permute-start.22 = (f32[96,360]{1,0:T(8,128)S(1)}, f32[96,360]{1,0:T(8,128)S(1)}, u32[]{:S(2)}, u32[]{:S(2)}) collective-permute-start(f32[96,360]{1,0:T(8,128)S(1)} %constant_dynamic-slice_fusion), channel_id=1, source_target_pairs={{0,1},{1,0},{2,3},{3,2},{4,5},{5,4},{6,7},{7,6},{8,9},{9,8},{10,11... | collective-permute-start | bytes 414728 | tf_op jit(solution)/shard_map/ppermute | solution.py:85
  150.2 5.2 %collective-permute-done.22 = f32[96,360]{1,0:T(8,128)S(1)} collective-permute-done((f32[96,360]{1,0:T(8,128)S(1)}, f32[96,360]{1,0:T(8,128)S(1)}, u32[]{:S(2)}, u32[]{:S(2)}) %collective-permute-start.22) | collective-permute-done | bytes 138272 | tf_op jit(solution)/shard_map/ppermute | solution.py:85
  (51 shorter events, 26.9 us)
Async XLA Ops:
  0.0 3.7 %collective-permute-start = (f32[192,360]{1,0:T(8,128)}, f32[192,360]{1,0:T(8,128)S(1)}, u32[]{:S(2)}, u32[]{:S(2)}) collective-permute-start(f32[192,360]{1,0:T(8,128)} %param.2), channel_id=1, source_target_pairs={{0,2},{2,0},{4,6},{6,4},{8,10},{10,8},{12,14},{14,12},{16,18},{18,... | collective-permute-start | bytes 829448 | tf_op jit(solution)/shard_map/ppermute | solution.py:15
  4.8 17.3 %collective-permute-start.1 = (f32[2,192,360]{2,1,0:T(8,128)S(1)}, f32[2,192,360]{2,1,0:T(8,128)S(1)}, u32[]{:S(2)}, u32[]{:S(2)}) collective-permute-start(f32[2,192,360]{2,1,0:T(8,128)S(1)} %maximum_select_fusion.1), channel_id=1, source_target_pairs={{0,4},{2,6},{4,0},{6,2},{8,12},{10,14},{12,8},{14,10},{16,20},{18,... | collective-permute-start | bytes 1658888 | tf_op jit(solution)/shard_map/ppermute | solution.py:17
  7.5 24.3 %collective-permute-start.6 = (f32[360,360]{1,0:T(8,128)}, f32[360,360]{1,0:T(8,128)}, u32[]{:S(2)}, u32[]{:S(2)}) collective-permute-start(f32[360,360]{1,0:T(8,128)} %param.3), channel_id=1, source_target_pairs={{0,32},{32,64},{64,96},{96,128},{128,160},{160,192},{192,224},{224... | collective-permute-start | bytes 1555208 | tf_op jit(solution)/shard_map/ppermute | solution.py:61
  11.4 22.4 %collective-permute-start.7 = (f32[360,360]{1,0:T(8,128)}, f32[360,360]{1,0:T(8,128)}, u32[]{:S(2)}, u32[]{:S(2)}) collective-permute-start(f32[360,360]{1,0:T(8,128)} %param.3), channel_id=1, source_target_pairs={{0,480},{32,0},{64,32},{96,64},{128,96},{160,128},{192,160},{224,1... | collective-permute-start | bytes 1555208 | tf_op jit(solution)/shard_map/ppermute | solution.py:63
  22.1 37.4 %collective-permute-start.3 = (f32[4,192,360]{2,1,0:T(8,128)S(1)}, f32[4,192,360]{2,1,0:T(8,128)S(1)}, u32[]{:S(2)}, u32[]{:S(2)}) collective-permute-start(f32[4,192,360]{2,1,0:T(8,128)S(1)} %maximum_select_fusion), channel_id=1, source_target_pairs={{0,8},{2,10},{4,12},{6,14},{8,16},{10,18},{12,20},{14,22},{16,24},... | collective-permute-start | bytes 3317768 | tf_op jit(solution)/shard_map/ppermute | solution.py:21
  25.6 37.0 %collective-permute-start.2 = (f32[4,192,360]{2,1,0:T(8,128)S(1)}, f32[4,192,360]{2,1,0:T(8,128)S(1)}, u32[]{:S(2)}, u32[]{:S(2)}) collective-permute-start(f32[4,192,360]{2,1,0:T(8,128)S(1)} %maximum_select_fusion), channel_id=1, source_target_pairs={{0,24},{2,26},{4,28},{6,30},{8,0},{10,2},{12,4},{14,6},{16,8},{18,... | collective-permute-start | bytes 3317768 | tf_op jit(solution)/shard_map/ppermute | solution.py:22
  31.8 20.6 %collective-permute-start.8 = (f32[360,360]{1,0:T(8,128)}, f32[360,360]{1,0:T(8,128)S(1)}, u32[]{:S(2)}, u32[]{:S(2)}) collective-permute-start(f32[360,360]{1,0:T(8,128)} %collective-permute-done.6), channel_id=1, source_target_pairs={{0,32},{32,64},{64,96},{96,128},{128,160},{160,192},{192,224},{224... | collective-permute-start | bytes 1555208 | tf_op jit(solution)/shard_map/ppermute | solution.py:61
  33.7 20.6 %collective-permute-start.9 = (f32[360,360]{1,0:T(8,128)}, f32[360,360]{1,0:T(8,128)S(1)}, u32[]{:S(2)}, u32[]{:S(2)}) collective-permute-start(f32[360,360]{1,0:T(8,128)} %collective-permute-done.7), channel_id=1, source_target_pairs={{0,480},{32,0},{64,32},{96,64},{128,96},{160,128},{192,160},{224,1... | collective-permute-start | bytes 1555208 | tf_op jit(solution)/shard_map/ppermute | solution.py:63
  52.4 10.2 %copy-start.1 = (f32[360,360]{1,0:T(8,128)}, f32[360,360]{1,0:T(8,128)S(1)}, u32[]{:S(2)}) copy-start(f32[360,360]{1,0:T(8,128)S(1)} %collective-permute-done.8) | copy-start | bytes 1555204
  52.4 15.9 %collective-permute-start.10 = (f32[360,360]{1,0:T(8,128)S(1)}, f32[360,360]{1,0:T(8,128)}, u32[]{:S(2)}, u32[]{:S(2)}) collective-permute-start(f32[360,360]{1,0:T(8,128)S(1)} %collective-permute-done.8), channel_id=1, source_target_pairs={{0,32},{32,64},{64,96},{96,128},{128,160},{160,192},{192,224},{224... | collective-permute-start | bytes 1555208 | tf_op jit(solution)/shard_map/ppermute | solution.py:61
  54.4 14.0 %copy-start.3 = (f32[360,360]{1,0:T(8,128)}, f32[360,360]{1,0:T(8,128)S(1)}, u32[]{:S(2)}) copy-start(f32[360,360]{1,0:T(8,128)S(1)} %collective-permute-done.9) | copy-start | bytes 1555204
  54.4 15.9 %collective-permute-start.13 = (f32[360,360]{1,0:T(8,128)S(1)}, f32[360,360]{1,0:T(8,128)}, u32[]{:S(2)}, u32[]{:S(2)}) collective-permute-start(f32[360,360]{1,0:T(8,128)S(1)} %collective-permute-done.9), channel_id=1, source_target_pairs={{0,480},{32,0},{64,32},{96,64},{128,96},{160,128},{192,160},{224,1... | collective-permute-start | bytes 1555208 | tf_op jit(solution)/shard_map/ppermute | solution.py:63
  60.4 30.5 %collective-permute-start.4 = (f32[4,96,360]{2,1,0:T(8,128)}, f32[4,96,360]{2,1,0:T(8,128)}, u32[]{:S(2)}, u32[]{:S(2)}) collective-permute-start(f32[4,96,360]{2,1,0:T(8,128)} %slice.24), channel_id=1, source_target_pairs={{0,8},{2,10},{4,12},{6,14},{8,16},{10,18},{12,20},{14,22},{16,24},... | collective-permute-start | bytes 1658888 | tf_op jit(solution)/shard_map/ppermute | solution.py:24
  63.5 27.4 %collective-permute-start.5 = (f32[4,96,360]{2,1,0:T(8,128)}, f32[4,96,360]{2,1,0:T(8,128)}, u32[]{:S(2)}, u32[]{:S(2)}) collective-permute-start(f32[4,96,360]{2,1,0:T(8,128)} %slice.25), channel_id=1, source_target_pairs={{0,24},{2,26},{4,28},{6,30},{8,0},{10,2},{12,4},{14,6},{16,8},{18,... | collective-permute-start | bytes 1658888 | tf_op jit(solution)/shard_map/ppermute | solution.py:25
  68.4 15.5 %collective-permute-start.11 = (f32[360,360]{1,0:T(8,128)}, f32[360,360]{1,0:T(8,128)}, u32[]{:S(2)}, u32[]{:S(2)}) collective-permute-start(f32[360,360]{1,0:T(8,128)} %collective-permute-done.10), channel_id=1, source_target_pairs={{0,32},{32,64},{64,96},{96,128},{128,160},{160,192},{192,224},{224... | collective-permute-start | bytes 1555208 | tf_op jit(solution)/shard_map/ppermute | solution.py:61
  70.3 15.4 %collective-permute-start.14 = (f32[360,360]{1,0:T(8,128)}, f32[360,360]{1,0:T(8,128)}, u32[]{:S(2)}, u32[]{:S(2)}) collective-permute-start(f32[360,360]{1,0:T(8,128)} %collective-permute-done.13), channel_id=1, source_target_pairs={{0,480},{32,0},{64,32},{96,64},{128,96},{160,128},{192,160},{224,1... | collective-permute-start | bytes 1555208 | tf_op jit(solution)/shard_map/ppermute | solution.py:63
  83.8 20.7 %collective-permute-start.12 = (f32[360,360]{1,0:T(8,128)}, f32[360,360]{1,0:T(8,128)S(1)}, u32[]{:S(2)}, u32[]{:S(2)}) collective-permute-start(f32[360,360]{1,0:T(8,128)} %collective-permute-done.11), channel_id=1, source_target_pairs={{0,32},{32,64},{64,96},{96,128},{128,160},{160,192},{192,224},{224... | collective-permute-start | bytes 1555208 | tf_op jit(solution)/shard_map/ppermute | solution.py:61
  85.7 18.8 %collective-permute-start.15 = (f32[360,360]{1,0:T(8,128)}, f32[360,360]{1,0:T(8,128)S(1)}, u32[]{:S(2)}, u32[]{:S(2)}) collective-permute-start(f32[360,360]{1,0:T(8,128)} %collective-permute-done.14), channel_id=1, source_target_pairs={{0,480},{32,0},{64,32},{96,64},{128,96},{160,128},{192,160},{224,1... | collective-permute-start | bytes 1555208 | tf_op jit(solution)/shard_map/ppermute | solution.py:63
  93.0 9.2 %copy-start.4 = (f32[360,360]{1,0:T(8,128)S(1)}, f32[360,360]{1,0:T(8,128)}, u32[]{:S(2)}) copy-start(f32[360,360]{1,0:T(8,128)} %copy-done.3) | copy-start | bytes 1555204
  93.0 10.0 %copy-start = (f32[360,360]{1,0:T(8,128)S(1)}, f32[360,360]{1,0:T(8,128)}, u32[]{:S(2)}) copy-start(f32[360,360]{1,0:T(8,128)} %param.3) | copy-start | bytes 1555204
  93.0 10.8 %copy-start.2 = (f32[360,360]{1,0:T(8,128)S(1)}, f32[360,360]{1,0:T(8,128)}, u32[]{:S(2)}) copy-start(f32[360,360]{1,0:T(8,128)} %copy-done.1) | copy-start | bytes 1555204
  104.6 13.7 %collective-permute-start.16 = (f32[360,360]{1,0:T(8,128)S(1)}, f32[360,360]{1,0:T(8,128)S(1)}, u32[]{:S(2)}, u32[]{:S(2)}) collective-permute-start(f32[360,360]{1,0:T(8,128)S(1)} %collective-permute-done.12), channel_id=1, source_target_pairs={{0,32},{32,64},{64,96},{96,128},{128,160},{160,192},{192,224},{224... | collective-permute-start | bytes 1555208 | tf_op jit(solution)/shard_map/ppermute | solution.py:61
  106.5 12.9 %collective-permute-start.17 = (f32[360,360]{1,0:T(8,128)S(1)}, f32[360,360]{1,0:T(8,128)S(1)}, u32[]{:S(2)}, u32[]{:S(2)}) collective-permute-start(f32[360,360]{1,0:T(8,128)S(1)} %collective-permute-done.15), channel_id=1, source_target_pairs={{0,480},{32,0},{64,32},{96,64},{128,96},{160,128},{192,160},{224,1... | collective-permute-start | bytes 1555208 | tf_op jit(solution)/shard_map/ppermute | solution.py:63
  119.4 13.2 %collective-permute-start.18 = (f32[360,360]{1,0:T(8,128)S(1)}, f32[360,360]{1,0:T(8,128)S(1)}, u32[]{:S(2)}, u32[]{:S(2)}) collective-permute-start(f32[360,360]{1,0:T(8,128)S(1)} %collective-permute-done.16), channel_id=1, source_target_pairs={{0,32},{32,64},{64,96},{96,128},{128,160},{160,192},{192,224},{224... | collective-permute-start | bytes 1555208 | tf_op jit(solution)/shard_map/ppermute | solution.py:61
  121.4 12.8 %collective-permute-start.19 = (f32[360,360]{1,0:T(8,128)S(1)}, f32[360,360]{1,0:T(8,128)S(1)}, u32[]{:S(2)}, u32[]{:S(2)}) collective-permute-start(f32[360,360]{1,0:T(8,128)S(1)} %collective-permute-done.17), channel_id=1, source_target_pairs={{0,480},{32,0},{64,32},{96,64},{128,96},{160,128},{192,160},{224,1... | collective-permute-start | bytes 1555208 | tf_op jit(solution)/shard_map/ppermute | solution.py:63
  134.2 10.2 %collective-permute-start.20 = (f32[180,360]{1,0:T(8,128)S(1)}, f32[180,360]{1,0:T(8,128)S(1)}, u32[]{:S(2)}, u32[]{:S(2)}) collective-permute-start(f32[180,360]{1,0:T(8,128)S(1)} %slice.20), channel_id=1, source_target_pairs={{0,32},{32,64},{64,96},{96,128},{128,160},{160,192},{192,224},{224... | collective-permute-start | bytes 777608 | tf_op jit(solution)/shard_map/ppermute | solution.py:67
  136.1 9.7 %collective-permute-start.21 = (f32[180,360]{1,0:T(8,128)S(1)}, f32[180,360]{1,0:T(8,128)S(1)}, u32[]{:S(2)}, u32[]{:S(2)}) collective-permute-start(f32[180,360]{1,0:T(8,128)S(1)} %slice.21), channel_id=1, source_target_pairs={{0,480},{32,0},{64,32},{96,64},{128,96},{160,128},{192,160},{224,1... | collective-permute-start | bytes 777608 | tf_op jit(solution)/shard_map/ppermute | solution.py:68
  146.9 8.5 %collective-permute-start.22 = (f32[96,360]{1,0:T(8,128)S(1)}, f32[96,360]{1,0:T(8,128)S(1)}, u32[]{:S(2)}, u32[]{:S(2)}) collective-permute-start(f32[96,360]{1,0:T(8,128)S(1)} %constant_dynamic-slice_fusion), channel_id=1, source_target_pairs={{0,1},{1,0},{2,3},{3,2},{4,5},{5,4},{6,7},{7,6},{8,9},{9,8},{10,11... | collective-permute-start | bytes 414728 | tf_op jit(solution)/shard_map/ppermute | solution.py:85

commit v5 on v3

v5 whole, which is shorter than its diff:
```python
import jax
import jax.numpy as jnp
from jax import lax
from jax.sharding import PartitionSpec as P

CHUNKS = 4


def gather_col(block):
    n = lax.axis_size("col")
    c = lax.axis_index("col")
    core, xlo, y = c % 2, (c // 2) % 2, c // 4
    ny = n // 4
    other = lax.ppermute(block, "col", [(i, i ^ 1) for i in range(n)])
    pair = jnp.where(core == 0, jnp.stack([block, other]), jnp.stack([other, block]))
    far = lax.ppermute(pair, "col", [(i, i ^ 2) for i in range(n)])
    quad = jnp.where(xlo == 0, jnp.concatenate([pair, far]), jnp.concatenate([far, pair]))
    up = [(i, (i + 4) % n) for i in range(n)]
    down = [(i, (i - 4) % n) for i in range(n)]
    below = lax.ppermute(quad, "col", up)
    above = lax.ppermute(quad, "col", down)
    h = quad.shape[1] // 2
    opp_a = lax.ppermute(below[:, :h], "col", up)
    opp_b = lax.ppermute(above[:, h:], "col", down)
    opposite = jnp.concatenate([opp_a, opp_b], axis=1)
    stack = jnp.concatenate([quad, above, opposite, below])

    def place(owner):
        return ((owner // 4 - y) % ny) * 4 + owner % 4

    return stack, place


def local(amplitudes, integrals):
    d = lax.axis_index("depth")
    rows = amplitudes.shape[0]
    half = rows // 2
    width = integrals.shape[1]

    stack, place = gather_col(amplitudes)
    n = stack.shape[0]
    order = jnp.stack([place(jnp.int32(k)) for k in range(n)])
    strip = jnp.take(stack, order, axis=0)

    outs = []
    step = width // CHUNKS
    for k in range(CHUNKS):
        piece = lax.all_gather(integrals[:, k * step:(k + 1) * step], "row", axis=0, tiled=False)
        total = lax.dot_general(strip, piece, (((0, 2), (0, 1)), ((), ())),
                                precision=lax.Precision.HIGHEST,
                                preferred_element_type=jnp.float32)
        mine = lax.dynamic_slice_in_dim(total, d * half, half, axis=0)
        other = lax.dynamic_slice_in_dim(total, (1 - d) * half, half, axis=0)
        other = lax.ppermute(other, "depth", [(0, 1), (1, 0)])
        outs.append(0.5 * (mine + other))
    return jnp.concatenate(outs, axis=1)


def solution(mesh):
    placed = (P("row", ("col", "depth")), P(("row", "depth"), "col"))
    return jax.shard_map(
        local, mesh=mesh, in_specs=placed, out_specs=P(("row", "depth"), "col"), check_vma=False
    )
```

time: 830 us -> 329 us (0.40)
  waiting for transfers between devices: 795 us -> 235 us
  starting transfers between devices: 5.61 us -> 37.6 us
  matrix products: 12.2 us -> 27 us
  local copies, waits for them, and re-layouts: 0.73 us -> 10.3 us
    reduce_scatter x1 -> x0, waiting for transfers between devices: 698 us -> none  [local(): lax.psum_scatter(partial, ('row', 'depth'), scatter_dimension=0, tiled=True)]
    all_gather x1 -> x4, waiting for transfers between devices: 49 us -> 181 us  [local(): lax.all_gather(integrals[:, k * step:(k + 1) * step], 'row', axis=0, tile...]
    ppermute x1 -> x10, starting transfers between devices: 5.56 us -> 37.5 us  [the longest x4 18.7 us: local(): other = lax.ppermute(other, 'depth', [(0, 1), (1, 0)])]
    dot_general x1 -> x4, matrix products: 12.2 us -> 27 us  [local(): lax.dot_general(strip, piece, (((0, 2), (0, 1)), ((), ())), precision=lax...]
    ppermute x1 -> x10, waiting for transfers between devices: 47.4 us -> 53.3 us  [the longest x1 23 us: gather_col(): below = lax.ppermute(quad, 'col', up)]
  transfers between devices with their start and end apart: 3 -> 14, of which waited for: 3 -> 9; matrix products, arithmetic and copies ran while one was open for 0% -> 12% of each run, Pallas kernels for 0% -> 0%
where the time goes in v5:
time: 329 us
  waiting for transfers between devices  235 us (71%)
  starting transfers between devices  37.6 us (11%)
  matrix products  27 us (8%)
  between operations  13.5 us (4%)
  local copies, waits for them, and re-layouts  10.3 us (3%)
  other arithmetic  5.32 us (2%)
    all_gather x4, waiting for transfers between devices, local(): lax.all_gather(integrals[:, k * step:(k + 1) * step], 'row', axis=0, tile...  181 us
    dot_general x4, matrix products, local(): lax.dot_general(strip, piece, (((0, 2), (0, 1)), ((), ())), precision=lax...  27 us
    ppermute x1, waiting for transfers between devices, gather_col(): below = lax.ppermute(quad, 'col', up)  23 us
    ppermute x4, starting transfers between devices, local(): other = lax.ppermute(other, 'depth', [(0, 1), (1, 0)])  18.7 us
    ppermute x1, waiting for transfers between devices, gather_col(): far = lax.ppermute(pair, 'col', [(i, i ^ 2) for i in range(n)])  13.7 us
    ppermute x1, waiting for transfers between devices, gather_col(): opp_a = lax.ppermute(below[:, :h], 'col', up)  9.62 us
  transfers between devices with their start and end apart: 14, of which 9 were waited for; matrix products, arithmetic and copies ran while one was open for 12% of the time, Pallas kernels for 0%

profile of v5, /device:TPU:6, one launch (start us, length us, event | category | flops | bytes accessed | tf_op | source)
XLA Modules:
  0.0 328.6 jit_solution(8505273491444959639)
XLA Ops:
  6.5 1.4 fusion.33
  8.0 0.8 copy.11
  8.9 0.8 copy.12
  9.7 0.8 copy.13
  10.6 1.9 collective-permute-start
  12.5 1.7 collective-permute-done
  14.3 1.1 maximum_select_fusion.1
  15.4 2.7 collective-permute-start.1
  18.1 0.8 copy.14
  19.0 13.7 %collective-permute-done.1 = f32[2,192,360]{2,1,0:T(8,128)S(1)} collective-permute-done((f32[2,192,360]{2,1,0:T(8,128)S(1)}, f32[2,192,360]{2,1,0:T(8,128)S(1)}, u32[]{:S(2)}, u32[]{:S(2)}) %collective-permute-start.1) | collective-permute-done | bytes 552992 | tf_op jit(solution)/shard_map/ppermute | solution.py:16
  32.7 3.5 %collective-permute-start.3 = (f32[4,192,360]{2,1,0:T(8,128)S(1)}, f32[4,192,360]{2,1,0:T(8,128)S(1)}, u32[]{:S(2)}, u32[]{:S(2)}) collective-permute-start(f32[4,192,360]{2,1,0:T(8,128)S(1)} %maximum_select_fusion), channel_id=1, source_target_pairs={{0,8},{2,10},{4,12},{6,14},{8,16},{10,18},{12,20},{14,22},{16,24},... | collective-permute-start | bytes 3317768 | tf_op jit(solution)/shard_map/ppermute | solution.py:20
  36.2 3.6 %collective-permute-start.2 = (f32[4,192,360]{2,1,0:T(8,128)S(1)}, f32[4,192,360]{2,1,0:T(8,128)S(1)}, u32[]{:S(2)}, u32[]{:S(2)}) collective-permute-start(f32[4,192,360]{2,1,0:T(8,128)S(1)} %maximum_select_fusion), channel_id=1, source_target_pairs={{0,24},{2,26},{4,28},{6,30},{8,0},{10,2},{12,4},{14,6},{16,8},{18,... | collective-permute-start | bytes 3317768 | tf_op jit(solution)/shard_map/ppermute | solution.py:21
  40.1 23.0 %collective-permute-done.3 = f32[4,192,360]{2,1,0:T(8,128)S(1)} collective-permute-done((f32[4,192,360]{2,1,0:T(8,128)S(1)}, f32[4,192,360]{2,1,0:T(8,128)S(1)}, u32[]{:S(2)}, u32[]{:S(2)}) %collective-permute-start.3) | collective-permute-done | bytes 1105952 | tf_op jit(solution)/shard_map/ppermute | solution.py:20
  63.1 2.2 collective-permute-start.4
  65.4 4.8 %collective-permute-start.5 = (f32[4,96,360]{2,1,0:T(8,128)S(1)}, f32[4,96,360]{2,1,0:T(8,128)S(1)}, u32[]{:S(2)}, u32[]{:S(2)}) collective-permute-start(f32[4,96,360]{2,1,0:T(8,128)S(1)} %slice.27), channel_id=1, source_target_pairs={{0,24},{2,26},{4,28},{6,30},{8,0},{10,2},{12,4},{14,6},{16,8},{18,... | collective-permute-start | bytes 1658888 | tf_op jit(solution)/shard_map/ppermute | solution.py:24
  70.3 9.6 %collective-permute-done.4 = f32[4,96,360]{2,1,0:T(8,128)S(1)} collective-permute-done((f32[4,96,360]{2,1,0:T(8,128)S(1)}, f32[4,96,360]{2,1,0:T(8,128)S(1)}, u32[]{:S(2)}, u32[]{:S(2)}) %collective-permute-start.4) | collective-permute-done | bytes 552992 | tf_op jit(solution)/shard_map/ppermute | solution.py:23
  79.9 1.2 collective-permute-done.5
  81.2 3.2 pad_maximum_fusion
  84.4 5.3 %gather_fusion = f32[16,192,360]{2,1,0:T(8,128)} fusion(f32[16,192,360]{2,1,0:T(8,128)} %pad_maximum_fusion, s32[1024]{0:T(1024)S(1)} %pad_clamp_fusion), kind=kCustom, calls=%fused_computation | custom fusion | bytes 8847424 | tf_op jit(solution)/shard_map/jit(_take)/gather | solution.py:43
  89.8 6.8 %fusion.16 = f32[192,90]{1,0:T(8,128)S(1)} fusion(f32[16,360,90]{1,2,0:T(8,128)} %all-gather.13.cloned.1.call-done, f32[16,192,360]{2,1,0:T(8,128)} %gather_fusion, pred[16]{0:T(512)(128)(4,1)S(1)} %compare_and_fusion), kind=kOutput, calls=%fused_computation.19 | convolution fusion | flops 1195499520 | bytes 6566416 | tf_op jit(solution)/shard_map/dot_general | solution.py:49
  96.5 8.3 %collective-permute-start.6 = (f32[96,90]{1,0:T(8,128)S(1)}, f32[96,90]{1,0:T(8,128)S(1)}, u32[]{:S(2)}, u32[]{:S(2)}) collective-permute-start(f32[96,90]{1,0:T(8,128)S(1)} %constant_dynamic-slice_fusion.3), channel_id=1, source_target_pairs={{0,1},{1,0},{2,3},{3,2},{4,5},{5,4},{6,7},{7,6},{8,9},{9,8},{10,11... | collective-permute-start | bytes 103688 | tf_op jit(solution)/shard_map/ppermute | solution.py:54
  104.9 56.2 %all-gather.15.cloned.1.call-done = f32[16,360,90]{1,2,0:T(8,128)} async-done(((f32[1,360,90]{1,2,0:T(8,128)}), f32[16,360,90]{1,2,0:T(8,128)}) %all-gather.15.cloned.1.call-update) | async-done | bytes 2073616 | tf_op jit(solution)/shard_map/all_gather | solution.py:48
  161.1 6.8 %fusion.19 = f32[192,90]{1,0:T(8,128)S(1)} fusion(f32[16,360,90]{1,2,0:T(8,128)} %all-gather.15.cloned.1.call-done, f32[16,192,360]{2,1,0:T(8,128)} %gather_fusion, pred[16]{0:T(512)(128)(4,1)S(1)} %compare_and_fusion), kind=kOutput, calls=%fused_computation.20 | convolution fusion | flops 1195499520 | bytes 6566416 | tf_op jit(solution)/shard_map/dot_general | solution.py:49
  167.8 3.5 %collective-permute-start.7 = (f32[96,90]{1,0:T(8,128)S(1)}, f32[96,90]{1,0:T(8,128)S(1)}, u32[]{:S(2)}, u32[]{:S(2)}) collective-permute-start(f32[96,90]{1,0:T(8,128)S(1)} %constant_dynamic-slice_fusion.2), channel_id=1, source_target_pairs={{0,1},{1,0},{2,3},{3,2},{4,5},{5,4},{6,7},{7,6},{8,9},{9,8},{10,11... | collective-permute-start | bytes 103688 | tf_op jit(solution)/shard_map/ppermute | solution.py:54
  171.3 62.7 %all-gather.17.cloned.1.call-done = f32[16,360,90]{1,2,0:T(8,128)} async-done(((f32[1,360,90]{1,2,0:T(8,128)}), f32[16,360,90]{1,2,0:T(8,128)}) %all-gather.17.cloned.1.call-update) | async-done | bytes 2073616 | tf_op jit(solution)/shard_map/all_gather | solution.py:48
  234.1 6.8 %fusion.22 = f32[192,90]{1,0:T(8,128)S(1)} fusion(f32[16,360,90]{1,2,0:T(8,128)} %all-gather.17.cloned.1.call-done, f32[16,192,360]{2,1,0:T(8,128)} %gather_fusion, pred[16]{0:T(512)(128)(4,1)S(1)} %compare_and_fusion), kind=kOutput, calls=%fused_computation.21 | convolution fusion | flops 1195499520 | bytes 6566416 | tf_op jit(solution)/shard_map/dot_general | solution.py:49
  240.8 3.5 %collective-permute-start.8 = (f32[96,90]{1,0:T(8,128)S(1)}, f32[96,90]{1,0:T(8,128)S(1)}, u32[]{:S(2)}, u32[]{:S(2)}) collective-permute-start(f32[96,90]{1,0:T(8,128)S(1)} %constant_dynamic-slice_fusion.1), channel_id=1, source_target_pairs={{0,1},{1,0},{2,3},{3,2},{4,5},{5,4},{6,7},{7,6},{8,9},{9,8},{10,11... | collective-permute-start | bytes 103688 | tf_op jit(solution)/shard_map/ppermute | solution.py:54
  244.4 62.6 %all-gather.19.cloned.1.call-done = f32[16,360,90]{1,2,0:T(8,128)} async-done(((f32[1,360,90]{1,2,0:T(8,128)}), f32[16,360,90]{1,2,0:T(8,128)}) %all-gather.19.cloned.1.call-update) | async-done | bytes 2073616 | tf_op jit(solution)/shard_map/all_gather | solution.py:48
  306.9 6.8 %fusion.25 = f32[192,90]{1,0:T(8,128)S(1)} fusion(f32[16,360,90]{1,2,0:T(8,128)} %all-gather.19.cloned.1.call-done, f32[16,192,360]{2,1,0:T(8,128)} %gather_fusion, pred[16]{0:T(512)(128)(4,1)S(1)} %compare_and_fusion), kind=kOutput, calls=%fused_computation.22 | convolution fusion | flops 1195499520 | bytes 6566416 | tf_op jit(solution)/shard_map/dot_general | solution.py:49
  313.7 3.4 %collective-permute-start.9 = (f32[96,90]{1,0:T(8,128)S(1)}, f32[96,90]{1,0:T(8,128)S(1)}, u32[]{:S(2)}, u32[]{:S(2)}) collective-permute-start(f32[96,90]{1,0:T(8,128)S(1)} %constant_dynamic-slice_fusion), channel_id=1, source_target_pairs={{0,1},{1,0},{2,3},{3,2},{4,5},{5,4},{6,7},{7,6},{8,9},{9,8},{10,11... | collective-permute-start | bytes 103688 | tf_op jit(solution)/shard_map/ppermute | solution.py:54
  317.2 4.0 %collective-permute-done.9 = f32[96,90]{1,0:T(8,128)S(1)} collective-permute-done((f32[96,90]{1,0:T(8,128)S(1)}, f32[96,90]{1,0:T(8,128)S(1)}, u32[]{:S(2)}, u32[]{:S(2)}) %collective-permute-start.9) | collective-permute-done | bytes 34592 | tf_op jit(solution)/shard_map/ppermute | solution.py:54
  321.2 0.8 pad_maximum_fusion.1
  (29 shorter events, 0.7 us)
Async XLA Ops:
  6.5 83.2 %all-gather.13.cloned.1.call-start = ((), (), s32[]{:S(2)}) async-start(), calls=%async_computation | async-start | bytes 2506752 | tf_op jit(solution)/shard_map/all_gather | solution.py:48
  8.8 152.2 %all-gather.15.cloned.1.call-start = ((), (), s32[]{:S(2)}) async-start(), calls=%async_computation.1 | async-start | bytes 2506752 | tf_op jit(solution)/shard_map/all_gather | solution.py:48
  9.7 224.4 %all-gather.17.cloned.1.call-start = ((), (), s32[]{:S(2)}) async-start(), calls=%async_computation.2 | async-start | bytes 2506752 | tf_op jit(solution)/shard_map/all_gather | solution.py:48
  10.5 296.4 %all-gather.19.cloned.1.call-start = ((), (), s32[]{:S(2)}) async-start(), calls=%async_computation.3 | async-start | bytes 2506752 | tf_op jit(solution)/shard_map/all_gather | solution.py:48
  10.6 3.7 %collective-permute-start = (f32[192,360]{1,0:T(8,128)}, f32[192,360]{1,0:T(8,128)S(1)}, u32[]{:S(2)}, u32[]{:S(2)}) collective-permute-start(f32[192,360]{1,0:T(8,128)} %param.2), channel_id=1, source_target_pairs={{0,2},{2,0},{4,6},{6,4},{8,10},{10,8},{12,14},{14,12},{16,18},{18,... | collective-permute-start | bytes 829448 | tf_op jit(solution)/shard_map/ppermute | solution.py:14
  15.4 17.3 %collective-permute-start.1 = (f32[2,192,360]{2,1,0:T(8,128)S(1)}, f32[2,192,360]{2,1,0:T(8,128)S(1)}, u32[]{:S(2)}, u32[]{:S(2)}) collective-permute-start(f32[2,192,360]{2,1,0:T(8,128)S(1)} %maximum_select_fusion.1), channel_id=1, source_target_pairs={{0,4},{2,6},{4,0},{6,2},{8,12},{10,14},{12,8},{14,10},{16,20},{18,... | collective-permute-start | bytes 1658888 | tf_op jit(solution)/shard_map/ppermute | solution.py:16
  32.7 30.4 %collective-permute-start.3 = (f32[4,192,360]{2,1,0:T(8,128)S(1)}, f32[4,192,360]{2,1,0:T(8,128)S(1)}, u32[]{:S(2)}, u32[]{:S(2)}) collective-permute-start(f32[4,192,360]{2,1,0:T(8,128)S(1)} %maximum_select_fusion), channel_id=1, source_target_pairs={{0,8},{2,10},{4,12},{6,14},{8,16},{10,18},{12,20},{14,22},{16,24},... | collective-permute-start | bytes 3317768 | tf_op jit(solution)/shard_map/ppermute | solution.py:20
  36.2 29.1 %collective-permute-start.2 = (f32[4,192,360]{2,1,0:T(8,128)S(1)}, f32[4,192,360]{2,1,0:T(8,128)S(1)}, u32[]{:S(2)}, u32[]{:S(2)}) collective-permute-start(f32[4,192,360]{2,1,0:T(8,128)S(1)} %maximum_select_fusion), channel_id=1, source_target_pairs={{0,24},{2,26},{4,28},{6,30},{8,0},{10,2},{12,4},{14,6},{16,8},{18,... | collective-permute-start | bytes 3317768 | tf_op jit(solution)/shard_map/ppermute | solution.py:21
  63.1 16.8 %collective-permute-start.4 = (f32[4,96,360]{2,1,0:T(8,128)S(1)}, f32[4,96,360]{2,1,0:T(8,128)S(1)}, u32[]{:S(2)}, u32[]{:S(2)}) collective-permute-start(f32[4,96,360]{2,1,0:T(8,128)S(1)} %slice.26), channel_id=1, source_target_pairs={{0,8},{2,10},{4,12},{6,14},{8,16},{10,18},{12,20},{14,22},{16,24},... | collective-permute-start | bytes 1658888 | tf_op jit(solution)/shard_map/ppermute | solution.py:23
  65.4 15.8 %collective-permute-start.5 = (f32[4,96,360]{2,1,0:T(8,128)S(1)}, f32[4,96,360]{2,1,0:T(8,128)S(1)}, u32[]{:S(2)}, u32[]{:S(2)}) collective-permute-start(f32[4,96,360]{2,1,0:T(8,128)S(1)} %slice.27), channel_id=1, source_target_pairs={{0,24},{2,26},{4,28},{6,30},{8,0},{10,2},{12,4},{14,6},{16,8},{18,... | collective-permute-start | bytes 1658888 | tf_op jit(solution)/shard_map/ppermute | solution.py:24
  96.5 220.6 %collective-permute-start.6 = (f32[96,90]{1,0:T(8,128)S(1)}, f32[96,90]{1,0:T(8,128)S(1)}, u32[]{:S(2)}, u32[]{:S(2)}) collective-permute-start(f32[96,90]{1,0:T(8,128)S(1)} %constant_dynamic-slice_fusion.3), channel_id=1, source_target_pairs={{0,1},{1,0},{2,3},{3,2},{4,5},{5,4},{6,7},{7,6},{8,9},{9,8},{10,11... | collective-permute-start | bytes 103688 | tf_op jit(solution)/shard_map/ppermute | solution.py:54
  167.8 149.3 %collective-permute-start.7 = (f32[96,90]{1,0:T(8,128)S(1)}, f32[96,90]{1,0:T(8,128)S(1)}, u32[]{:S(2)}, u32[]{:S(2)}) collective-permute-start(f32[96,90]{1,0:T(8,128)S(1)} %constant_dynamic-slice_fusion.2), channel_id=1, source_target_pairs={{0,1},{1,0},{2,3},{3,2},{4,5},{5,4},{6,7},{7,6},{8,9},{9,8},{10,11... | collective-permute-start | bytes 103688 | tf_op jit(solution)/shard_map/ppermute | solution.py:54
  240.8 76.3 %collective-permute-start.8 = (f32[96,90]{1,0:T(8,128)S(1)}, f32[96,90]{1,0:T(8,128)S(1)}, u32[]{:S(2)}, u32[]{:S(2)}) collective-permute-start(f32[96,90]{1,0:T(8,128)S(1)} %constant_dynamic-slice_fusion.1), channel_id=1, source_target_pairs={{0,1},{1,0},{2,3},{3,2},{4,5},{5,4},{6,7},{7,6},{8,9},{9,8},{10,11... | collective-permute-start | bytes 103688 | tf_op jit(solution)/shard_map/ppermute | solution.py:54
  313.7 7.5 %collective-permute-start.9 = (f32[96,90]{1,0:T(8,128)S(1)}, f32[96,90]{1,0:T(8,128)S(1)}, u32[]{:S(2)}, u32[]{:S(2)}) collective-permute-start(f32[96,90]{1,0:T(8,128)S(1)} %constant_dynamic-slice_fusion), channel_id=1, source_target_pairs={{0,1},{1,0},{2,3},{3,2},{4,5},{5,4},{6,7},{7,6},{8,9},{9,8},{10,11... | collective-permute-start | bytes 103688 | tf_op jit(solution)/shard_map/ppermute | solution.py:54
Sparse Core Ops, SparseCore 0:
  9.4 78.5 all-gather.12
  90.1 70.8 all-gather.14
  163.1 70.8 all-gather.16
  236.0 70.9 all-gather.18

commit v6 on v4

--- a/solution.py
+++ b/solution.py
@@ -1,10 +1,15 @@
+import functools
+
 import jax
 import jax.numpy as jnp
 from jax import lax
+from jax.experimental import pallas as pl
+from jax.experimental.pallas import tpu as pltpu
 from jax.sharding import PartitionSpec as P
 
 FIRST_DOT_STEP = 5
 DOTS_PER_STEP = 5
+SHARE = 180
 
 
 def gather_col(block):
@@ -32,20 +37,52 @@
     return stack, place
 
 
+def _stacked_kernel(share, places, a_ref, b_ref, o_ref):
+    @pl.when(pl.program_id(0) == 0)
+    def _():
+        o_ref[...] = jnp.zeros_like(o_ref)
+
+    a = a_ref[0, :, :share]
+    o_ref[...] += jnp.dot(a, b_ref[0], precision=lax.Precision.HIGHEST,
+                          preferred_element_type=jnp.float32)
+
+
+def stacked_product(places, stack, gathered):
+    n, rows, kb = stack.shape
+    share, width = gathered.shape[1], gathered.shape[2]
+    grid_spec = pltpu.PrefetchScalarGridSpec(
+        num_scalar_prefetch=1,
+        grid=(n,),
+        in_specs=[
+            pl.BlockSpec((1, rows, kb), lambda b, pr: (pr[b], 0, 0)),
+            pl.BlockSpec((1, share, width), lambda b, pr: (b, 0, 0)),
+        ],
+        out_specs=pl.BlockSpec((rows, width), lambda b, pr: (0, 0)),
+    )
+    return pl.pallas_call(
+        functools.partial(_stacked_kernel, share),
+        grid_spec=grid_spec,
+        out_shape=jax.ShapeDtypeStruct((rows, width), jnp.float32),
+    )(places, stack, gathered)
+
+
 def local(amplitudes, integrals):
     n = lax.axis_size("row")
     me = lax.axis_index("row")
     d = lax.axis_index("depth")
-    kb = integrals.shape[0]
+    kb = integrals.shape[0] - SHARE
     rows = amplitudes.shape[0]
     half = rows // 2
 
     strip, place = gather_col(amplitudes)
+    upper = lax.all_gather(integrals[:SHARE], "row", axis=0, tiled=False)
+    places = jnp.stack([place(jnp.int32(k)) for k in range(n)]).astype(jnp.int32)
+    integrals = integrals[SHARE:]
 
     def product(block, owner, lo=0, hi=None):
         hi = kb if hi is None else hi
         cols = lax.dynamic_index_in_dim(strip, place(owner), axis=0, keepdims=False)
-        return jnp.dot(cols[:, lo:hi], block, precision=lax.Precision.HIGHEST,
+        return jnp.dot(cols[:, SHARE + lo:SHARE + hi], block, precision=lax.Precision.HIGHEST,
                        preferred_element_type=jnp.float32)
 
     fwd = [(i, (i + 1) % n) for i in range(n)]
@@ -80,6 +117,7 @@
         part = product(block, owner, lo, hi)
         total = part if total is None else total + part
 
+    total = total + stacked_product(places, strip, upper)
     mine = lax.dynamic_slice_in_dim(total, d * half, half, axis=0)
     other = lax.dynamic_slice_in_dim(total, (1 - d) * half, half, axis=0)
     other = lax.ppermute(other, "depth", [(0, 1), (1, 0)])

time: 157 us -> 191 us (1.22)
  Pallas kernels: 0 us -> 14.6 us
  between operations: 1.5 us -> 15.1 us
  waiting for transfers between devices: 40.5 us -> 51.3 us
  matrix products: 18.8 us -> 12.5 us
  local copies, waits for them, and re-layouts: 1.84 us -> 7.31 us
  starting transfers between devices: 89.5 us -> 85.2 us
    pallas_call x0 -> x1, Pallas kernels: none -> 14.6 us  [stacked_product(): pl.pallas_call(functools.partial(_stacked_kernel, share), grid_spec=grid_...]
    ppermute x1, waiting for transfers between devices: 1.14 us -> 14.5 us  [gather_col(): far = lax.ppermute(pair, 'col', [(i, i ^ 2) for i in range(n)])]
    dot_general x17, matrix products: 18.8 us -> 12.5 us  [product(): jnp.dot(cols[:, SHARE + lo:SHARE + hi], block, precision=lax.Precision.HI...]
    ppermute x7, starting transfers between devices: 44.6 us -> 40.3 us  [local(): behind = lax.ppermute(behind, 'row', bwd)]
    unnamed x10 -> x24, local copies, waits for them, and re-layouts: 0.02 us -> 2.46 us
    slice x0 -> x1, local copies, waits for them, and re-layouts: none -> 1.98 us  [local(): integrals = integrals[SHARE:]]
  transfers between devices with their start and end apart: 23 -> 24, of which waited for: 12 -> 11; matrix products, arithmetic and copies ran while one was open for 14% -> 9% of each run, Pallas kernels for 0% -> 0%
where the time goes in v6:
time: 191 us; the launch traced here: 190 us
  starting transfers between devices  85.2 us (45%)
  waiting for transfers between devices  51.3 us (27%)
  between operations  15.1 us (8%)
  Pallas kernels  14.6 us (8%)
  matrix products  12.5 us (7%)
  local copies, waits for them, and re-layouts  7.31 us (4%)
  other arithmetic  3.91 us (2%)
    ppermute x7, starting transfers between devices, local(): behind = lax.ppermute(behind, 'row', bwd)  40.3 us
    ppermute x7, waiting for transfers between devices, local(): ahead = lax.ppermute(ahead, 'row', fwd)  27 us
    ppermute x7, starting transfers between devices, local(): ahead = lax.ppermute(ahead, 'row', fwd)  15.3 us
    pallas_call x1, Pallas kernels, stacked_product(): pl.pallas_call(functools.partial(_stacked_kernel, share), grid_spec=grid_...  14.6 us
    ppermute x1, waiting for transfers between devices, gather_col(): far = lax.ppermute(pair, 'col', [(i, i ^ 2) for i in range(n)])  14.5 us
    dot_general x17, matrix products, product(): jnp.dot(cols[:, SHARE + lo:SHARE + hi], block, precision=lax.Precision.HI...  12.5 us
    ppermute x1, starting transfers between devices, local(): bottom = lax.ppermute(behind[m:], 'row', bwd)  5.6 us
    ppermute x1, waiting for transfers between devices, local(): other = lax.ppermute(other, 'depth', [(0, 1), (1, 0)])  5.17 us
  transfers between devices with their start and end apart: 24, of which 11 were waited for; matrix products, arithmetic and copies ran while one was open for 9% of the time, Pallas kernels for 0%

profile of v6, /device:TPU:6, one launch (start us, length us, event | category | flops | bytes accessed | tf_op | source)
XLA Modules:
  0.0 189.9 jit_solution(3346451919078152278)
XLA Ops:
  6.5 2.0 %fusion.36 = (f32[180,360]{1,0:T(8,128)}, f32[1,180,360]{2,1,0:T(8,128)}) fusion(f32[360,360]{1,0:T(8,128)} %param.3), kind=kLoop, calls=%fused_computation.63 | loop fusion | bytes 1036800 | tf_op jit(solution)/shard_map/slice | solution.py:80
  8.6 1.9 %collective-permute-start = (f32[192,360]{1,0:T(8,128)S(1)}, f32[192,360]{1,0:T(8,128)S(1)}, u32[]{:S(2)}, u32[]{:S(2)}) collective-permute-start(f32[192,360]{1,0:T(8,128)S(1)} %copy-done.2), channel_id=1, source_target_pairs={{0,2},{2,0},{4,6},{6,4},{8,10},{10,8},{12,14},{14,12},{16,18},{18,... | collective-permute-start | bytes 829448 | tf_op jit(solution)/shard_map/ppermute | solution.py:20
  12.1 2.7 %collective-permute-start.1 = (f32[2,192,360]{2,1,0:T(8,128)S(1)}, f32[2,192,360]{2,1,0:T(8,128)S(1)}, u32[]{:S(2)}, u32[]{:S(2)}) collective-permute-start(f32[2,192,360]{2,1,0:T(8,128)S(1)} %maximum_select_fusion.1), channel_id=1, source_target_pairs={{0,4},{2,6},{4,0},{6,2},{8,12},{10,14},{12,8},{14,10},{16,20},{18,... | collective-permute-start | bytes 1658888 | tf_op jit(solution)/shard_map/ppermute | solution.py:22
  14.9 14.5 %collective-permute-done.1 = f32[2,192,360]{2,1,0:T(8,128)S(1)} collective-permute-done((f32[2,192,360]{2,1,0:T(8,128)S(1)}, f32[2,192,360]{2,1,0:T(8,128)S(1)}, u32[]{:S(2)}, u32[]{:S(2)}) %collective-permute-start.1) | collective-permute-done | bytes 552992 | tf_op jit(solution)/shard_map/ppermute | solution.py:22
  29.4 3.5 %collective-permute-start.3 = (f32[4,192,360]{2,1,0:T(8,128)S(1)}, f32[4,192,360]{2,1,0:T(8,128)S(1)}, u32[]{:S(2)}, u32[]{:S(2)}) collective-permute-start(f32[4,192,360]{2,1,0:T(8,128)S(1)} %maximum_select_fusion), channel_id=1, source_target_pairs={{0,8},{2,10},{4,12},{6,14},{8,16},{10,18},{12,20},{14,22},{16,24},... | collective-permute-start | bytes 3317768 | tf_op jit(solution)/shard_map/ppermute | solution.py:26
  32.9 3.6 %collective-permute-start.2 = (f32[4,192,360]{2,1,0:T(8,128)S(1)}, f32[4,192,360]{2,1,0:T(8,128)S(1)}, u32[]{:S(2)}, u32[]{:S(2)}) collective-permute-start(f32[4,192,360]{2,1,0:T(8,128)S(1)} %maximum_select_fusion), channel_id=1, source_target_pairs={{0,24},{2,26},{4,28},{6,30},{8,0},{10,2},{12,4},{14,6},{16,8},{18,... | collective-permute-start | bytes 3317768 | tf_op jit(solution)/shard_map/ppermute | solution.py:27
  36.5 3.8 %collective-permute-start.6 = (f32[180,360]{1,0:T(8,128)S(1)}, f32[180,360]{1,0:T(8,128)S(1)}, u32[]{:S(2)}, u32[]{:S(2)}) collective-permute-start(f32[180,360]{1,0:T(8,128)S(1)} %copy-done.11), channel_id=1, source_target_pairs={{0,32},{32,64},{64,96},{96,128},{128,160},{160,192},{192,224},{224... | collective-permute-start | bytes 777608 | tf_op jit(solution)/shard_map/ppermute | solution.py:98
  40.3 9.5 %collective-permute-start.7 = (f32[180,360]{1,0:T(8,128)S(1)}, f32[180,360]{1,0:T(8,128)S(1)}, u32[]{:S(2)}, u32[]{:S(2)}) collective-permute-start(f32[180,360]{1,0:T(8,128)S(1)} %copy-done.11), channel_id=1, source_target_pairs={{0,480},{32,0},{64,32},{96,64},{128,96},{160,128},{192,160},{224,1... | collective-permute-start | bytes 777608 | tf_op jit(solution)/shard_map/ppermute | solution.py:100
  49.8 10.4 %collective-permute-done.6 = f32[180,360]{1,0:T(8,128)S(1)} collective-permute-done((f32[180,360]{1,0:T(8,128)S(1)}, f32[180,360]{1,0:T(8,128)S(1)}, u32[]{:S(2)}, u32[]{:S(2)}) %collective-permute-start.6) | collective-permute-done | bytes 259232 | tf_op jit(solution)/shard_map/ppermute | solution.py:98
  60.2 1.9 %collective-permute-start.8 = (f32[180,360]{1,0:T(8,128)S(1)}, f32[180,360]{1,0:T(8,128)S(1)}, u32[]{:S(2)}, u32[]{:S(2)}) collective-permute-start(f32[180,360]{1,0:T(8,128)S(1)} %collective-permute-done.6), channel_id=1, source_target_pairs={{0,32},{32,64},{64,96},{96,128},{128,160},{160,192},{192,224},{224... | collective-permute-start | bytes 777608 | tf_op jit(solution)/shard_map/ppermute | solution.py:98
  62.2 5.1 %collective-permute-start.9 = (f32[180,360]{1,0:T(8,128)S(1)}, f32[180,360]{1,0:T(8,128)S(1)}, u32[]{:S(2)}, u32[]{:S(2)}) collective-permute-start(f32[180,360]{1,0:T(8,128)S(1)} %collective-permute-done.7), channel_id=1, source_target_pairs={{0,480},{32,0},{64,32},{96,64},{128,96},{160,128},{192,160},{224,1... | collective-permute-start | bytes 777608 | tf_op jit(solution)/shard_map/ppermute | solution.py:100
  68.2 2.6 %collective-permute-start.4 = (f32[4,96,360]{2,1,0:T(8,128)}, f32[4,96,360]{2,1,0:T(8,128)}, u32[]{:S(2)}, u32[]{:S(2)}) collective-permute-start(f32[4,96,360]{2,1,0:T(8,128)} %slice.92), channel_id=1, source_target_pairs={{0,8},{2,10},{4,12},{6,14},{8,16},{10,18},{12,20},{14,22},{16,24},... | collective-permute-start | bytes 1658888 | tf_op jit(solution)/shard_map/ppermute | solution.py:29
  71.7 4.4 %collective-permute-start.5 = (f32[4,96,360]{2,1,0:T(8,128)}, f32[4,96,360]{2,1,0:T(8,128)}, u32[]{:S(2)}, u32[]{:S(2)}) collective-permute-start(f32[4,96,360]{2,1,0:T(8,128)} %slice.93), channel_id=1, source_target_pairs={{0,24},{2,26},{4,28},{6,30},{8,0},{10,2},{12,4},{14,6},{16,8},{18,... | collective-permute-start | bytes 1658888 | tf_op jit(solution)/shard_map/ppermute | solution.py:30
  78.5 1.9 %collective-permute-start.10 = (f32[180,360]{1,0:T(8,128)S(1)}, f32[180,360]{1,0:T(8,128)}, u32[]{:S(2)}, u32[]{:S(2)}) collective-permute-start(f32[180,360]{1,0:T(8,128)S(1)} %collective-permute-done.8), channel_id=1, source_target_pairs={{0,32},{32,64},{64,96},{96,128},{128,160},{160,192},{192,224},{224... | collective-permute-start | bytes 777608 | tf_op jit(solution)/shard_map/ppermute | solution.py:98
  80.4 5.1 %collective-permute-start.13 = (f32[180,360]{1,0:T(8,128)S(1)}, f32[180,360]{1,0:T(8,128)}, u32[]{:S(2)}, u32[]{:S(2)}) collective-permute-start(f32[180,360]{1,0:T(8,128)S(1)} %collective-permute-done.9), channel_id=1, source_target_pairs={{0,480},{32,0},{64,32},{96,64},{128,96},{160,128},{192,160},{224,1... | collective-permute-start | bytes 777608 | tf_op jit(solution)/shard_map/ppermute | solution.py:100
  85.6 10.0 %collective-permute-done.10 = f32[180,360]{1,0:T(8,128)} collective-permute-done((f32[180,360]{1,0:T(8,128)S(1)}, f32[180,360]{1,0:T(8,128)}, u32[]{:S(2)}, u32[]{:S(2)}) %collective-permute-start.10) | collective-permute-done | bytes 259232 | tf_op jit(solution)/shard_map/ppermute | solution.py:98
  95.6 1.9 %collective-permute-start.11 = (f32[180,360]{1,0:T(8,128)}, f32[180,360]{1,0:T(8,128)}, u32[]{:S(2)}, u32[]{:S(2)}) collective-permute-start(f32[180,360]{1,0:T(8,128)} %collective-permute-done.10), channel_id=1, source_target_pairs={{0,32},{32,64},{64,96},{96,128},{128,160},{160,192},{192,224},{224... | collective-permute-start | bytes 777608 | tf_op jit(solution)/shard_map/ppermute | solution.py:98
  97.6 5.1 %collective-permute-start.14 = (f32[180,360]{1,0:T(8,128)}, f32[180,360]{1,0:T(8,128)}, u32[]{:S(2)}, u32[]{:S(2)}) collective-permute-start(f32[180,360]{1,0:T(8,128)} %collective-permute-done.13), channel_id=1, source_target_pairs={{0,480},{32,0},{64,32},{96,64},{128,96},{160,128},{192,160},{224,1... | collective-permute-start | bytes 777608 | tf_op jit(solution)/shard_map/ppermute | solution.py:100
  104.5 3.8 %collective-permute-done.11 = f32[180,360]{1,0:T(8,128)} collective-permute-done((f32[180,360]{1,0:T(8,128)}, f32[180,360]{1,0:T(8,128)}, u32[]{:S(2)}, u32[]{:S(2)}) %collective-permute-start.11) | collective-permute-done | bytes 259232 | tf_op jit(solution)/shard_map/ppermute | solution.py:98
  108.3 1.9 %collective-permute-start.12 = (f32[180,360]{1,0:T(8,128)}, f32[180,360]{1,0:T(8,128)S(1)}, u32[]{:S(2)}, u32[]{:S(2)}) collective-permute-start(f32[180,360]{1,0:T(8,128)} %collective-permute-done.11), channel_id=1, source_target_pairs={{0,32},{32,64},{64,96},{96,128},{128,160},{160,192},{192,224},{224... | collective-permute-start | bytes 777608 | tf_op jit(solution)/shard_map/ppermute | solution.py:98
  110.2 5.1 %collective-permute-start.15 = (f32[180,360]{1,0:T(8,128)}, f32[180,360]{1,0:T(8,128)S(1)}, u32[]{:S(2)}, u32[]{:S(2)}) collective-permute-start(f32[180,360]{1,0:T(8,128)} %collective-permute-done.14), channel_id=1, source_target_pairs={{0,480},{32,0},{64,32},{96,64},{128,96},{160,128},{192,160},{224,1... | collective-permute-start | bytes 777608 | tf_op jit(solution)/shard_map/ppermute | solution.py:100
  115.4 2.1 %pad_maximum_fusion.a_ref = f32[16,192,360]{2,1,0:T(8,128)S(1)} fusion(f32[4,192,360]{2,1,0:T(8,128)S(1)} %collective-permute-done.3, f32[4,96,360]{2,1,0:T(8,128)} %collective-permute-done.5, f32[4,96,360]{2,1,0:T(8,128)} %collective-permute-done.4, f32[4,192,360]{2,1,0:T(8,128)S(1)} %collective-permute-done.2, f32[4,192,360]{2,1,0:T(8,128)S(1)} %maximum_select_fusion), kind=kLoop, calls=%fused_computation | loop fusion | flops 4423680 | bytes 8847360 | tf_op jit(solution)/shard_map/concatenate | solution.py:32
  117.9 1.7 copy-done
  122.4 1.9 %collective-permute-start.16 = (f32[180,360]{1,0:T(8,128)S(1)}, f32[180,360]{1,0:T(8,128)S(1)}, u32[]{:S(2)}, u32[]{:S(2)}) collective-permute-start(f32[180,360]{1,0:T(8,128)S(1)} %collective-permute-done.12), channel_id=1, source_target_pairs={{0,32},{32,64},{64,96},{96,128},{128,160},{160,192},{192,224},{224... | collective-permute-start | bytes 777608 | tf_op jit(solution)/shard_map/ppermute | solution.py:98
  124.3 5.1 %collective-permute-start.17 = (f32[180,360]{1,0:T(8,128)S(1)}, f32[180,360]{1,0:T(8,128)S(1)}, u32[]{:S(2)}, u32[]{:S(2)}) collective-permute-start(f32[180,360]{1,0:T(8,128)S(1)} %collective-permute-done.15), channel_id=1, source_target_pairs={{0,480},{32,0},{64,32},{96,64},{128,96},{160,128},{192,160},{224,1... | collective-permute-start | bytes 777608 | tf_op jit(solution)/shard_map/ppermute | solution.py:100
  135.9 1.9 %collective-permute-start.18 = (f32[180,360]{1,0:T(8,128)S(1)}, f32[180,360]{1,0:T(8,128)S(1)}, u32[]{:S(2)}, u32[]{:S(2)}) collective-permute-start(f32[180,360]{1,0:T(8,128)S(1)} %collective-permute-done.16), channel_id=1, source_target_pairs={{0,32},{32,64},{64,96},{96,128},{128,160},{160,192},{192,224},{224... | collective-permute-start | bytes 777608 | tf_op jit(solution)/shard_map/ppermute | solution.py:98
  137.9 5.1 %collective-permute-start.19 = (f32[180,360]{1,0:T(8,128)S(1)}, f32[180,360]{1,0:T(8,128)S(1)}, u32[]{:S(2)}, u32[]{:S(2)}) collective-permute-start(f32[180,360]{1,0:T(8,128)S(1)} %collective-permute-done.17), channel_id=1, source_target_pairs={{0,480},{32,0},{64,32},{96,64},{128,96},{160,128},{192,160},{224,1... | collective-permute-start | bytes 777608 | tf_op jit(solution)/shard_map/ppermute | solution.py:100
  147.1 1.9 %collective-permute-start.20 = (f32[90,360]{1,0:T(8,128)S(1)}, f32[90,360]{1,0:T(8,128)S(1)}, u32[]{:S(2)}, u32[]{:S(2)}) collective-permute-start(f32[90,360]{1,0:T(8,128)S(1)} %slice.87), channel_id=1, source_target_pairs={{0,32},{32,64},{64,96},{96,128},{128,160},{160,192},{192,224},{224... | collective-permute-start | bytes 388808 | tf_op jit(solution)/shard_map/ppermute | solution.py:104
  149.0 5.6 %collective-permute-start.21 = (f32[90,360]{1,0:T(8,128)S(1)}, f32[90,360]{1,0:T(8,128)S(1)}, u32[]{:S(2)}, u32[]{:S(2)}) collective-permute-start(f32[90,360]{1,0:T(8,128)S(1)} %slice.88), channel_id=1, source_target_pairs={{0,480},{32,0},{64,32},{96,64},{128,96},{160,128},{192,160},{224,1... | collective-permute-start | bytes 388808 | tf_op jit(solution)/shard_map/ppermute | solution.py:105
  158.2 14.6 %shard_map.28 = f32[192,360]{1,0:T(8,128)} custom-call(s32[16]{0:T(128)} %stack.85.places, f32[16,192,360]{2,1,0:T(8,128)} %copy-done, f32[16,180,360]{2,1,0:T(8,128)} %all-gather.4.cloned.1.call-done.b_ref), custom_call_target="tpu_custom_call" | custom-call | tf_op jit(solution)/shard_map/pallas_call | solution.py:62
  173.8 3.4 %collective-permute-start.22 = (f32[96,360]{1,0:T(8,128)S(1)}, f32[96,360]{1,0:T(8,128)S(1)}, u32[]{:S(2)}, u32[]{:S(2)}) collective-permute-start(f32[96,360]{1,0:T(8,128)S(1)} %constant_dynamic-slice_fusion), channel_id=1, source_target_pairs={{0,1},{1,0},{2,3},{3,2},{4,5},{5,4},{6,7},{7,6},{8,9},{9,8},{10,11... | collective-permute-start | bytes 414728 | tf_op jit(solution)/shard_map/ppermute | solution.py:123
  177.2 5.2 %collective-permute-done.22 = f32[96,360]{1,0:T(8,128)S(1)} collective-permute-done((f32[96,360]{1,0:T(8,128)S(1)}, f32[96,360]{1,0:T(8,128)S(1)}, u32[]{:S(2)}, u32[]{:S(2)}) %collective-permute-start.22) | collective-permute-done | bytes 138272 | tf_op jit(solution)/shard_map/ppermute | solution.py:123
  (72 shorter events, 25.3 us)
Async XLA Ops:
  6.5 2.0 %copy-start.2 = (f32[192,360]{1,0:T(8,128)S(1)}, f32[192,360]{1,0:T(8,128)}, u32[]{:S(2)}) copy-start(f32[192,360]{1,0:T(8,128)} %param.2) | copy-start | bytes 829444
  6.5 151.7 %all-gather.4.cloned.1.call-start = ((), (), s32[]{:S(2)}) async-start(), calls=%async_computation | async-start | bytes 4804608 | tf_op jit(solution)/shard_map/all_gather | solution.py:78
  8.6 3.5 %collective-permute-start = (f32[192,360]{1,0:T(8,128)S(1)}, f32[192,360]{1,0:T(8,128)S(1)}, u32[]{:S(2)}, u32[]{:S(2)}) collective-permute-start(f32[192,360]{1,0:T(8,128)S(1)} %copy-done.2), channel_id=1, source_target_pairs={{0,2},{2,0},{4,6},{6,4},{8,10},{10,8},{12,14},{14,12},{16,18},{18,... | collective-permute-start | bytes 829448 | tf_op jit(solution)/shard_map/ppermute | solution.py:20
  12.1 17.3 %collective-permute-start.1 = (f32[2,192,360]{2,1,0:T(8,128)S(1)}, f32[2,192,360]{2,1,0:T(8,128)S(1)}, u32[]{:S(2)}, u32[]{:S(2)}) collective-permute-start(f32[2,192,360]{2,1,0:T(8,128)S(1)} %maximum_select_fusion.1), channel_id=1, source_target_pairs={{0,4},{2,6},{4,0},{6,2},{8,12},{10,14},{12,8},{14,10},{16,20},{18,... | collective-permute-start | bytes 1658888 | tf_op jit(solution)/shard_map/ppermute | solution.py:22
  14.8 21.6 %copy-start.11 = (f32[180,360]{1,0:T(8,128)S(1)}, f32[180,360]{1,0:T(8,128)}, u32[]{:S(2)}) copy-start(f32[180,360]{1,0:T(8,128)} %get-tuple-element.41) | copy-start | bytes 777604
  29.4 37.9 %collective-permute-start.3 = (f32[4,192,360]{2,1,0:T(8,128)S(1)}, f32[4,192,360]{2,1,0:T(8,128)S(1)}, u32[]{:S(2)}, u32[]{:S(2)}) collective-permute-start(f32[4,192,360]{2,1,0:T(8,128)S(1)} %maximum_select_fusion), channel_id=1, source_target_pairs={{0,8},{2,10},{4,12},{6,14},{8,16},{10,18},{12,20},{14,22},{16,24},... | collective-permute-start | bytes 3317768 | tf_op jit(solution)/shard_map/ppermute | solution.py:26
  32.9 38.0 %collective-permute-start.2 = (f32[4,192,360]{2,1,0:T(8,128)S(1)}, f32[4,192,360]{2,1,0:T(8,128)S(1)}, u32[]{:S(2)}, u32[]{:S(2)}) collective-permute-start(f32[4,192,360]{2,1,0:T(8,128)S(1)} %maximum_select_fusion), channel_id=1, source_target_pairs={{0,24},{2,26},{4,28},{6,30},{8,0},{10,2},{12,4},{14,6},{16,8},{18,... | collective-permute-start | bytes 3317768 | tf_op jit(solution)/shard_map/ppermute | solution.py:27
  36.5 23.7 %collective-permute-start.6 = (f32[180,360]{1,0:T(8,128)S(1)}, f32[180,360]{1,0:T(8,128)S(1)}, u32[]{:S(2)}, u32[]{:S(2)}) collective-permute-start(f32[180,360]{1,0:T(8,128)S(1)} %copy-done.11), channel_id=1, source_target_pairs={{0,32},{32,64},{64,96},{96,128},{128,160},{160,192},{192,224},{224... | collective-permute-start | bytes 777608 | tf_op jit(solution)/shard_map/ppermute | solution.py:98
  40.3 21.8 %collective-permute-start.7 = (f32[180,360]{1,0:T(8,128)S(1)}, f32[180,360]{1,0:T(8,128)S(1)}, u32[]{:S(2)}, u32[]{:S(2)}) collective-permute-start(f32[180,360]{1,0:T(8,128)S(1)} %copy-done.11), channel_id=1, source_target_pairs={{0,480},{32,0},{64,32},{96,64},{128,96},{160,128},{192,160},{224,1... | collective-permute-start | bytes 777608 | tf_op jit(solution)/shard_map/ppermute | solution.py:100
  60.2 10.6 %copy-start.3 = (f32[180,360]{1,0:T(8,128)}, f32[180,360]{1,0:T(8,128)S(1)}, u32[]{:S(2)}) copy-start(f32[180,360]{1,0:T(8,128)S(1)} %collective-permute-done.6) | copy-start | bytes 777604
  60.2 17.6 %collective-permute-start.8 = (f32[180,360]{1,0:T(8,128)S(1)}, f32[180,360]{1,0:T(8,128)S(1)}, u32[]{:S(2)}, u32[]{:S(2)}) collective-permute-start(f32[180,360]{1,0:T(8,128)S(1)} %collective-permute-done.6), channel_id=1, source_target_pairs={{0,32},{32,64},{64,96},{96,128},{128,160},{160,192},{192,224},{224... | collective-permute-start | bytes 777608 | tf_op jit(solution)/shard_map/ppermute | solution.py:98
  62.2 33.5 %copy-start.7 = (f32[180,360]{1,0:T(8,128)}, f32[180,360]{1,0:T(8,128)S(1)}, u32[]{:S(2)}) copy-start(f32[180,360]{1,0:T(8,128)S(1)} %collective-permute-done.7) | copy-start | bytes 777604
  62.2 18.2 %collective-permute-start.9 = (f32[180,360]{1,0:T(8,128)S(1)}, f32[180,360]{1,0:T(8,128)S(1)}, u32[]{:S(2)}, u32[]{:S(2)}) collective-permute-start(f32[180,360]{1,0:T(8,128)S(1)} %collective-permute-done.7), channel_id=1, source_target_pairs={{0,480},{32,0},{64,32},{96,64},{128,96},{160,128},{192,160},{224,1... | collective-permute-start | bytes 777608 | tf_op jit(solution)/shard_map/ppermute | solution.py:100
  68.2 47.1 %collective-permute-start.4 = (f32[4,96,360]{2,1,0:T(8,128)}, f32[4,96,360]{2,1,0:T(8,128)}, u32[]{:S(2)}, u32[]{:S(2)}) collective-permute-start(f32[4,96,360]{2,1,0:T(8,128)} %slice.92), channel_id=1, source_target_pairs={{0,8},{2,10},{4,12},{6,14},{8,16},{10,18},{12,20},{14,22},{16,24},... | collective-permute-start | bytes 1658888 | tf_op jit(solution)/shard_map/ppermute | solution.py:29
  71.7 43.6 %collective-permute-start.5 = (f32[4,96,360]{2,1,0:T(8,128)}, f32[4,96,360]{2,1,0:T(8,128)}, u32[]{:S(2)}, u32[]{:S(2)}) collective-permute-start(f32[4,96,360]{2,1,0:T(8,128)} %slice.93), channel_id=1, source_target_pairs={{0,24},{2,26},{4,28},{6,30},{8,0},{10,2},{12,4},{14,6},{16,8},{18,... | collective-permute-start | bytes 1658888 | tf_op jit(solution)/shard_map/ppermute | solution.py:30
  78.5 17.1 %collective-permute-start.10 = (f32[180,360]{1,0:T(8,128)S(1)}, f32[180,360]{1,0:T(8,128)}, u32[]{:S(2)}, u32[]{:S(2)}) collective-permute-start(f32[180,360]{1,0:T(8,128)S(1)} %collective-permute-done.8), channel_id=1, source_target_pairs={{0,32},{32,64},{64,96},{96,128},{128,160},{160,192},{192,224},{224... | collective-permute-start | bytes 777608 | tf_op jit(solution)/shard_map/ppermute | solution.py:98
  80.4 17.1 %copy-start.9 = (f32[180,360]{1,0:T(8,128)}, f32[180,360]{1,0:T(8,128)S(1)}, u32[]{:S(2)}) copy-start(f32[180,360]{1,0:T(8,128)S(1)} %collective-permute-done.9) | copy-start | bytes 777604
  80.4 17.1 %collective-permute-start.13 = (f32[180,360]{1,0:T(8,128)S(1)}, f32[180,360]{1,0:T(8,128)}, u32[]{:S(2)}, u32[]{:S(2)}) collective-permute-start(f32[180,360]{1,0:T(8,128)S(1)} %collective-permute-done.9), channel_id=1, source_target_pairs={{0,480},{32,0},{64,32},{96,64},{128,96},{160,128},{192,160},{224,1... | collective-permute-start | bytes 777608 | tf_op jit(solution)/shard_map/ppermute | solution.py:100
  95.6 12.7 %collective-permute-start.11 = (f32[180,360]{1,0:T(8,128)}, f32[180,360]{1,0:T(8,128)}, u32[]{:S(2)}, u32[]{:S(2)}) collective-permute-start(f32[180,360]{1,0:T(8,128)} %collective-permute-done.10), channel_id=1, source_target_pairs={{0,32},{32,64},{64,96},{96,128},{128,160},{160,192},{192,224},{224... | collective-permute-start | bytes 777608 | tf_op jit(solution)/shard_map/ppermute | solution.py:98
  97.6 12.6 %collective-permute-start.14 = (f32[180,360]{1,0:T(8,128)}, f32[180,360]{1,0:T(8,128)}, u32[]{:S(2)}, u32[]{:S(2)}) collective-permute-start(f32[180,360]{1,0:T(8,128)} %collective-permute-done.13), channel_id=1, source_target_pairs={{0,480},{32,0},{64,32},{96,64},{128,96},{160,128},{192,160},{224,1... | collective-permute-start | bytes 777608 | tf_op jit(solution)/shard_map/ppermute | solution.py:100
  108.3 14.1 %collective-permute-start.12 = (f32[180,360]{1,0:T(8,128)}, f32[180,360]{1,0:T(8,128)S(1)}, u32[]{:S(2)}, u32[]{:S(2)}) collective-permute-start(f32[180,360]{1,0:T(8,128)} %collective-permute-done.11), channel_id=1, source_target_pairs={{0,32},{32,64},{64,96},{96,128},{128,160},{160,192},{192,224},{224... | collective-permute-start | bytes 777608 | tf_op jit(solution)/shard_map/ppermute | solution.py:98
  110.2 12.1 %collective-permute-start.15 = (f32[180,360]{1,0:T(8,128)}, f32[180,360]{1,0:T(8,128)S(1)}, u32[]{:S(2)}, u32[]{:S(2)}) collective-permute-start(f32[180,360]{1,0:T(8,128)} %collective-permute-done.14), channel_id=1, source_target_pairs={{0,480},{32,0},{64,32},{96,64},{128,96},{160,128},{192,160},{224,1... | collective-permute-start | bytes 777608 | tf_op jit(solution)/shard_map/ppermute | solution.py:100
  117.5 2.1 %copy-start = (f32[16,192,360]{2,1,0:T(8,128)}, f32[16,192,360]{2,1,0:T(8,128)S(1)}, u32[]{:S(2)}) copy-start(f32[16,192,360]{2,1,0:T(8,128)S(1)} %pad_maximum_fusion.a_ref) | copy-start | bytes 13271044
  117.5 2.1 %copy-start.1 = (f32[360,360]{1,0:T(8,128)S(1)}, f32[360,360]{1,0:T(8,128)}, u32[]{:S(2)}) copy-start(f32[360,360]{1,0:T(8,128)} %param.3) | copy-start | bytes 1555204
  117.5 2.7 %copy-start.4 = (f32[180,360]{1,0:T(8,128)S(1)}, f32[180,360]{1,0:T(8,128)}, u32[]{:S(2)}) copy-start(f32[180,360]{1,0:T(8,128)} %copy-done.3) | copy-start | bytes 777604
  122.4 13.5 %collective-permute-start.16 = (f32[180,360]{1,0:T(8,128)S(1)}, f32[180,360]{1,0:T(8,128)S(1)}, u32[]{:S(2)}, u32[]{:S(2)}) collective-permute-start(f32[180,360]{1,0:T(8,128)S(1)} %collective-permute-done.12), channel_id=1, source_target_pairs={{0,32},{32,64},{64,96},{96,128},{128,160},{160,192},{192,224},{224... | collective-permute-start | bytes 777608 | tf_op jit(solution)/shard_map/ppermute | solution.py:98
  124.3 11.6 %collective-permute-start.17 = (f32[180,360]{1,0:T(8,128)S(1)}, f32[180,360]{1,0:T(8,128)S(1)}, u32[]{:S(2)}, u32[]{:S(2)}) collective-permute-start(f32[180,360]{1,0:T(8,128)S(1)} %collective-permute-done.15), channel_id=1, source_target_pairs={{0,480},{32,0},{64,32},{96,64},{128,96},{160,128},{192,160},{224,1... | collective-permute-start | bytes 777608 | tf_op jit(solution)/shard_map/ppermute | solution.py:100
  135.9 9.7 %collective-permute-start.18 = (f32[180,360]{1,0:T(8,128)S(1)}, f32[180,360]{1,0:T(8,128)S(1)}, u32[]{:S(2)}, u32[]{:S(2)}) collective-permute-start(f32[180,360]{1,0:T(8,128)S(1)} %collective-permute-done.16), channel_id=1, source_target_pairs={{0,32},{32,64},{64,96},{96,128},{128,160},{160,192},{192,224},{224... | collective-permute-start | bytes 777608 | tf_op jit(solution)/shard_map/ppermute | solution.py:98
  137.9 9.2 %collective-permute-start.19 = (f32[180,360]{1,0:T(8,128)S(1)}, f32[180,360]{1,0:T(8,128)S(1)}, u32[]{:S(2)}, u32[]{:S(2)}) collective-permute-start(f32[180,360]{1,0:T(8,128)S(1)} %collective-permute-done.17), channel_id=1, source_target_pairs={{0,480},{32,0},{64,32},{96,64},{128,96},{160,128},{192,160},{224,1... | collective-permute-start | bytes 777608 | tf_op jit(solution)/shard_map/ppermute | solution.py:100
  147.1 8.7 %collective-permute-start.20 = (f32[90,360]{1,0:T(8,128)S(1)}, f32[90,360]{1,0:T(8,128)S(1)}, u32[]{:S(2)}, u32[]{:S(2)}) collective-permute-start(f32[90,360]{1,0:T(8,128)S(1)} %slice.87), channel_id=1, source_target_pairs={{0,32},{32,64},{64,96},{96,128},{128,160},{160,192},{192,224},{224... | collective-permute-start | bytes 388808 | tf_op jit(solution)/shard_map/ppermute | solution.py:104
  149.0 8.3 %collective-permute-start.21 = (f32[90,360]{1,0:T(8,128)S(1)}, f32[90,360]{1,0:T(8,128)S(1)}, u32[]{:S(2)}, u32[]{:S(2)}) collective-permute-start(f32[90,360]{1,0:T(8,128)S(1)} %slice.88), channel_id=1, source_target_pairs={{0,480},{32,0},{64,32},{96,64},{128,96},{160,128},{192,160},{224,1... | collective-permute-start | bytes 388808 | tf_op jit(solution)/shard_map/ppermute | solution.py:105
  173.8 8.5 %collective-permute-start.22 = (f32[96,360]{1,0:T(8,128)S(1)}, f32[96,360]{1,0:T(8,128)S(1)}, u32[]{:S(2)}, u32[]{:S(2)}) collective-permute-start(f32[96,360]{1,0:T(8,128)S(1)} %constant_dynamic-slice_fusion), channel_id=1, source_target_pairs={{0,1},{1,0},{2,3},{3,2},{4,5},{5,4},{6,7},{7,6},{8,9},{9,8},{10,11... | collective-permute-start | bytes 414728 | tf_op jit(solution)/shard_map/ppermute | solution.py:123
  (4 other events, 4.0 us)
Sparse Core Ops, SparseCore 0:
  9.4 98.4 all-gather.3

commit v7 on v4

--- a/solution.py
+++ b/solution.py
@@ -1,6 +1,10 @@
+import functools
+
 import jax
 import jax.numpy as jnp
 from jax import lax
+from jax.experimental import pallas as pl
+from jax.experimental.pallas import tpu as pltpu
 from jax.sharding import PartitionSpec as P
 
 FIRST_DOT_STEP = 5
@@ -32,6 +36,42 @@
     return stack, place
 
 
+def _accumulate_kernel(lo, hi, first, place_ref, a_ref, b_ref, *refs):
+    o_ref = refs[-1]
+    part = jnp.dot(a_ref[0, :, lo:hi], b_ref[...], precision=lax.Precision.HIGHEST,
+                   preferred_element_type=jnp.float32)
+    if first:
+        o_ref[...] = part
+    else:
+        o_ref[...] = refs[0][...] + part
+
+
+def accumulate(total, stack, block, where, lo, hi):
+    _, rows, kb = stack.shape
+    width = block.shape[1]
+    first = total is None
+    in_specs = [
+        pl.BlockSpec((1, rows, kb), lambda i, pr: (pr[0], 0, 0)),
+        pl.BlockSpec(block.shape, lambda i, pr: (0, 0)),
+    ]
+    args = [stack, block]
+    if not first:
+        in_specs.append(pl.BlockSpec((rows, width), lambda i, pr: (0, 0)))
+        args.append(total)
+    grid_spec = pltpu.PrefetchScalarGridSpec(
+        num_scalar_prefetch=1,
+        grid=(1,),
+        in_specs=in_specs,
+        out_specs=pl.BlockSpec((rows, width), lambda i, pr: (0, 0)),
+    )
+    return pl.pallas_call(
+        functools.partial(_accumulate_kernel, lo, hi, first),
+        grid_spec=grid_spec,
+        out_shape=jax.ShapeDtypeStruct((rows, width), jnp.float32),
+        input_output_aliases={} if first else {3: 0},
+    )(jnp.reshape(where, (1,)).astype(jnp.int32), *args)
+
+
 def local(amplitudes, integrals):
     n = lax.axis_size("row")
     me = lax.axis_index("row")
@@ -42,11 +82,6 @@
 
     strip, place = gather_col(amplitudes)
 
-    def product(block, owner, lo=0, hi=None):
-        hi = kb if hi is None else hi
-        cols = lax.dynamic_index_in_dim(strip, place(owner), axis=0, keepdims=False)
-        return jnp.dot(cols[:, lo:hi], block, precision=lax.Precision.HIGHEST,
-                       preferred_element_type=jnp.float32)
 
     fwd = [(i, (i + 1) % n) for i in range(n)]
     bwd = [(i, (i - 1) % n) for i in range(n)]
@@ -71,14 +106,12 @@
             ahead, behind = top, bottom
         if step >= FIRST_DOT_STEP:
             for block, owner, lo, hi in pending[:DOTS_PER_STEP]:
-                part = product(block, owner, lo, hi)
-                total = part if total is None else total + part
+                total = accumulate(total, strip, block, place(owner), lo, hi)
             pending = pending[DOTS_PER_STEP:]
             total, ahead, behind = lax.optimization_barrier((total, ahead, behind))
         pending = pending + arrived
     for block, owner, lo, hi in pending:
-        part = product(block, owner, lo, hi)
-        total = part if total is None else total + part
+        total = accumulate(total, strip, block, place(owner), lo, hi)
 
     mine = lax.dynamic_slice_in_dim(total, d * half, half, axis=0)
     other = lax.dynamic_slice_in_dim(total, (1 - d) * half, half, axis=0)

time: 157 us -> 176 us (1.12)
  Pallas kernels: 0 us -> 44.7 us
  matrix products: 18.8 us -> 0 us
  starting transfers between devices: 89.5 us -> 83 us
  waiting for transfers between devices: 40.5 us -> 35.3 us
  other arithmetic: 3.96 us -> 6.27 us
    pallas_call x0 -> x17, Pallas kernels: none -> 44.7 us  [accumulate(): pl.pallas_call(functools.partial(_accumulate_kernel, lo, hi, first), grid...]
    dot_general x17 -> x0, matrix products: 18.8 us -> none  [product(): jnp.dot(cols[:, lo:hi], block, precision=lax.Precision.HIGHEST, preferred...]
    ppermute x7, starting transfers between devices: 44.6 us -> 37.5 us  [local(): behind = lax.ppermute(behind, 'row', bwd)]
    ppermute x7, waiting for transfers between devices: 27.2 us -> 22.7 us  [local(): ahead = lax.ppermute(ahead, 'row', fwd)]
    ppermute x1, waiting for transfers between devices: 0.01 us -> 2.82 us  [gather_col(): opp_b = lax.ppermute(above[:, h:], 'col', down)]
    ppermute x7, waiting for transfers between devices: 2.67 us -> 0.02 us  [local(): behind = lax.ppermute(behind, 'row', bwd)]
  transfers between devices with their start and end apart: 23 -> 23, of which waited for: 12 -> 8; matrix products, arithmetic and copies ran while one was open for 14% -> 3% of each run, Pallas kernels for 0% -> 23%
where the time goes in v7:
time: 176 us; the launch traced here: 174 us
  starting transfers between devices  83 us (47%)
  Pallas kernels  44.7 us (25%)
  waiting for transfers between devices  35.3 us (20%)
  other arithmetic  6.27 us (4%)
  local copies, waits for them, and re-layouts  3.46 us (2%)
    pallas_call x17, Pallas kernels, accumulate(): pl.pallas_call(functools.partial(_accumulate_kernel, lo, hi, first), grid...  44.7 us
    ppermute x7, starting transfers between devices, local(): behind = lax.ppermute(behind, 'row', bwd)  37.5 us
    ppermute x7, waiting for transfers between devices, local(): ahead = lax.ppermute(ahead, 'row', fwd)  22.7 us
    ppermute x7, starting transfers between devices, local(): ahead = lax.ppermute(ahead, 'row', fwd)  17 us
    ppermute x1, waiting for transfers between devices, local(): other = lax.ppermute(other, 'depth', [(0, 1), (1, 0)])  5.53 us
    ppermute x1, starting transfers between devices, local(): bottom = lax.ppermute(behind[m:], 'row', bwd)  4.68 us
    ppermute x1, starting transfers between devices, gather_col(): above = lax.ppermute(quad, 'col', down)  3.57 us
    ppermute x1, starting transfers between devices, gather_col(): opp_b = lax.ppermute(above[:, h:], 'col', down)  3.56 us
  transfers between devices with their start and end apart: 23, of which 8 were waited for; matrix products, arithmetic and copies ran while one was open for 3% of the time, Pallas kernels for 23%

profile of v7, /device:TPU:6, one launch (start us, length us, event | category | flops | bytes accessed | tf_op | source)
XLA Modules:
  0.0 174.2 jit_solution(2809253342008538288)
XLA Ops:
  5.0 2.7 %collective-permute-start.1 = (f32[2,192,360]{2,1,0:T(8,128)S(1)}, f32[2,192,360]{2,1,0:T(8,128)S(1)}, u32[]{:S(2)}, u32[]{:S(2)}) collective-permute-start(f32[2,192,360]{2,1,0:T(8,128)S(1)} %maximum_select_fusion.1), channel_id=1, source_target_pairs={{0,4},{2,6},{4,0},{6,2},{8,12},{10,14},{12,8},{14,10},{16,20},{18,... | collective-permute-start | bytes 1658888 | tf_op jit(solution)/shard_map/ppermute | solution.py:21
  7.7 3.8 %collective-permute-start.8 = (f32[360,360]{1,0:T(8,128)S(1)}, f32[360,360]{1,0:T(8,128)}, u32[]{:S(2)}, u32[]{:S(2)}) collective-permute-start(f32[360,360]{1,0:T(8,128)S(1)} %copy-done.2), channel_id=1, source_target_pairs={{0,32},{32,64},{64,96},{96,128},{128,160},{160,192},{192,224},{224... | collective-permute-start | bytes 1555208 | tf_op jit(solution)/shard_map/ppermute | solution.py:96
  11.5 9.5 %collective-permute-start.6 = (f32[360,360]{1,0:T(8,128)S(1)}, f32[360,360]{1,0:T(8,128)}, u32[]{:S(2)}, u32[]{:S(2)}) collective-permute-start(f32[360,360]{1,0:T(8,128)S(1)} %copy-done.2), channel_id=1, source_target_pairs={{0,480},{32,0},{64,32},{96,64},{128,96},{160,128},{192,160},{224,1... | collective-permute-start | bytes 1555208 | tf_op jit(solution)/shard_map/ppermute | solution.py:98
  21.0 10.7 %collective-permute-done.8.b_ref = f32[360,360]{1,0:T(8,128)} collective-permute-done((f32[360,360]{1,0:T(8,128)S(1)}, f32[360,360]{1,0:T(8,128)}, u32[]{:S(2)}, u32[]{:S(2)}) %collective-permute-start.8) | collective-permute-done | bytes 518432 | tf_op jit(solution)/shard_map/ppermute | solution.py:96
  33.7 5.1 %collective-permute-start.7 = (f32[360,360]{1,0:T(8,128)}, f32[360,360]{1,0:T(8,128)}, u32[]{:S(2)}, u32[]{:S(2)}) collective-permute-start(f32[360,360]{1,0:T(8,128)} %collective-permute-done.6.b_ref), channel_id=1, source_target_pairs={{0,480},{32,0},{64,32},{96,64},{128,96},{160,128},{192,160},{224,1... | collective-permute-start | bytes 1555208 | tf_op jit(solution)/shard_map/ppermute | solution.py:98
  39.0 3.5 %collective-permute-start.3 = (f32[4,192,360]{2,1,0:T(8,128)S(1)}, f32[4,192,360]{2,1,0:T(8,128)S(1)}, u32[]{:S(2)}, u32[]{:S(2)}) collective-permute-start(f32[4,192,360]{2,1,0:T(8,128)S(1)} %maximum_select_fusion), channel_id=1, source_target_pairs={{0,8},{2,10},{4,12},{6,14},{8,16},{10,18},{12,20},{14,22},{16,24},... | collective-permute-start | bytes 3317768 | tf_op jit(solution)/shard_map/ppermute | solution.py:25
  42.5 3.6 %collective-permute-start.2 = (f32[4,192,360]{2,1,0:T(8,128)S(1)}, f32[4,192,360]{2,1,0:T(8,128)S(1)}, u32[]{:S(2)}, u32[]{:S(2)}) collective-permute-start(f32[4,192,360]{2,1,0:T(8,128)S(1)} %maximum_select_fusion), channel_id=1, source_target_pairs={{0,24},{2,26},{4,28},{6,30},{8,0},{10,2},{12,4},{14,6},{16,8},{18,... | collective-permute-start | bytes 3317768 | tf_op jit(solution)/shard_map/ppermute | solution.py:26
  46.0 2.9 %collective-permute-done.9.b_ref = f32[360,360]{1,0:T(8,128)} collective-permute-done((f32[360,360]{1,0:T(8,128)}, f32[360,360]{1,0:T(8,128)}, u32[]{:S(2)}, u32[]{:S(2)}) %collective-permute-start.9) | collective-permute-done | bytes 518432 | tf_op jit(solution)/shard_map/ppermute | solution.py:96
  50.9 5.1 %collective-permute-start.13 = (f32[360,360]{1,0:T(8,128)}, f32[360,360]{1,0:T(8,128)S(1)}, u32[]{:S(2)}, u32[]{:S(2)}) collective-permute-start(f32[360,360]{1,0:T(8,128)} %collective-permute-done.7.b_ref), channel_id=1, source_target_pairs={{0,480},{32,0},{64,32},{96,64},{128,96},{160,128},{192,160},{224,1... | collective-permute-start | bytes 1555208 | tf_op jit(solution)/shard_map/ppermute | solution.py:98
  56.0 9.1 %collective-permute-done.10.b_ref = f32[360,360]{1,0:T(8,128)S(1)} collective-permute-done((f32[360,360]{1,0:T(8,128)}, f32[360,360]{1,0:T(8,128)S(1)}, u32[]{:S(2)}, u32[]{:S(2)}) %collective-permute-start.10) | collective-permute-done | bytes 518432 | tf_op jit(solution)/shard_map/ppermute | solution.py:96
  67.0 5.1 %collective-permute-start.14 = (f32[360,360]{1,0:T(8,128)S(1)}, f32[360,360]{1,0:T(8,128)}, u32[]{:S(2)}, u32[]{:S(2)}) collective-permute-start(f32[360,360]{1,0:T(8,128)S(1)} %collective-permute-done.13.b_ref), channel_id=1, source_target_pairs={{0,480},{32,0},{64,32},{96,64},{128,96},{160,128},{192,160},{224,1... | collective-permute-start | bytes 1555208 | tf_op jit(solution)/shard_map/ppermute | solution.py:98
  73.0 3.5 %collective-permute-start.4 = (f32[4,96,360]{2,1,0:T(8,128)}, f32[4,96,360]{2,1,0:T(8,128)}, u32[]{:S(2)}, u32[]{:S(2)}) collective-permute-start(f32[4,96,360]{2,1,0:T(8,128)} %slice.16), channel_id=1, source_target_pairs={{0,8},{2,10},{4,12},{6,14},{8,16},{10,18},{12,20},{14,22},{16,24},... | collective-permute-start | bytes 1658888 | tf_op jit(solution)/shard_map/ppermute | solution.py:28
  77.4 3.6 %collective-permute-start.5 = (f32[4,96,360]{2,1,0:T(8,128)}, f32[4,96,360]{2,1,0:T(8,128)}, u32[]{:S(2)}, u32[]{:S(2)}) collective-permute-start(f32[4,96,360]{2,1,0:T(8,128)} %slice.17), channel_id=1, source_target_pairs={{0,24},{2,26},{4,28},{6,30},{8,0},{10,2},{12,4},{14,6},{16,8},{18,... | collective-permute-start | bytes 1658888 | tf_op jit(solution)/shard_map/ppermute | solution.py:29
  82.9 5.1 %collective-permute-start.15 = (f32[360,360]{1,0:T(8,128)}, f32[360,360]{1,0:T(8,128)}, u32[]{:S(2)}, u32[]{:S(2)}) collective-permute-start(f32[360,360]{1,0:T(8,128)} %collective-permute-done.14.b_ref), channel_id=1, source_target_pairs={{0,480},{32,0},{64,32},{96,64},{128,96},{160,128},{192,160},{224,1... | collective-permute-start | bytes 1555208 | tf_op jit(solution)/shard_map/ppermute | solution.py:98
  88.6 2.8 %collective-permute-done.5 = f32[4,96,360]{2,1,0:T(8,128)} collective-permute-done((f32[4,96,360]{2,1,0:T(8,128)}, f32[4,96,360]{2,1,0:T(8,128)}, u32[]{:S(2)}, u32[]{:S(2)}) %collective-permute-start.5) | collective-permute-done | bytes 552992 | tf_op jit(solution)/shard_map/ppermute | solution.py:29
  91.4 3.5 %pad_maximum_fusion.a_ref = f32[16,192,360]{2,1,0:T(8,128)} fusion(f32[4,192,360]{2,1,0:T(8,128)S(1)} %collective-permute-done.3, f32[4,96,360]{2,1,0:T(8,128)} %collective-permute-done.5, f32[4,96,360]{2,1,0:T(8,128)} %collective-permute-done.4, f32[4,192,360]{2,1,0:T(8,128)S(1)} %collective-permute-done.2, f32[4,192,360]{2,1,0:T(8,128)S(1)} %maximum_select_fusion), kind=kLoop, calls=%fused_computation | loop fusion | flops 4423680 | bytes 8847360 | tf_op jit(solution)/shard_map/concatenate | solution.py:31
  97.5 2.7 %shard_map.29.refs_0_ = f32[192,360]{1,0:T(8,128)} custom-call(s32[1]{0:T(128)} %bitcast.7.place_ref, f32[16,192,360]{2,1,0:T(8,128)} %pad_maximum_fusion.a_ref, f32[360,360]{1,0:T(8,128)} %collective-permute-done.8.b_ref, f32[192,360]{1,0:T(8,128)} %shard_map.28.refs_0_), custom_call_target="tpu_custom_call", output_to_operand_aliasing={{}: (3, {})} | custom-call | tf_op jit(solution)/shard_map/pallas_call | solution.py:67
  100.2 2.7 %shard_map.30.refs_0_ = f32[192,360]{1,0:T(8,128)} custom-call(s32[1]{0:T(128)} %bitcast.6.place_ref, f32[16,192,360]{2,1,0:T(8,128)} %pad_maximum_fusion.a_ref, f32[360,360]{1,0:T(8,128)} %collective-permute-done.6.b_ref, f32[192,360]{1,0:T(8,128)} %shard_map.29.refs_0_), custom_call_target="tpu_custom_call", output_to_operand_aliasing={{}: (3, {})} | custom-call | tf_op jit(solution)/shard_map/pallas_call | solution.py:67
  102.8 2.7 %shard_map.31.refs_0_ = f32[192,360]{1,0:T(8,128)} custom-call(s32[1]{0:T(128)} %bitcast.5.place_ref, f32[16,192,360]{2,1,0:T(8,128)} %pad_maximum_fusion.a_ref, f32[360,360]{1,0:T(8,128)} %collective-permute-done.9.b_ref, f32[192,360]{1,0:T(8,128)} %shard_map.30.refs_0_), custom_call_target="tpu_custom_call", output_to_operand_aliasing={{}: (3, {})} | custom-call | tf_op jit(solution)/shard_map/pallas_call | solution.py:67
  105.5 2.7 %shard_map.32.refs_0_ = f32[192,360]{1,0:T(8,128)} custom-call(s32[1]{0:T(128)} %bitcast.4.place_ref, f32[16,192,360]{2,1,0:T(8,128)} %pad_maximum_fusion.a_ref, f32[360,360]{1,0:T(8,128)} %collective-permute-done.7.b_ref, f32[192,360]{1,0:T(8,128)} %shard_map.31.refs_0_), custom_call_target="tpu_custom_call", output_to_operand_aliasing={{}: (3, {})} | custom-call | tf_op jit(solution)/shard_map/pallas_call | solution.py:67
  110.4 3.6 %collective-permute-start.17 = (f32[360,360]{1,0:T(8,128)}, f32[360,360]{1,0:T(8,128)S(1)}, u32[]{:S(2)}, u32[]{:S(2)}) collective-permute-start(f32[360,360]{1,0:T(8,128)} %collective-permute-done.12.b_ref), channel_id=1, source_target_pairs={{0,32},{32,64},{64,96},{96,128},{128,160},{160,192},{192,224},{224... | collective-permute-start | bytes 1555208 | tf_op jit(solution)/shard_map/ppermute | solution.py:96
  114.3 2.7 %shard_map.33.refs_0_ = f32[192,360]{1,0:T(8,128)} custom-call(s32[1]{0:T(128)} %bitcast.15.place_ref, f32[16,192,360]{2,1,0:T(8,128)} %pad_maximum_fusion.a_ref, f32[360,360]{1,0:T(8,128)} %copy-done.3, f32[192,360]{1,0:T(8,128)} %shard_map.32.refs_0_), custom_call_target="tpu_custom_call", output_to_operand_aliasing={{}: (3, {})} | custom-call | tf_op jit(solution)/shard_map/pallas_call | solution.py:67
  117.0 2.7 %shard_map.34.refs_0_ = f32[192,360]{1,0:T(8,128)} custom-call(s32[1]{0:T(128)} %bitcast.14.place_ref, f32[16,192,360]{2,1,0:T(8,128)} %pad_maximum_fusion.a_ref, f32[360,360]{1,0:T(8,128)} %copy-done.4, f32[192,360]{1,0:T(8,128)} %shard_map.33.refs_0_), custom_call_target="tpu_custom_call", output_to_operand_aliasing={{}: (3, {})} | custom-call | tf_op jit(solution)/shard_map/pallas_call | solution.py:67
  129.7 5.3 %collective-permute-start.19 = (f32[360,360]{1,0:T(8,128)S(1)}, f32[360,360]{1,0:T(8,128)S(1)}, u32[]{:S(2)}, u32[]{:S(2)}) collective-permute-start(f32[360,360]{1,0:T(8,128)S(1)} %collective-permute-done.16.b_ref), channel_id=1, source_target_pairs={{0,480},{32,0},{64,32},{96,64},{128,96},{160,128},{192,160},{224,1... | collective-permute-start | bytes 1555208 | tf_op jit(solution)/shard_map/ppermute | solution.py:98
  135.1 2.7 %shard_map.38.refs_0_ = f32[192,360]{1,0:T(8,128)} custom-call(s32[1]{0:T(128)} %bitcast.10.place_ref, f32[16,192,360]{2,1,0:T(8,128)} %pad_maximum_fusion.a_ref, f32[360,360]{1,0:T(8,128)} %collective-permute-done.15.b_ref, f32[192,360]{1,0:T(8,128)} %shard_map.37.refs_0_), custom_call_target="tpu_custom_call", output_to_operand_aliasing={{}: (3, {})} | custom-call | tf_op jit(solution)/shard_map/pallas_call | solution.py:67
  137.8 2.7 %shard_map.39.refs_0_ = f32[192,360]{1,0:T(8,128)} custom-call(s32[1]{0:T(128)} %bitcast.9.place_ref, f32[16,192,360]{2,1,0:T(8,128)} %pad_maximum_fusion.a_ref, f32[360,360]{1,0:T(8,128)} %copy-done.6, f32[192,360]{1,0:T(8,128)} %shard_map.38.refs_0_), custom_call_target="tpu_custom_call", output_to_operand_aliasing={{}: (3, {})} | custom-call | tf_op jit(solution)/shard_map/pallas_call | solution.py:67
  140.5 2.7 %shard_map.40.refs_0_ = f32[192,360]{1,0:T(8,128)} custom-call(s32[1]{0:T(128)} %bitcast.3.place_ref, f32[16,192,360]{2,1,0:T(8,128)} %pad_maximum_fusion.a_ref, f32[360,360]{1,0:T(8,128)} %copy-done.5, f32[192,360]{1,0:T(8,128)} %shard_map.39.refs_0_), custom_call_target="tpu_custom_call", output_to_operand_aliasing={{}: (3, {})} | custom-call | tf_op jit(solution)/shard_map/pallas_call | solution.py:67
  143.2 4.7 %collective-permute-start.20 = (f32[180,360]{1,0:T(8,128)S(1)}, f32[180,360]{1,0:T(8,128)S(1)}, u32[]{:S(2)}, u32[]{:S(2)}) collective-permute-start(f32[180,360]{1,0:T(8,128)S(1)} %slice.14), channel_id=1, source_target_pairs={{0,480},{32,0},{64,32},{96,64},{128,96},{160,128},{192,160},{224,1... | collective-permute-start | bytes 777608 | tf_op jit(solution)/shard_map/ppermute | solution.py:103
  150.1 2.7 %shard_map.41.refs_0_ = f32[192,360]{1,0:T(8,128)} custom-call(s32[1]{0:T(128)} %bitcast.17.place_ref, f32[16,192,360]{2,1,0:T(8,128)} %pad_maximum_fusion.a_ref, f32[360,360]{1,0:T(8,128)} %copy-done, f32[192,360]{1,0:T(8,128)} %shard_map.40.refs_0_), custom_call_target="tpu_custom_call", output_to_operand_aliasing={{}: (3, {})} | custom-call | tf_op jit(solution)/shard_map/pallas_call | solution.py:67
  152.7 2.7 %shard_map.42.refs_0_ = f32[192,360]{1,0:T(8,128)} custom-call(s32[1]{0:T(128)} %bitcast.16.place_ref, f32[16,192,360]{2,1,0:T(8,128)} %pad_maximum_fusion.a_ref, f32[360,360]{1,0:T(8,128)} %copy-done.1, f32[192,360]{1,0:T(8,128)} %shard_map.41.refs_0_), custom_call_target="tpu_custom_call", output_to_operand_aliasing={{}: (3, {})} | custom-call | tf_op jit(solution)/shard_map/pallas_call | solution.py:67
  164.0 3.0 %collective-permute-start.22 = (f32[96,360]{1,0:T(8,128)S(1)}, f32[96,360]{1,0:T(8,128)S(1)}, u32[]{:S(2)}, u32[]{:S(2)}) collective-permute-start(f32[96,360]{1,0:T(8,128)S(1)} %constant_dynamic-slice_fusion), channel_id=1, source_target_pairs={{0,1},{1,0},{2,3},{3,2},{4,5},{5,4},{6,7},{7,6},{8,9},{9,8},{10,11... | collective-permute-start | bytes 414728 | tf_op jit(solution)/shard_map/ppermute | solution.py:118
  167.0 5.5 %collective-permute-done.22 = f32[96,360]{1,0:T(8,128)S(1)} collective-permute-done((f32[96,360]{1,0:T(8,128)S(1)}, f32[96,360]{1,0:T(8,128)S(1)}, u32[]{:S(2)}, u32[]{:S(2)}) %collective-permute-start.22) | collective-permute-done | bytes 138272 | tf_op jit(solution)/shard_map/ppermute | solution.py:118
  (58 shorter events, 41.6 us)
Async XLA Ops:
  0.0 7.7 %copy-start.2 = (f32[360,360]{1,0:T(8,128)S(1)}, f32[360,360]{1,0:T(8,128)}, u32[]{:S(2)}) copy-start(f32[360,360]{1,0:T(8,128)} %b_ref.1) | copy-start | bytes 1555204
  0.0 3.8 %collective-permute-start = (f32[192,360]{1,0:T(8,128)}, f32[192,360]{1,0:T(8,128)S(1)}, u32[]{:S(2)}, u32[]{:S(2)}) collective-permute-start(f32[192,360]{1,0:T(8,128)} %param.2), channel_id=1, source_target_pairs={{0,2},{2,0},{4,6},{6,4},{8,10},{10,8},{12,14},{14,12},{16,18},{18,... | collective-permute-start | bytes 829448 | tf_op jit(solution)/shard_map/ppermute | solution.py:19
  5.0 33.9 %collective-permute-start.1 = (f32[2,192,360]{2,1,0:T(8,128)S(1)}, f32[2,192,360]{2,1,0:T(8,128)S(1)}, u32[]{:S(2)}, u32[]{:S(2)}) collective-permute-start(f32[2,192,360]{2,1,0:T(8,128)S(1)} %maximum_select_fusion.1), channel_id=1, source_target_pairs={{0,4},{2,6},{4,0},{6,2},{8,12},{10,14},{12,8},{14,10},{16,20},{18,... | collective-permute-start | bytes 1658888 | tf_op jit(solution)/shard_map/ppermute | solution.py:21
  7.7 24.1 %collective-permute-start.8 = (f32[360,360]{1,0:T(8,128)S(1)}, f32[360,360]{1,0:T(8,128)}, u32[]{:S(2)}, u32[]{:S(2)}) collective-permute-start(f32[360,360]{1,0:T(8,128)S(1)} %copy-done.2), channel_id=1, source_target_pairs={{0,32},{32,64},{64,96},{96,128},{128,160},{160,192},{192,224},{224... | collective-permute-start | bytes 1555208 | tf_op jit(solution)/shard_map/ppermute | solution.py:96
  11.5 22.1 %collective-permute-start.6 = (f32[360,360]{1,0:T(8,128)S(1)}, f32[360,360]{1,0:T(8,128)}, u32[]{:S(2)}, u32[]{:S(2)}) collective-permute-start(f32[360,360]{1,0:T(8,128)S(1)} %copy-done.2), channel_id=1, source_target_pairs={{0,480},{32,0},{64,32},{96,64},{128,96},{160,128},{192,160},{224,1... | collective-permute-start | bytes 1555208 | tf_op jit(solution)/shard_map/ppermute | solution.py:98
  31.8 17.2 %collective-permute-start.9 = (f32[360,360]{1,0:T(8,128)}, f32[360,360]{1,0:T(8,128)}, u32[]{:S(2)}, u32[]{:S(2)}) collective-permute-start(f32[360,360]{1,0:T(8,128)} %collective-permute-done.8.b_ref), channel_id=1, source_target_pairs={{0,32},{32,64},{64,96},{96,128},{128,160},{160,192},{192,224},{224... | collective-permute-start | bytes 1555208 | tf_op jit(solution)/shard_map/ppermute | solution.py:96
  33.7 17.2 %collective-permute-start.7 = (f32[360,360]{1,0:T(8,128)}, f32[360,360]{1,0:T(8,128)}, u32[]{:S(2)}, u32[]{:S(2)}) collective-permute-start(f32[360,360]{1,0:T(8,128)} %collective-permute-done.6.b_ref), channel_id=1, source_target_pairs={{0,480},{32,0},{64,32},{96,64},{128,96},{160,128},{192,160},{224,1... | collective-permute-start | bytes 1555208 | tf_op jit(solution)/shard_map/ppermute | solution.py:98
  39.0 33.2 %collective-permute-start.3 = (f32[4,192,360]{2,1,0:T(8,128)S(1)}, f32[4,192,360]{2,1,0:T(8,128)S(1)}, u32[]{:S(2)}, u32[]{:S(2)}) collective-permute-start(f32[4,192,360]{2,1,0:T(8,128)S(1)} %maximum_select_fusion), channel_id=1, source_target_pairs={{0,8},{2,10},{4,12},{6,14},{8,16},{10,18},{12,20},{14,22},{16,24},... | collective-permute-start | bytes 3317768 | tf_op jit(solution)/shard_map/ppermute | solution.py:25
  42.5 34.0 %collective-permute-start.2 = (f32[4,192,360]{2,1,0:T(8,128)S(1)}, f32[4,192,360]{2,1,0:T(8,128)S(1)}, u32[]{:S(2)}, u32[]{:S(2)}) collective-permute-start(f32[4,192,360]{2,1,0:T(8,128)S(1)} %maximum_select_fusion), channel_id=1, source_target_pairs={{0,24},{2,26},{4,28},{6,30},{8,0},{10,2},{12,4},{14,6},{16,8},{18,... | collective-permute-start | bytes 3317768 | tf_op jit(solution)/shard_map/ppermute | solution.py:26
  48.9 16.1 %collective-permute-start.10 = (f32[360,360]{1,0:T(8,128)}, f32[360,360]{1,0:T(8,128)S(1)}, u32[]{:S(2)}, u32[]{:S(2)}) collective-permute-start(f32[360,360]{1,0:T(8,128)} %collective-permute-done.9.b_ref), channel_id=1, source_target_pairs={{0,32},{32,64},{64,96},{96,128},{128,160},{160,192},{192,224},{224... | collective-permute-start | bytes 1555208 | tf_op jit(solution)/shard_map/ppermute | solution.py:96
  50.9 16.1 %collective-permute-start.13 = (f32[360,360]{1,0:T(8,128)}, f32[360,360]{1,0:T(8,128)S(1)}, u32[]{:S(2)}, u32[]{:S(2)}) collective-permute-start(f32[360,360]{1,0:T(8,128)} %collective-permute-done.7.b_ref), channel_id=1, source_target_pairs={{0,480},{32,0},{64,32},{96,64},{128,96},{160,128},{192,160},{224,1... | collective-permute-start | bytes 1555208 | tf_op jit(solution)/shard_map/ppermute | solution.py:98
  65.1 11.4 %copy-start.3 = (f32[360,360]{1,0:T(8,128)}, f32[360,360]{1,0:T(8,128)S(1)}, u32[]{:S(2)}) copy-start(f32[360,360]{1,0:T(8,128)S(1)} %collective-permute-done.10.b_ref) | copy-start | bytes 1555204
  65.1 15.9 %collective-permute-start.11 = (f32[360,360]{1,0:T(8,128)S(1)}, f32[360,360]{1,0:T(8,128)}, u32[]{:S(2)}, u32[]{:S(2)}) collective-permute-start(f32[360,360]{1,0:T(8,128)S(1)} %collective-permute-done.10.b_ref), channel_id=1, source_target_pairs={{0,32},{32,64},{64,96},{96,128},{128,160},{160,192},{192,224},{224... | collective-permute-start | bytes 1555208 | tf_op jit(solution)/shard_map/ppermute | solution.py:96
  67.0 14.0 %copy-start.4 = (f32[360,360]{1,0:T(8,128)}, f32[360,360]{1,0:T(8,128)S(1)}, u32[]{:S(2)}) copy-start(f32[360,360]{1,0:T(8,128)S(1)} %collective-permute-done.13.b_ref) | copy-start | bytes 1555204
  67.0 15.9 %collective-permute-start.14 = (f32[360,360]{1,0:T(8,128)S(1)}, f32[360,360]{1,0:T(8,128)}, u32[]{:S(2)}, u32[]{:S(2)}) collective-permute-start(f32[360,360]{1,0:T(8,128)S(1)} %collective-permute-done.13.b_ref), channel_id=1, source_target_pairs={{0,480},{32,0},{64,32},{96,64},{128,96},{160,128},{192,160},{224,1... | collective-permute-start | bytes 1555208 | tf_op jit(solution)/shard_map/ppermute | solution.py:98
  73.0 15.6 %collective-permute-start.4 = (f32[4,96,360]{2,1,0:T(8,128)}, f32[4,96,360]{2,1,0:T(8,128)}, u32[]{:S(2)}, u32[]{:S(2)}) collective-permute-start(f32[4,96,360]{2,1,0:T(8,128)} %slice.16), channel_id=1, source_target_pairs={{0,8},{2,10},{4,12},{6,14},{8,16},{10,18},{12,20},{14,22},{16,24},... | collective-permute-start | bytes 1658888 | tf_op jit(solution)/shard_map/ppermute | solution.py:28
  77.4 14.1 %collective-permute-start.5 = (f32[4,96,360]{2,1,0:T(8,128)}, f32[4,96,360]{2,1,0:T(8,128)}, u32[]{:S(2)}, u32[]{:S(2)}) collective-permute-start(f32[4,96,360]{2,1,0:T(8,128)} %slice.17), channel_id=1, source_target_pairs={{0,24},{2,26},{4,28},{6,30},{8,0},{10,2},{12,4},{14,6},{16,8},{18,... | collective-permute-start | bytes 1658888 | tf_op jit(solution)/shard_map/ppermute | solution.py:29
  81.0 27.2 %collective-permute-start.12 = (f32[360,360]{1,0:T(8,128)}, f32[360,360]{1,0:T(8,128)}, u32[]{:S(2)}, u32[]{:S(2)}) collective-permute-start(f32[360,360]{1,0:T(8,128)} %collective-permute-done.11.b_ref), channel_id=1, source_target_pairs={{0,32},{32,64},{64,96},{96,128},{128,160},{160,192},{192,224},{224... | collective-permute-start | bytes 1555208 | tf_op jit(solution)/shard_map/ppermute | solution.py:96
  82.9 25.3 %collective-permute-start.15 = (f32[360,360]{1,0:T(8,128)}, f32[360,360]{1,0:T(8,128)}, u32[]{:S(2)}, u32[]{:S(2)}) collective-permute-start(f32[360,360]{1,0:T(8,128)} %collective-permute-done.14.b_ref), channel_id=1, source_target_pairs={{0,480},{32,0},{64,32},{96,64},{128,96},{160,128},{192,160},{224,1... | collective-permute-start | bytes 1555208 | tf_op jit(solution)/shard_map/ppermute | solution.py:98
  108.2 19.5 %collective-permute-start.16 = (f32[360,360]{1,0:T(8,128)}, f32[360,360]{1,0:T(8,128)S(1)}, u32[]{:S(2)}, u32[]{:S(2)}) collective-permute-start(f32[360,360]{1,0:T(8,128)} %collective-permute-done.15.b_ref), channel_id=1, source_target_pairs={{0,480},{32,0},{64,32},{96,64},{128,96},{160,128},{192,160},{224,1... | collective-permute-start | bytes 1555208 | tf_op jit(solution)/shard_map/ppermute | solution.py:98
  110.4 17.3 %collective-permute-start.17 = (f32[360,360]{1,0:T(8,128)}, f32[360,360]{1,0:T(8,128)S(1)}, u32[]{:S(2)}, u32[]{:S(2)}) collective-permute-start(f32[360,360]{1,0:T(8,128)} %collective-permute-done.12.b_ref), channel_id=1, source_target_pairs={{0,32},{32,64},{64,96},{96,128},{128,160},{160,192},{192,224},{224... | collective-permute-start | bytes 1555208 | tf_op jit(solution)/shard_map/ppermute | solution.py:96
  127.7 10.1 %copy-start.5 = (f32[360,360]{1,0:T(8,128)}, f32[360,360]{1,0:T(8,128)S(1)}, u32[]{:S(2)}) copy-start(f32[360,360]{1,0:T(8,128)S(1)} %collective-permute-done.16.b_ref) | copy-start | bytes 1555204
  127.7 10.1 %copy-start.6 = (f32[360,360]{1,0:T(8,128)}, f32[360,360]{1,0:T(8,128)S(1)}, u32[]{:S(2)}) copy-start(f32[360,360]{1,0:T(8,128)S(1)} %collective-permute-done.17.b_ref) | copy-start | bytes 1555204
  127.7 15.5 %collective-permute-start.18 = (f32[360,360]{1,0:T(8,128)S(1)}, f32[360,360]{1,0:T(8,128)S(1)}, u32[]{:S(2)}, u32[]{:S(2)}) collective-permute-start(f32[360,360]{1,0:T(8,128)S(1)} %collective-permute-done.17.b_ref), channel_id=1, source_target_pairs={{0,32},{32,64},{64,96},{96,128},{128,160},{160,192},{192,224},{224... | collective-permute-start | bytes 1555208 | tf_op jit(solution)/shard_map/ppermute | solution.py:96
  129.7 13.5 %collective-permute-start.19 = (f32[360,360]{1,0:T(8,128)S(1)}, f32[360,360]{1,0:T(8,128)S(1)}, u32[]{:S(2)}, u32[]{:S(2)}) collective-permute-start(f32[360,360]{1,0:T(8,128)S(1)} %collective-permute-done.16.b_ref), channel_id=1, source_target_pairs={{0,480},{32,0},{64,32},{96,64},{128,96},{160,128},{192,160},{224,1... | collective-permute-start | bytes 1555208 | tf_op jit(solution)/shard_map/ppermute | solution.py:98
  143.2 6.9 %copy-start = (f32[360,360]{1,0:T(8,128)}, f32[360,360]{1,0:T(8,128)S(1)}, u32[]{:S(2)}) copy-start(f32[360,360]{1,0:T(8,128)S(1)} %collective-permute-done.18.b_ref) | copy-start | bytes 1555204
  143.2 9.6 %copy-start.1 = (f32[360,360]{1,0:T(8,128)}, f32[360,360]{1,0:T(8,128)S(1)}, u32[]{:S(2)}) copy-start(f32[360,360]{1,0:T(8,128)S(1)} %collective-permute-done.19.b_ref) | copy-start | bytes 1555204
  143.2 12.2 %collective-permute-start.20 = (f32[180,360]{1,0:T(8,128)S(1)}, f32[180,360]{1,0:T(8,128)S(1)}, u32[]{:S(2)}, u32[]{:S(2)}) collective-permute-start(f32[180,360]{1,0:T(8,128)S(1)} %slice.14), channel_id=1, source_target_pairs={{0,480},{32,0},{64,32},{96,64},{128,96},{160,128},{192,160},{224,1... | collective-permute-start | bytes 777608 | tf_op jit(solution)/shard_map/ppermute | solution.py:103
  147.9 9.7 %collective-permute-start.21 = (f32[180,360]{1,0:T(8,128)S(1)}, f32[180,360]{1,0:T(8,128)S(1)}, u32[]{:S(2)}, u32[]{:S(2)}) collective-permute-start(f32[180,360]{1,0:T(8,128)S(1)} %slice.15), channel_id=1, source_target_pairs={{0,32},{32,64},{64,96},{96,128},{128,160},{160,192},{192,224},{224... | collective-permute-start | bytes 777608 | tf_op jit(solution)/shard_map/ppermute | solution.py:102
  155.4 5.3 %copy-start.7 = (f32[180,360]{1,0:T(8,128)}, f32[180,360]{1,0:T(8,128)S(1)}, u32[]{:S(2)}) copy-start(f32[180,360]{1,0:T(8,128)S(1)} %collective-permute-done.20.b_ref) | copy-start | bytes 777604
  157.6 0.7 copy-start.8
  164.0 8.5 %collective-permute-start.22 = (f32[96,360]{1,0:T(8,128)S(1)}, f32[96,360]{1,0:T(8,128)S(1)}, u32[]{:S(2)}, u32[]{:S(2)}) collective-permute-start(f32[96,360]{1,0:T(8,128)S(1)} %constant_dynamic-slice_fusion), channel_id=1, source_target_pairs={{0,1},{1,0},{2,3},{3,2},{4,5},{5,4},{6,7},{7,6},{8,9},{9,8},{10,11... | collective-permute-start | bytes 414728 | tf_op jit(solution)/shard_map/ppermute | solution.py:118

commit v8 on v3

v8 whole, which is shorter than its diff:
```python
import jax
import jax.numpy as jnp
from jax import lax
from jax.sharding import PartitionSpec as P


def ring_reduce(gathered, integrals, me, n):
    fwd = [(i, (i + 1) % n) for i in range(n)]
    bwd = [(i, (i - 1) % n) for i in range(n)]

    def part(t):
        block = lax.dynamic_index_in_dim(gathered, t % n, axis=0, keepdims=False)
        return jnp.dot(block, integrals, precision=lax.Precision.HIGHEST,
                       preferred_element_type=jnp.float32)

    back = n // 2
    ahead = n - 1 - back
    acc_f = part(me + ahead)
    acc_b = part(me - back)
    for s in range(1, back + 1):
        if s <= ahead:
            acc_f = lax.ppermute(acc_f, "row", fwd) + part(me + ahead - s)
        got = lax.ppermute(acc_b, "row", bwd)
        acc_b = got + part(me - back + s) if s < back else got
    return acc_f + acc_b


def local(amplitudes, integrals):
    n = lax.axis_size("row")
    me = lax.axis_index("row")
    d = lax.axis_index("depth")
    rows = amplitudes.shape[0]
    half = rows // 2

    swap = [(i * n + c, c * n + i) for i in range(n) for c in range(n)]
    moved = lax.ppermute(amplitudes, ("row", "col"), swap)
    theirs = lax.dynamic_slice_in_dim(moved, (1 - d) * half, half, axis=0)
    mine = lax.dynamic_slice_in_dim(moved, d * half, half, axis=0)
    g_theirs = lax.all_gather(theirs, "col", axis=0, tiled=False)
    g_mine = lax.all_gather(mine, "col", axis=0, tiled=False)

    sent = ring_reduce(g_theirs, integrals, me, n)
    got = lax.ppermute(sent, "depth", [(0, 1), (1, 0)])
    own = ring_reduce(g_mine, integrals, me, n)
    return 0.5 * (own + got)


def solution(mesh):
    placed = (P("row", ("col", "depth")), P(("row", "depth"), "col"))
    return jax.shard_map(
        local, mesh=mesh, in_specs=placed, out_specs=P(("row", "depth"), "col"), check_vma=False
    )
```

time: 830 us -> 288 us (0.35)
  waiting for transfers between devices: 795 us -> 138 us
  starting transfers between devices: 5.61 us -> 110 us
  matrix products: 12.2 us -> 21.8 us
    reduce_scatter x1 -> x0, waiting for transfers between devices: 698 us -> none  [local(): lax.psum_scatter(partial, ('row', 'depth'), scatter_dimension=0, tiled=True)]
    ppermute x0 -> x31, starting transfers between devices: none -> 104 us  [the longest x16 61.7 us: ring_reduce(): got = lax.ppermute(acc_b, 'row', bwd)]
    all_gather x1 -> x2, waiting for transfers between devices: 49 us -> 85.4 us  [the longest x1 44 us: local(): g_theirs = lax.all_gather(theirs, 'col', axis=0, tiled=False)]
    dot_general x1 -> x32, matrix products: 12.2 us -> 21.8 us  [part(): jnp.dot(block, integrals, precision=lax.Precision.HIGHEST, preferred_elem...]
  transfers between devices with their start and end apart: 3 -> 34, of which waited for: 3 -> 4; matrix products, arithmetic and copies ran while one was open for 0% -> 3% of each run, Pallas kernels for 0% -> 0%
where the time goes in v8:
time: 288 us; the launch traced here: 286 us
  waiting for transfers between devices  138 us (48%)
  starting transfers between devices  110 us (38%)
  matrix products  21.8 us (8%)
  between operations  14.6 us (5%)
    ppermute x16, starting transfers between devices, ring_reduce(): got = lax.ppermute(acc_b, 'row', bwd)  61.7 us
    ppermute x1, waiting for transfers between devices, local(): moved = lax.ppermute(amplitudes, ('row', 'col'), swap)  47.4 us
    all_gather x1, waiting for transfers between devices, local(): g_theirs = lax.all_gather(theirs, 'col', axis=0, tiled=False)  44 us
    all_gather x1, waiting for transfers between devices, local(): g_mine = lax.all_gather(mine, 'col', axis=0, tiled=False)  41.5 us
    ppermute x14, starting transfers between devices, ring_reduce(): acc_f = lax.ppermute(acc_f, 'row', fwd) + part(me + ahead - s)  39.1 us
    dot_general x32, matrix products, part(): jnp.dot(block, integrals, precision=lax.Precision.HIGHEST, preferred_elem...  21.8 us
  transfers between devices with their start and end apart: 34, of which 4 were waited for; matrix products, arithmetic and copies ran while one was open for 3% of the time, Pallas kernels for 0%

profile of v8, /device:TPU:6, one launch (start us, length us, event | category | flops | bytes accessed | tf_op | source)
XLA Modules:
  0.0 286.3 jit_solution(15030127259101195216)
XLA Ops:
  6.5 5.6 %collective-permute-start = (f32[192,360]{1,0:T(8,128)}, f32[192,360]{1,0:T(8,128)S(1)}, u32[]{:S(2)}, u32[]{:S(2)}) collective-permute-start(f32[192,360]{1,0:T(8,128)} %param.2), channel_id=1, source_target_pairs={{0,0},{2,32},{4,64},{6,96},{8,128},{10,160},{12,192},{14,224},{16,... | collective-permute-start | bytes 829448 | tf_op jit(solution)/shard_map/ppermute | solution.py:36
  12.1 47.4 %collective-permute-done = f32[192,360]{1,0:T(8,128)S(1)} collective-permute-done((f32[192,360]{1,0:T(8,128)}, f32[192,360]{1,0:T(8,128)S(1)}, u32[]{:S(2)}, u32[]{:S(2)}) %collective-permute-start) | collective-permute-done | bytes 276512 | tf_op jit(solution)/shard_map/ppermute | solution.py:36
  61.3 44.0 %all-gather.7.cloned.1.call-done = f32[1536,360]{1,0:T(8,128)} async-done(((f32[96,360]{1,0:T(8,128)}), f32[1536,360]{1,0:T(8,128)}) %all-gather.7.cloned.1.call-update) | async-done | bytes 2211856 | tf_op jit(solution)/shard_map/all_gather | solution.py:39
  108.1 41.5 %all-gather.5.cloned.1.call-done = f32[1536,360]{1,0:T(8,128)} async-done(((f32[96,360]{1,0:T(8,128)}), f32[1536,360]{1,0:T(8,128)}) %all-gather.5.cloned.1.call-update) | async-done | bytes 2211856 | tf_op jit(solution)/shard_map/all_gather | solution.py:40
  162.6 6.0 %collective-permute-start.23 = (f32[96,360]{1,0:T(8,128)S(1)}, f32[96,360]{1,0:T(8,128)S(1)}, u32[]{:S(2)}, u32[]{:S(2)}) collective-permute-start(f32[96,360]{1,0:T(8,128)S(1)} %fusion.13), channel_id=1, source_target_pairs={{0,480},{32,0},{64,32},{96,64},{128,96},{160,128},{192,160},{224,1... | collective-permute-start | bytes 414728 | tf_op jit(solution)/shard_map/ppermute | solution.py:23
  168.6 1.9 collective-permute-start.16
  171.0 5.1 %collective-permute-start.8 = (f32[96,360]{1,0:T(8,128)S(1)}, f32[96,360]{1,0:T(8,128)S(1)}, u32[]{:S(2)}, u32[]{:S(2)}) collective-permute-start(f32[96,360]{1,0:T(8,128)S(1)} %fusion.43), channel_id=1, source_target_pairs={{0,480},{32,0},{64,32},{96,64},{128,96},{160,128},{192,160},{224,1... | collective-permute-start | bytes 414728 | tf_op jit(solution)/shard_map/ppermute | solution.py:23
  176.2 1.9 collective-permute-start.1
  179.2 5.1 %collective-permute-start.24 = (f32[96,360]{1,0:T(8,128)S(1)}, f32[96,360]{1,0:T(8,128)S(1)}, u32[]{:S(2)}, u32[]{:S(2)}) collective-permute-start(f32[96,360]{1,0:T(8,128)S(1)} %convolution_add_fusion), channel_id=1, source_target_pairs={{0,480},{32,0},{64,32},{96,64},{128,96},{160,128},{192,160},{224,1... | collective-permute-start | bytes 414728 | tf_op jit(solution)/shard_map/ppermute | solution.py:23
  184.8 2.1 collective-permute-start.17
  187.5 5.1 %collective-permute-start.9 = (f32[96,360]{1,0:T(8,128)S(1)}, f32[96,360]{1,0:T(8,128)S(1)}, u32[]{:S(2)}, u32[]{:S(2)}) collective-permute-start(f32[96,360]{1,0:T(8,128)S(1)} %convolution_add_fusion.2), channel_id=1, source_target_pairs={{0,480},{32,0},{64,32},{96,64},{128,96},{160,128},{192,160},{224,1... | collective-permute-start | bytes 414728 | tf_op jit(solution)/shard_map/ppermute | solution.py:23
  192.6 1.9 collective-permute-start.25
  195.1 3.9 %collective-permute-start.2 = (f32[96,360]{1,0:T(8,128)S(1)}, f32[96,360]{1,0:T(8,128)S(1)}, u32[]{:S(2)}, u32[]{:S(2)}) collective-permute-start(f32[96,360]{1,0:T(8,128)S(1)} %convolution_add_fusion.3), channel_id=1, source_target_pairs={{0,32},{32,64},{64,96},{96,128},{128,160},{160,192},{192,224},{224... | collective-permute-start | bytes 414728 | tf_op jit(solution)/shard_map/ppermute | solution.py:22
  199.1 1.9 collective-permute-start.18
  201.0 5.1 %collective-permute-start.10 = (f32[96,360]{1,0:T(8,128)S(1)}, f32[96,360]{1,0:T(8,128)S(1)}, u32[]{:S(2)}, u32[]{:S(2)}) collective-permute-start(f32[96,360]{1,0:T(8,128)S(1)} %add.345), channel_id=1, source_target_pairs={{0,480},{32,0},{64,32},{96,64},{128,96},{160,128},{192,160},{224,1... | collective-permute-start | bytes 414728 | tf_op jit(solution)/shard_map/ppermute | solution.py:23
  206.2 1.9 collective-permute-start.26
  208.7 3.9 %collective-permute-start.3 = (f32[96,360]{1,0:T(8,128)S(1)}, f32[96,360]{1,0:T(8,128)S(1)}, u32[]{:S(2)}, u32[]{:S(2)}) collective-permute-start(f32[96,360]{1,0:T(8,128)S(1)} %add.320), channel_id=1, source_target_pairs={{0,32},{32,64},{64,96},{96,128},{128,160},{160,192},{192,224},{224... | collective-permute-start | bytes 414728 | tf_op jit(solution)/shard_map/ppermute | solution.py:22
  214.6 5.1 %collective-permute-start.11 = (f32[96,360]{1,0:T(8,128)S(1)}, f32[96,360]{1,0:T(8,128)S(1)}, u32[]{:S(2)}, u32[]{:S(2)}) collective-permute-start(f32[96,360]{1,0:T(8,128)S(1)} %add.349), channel_id=1, source_target_pairs={{0,480},{32,0},{64,32},{96,64},{128,96},{160,128},{192,160},{224,1... | collective-permute-start | bytes 414728 | tf_op jit(solution)/shard_map/ppermute | solution.py:23
  219.8 1.9 collective-permute-start.27
  222.3 3.9 %collective-permute-start.4 = (f32[96,360]{1,0:T(8,128)S(1)}, f32[96,360]{1,0:T(8,128)S(1)}, u32[]{:S(2)}, u32[]{:S(2)}) collective-permute-start(f32[96,360]{1,0:T(8,128)S(1)} %add.323), channel_id=1, source_target_pairs={{0,32},{32,64},{64,96},{96,128},{128,160},{160,192},{192,224},{224... | collective-permute-start | bytes 414728 | tf_op jit(solution)/shard_map/ppermute | solution.py:22
  226.2 1.9 collective-permute-start.20
  228.2 5.1 %collective-permute-start.12 = (f32[96,360]{1,0:T(8,128)S(1)}, f32[96,360]{1,0:T(8,128)S(1)}, u32[]{:S(2)}, u32[]{:S(2)}) collective-permute-start(f32[96,360]{1,0:T(8,128)S(1)} %add.353), channel_id=1, source_target_pairs={{0,480},{32,0},{64,32},{96,64},{128,96},{160,128},{192,160},{224,1... | collective-permute-start | bytes 414728 | tf_op jit(solution)/shard_map/ppermute | solution.py:23
  233.4 1.9 collective-permute-start.28
  235.9 3.9 %collective-permute-start.5 = (f32[96,360]{1,0:T(8,128)S(1)}, f32[96,360]{1,0:T(8,128)S(1)}, u32[]{:S(2)}, u32[]{:S(2)}) collective-permute-start(f32[96,360]{1,0:T(8,128)S(1)} %add.326), channel_id=1, source_target_pairs={{0,32},{32,64},{64,96},{96,128},{128,160},{160,192},{192,224},{224... | collective-permute-start | bytes 414728 | tf_op jit(solution)/shard_map/ppermute | solution.py:22
  241.8 5.1 %collective-permute-start.13 = (f32[96,360]{1,0:T(8,128)S(1)}, f32[96,360]{1,0:T(8,128)S(1)}, u32[]{:S(2)}, u32[]{:S(2)}) collective-permute-start(f32[96,360]{1,0:T(8,128)S(1)} %add.357), channel_id=1, source_target_pairs={{0,480},{32,0},{64,32},{96,64},{128,96},{160,128},{192,160},{224,1... | collective-permute-start | bytes 414728 | tf_op jit(solution)/shard_map/ppermute | solution.py:23
  249.4 3.9 %collective-permute-start.6 = (f32[96,360]{1,0:T(8,128)S(1)}, f32[96,360]{1,0:T(8,128)S(1)}, u32[]{:S(2)}, u32[]{:S(2)}) collective-permute-start(f32[96,360]{1,0:T(8,128)S(1)} %add.329), channel_id=1, source_target_pairs={{0,32},{32,64},{64,96},{96,128},{128,160},{160,192},{192,224},{224... | collective-permute-start | bytes 414728 | tf_op jit(solution)/shard_map/ppermute | solution.py:22
  255.4 5.1 %collective-permute-start.14 = (f32[96,360]{1,0:T(8,128)S(1)}, f32[96,360]{1,0:T(8,128)S(1)}, u32[]{:S(2)}, u32[]{:S(2)}) collective-permute-start(f32[96,360]{1,0:T(8,128)S(1)} %add.361), channel_id=1, source_target_pairs={{0,480},{32,0},{64,32},{96,64},{128,96},{160,128},{192,160},{224,1... | collective-permute-start | bytes 414728 | tf_op jit(solution)/shard_map/ppermute | solution.py:23
  260.6 1.9 collective-permute-start.30
  263.0 3.9 %collective-permute-start.7 = (f32[96,360]{1,0:T(8,128)S(1)}, f32[96,360]{1,0:T(8,128)S(1)}, u32[]{:S(2)}, u32[]{:S(2)}) collective-permute-start(f32[96,360]{1,0:T(8,128)S(1)} %add.332), channel_id=1, source_target_pairs={{0,32},{32,64},{64,96},{96,128},{128,160},{160,192},{192,224},{224... | collective-permute-start | bytes 414728 | tf_op jit(solution)/shard_map/ppermute | solution.py:22
  267.0 3.1 %collective-permute-start.15 = (f32[96,360]{1,0:T(8,128)S(1)}, f32[96,360]{1,0:T(8,128)S(1)}, u32[]{:S(2)}, u32[]{:S(2)}) collective-permute-start(f32[96,360]{1,0:T(8,128)S(1)} %add.365), channel_id=1, source_target_pairs={{0,480},{32,0},{64,32},{96,64},{128,96},{160,128},{192,160},{224,1... | collective-permute-start | bytes 414728 | tf_op jit(solution)/shard_map/ppermute | solution.py:23
  270.2 3.5 %collective-permute-start.31 = (f32[96,360]{1,0:T(8,128)S(1)}, f32[96,360]{1,0:T(8,128)S(1)}, u32[]{:S(2)}, u32[]{:S(2)}) collective-permute-start(f32[96,360]{1,0:T(8,128)S(1)} %add_add_fusion), channel_id=1, source_target_pairs={{0,1},{1,0},{2,3},{3,2},{4,5},{5,4},{6,7},{7,6},{8,9},{9,8},{10,11... | collective-permute-start | bytes 414728 | tf_op jit(solution)/shard_map/ppermute | solution.py:43
  274.3 4.5 %collective-permute-done.31 = f32[96,360]{1,0:T(8,128)S(1)} collective-permute-done((f32[96,360]{1,0:T(8,128)S(1)}, f32[96,360]{1,0:T(8,128)S(1)}, u32[]{:S(2)}, u32[]{:S(2)}) %collective-permute-start.31) | collective-permute-done | bytes 138272 | tf_op jit(solution)/shard_map/ppermute | solution.py:43
  (101 shorter events, 32.2 us)
Async XLA Ops:
  6.5 98.7 %all-gather.7.cloned.1.call-start = ((), (), s32[]{:S(2)}) async-start(), calls=%async_computation.1 | async-start | bytes 2506752 | tf_op jit(solution)/shard_map/all_gather | solution.py:39
  6.5 53.0 %collective-permute-start = (f32[192,360]{1,0:T(8,128)}, f32[192,360]{1,0:T(8,128)S(1)}, u32[]{:S(2)}, u32[]{:S(2)}) collective-permute-start(f32[192,360]{1,0:T(8,128)} %param.2), channel_id=1, source_target_pairs={{0,0},{2,32},{4,64},{6,96},{8,128},{10,160},{12,192},{14,224},{16,... | collective-permute-start | bytes 829448 | tf_op jit(solution)/shard_map/ppermute | solution.py:36
  60.3 89.3 %all-gather.5.cloned.1.call-start = ((), (), s32[]{:S(2)}) async-start(), calls=%async_computation | async-start | bytes 2506752 | tf_op jit(solution)/shard_map/all_gather | solution.py:40
  162.6 16.0 %collective-permute-start.23 = (f32[96,360]{1,0:T(8,128)S(1)}, f32[96,360]{1,0:T(8,128)S(1)}, u32[]{:S(2)}, u32[]{:S(2)}) collective-permute-start(f32[96,360]{1,0:T(8,128)S(1)} %fusion.13), channel_id=1, source_target_pairs={{0,480},{32,0},{64,32},{96,64},{128,96},{160,128},{192,160},{224,1... | collective-permute-start | bytes 414728 | tf_op jit(solution)/shard_map/ppermute | solution.py:23
  168.6 15.7 %collective-permute-start.16 = (f32[96,360]{1,0:T(8,128)S(1)}, f32[96,360]{1,0:T(8,128)S(1)}, u32[]{:S(2)}, u32[]{:S(2)}) collective-permute-start(f32[96,360]{1,0:T(8,128)S(1)} %fusion.28), channel_id=1, source_target_pairs={{0,32},{32,64},{64,96},{96,128},{128,160},{160,192},{192,224},{224... | collective-permute-start | bytes 414728 | tf_op jit(solution)/shard_map/ppermute | solution.py:22
  171.0 15.9 %collective-permute-start.8 = (f32[96,360]{1,0:T(8,128)S(1)}, f32[96,360]{1,0:T(8,128)S(1)}, u32[]{:S(2)}, u32[]{:S(2)}) collective-permute-start(f32[96,360]{1,0:T(8,128)S(1)} %fusion.43), channel_id=1, source_target_pairs={{0,480},{32,0},{64,32},{96,64},{128,96},{160,128},{192,160},{224,1... | collective-permute-start | bytes 414728 | tf_op jit(solution)/shard_map/ppermute | solution.py:23
  176.2 18.4 %collective-permute-start.1 = (f32[96,360]{1,0:T(8,128)S(1)}, f32[96,360]{1,0:T(8,128)S(1)}, u32[]{:S(2)}, u32[]{:S(2)}) collective-permute-start(f32[96,360]{1,0:T(8,128)S(1)} %fusion.58), channel_id=1, source_target_pairs={{0,32},{32,64},{64,96},{96,128},{128,160},{160,192},{192,224},{224... | collective-permute-start | bytes 414728 | tf_op jit(solution)/shard_map/ppermute | solution.py:22
  179.2 13.4 %collective-permute-start.24 = (f32[96,360]{1,0:T(8,128)S(1)}, f32[96,360]{1,0:T(8,128)S(1)}, u32[]{:S(2)}, u32[]{:S(2)}) collective-permute-start(f32[96,360]{1,0:T(8,128)S(1)} %convolution_add_fusion), channel_id=1, source_target_pairs={{0,480},{32,0},{64,32},{96,64},{128,96},{160,128},{192,160},{224,1... | collective-permute-start | bytes 414728 | tf_op jit(solution)/shard_map/ppermute | solution.py:23
  184.8 14.2 %collective-permute-start.17 = (f32[96,360]{1,0:T(8,128)S(1)}, f32[96,360]{1,0:T(8,128)S(1)}, u32[]{:S(2)}, u32[]{:S(2)}) collective-permute-start(f32[96,360]{1,0:T(8,128)S(1)} %convolution_add_fusion.1), channel_id=1, source_target_pairs={{0,32},{32,64},{64,96},{96,128},{128,160},{160,192},{192,224},{224... | collective-permute-start | bytes 414728 | tf_op jit(solution)/shard_map/ppermute | solution.py:22
  187.5 13.5 %collective-permute-start.9 = (f32[96,360]{1,0:T(8,128)S(1)}, f32[96,360]{1,0:T(8,128)S(1)}, u32[]{:S(2)}, u32[]{:S(2)}) collective-permute-start(f32[96,360]{1,0:T(8,128)S(1)} %convolution_add_fusion.2), channel_id=1, source_target_pairs={{0,480},{32,0},{64,32},{96,64},{128,96},{160,128},{192,160},{224,1... | collective-permute-start | bytes 414728 | tf_op jit(solution)/shard_map/ppermute | solution.py:23
  192.6 13.5 %collective-permute-start.25 = (f32[96,360]{1,0:T(8,128)S(1)}, f32[96,360]{1,0:T(8,128)S(1)}, u32[]{:S(2)}, u32[]{:S(2)}) collective-permute-start(f32[96,360]{1,0:T(8,128)S(1)} %add.376), channel_id=1, source_target_pairs={{0,480},{32,0},{64,32},{96,64},{128,96},{160,128},{192,160},{224,1... | collective-permute-start | bytes 414728 | tf_op jit(solution)/shard_map/ppermute | solution.py:23
  195.1 13.6 %collective-permute-start.2 = (f32[96,360]{1,0:T(8,128)S(1)}, f32[96,360]{1,0:T(8,128)S(1)}, u32[]{:S(2)}, u32[]{:S(2)}) collective-permute-start(f32[96,360]{1,0:T(8,128)S(1)} %convolution_add_fusion.3), channel_id=1, source_target_pairs={{0,32},{32,64},{64,96},{96,128},{128,160},{160,192},{192,224},{224... | collective-permute-start | bytes 414728 | tf_op jit(solution)/shard_map/ppermute | solution.py:22
  199.1 13.6 %collective-permute-start.18 = (f32[96,360]{1,0:T(8,128)S(1)}, f32[96,360]{1,0:T(8,128)S(1)}, u32[]{:S(2)}, u32[]{:S(2)}) collective-permute-start(f32[96,360]{1,0:T(8,128)S(1)} %add.369), channel_id=1, source_target_pairs={{0,32},{32,64},{64,96},{96,128},{128,160},{160,192},{192,224},{224... | collective-permute-start | bytes 414728 | tf_op jit(solution)/shard_map/ppermute | solution.py:22
  201.0 13.6 %collective-permute-start.10 = (f32[96,360]{1,0:T(8,128)S(1)}, f32[96,360]{1,0:T(8,128)S(1)}, u32[]{:S(2)}, u32[]{:S(2)}) collective-permute-start(f32[96,360]{1,0:T(8,128)S(1)} %add.345), channel_id=1, source_target_pairs={{0,480},{32,0},{64,32},{96,64},{128,96},{160,128},{192,160},{224,1... | collective-permute-start | bytes 414728 | tf_op jit(solution)/shard_map/ppermute | solution.py:23
  206.2 13.6 %collective-permute-start.26 = (f32[96,360]{1,0:T(8,128)S(1)}, f32[96,360]{1,0:T(8,128)S(1)}, u32[]{:S(2)}, u32[]{:S(2)}) collective-permute-start(f32[96,360]{1,0:T(8,128)S(1)} %add.377), channel_id=1, source_target_pairs={{0,480},{32,0},{64,32},{96,64},{128,96},{160,128},{192,160},{224,1... | collective-permute-start | bytes 414728 | tf_op jit(solution)/shard_map/ppermute | solution.py:23
  208.7 13.6 %collective-permute-start.3 = (f32[96,360]{1,0:T(8,128)S(1)}, f32[96,360]{1,0:T(8,128)S(1)}, u32[]{:S(2)}, u32[]{:S(2)}) collective-permute-start(f32[96,360]{1,0:T(8,128)S(1)} %add.320), channel_id=1, source_target_pairs={{0,32},{32,64},{64,96},{96,128},{128,160},{160,192},{192,224},{224... | collective-permute-start | bytes 414728 | tf_op jit(solution)/shard_map/ppermute | solution.py:22
  212.6 13.6 %collective-permute-start.19 = (f32[96,360]{1,0:T(8,128)S(1)}, f32[96,360]{1,0:T(8,128)S(1)}, u32[]{:S(2)}, u32[]{:S(2)}) collective-permute-start(f32[96,360]{1,0:T(8,128)S(1)} %add.370), channel_id=1, source_target_pairs={{0,32},{32,64},{64,96},{96,128},{128,160},{160,192},{192,224},{224... | collective-permute-start | bytes 414728 | tf_op jit(solution)/shard_map/ppermute | solution.py:22
  214.6 13.6 %collective-permute-start.11 = (f32[96,360]{1,0:T(8,128)S(1)}, f32[96,360]{1,0:T(8,128)S(1)}, u32[]{:S(2)}, u32[]{:S(2)}) collective-permute-start(f32[96,360]{1,0:T(8,128)S(1)} %add.349), channel_id=1, source_target_pairs={{0,480},{32,0},{64,32},{96,64},{128,96},{160,128},{192,160},{224,1... | collective-permute-start | bytes 414728 | tf_op jit(solution)/shard_map/ppermute | solution.py:23
  219.8 13.6 %collective-permute-start.27 = (f32[96,360]{1,0:T(8,128)S(1)}, f32[96,360]{1,0:T(8,128)S(1)}, u32[]{:S(2)}, u32[]{:S(2)}) collective-permute-start(f32[96,360]{1,0:T(8,128)S(1)} %add.378), channel_id=1, source_target_pairs={{0,480},{32,0},{64,32},{96,64},{128,96},{160,128},{192,160},{224,1... | collective-permute-start | bytes 414728 | tf_op jit(solution)/shard_map/ppermute | solution.py:23
  222.3 13.6 %collective-permute-start.4 = (f32[96,360]{1,0:T(8,128)S(1)}, f32[96,360]{1,0:T(8,128)S(1)}, u32[]{:S(2)}, u32[]{:S(2)}) collective-permute-start(f32[96,360]{1,0:T(8,128)S(1)} %add.323), channel_id=1, source_target_pairs={{0,32},{32,64},{64,96},{96,128},{128,160},{160,192},{192,224},{224... | collective-permute-start | bytes 414728 | tf_op jit(solution)/shard_map/ppermute | solution.py:22
  226.2 13.6 %collective-permute-start.20 = (f32[96,360]{1,0:T(8,128)S(1)}, f32[96,360]{1,0:T(8,128)S(1)}, u32[]{:S(2)}, u32[]{:S(2)}) collective-permute-start(f32[96,360]{1,0:T(8,128)S(1)} %add.371), channel_id=1, source_target_pairs={{0,32},{32,64},{64,96},{96,128},{128,160},{160,192},{192,224},{224... | collective-permute-start | bytes 414728 | tf_op jit(solution)/shard_map/ppermute | solution.py:22
  228.2 13.6 %collective-permute-start.12 = (f32[96,360]{1,0:T(8,128)S(1)}, f32[96,360]{1,0:T(8,128)S(1)}, u32[]{:S(2)}, u32[]{:S(2)}) collective-permute-start(f32[96,360]{1,0:T(8,128)S(1)} %add.353), channel_id=1, source_target_pairs={{0,480},{32,0},{64,32},{96,64},{128,96},{160,128},{192,160},{224,1... | collective-permute-start | bytes 414728 | tf_op jit(solution)/shard_map/ppermute | solution.py:23
  233.4 13.6 %collective-permute-start.28 = (f32[96,360]{1,0:T(8,128)S(1)}, f32[96,360]{1,0:T(8,128)S(1)}, u32[]{:S(2)}, u32[]{:S(2)}) collective-permute-start(f32[96,360]{1,0:T(8,128)S(1)} %add.379), channel_id=1, source_target_pairs={{0,480},{32,0},{64,32},{96,64},{128,96},{160,128},{192,160},{224,1... | collective-permute-start | bytes 414728 | tf_op jit(solution)/shard_map/ppermute | solution.py:23
  235.9 13.6 %collective-permute-start.5 = (f32[96,360]{1,0:T(8,128)S(1)}, f32[96,360]{1,0:T(8,128)S(1)}, u32[]{:S(2)}, u32[]{:S(2)}) collective-permute-start(f32[96,360]{1,0:T(8,128)S(1)} %add.326), channel_id=1, source_target_pairs={{0,32},{32,64},{64,96},{96,128},{128,160},{160,192},{192,224},{224... | collective-permute-start | bytes 414728 | tf_op jit(solution)/shard_map/ppermute | solution.py:22
  239.8 13.6 %collective-permute-start.21 = (f32[96,360]{1,0:T(8,128)S(1)}, f32[96,360]{1,0:T(8,128)S(1)}, u32[]{:S(2)}, u32[]{:S(2)}) collective-permute-start(f32[96,360]{1,0:T(8,128)S(1)} %add.372), channel_id=1, source_target_pairs={{0,32},{32,64},{64,96},{96,128},{128,160},{160,192},{192,224},{224... | collective-permute-start | bytes 414728 | tf_op jit(solution)/shard_map/ppermute | solution.py:22
  241.8 13.6 %collective-permute-start.13 = (f32[96,360]{1,0:T(8,128)S(1)}, f32[96,360]{1,0:T(8,128)S(1)}, u32[]{:S(2)}, u32[]{:S(2)}) collective-permute-start(f32[96,360]{1,0:T(8,128)S(1)} %add.357), channel_id=1, source_target_pairs={{0,480},{32,0},{64,32},{96,64},{128,96},{160,128},{192,160},{224,1... | collective-permute-start | bytes 414728 | tf_op jit(solution)/shard_map/ppermute | solution.py:23
  247.0 13.6 %collective-permute-start.29 = (f32[96,360]{1,0:T(8,128)S(1)}, f32[96,360]{1,0:T(8,128)S(1)}, u32[]{:S(2)}, u32[]{:S(2)}) collective-permute-start(f32[96,360]{1,0:T(8,128)S(1)} %add.380), channel_id=1, source_target_pairs={{0,480},{32,0},{64,32},{96,64},{128,96},{160,128},{192,160},{224,1... | collective-permute-start | bytes 414728 | tf_op jit(solution)/shard_map/ppermute | solution.py:23
  249.4 13.6 %collective-permute-start.6 = (f32[96,360]{1,0:T(8,128)S(1)}, f32[96,360]{1,0:T(8,128)S(1)}, u32[]{:S(2)}, u32[]{:S(2)}) collective-permute-start(f32[96,360]{1,0:T(8,128)S(1)} %add.329), channel_id=1, source_target_pairs={{0,32},{32,64},{64,96},{96,128},{128,160},{160,192},{192,224},{224... | collective-permute-start | bytes 414728 | tf_op jit(solution)/shard_map/ppermute | solution.py:22
  253.4 16.7 %collective-permute-start.22 = (f32[96,360]{1,0:T(8,128)S(1)}, f32[96,360]{1,0:T(8,128)S(1)}, u32[]{:S(2)}, u32[]{:S(2)}) collective-permute-start(f32[96,360]{1,0:T(8,128)S(1)} %add.373), channel_id=1, source_target_pairs={{0,32},{32,64},{64,96},{96,128},{128,160},{160,192},{192,224},{224... | collective-permute-start | bytes 414728 | tf_op jit(solution)/shard_map/ppermute | solution.py:22
  255.4 11.6 %collective-permute-start.14 = (f32[96,360]{1,0:T(8,128)S(1)}, f32[96,360]{1,0:T(8,128)S(1)}, u32[]{:S(2)}, u32[]{:S(2)}) collective-permute-start(f32[96,360]{1,0:T(8,128)S(1)} %add.361), channel_id=1, source_target_pairs={{0,480},{32,0},{64,32},{96,64},{128,96},{160,128},{192,160},{224,1... | collective-permute-start | bytes 414728 | tf_op jit(solution)/shard_map/ppermute | solution.py:23
  260.6 9.6 %collective-permute-start.30 = (f32[96,360]{1,0:T(8,128)S(1)}, f32[96,360]{1,0:T(8,128)S(1)}, u32[]{:S(2)}, u32[]{:S(2)}) collective-permute-start(f32[96,360]{1,0:T(8,128)S(1)} %add.381), channel_id=1, source_target_pairs={{0,480},{32,0},{64,32},{96,64},{128,96},{160,128},{192,160},{224,1... | collective-permute-start | bytes 414728 | tf_op jit(solution)/shard_map/ppermute | solution.py:23
  263.0 11.2 %collective-permute-start.7 = (f32[96,360]{1,0:T(8,128)S(1)}, f32[96,360]{1,0:T(8,128)S(1)}, u32[]{:S(2)}, u32[]{:S(2)}) collective-permute-start(f32[96,360]{1,0:T(8,128)S(1)} %add.332), channel_id=1, source_target_pairs={{0,32},{32,64},{64,96},{96,128},{128,160},{160,192},{192,224},{224... | collective-permute-start | bytes 414728 | tf_op jit(solution)/shard_map/ppermute | solution.py:22
  (5 other events, 125.8 us)
Sparse Core Ops, SparseCore 0:
  60.4 44.8 all-gather.6
  107.4 42.1 all-gather.4

commit v9 on v4

v9 whole, which is shorter than its diff:
```python
import jax
import jax.numpy as jnp
from jax import lax
from jax.sharding import PartitionSpec as P

FIRST_DOT_STEP = 5
DOTS_PER_STEP = 2


def gather_col(block):
    n = lax.axis_size("col")
    c = lax.axis_index("col")
    core, xlo, y = c % 2, (c // 2) % 2, c // 4
    ny = n // 4
    other = lax.ppermute(block, "col", [(i, i ^ 1) for i in range(n)])
    pair = jnp.where(core == 0, jnp.stack([block, other]), jnp.stack([other, block]))
    far = lax.ppermute(pair, "col", [(i, i ^ 2) for i in range(n)])
    quad = jnp.where(xlo == 0, jnp.concatenate([pair, far]), jnp.concatenate([far, pair]))
    up = [(i, (i + 4) % n) for i in range(n)]
    down = [(i, (i - 4) % n) for i in range(n)]
    below = lax.ppermute(quad, "col", up)
    above = lax.ppermute(quad, "col", down)
    h = quad.shape[1] // 2
    opp_a = lax.ppermute(below[:, :h], "col", up)
    opp_b = lax.ppermute(above[:, h:], "col", down)
    opposite = jnp.concatenate([opp_a, opp_b], axis=1)
    stack = jnp.concatenate([quad, above, opposite, below])

    def place(owner):
        return ((owner // 4 - y) % ny) * 4 + owner % 4

    return stack, place


def local(amplitudes, integrals):
    n = lax.axis_size("row")
    m = lax.axis_size("col")
    me = lax.axis_index("row")
    d = lax.axis_index("depth")
    core = lax.axis_index("col") % 2
    kb = integrals.shape[0]
    rows = amplitudes.shape[0]
    half = rows // 2
    sign = 2 * core - 1

    strip, place = gather_col(amplitudes)

    def cols(owner):
        return lax.dynamic_index_in_dim(strip, place(owner % n), axis=0, keepdims=False)

    def dot(a, b):
        return jnp.dot(a, b, precision=lax.Precision.HIGHEST,
                       preferred_element_type=jnp.float32)

    partner = lax.ppermute(integrals, "col", [(i, i ^ 1) for i in range(m)])
    pair = jnp.where(core == 0, jnp.stack([integrals, partner]),
                     jnp.stack([partner, integrals]))
    ring = [(r * m + c, ((r + 1 - 2 * (c % 2)) % n) * m + c)
            for r in range(n) for c in range(m)]

    sums = [None, None]
    own = dot(cols(me), integrals)
    pending = []
    held = pair
    last = n // 2
    for step in range(1, last + 1):
        owner = me + sign * step
        if step < last:
            held = lax.ppermute(held, ("row", "col"), ring)
            arrived = [(held, owner, None)]
        else:
            q = kb // 2
            held = lax.ppermute(lax.dynamic_slice_in_dim(held, core * q, q, axis=1),
                                ("row", "col"), ring)
            arrived = [(held, owner, q)]
        if step >= FIRST_DOT_STEP:
            for block, who, q in pending[:DOTS_PER_STEP]:
                a = cols(who)
                if q is not None:
                    a = lax.dynamic_slice_in_dim(a, core * q, q, axis=1)
                for k in range(2):
                    p = dot(a, block[k])
                    sums[k] = p if sums[k] is None else sums[k] + p
            pending = pending[DOTS_PER_STEP:]
            sums, held = lax.optimization_barrier((sums, held))
        pending = pending + arrived
    for block, who, q in pending:
        a = cols(who)
        if q is not None:
            a = lax.dynamic_slice_in_dim(a, core * q, q, axis=1)
        for k in range(2):
            p = dot(a, block[k])
            sums[k] = p if sums[k] is None else sums[k] + p

    mine = jnp.where(core == 0, sums[0], sums[1])
    theirs = jnp.where(core == 0, sums[1], sums[0])
    total = own + mine + lax.ppermute(theirs, "col", [(i, i ^ 1) for i in range(m)])

    mine = lax.dynamic_slice_in_dim(total, d * half, half, axis=0)
    other = lax.dynamic_slice_in_dim(total, (1 - d) * half, half, axis=0)
    other = lax.ppermute(other, "depth", [(0, 1), (1, 0)])
    return 0.5 * (mine + other)


def solution(mesh):
    placed = (P("row", ("col", "depth")), P(("row", "depth"), "col"))
    return jax.shard_map(
        local, mesh=mesh, in_specs=placed, out_specs=P(("row", "depth"), "col"), check_vma=False
    )
```

time: 157 us -> 186 us (1.18)
  waiting for transfers between devices: 40.5 us -> 98.4 us
  starting transfers between devices: 89.5 us -> 51.3 us
  local copies, waits for them, and re-layouts: 1.84 us -> 15.4 us
  matrix products: 18.8 us -> 13.4 us
    ppermute x16 -> x10, starting transfers between devices: 67.5 us -> 21.6 us  [the longest x7 15.5 us: local(): held = lax.ppermute(held, ('row', 'col'), ring)]
    ppermute x16 -> x10, waiting for transfers between devices: 32.4 us -> 56.9 us  [the longest x7 46.8 us: local(): held = lax.ppermute(held, ('row', 'col'), ring)]
    ppermute x1, waiting for transfers between devices: 0.01 us -> 17.6 us  [gather_col(): above = lax.ppermute(quad, 'col', down)]
    slice x2 -> x8, local copies, waits for them, and re-layouts: 0.04 us -> 11.6 us  [local(): p = dot(a, block[k])]
    ppermute x1, starting transfers between devices: 1.91 us -> 9.34 us  [gather_col(): other = lax.ppermute(block, 'col', [(i, i ^ 1) for i in range(n)])]
    ppermute x1, waiting for transfers between devices: 0.01 us -> 6.19 us  [gather_col(): opp_a = lax.ppermute(below[:, :h], 'col', up)]
    dot_general x17, matrix products: 18.8 us -> 13.4 us  [dot(): jnp.dot(a, b, precision=lax.Precision.HIGHEST, preferred_element_type=jnp...]
    ppermute x1, waiting for transfers between devices: 1.14 us -> 6.35 us  [gather_col(): far = lax.ppermute(pair, 'col', [(i, i ^ 2) for i in range(n)])]
  transfers between devices with their start and end apart: 23 -> 17, of which waited for: 12 -> 14; matrix products, arithmetic and copies ran while one was open for 14% -> 15% of each run, Pallas kernels for 0% -> 0%
where the time goes in v9:
time: 186 us; the launch traced here: 185 us
  waiting for transfers between devices  98.4 us (53%)
  starting transfers between devices  51.3 us (28%)
  local copies, waits for them, and re-layouts  15.4 us (8%)
  matrix products  13.4 us (7%)
  other arithmetic  5.75 us (3%)
    ppermute x7, waiting for transfers between devices, local(): held = lax.ppermute(held, ('row', 'col'), ring)  46.8 us
    ppermute x1, waiting for transfers between devices, gather_col(): above = lax.ppermute(quad, 'col', down)  17.6 us
    ppermute x7, starting transfers between devices, local(): held = lax.ppermute(held, ('row', 'col'), ring)  15.5 us
    dot_general x17, matrix products, dot(): jnp.dot(a, b, precision=lax.Precision.HIGHEST, preferred_element_type=jnp...  13.4 us
    slice x8, local copies, waits for them, and re-layouts, local(): p = dot(a, block[k])  11.6 us
    ppermute x1, starting transfers between devices, gather_col(): other = lax.ppermute(block, 'col', [(i, i ^ 1) for i in range(n)])  9.34 us
    ppermute x1, waiting for transfers between devices, local(): lax.ppermute(lax.dynamic_slice_in_dim(held, core * q, q, axis=1), ('row',...  7.97 us
    ppermute x1, waiting for transfers between devices, gather_col(): far = lax.ppermute(pair, 'col', [(i, i ^ 2) for i in range(n)])  6.35 us
  transfers between devices with their start and end apart: 17, of which 14 were waited for; matrix products, arithmetic and copies ran while one was open for 15% of the time, Pallas kernels for 0%

profile of v9, /device:TPU:6, one launch (start us, length us, event | category | flops | bytes accessed | tf_op | source)
XLA Modules:
  0.0 185.3 jit_solution(7374106718474202815)
XLA Ops:
  0.0 1.9 %collective-permute-start.6 = (f32[360,360]{1,0:T(8,128)}, f32[360,360]{1,0:T(8,128)S(1)}, u32[]{:S(2)}, u32[]{:S(2)}) collective-permute-start(f32[360,360]{1,0:T(8,128)} %param.3), channel_id=1, source_target_pairs={{0,2},{2,0},{4,6},{6,4},{8,10},{10,8},{12,14},{14,12},{16,18},{18,... | collective-permute-start | bytes 1555208 | tf_op jit(solution)/shard_map/ppermute | solution.py:55
  6.2 3.8 %collective-permute-start.7 = (f32[2,360,360]{2,0,1:T(2,128)S(1)}, f32[2,360,360]{2,0,1:T(2,128)}, u32[]{:S(2)}, u32[]{:S(2)}) collective-permute-start(f32[2,360,360]{2,0,1:T(2,128)S(1)} %maximum_select_fusion.1), channel_id=1, source_target_pairs={{0,32},{2,482},{4,36},{6,486},{8,40},{10,490},{12,44},{14,494},{16... | collective-permute-start | bytes 3110408 | tf_op jit(solution)/shard_map/ppermute | solution.py:69
  10.0 9.3 %collective-permute-start = (f32[192,360]{1,0:T(8,128)}, f32[192,360]{1,0:T(8,128)S(1)}, u32[]{:S(2)}, u32[]{:S(2)}) collective-permute-start(f32[192,360]{1,0:T(8,128)} %param.2), channel_id=1, source_target_pairs={{0,2},{2,0},{4,6},{6,4},{8,10},{10,8},{12,14},{14,12},{16,18},{18,... | collective-permute-start | bytes 829448 | tf_op jit(solution)/shard_map/ppermute | solution.py:15
  21.9 2.8 %collective-permute-start.1 = (f32[2,192,360]{2,1,0:T(8,128)S(1)}, f32[2,192,360]{2,1,0:T(8,128)S(1)}, u32[]{:S(2)}, u32[]{:S(2)}) collective-permute-start(f32[2,192,360]{2,1,0:T(8,128)S(1)} %maximum_select_fusion.2), channel_id=1, source_target_pairs={{0,4},{2,6},{4,0},{6,2},{8,12},{10,14},{12,8},{14,10},{16,20},{18,... | collective-permute-start | bytes 1658888 | tf_op jit(solution)/shard_map/ppermute | solution.py:17
  24.6 6.4 %collective-permute-done.7 = f32[2,360,360]{2,0,1:T(2,128)} collective-permute-done((f32[2,360,360]{2,0,1:T(2,128)S(1)}, f32[2,360,360]{2,0,1:T(2,128)}, u32[]{:S(2)}, u32[]{:S(2)}) %collective-permute-start.7) | collective-permute-done | bytes 1036832 | tf_op jit(solution)/shard_map/ppermute | solution.py:69
  31.1 1.9 %collective-permute-start.8 = (f32[2,360,360]{2,0,1:T(2,128)}, f32[2,360,360]{2,0,1:T(2,128)}, u32[]{:S(2)}, u32[]{:S(2)}) collective-permute-start(f32[2,360,360]{2,0,1:T(2,128)} %collective-permute-done.7), channel_id=1, source_target_pairs={{0,32},{2,482},{4,36},{6,486},{8,40},{10,490},{12,44},{14,494},{16... | collective-permute-start | bytes 3110408 | tf_op jit(solution)/shard_map/ppermute | solution.py:69
  33.0 6.3 %collective-permute-done.1 = f32[2,192,360]{2,1,0:T(8,128)S(1)} collective-permute-done((f32[2,192,360]{2,1,0:T(8,128)S(1)}, f32[2,192,360]{2,1,0:T(8,128)S(1)}, u32[]{:S(2)}, u32[]{:S(2)}) %collective-permute-start.1) | collective-permute-done | bytes 552992 | tf_op jit(solution)/shard_map/ppermute | solution.py:17
  39.5 4.9 %collective-permute-start.2 = (f32[4,192,360]{2,1,0:T(8,128)S(1)}, f32[4,192,360]{2,1,0:T(8,128)S(1)}, u32[]{:S(2)}, u32[]{:S(2)}) collective-permute-start(f32[4,192,360]{2,1,0:T(8,128)S(1)} %maximum_select_fusion), channel_id=1, source_target_pairs={{0,24},{2,26},{4,28},{6,30},{8,0},{10,2},{12,4},{14,6},{16,8},{18,... | collective-permute-start | bytes 3317768 | tf_op jit(solution)/shard_map/ppermute | solution.py:22
  44.4 1.9 %collective-permute-start.3 = (f32[4,192,360]{2,1,0:T(8,128)S(1)}, f32[4,192,360]{2,1,0:T(8,128)S(1)}, u32[]{:S(2)}, u32[]{:S(2)}) collective-permute-start(f32[4,192,360]{2,1,0:T(8,128)S(1)} %maximum_select_fusion), channel_id=1, source_target_pairs={{0,8},{2,10},{4,12},{6,14},{8,16},{10,18},{12,20},{14,22},{16,24},... | collective-permute-start | bytes 3317768 | tf_op jit(solution)/shard_map/ppermute | solution.py:21
  46.3 3.6 %collective-permute-done.8 = f32[2,360,360]{2,0,1:T(2,128)} collective-permute-done((f32[2,360,360]{2,0,1:T(2,128)}, f32[2,360,360]{2,0,1:T(2,128)}, u32[]{:S(2)}, u32[]{:S(2)}) %collective-permute-start.8) | collective-permute-done | bytes 1036832 | tf_op jit(solution)/shard_map/ppermute | solution.py:69
  49.9 1.9 %collective-permute-start.9 = (f32[2,360,360]{2,0,1:T(2,128)}, f32[2,360,360]{2,0,1:T(2,128)}, u32[]{:S(2)}, u32[]{:S(2)}) collective-permute-start(f32[2,360,360]{2,0,1:T(2,128)} %collective-permute-done.8), channel_id=1, source_target_pairs={{0,32},{2,482},{4,36},{6,486},{8,40},{10,490},{12,44},{14,494},{16... | collective-permute-start | bytes 3110408 | tf_op jit(solution)/shard_map/ppermute | solution.py:69
  51.8 17.6 %collective-permute-done.2 = f32[4,192,360]{2,1,0:T(8,128)S(1)} collective-permute-done((f32[4,192,360]{2,1,0:T(8,128)S(1)}, f32[4,192,360]{2,1,0:T(8,128)S(1)}, u32[]{:S(2)}, u32[]{:S(2)}) %collective-permute-start.2) | collective-permute-done | bytes 1105952 | tf_op jit(solution)/shard_map/ppermute | solution.py:22
  70.3 5.6 %collective-permute-start.5 = (f32[4,96,360]{2,1,0:T(8,128)}, f32[4,96,360]{2,1,0:T(8,128)}, u32[]{:S(2)}, u32[]{:S(2)}) collective-permute-start(f32[4,96,360]{2,1,0:T(8,128)} %slice.73), channel_id=1, source_target_pairs={{0,24},{2,26},{4,28},{6,30},{8,0},{10,2},{12,4},{14,6},{16,8},{18,... | collective-permute-start | bytes 1658888 | tf_op jit(solution)/shard_map/ppermute | solution.py:25
  76.8 1.9 %collective-permute-start.4 = (f32[4,96,360]{2,1,0:T(8,128)}, f32[4,96,360]{2,1,0:T(8,128)}, u32[]{:S(2)}, u32[]{:S(2)}) collective-permute-start(f32[4,96,360]{2,1,0:T(8,128)} %slice.72), channel_id=1, source_target_pairs={{0,8},{2,10},{4,12},{6,14},{8,16},{10,18},{12,20},{14,22},{16,24},... | collective-permute-start | bytes 1658888 | tf_op jit(solution)/shard_map/ppermute | solution.py:24
  79.2 1.9 %collective-permute-start.10 = (f32[2,360,360]{2,0,1:T(2,128)}, f32[2,360,360]{2,0,1:T(2,128)S(1)}, u32[]{:S(2)}, u32[]{:S(2)}) collective-permute-start(f32[2,360,360]{2,0,1:T(2,128)} %collective-permute-done.9), channel_id=1, source_target_pairs={{0,32},{2,482},{4,36},{6,486},{8,40},{10,490},{12,44},{14,494},{16... | collective-permute-start | bytes 3110408 | tf_op jit(solution)/shard_map/ppermute | solution.py:69
  81.2 2.6 %fusion.114 = (f32[1,360,360]{2,0,1:T(1,128)S(1)}, f32[1,360,360]{2,0,1:T(1,128)S(1)}) fusion(f32[2,360,360]{2,0,1:T(2,128)} %collective-permute-done.7), kind=kLoop, calls=%fused_computation.119 | loop fusion | bytes 2073600 | tf_op jit(solution)/shard_map/slice | solution.py:82
  83.7 4.0 %collective-permute-done.5 = f32[4,96,360]{2,1,0:T(8,128)} collective-permute-done((f32[4,96,360]{2,1,0:T(8,128)}, f32[4,96,360]{2,1,0:T(8,128)}, u32[]{:S(2)}, u32[]{:S(2)}) %collective-permute-start.5) | collective-permute-done | bytes 552992 | tf_op jit(solution)/shard_map/ppermute | solution.py:25
  87.7 6.2 %collective-permute-done.4 = f32[4,96,360]{2,1,0:T(8,128)} collective-permute-done((f32[4,96,360]{2,1,0:T(8,128)}, f32[4,96,360]{2,1,0:T(8,128)}, u32[]{:S(2)}, u32[]{:S(2)}) %collective-permute-start.4) | collective-permute-done | bytes 552992 | tf_op jit(solution)/shard_map/ppermute | solution.py:24
  93.9 2.0 %pad_maximum_fusion = f32[16,192,360]{2,1,0:T(8,128)S(1)} fusion(f32[4,192,360]{2,1,0:T(8,128)S(1)} %collective-permute-done.3, f32[4,96,360]{2,1,0:T(8,128)} %collective-permute-done.5, f32[4,96,360]{2,1,0:T(8,128)} %collective-permute-done.4, f32[4,192,360]{2,1,0:T(8,128)S(1)} %collective-permute-done.2, f32[4,192,360]{2,1,0:T(8,128)S(1)} %maximum_select_fusion), kind=kLoop, calls=%fused_computation | loop fusion | flops 4423680 | bytes 8847360 | tf_op jit(solution)/shard_map/concatenate | solution.py:27
  97.5 2.6 %fusion.113 = (f32[1,360,360]{2,0,1:T(1,128)S(1)}, f32[1,360,360]{2,0,1:T(1,128)S(1)}) fusion(f32[2,360,360]{2,0,1:T(2,128)} %collective-permute-done.8), kind=kLoop, calls=%fused_computation.118 | loop fusion | bytes 2073600 | tf_op jit(solution)/shard_map/slice | solution.py:82
  100.1 2.1 %collective-permute-start.11 = (f32[2,360,360]{2,0,1:T(2,128)S(1)}, f32[2,360,360]{2,0,1:T(2,128)S(1)}, u32[]{:S(2)}, u32[]{:S(2)}) collective-permute-start(f32[2,360,360]{2,0,1:T(2,128)S(1)} %collective-permute-done.10), channel_id=1, source_target_pairs={{0,32},{2,482},{4,36},{6,486},{8,40},{10,490},{12,44},{14,494},{16... | collective-permute-start | bytes 3110408 | tf_op jit(solution)/shard_map/ppermute | solution.py:69
  103.7 2.6 %fusion.111 = (f32[1,360,360]{2,0,1:T(1,128)S(1)}, f32[1,360,360]{2,0,1:T(1,128)S(1)}) fusion(f32[2,360,360]{2,0,1:T(2,128)} %collective-permute-done.9), kind=kLoop, calls=%fused_computation.116 | loop fusion | bytes 2073600 | tf_op jit(solution)/shard_map/slice | solution.py:82
  107.8 10.7 %collective-permute-done.11 = f32[2,360,360]{2,0,1:T(2,128)S(1)} collective-permute-done((f32[2,360,360]{2,0,1:T(2,128)S(1)}, f32[2,360,360]{2,0,1:T(2,128)S(1)}, u32[]{:S(2)}, u32[]{:S(2)}) %collective-permute-start.11) | collective-permute-done | bytes 1036832 | tf_op jit(solution)/shard_map/ppermute | solution.py:69
  118.6 1.9 %collective-permute-start.12 = (f32[2,360,360]{2,0,1:T(2,128)S(1)}, f32[2,360,360]{2,0,1:T(2,128)S(1)}, u32[]{:S(2)}, u32[]{:S(2)}) collective-permute-start(f32[2,360,360]{2,0,1:T(2,128)S(1)} %collective-permute-done.11), channel_id=1, source_target_pairs={{0,32},{2,482},{4,36},{6,486},{8,40},{10,490},{12,44},{14,494},{16... | collective-permute-start | bytes 3110408 | tf_op jit(solution)/shard_map/ppermute | solution.py:69
  123.7 13.3 %collective-permute-done.12 = f32[2,360,360]{2,0,1:T(2,128)S(1)} collective-permute-done((f32[2,360,360]{2,0,1:T(2,128)S(1)}, f32[2,360,360]{2,0,1:T(2,128)S(1)}, u32[]{:S(2)}, u32[]{:S(2)}) %collective-permute-start.12) | collective-permute-done | bytes 1036832 | tf_op jit(solution)/shard_map/ppermute | solution.py:69
  137.1 1.9 %collective-permute-start.13 = (f32[2,360,360]{2,0,1:T(2,128)S(1)}, f32[2,360,360]{2,0,1:T(2,128)S(1)}, u32[]{:S(2)}, u32[]{:S(2)}) collective-permute-start(f32[2,360,360]{2,0,1:T(2,128)S(1)} %collective-permute-done.12), channel_id=1, source_target_pairs={{0,32},{2,482},{4,36},{6,486},{8,40},{10,490},{12,44},{14,494},{16... | collective-permute-start | bytes 3110408 | tf_op jit(solution)/shard_map/ppermute | solution.py:69
  142.9 12.7 %collective-permute-done.13 = f32[2,360,360]{2,0,1:T(2,128)S(1)} collective-permute-done((f32[2,360,360]{2,0,1:T(2,128)S(1)}, f32[2,360,360]{2,0,1:T(2,128)S(1)}, u32[]{:S(2)}, u32[]{:S(2)}) %collective-permute-start.13) | collective-permute-done | bytes 1036832 | tf_op jit(solution)/shard_map/ppermute | solution.py:69
  155.8 2.3 %collective-permute-start.14 = (f32[2,180,360]{2,0,1:T(2,128)S(1)}, f32[2,180,360]{2,0,1:T(2,128)S(1)}, u32[]{:S(2)}, u32[]{:S(2)}) collective-permute-start(f32[2,180,360]{2,0,1:T(2,128)S(1)} %constant_dynamic-slice_fusion.1), channel_id=1, source_target_pairs={{0,32},{2,482},{4,36},{6,486},{8,40},{10,490},{12,44},{14,494},{16... | collective-permute-start | bytes 1555208 | tf_op jit(solution)/shard_map/ppermute | solution.py:73
  160.5 8.0 %collective-permute-done.14 = f32[2,180,360]{2,0,1:T(2,128)S(1)} collective-permute-done((f32[2,180,360]{2,0,1:T(2,128)S(1)}, f32[2,180,360]{2,0,1:T(2,128)S(1)}, u32[]{:S(2)}, u32[]{:S(2)}) %collective-permute-start.14) | collective-permute-done | bytes 518432 | tf_op jit(solution)/shard_map/ppermute | solution.py:73
  170.1 1.9 %collective-permute-start.15 = (f32[192,360]{1,0:T(8,128)S(1)}, f32[192,360]{1,0:T(8,128)S(1)}, u32[]{:S(2)}, u32[]{:S(2)}) collective-permute-start(f32[192,360]{1,0:T(8,128)S(1)} %get-tuple-element.43), channel_id=1, source_target_pairs={{0,2},{2,0},{4,6},{6,4},{8,10},{10,8},{12,14},{14,12},{16,18},{18,... | collective-permute-start | bytes 829448 | tf_op jit(solution)/shard_map/ppermute | solution.py:97
  175.3 3.3 %collective-permute-start.16 = (f32[96,360]{1,0:T(8,128)S(1)}, f32[96,360]{1,0:T(8,128)S(1)}, u32[]{:S(2)}, u32[]{:S(2)}) collective-permute-start(f32[96,360]{1,0:T(8,128)S(1)} %constant_dynamic-slice_fusion), channel_id=1, source_target_pairs={{0,1},{1,0},{2,3},{3,2},{4,5},{5,4},{6,7},{7,6},{8,9},{9,8},{10,11... | collective-permute-start | bytes 414728 | tf_op jit(solution)/shard_map/ppermute | solution.py:101
  178.6 6.0 %collective-permute-done.16 = f32[96,360]{1,0:T(8,128)S(1)} collective-permute-done((f32[96,360]{1,0:T(8,128)S(1)}, f32[96,360]{1,0:T(8,128)S(1)}, u32[]{:S(2)}, u32[]{:S(2)}) %collective-permute-start.16) | collective-permute-done | bytes 138272 | tf_op jit(solution)/shard_map/ppermute | solution.py:101
  (44 shorter events, 28.2 us)
Async XLA Ops:
  0.0 4.0 %collective-permute-start.6 = (f32[360,360]{1,0:T(8,128)}, f32[360,360]{1,0:T(8,128)S(1)}, u32[]{:S(2)}, u32[]{:S(2)}) collective-permute-start(f32[360,360]{1,0:T(8,128)} %param.3), channel_id=1, source_target_pairs={{0,2},{2,0},{4,6},{6,4},{8,10},{10,8},{12,14},{14,12},{16,18},{18,... | collective-permute-start | bytes 1555208 | tf_op jit(solution)/shard_map/ppermute | solution.py:55
  6.2 24.9 %collective-permute-start.7 = (f32[2,360,360]{2,0,1:T(2,128)S(1)}, f32[2,360,360]{2,0,1:T(2,128)}, u32[]{:S(2)}, u32[]{:S(2)}) collective-permute-start(f32[2,360,360]{2,0,1:T(2,128)S(1)} %maximum_select_fusion.1), channel_id=1, source_target_pairs={{0,32},{2,482},{4,36},{6,486},{8,40},{10,490},{12,44},{14,494},{16... | collective-permute-start | bytes 3110408 | tf_op jit(solution)/shard_map/ppermute | solution.py:69
  10.0 10.7 %collective-permute-start = (f32[192,360]{1,0:T(8,128)}, f32[192,360]{1,0:T(8,128)S(1)}, u32[]{:S(2)}, u32[]{:S(2)}) collective-permute-start(f32[192,360]{1,0:T(8,128)} %param.2), channel_id=1, source_target_pairs={{0,2},{2,0},{4,6},{6,4},{8,10},{10,8},{12,14},{14,12},{16,18},{18,... | collective-permute-start | bytes 829448 | tf_op jit(solution)/shard_map/ppermute | solution.py:15
  21.9 17.5 %collective-permute-start.1 = (f32[2,192,360]{2,1,0:T(8,128)S(1)}, f32[2,192,360]{2,1,0:T(8,128)S(1)}, u32[]{:S(2)}, u32[]{:S(2)}) collective-permute-start(f32[2,192,360]{2,1,0:T(8,128)S(1)} %maximum_select_fusion.2), channel_id=1, source_target_pairs={{0,4},{2,6},{4,0},{6,2},{8,12},{10,14},{12,8},{14,10},{16,20},{18,... | collective-permute-start | bytes 1658888 | tf_op jit(solution)/shard_map/ppermute | solution.py:17
  31.1 18.8 %collective-permute-start.8 = (f32[2,360,360]{2,0,1:T(2,128)}, f32[2,360,360]{2,0,1:T(2,128)}, u32[]{:S(2)}, u32[]{:S(2)}) collective-permute-start(f32[2,360,360]{2,0,1:T(2,128)} %collective-permute-done.7), channel_id=1, source_target_pairs={{0,32},{2,482},{4,36},{6,486},{8,40},{10,490},{12,44},{14,494},{16... | collective-permute-start | bytes 3110408 | tf_op jit(solution)/shard_map/ppermute | solution.py:69
  39.5 30.0 %collective-permute-start.2 = (f32[4,192,360]{2,1,0:T(8,128)S(1)}, f32[4,192,360]{2,1,0:T(8,128)S(1)}, u32[]{:S(2)}, u32[]{:S(2)}) collective-permute-start(f32[4,192,360]{2,1,0:T(8,128)S(1)} %maximum_select_fusion), channel_id=1, source_target_pairs={{0,24},{2,26},{4,28},{6,30},{8,0},{10,2},{12,4},{14,6},{16,8},{18,... | collective-permute-start | bytes 3317768 | tf_op jit(solution)/shard_map/ppermute | solution.py:22
  44.4 31.5 %collective-permute-start.3 = (f32[4,192,360]{2,1,0:T(8,128)S(1)}, f32[4,192,360]{2,1,0:T(8,128)S(1)}, u32[]{:S(2)}, u32[]{:S(2)}) collective-permute-start(f32[4,192,360]{2,1,0:T(8,128)S(1)} %maximum_select_fusion), channel_id=1, source_target_pairs={{0,8},{2,10},{4,12},{6,14},{8,16},{10,18},{12,20},{14,22},{16,24},... | collective-permute-start | bytes 3317768 | tf_op jit(solution)/shard_map/ppermute | solution.py:21
  49.9 29.3 %collective-permute-start.9 = (f32[2,360,360]{2,0,1:T(2,128)}, f32[2,360,360]{2,0,1:T(2,128)}, u32[]{:S(2)}, u32[]{:S(2)}) collective-permute-start(f32[2,360,360]{2,0,1:T(2,128)} %collective-permute-done.8), channel_id=1, source_target_pairs={{0,32},{2,482},{4,36},{6,486},{8,40},{10,490},{12,44},{14,494},{16... | collective-permute-start | bytes 3110408 | tf_op jit(solution)/shard_map/ppermute | solution.py:69
  70.3 17.4 %collective-permute-start.5 = (f32[4,96,360]{2,1,0:T(8,128)}, f32[4,96,360]{2,1,0:T(8,128)}, u32[]{:S(2)}, u32[]{:S(2)}) collective-permute-start(f32[4,96,360]{2,1,0:T(8,128)} %slice.73), channel_id=1, source_target_pairs={{0,24},{2,26},{4,28},{6,30},{8,0},{10,2},{12,4},{14,6},{16,8},{18,... | collective-permute-start | bytes 1658888 | tf_op jit(solution)/shard_map/ppermute | solution.py:25
  76.8 17.1 %collective-permute-start.4 = (f32[4,96,360]{2,1,0:T(8,128)}, f32[4,96,360]{2,1,0:T(8,128)}, u32[]{:S(2)}, u32[]{:S(2)}) collective-permute-start(f32[4,96,360]{2,1,0:T(8,128)} %slice.72), channel_id=1, source_target_pairs={{0,8},{2,10},{4,12},{6,14},{8,16},{10,18},{12,20},{14,22},{16,24},... | collective-permute-start | bytes 1658888 | tf_op jit(solution)/shard_map/ppermute | solution.py:24
  79.2 20.8 %collective-permute-start.10 = (f32[2,360,360]{2,0,1:T(2,128)}, f32[2,360,360]{2,0,1:T(2,128)S(1)}, u32[]{:S(2)}, u32[]{:S(2)}) collective-permute-start(f32[2,360,360]{2,0,1:T(2,128)} %collective-permute-done.9), channel_id=1, source_target_pairs={{0,32},{2,482},{4,36},{6,486},{8,40},{10,490},{12,44},{14,494},{16... | collective-permute-start | bytes 3110408 | tf_op jit(solution)/shard_map/ppermute | solution.py:69
  95.9 73.6 %copy-start = (f32[16,192,360]{2,1,0:T(8,128)}, f32[16,192,360]{2,1,0:T(8,128)S(1)}, u32[]{:S(2)}) copy-start(f32[16,192,360]{2,1,0:T(8,128)S(1)} %pad_maximum_fusion) | copy-start | bytes 13271044
  100.1 18.5 %collective-permute-start.11 = (f32[2,360,360]{2,0,1:T(2,128)S(1)}, f32[2,360,360]{2,0,1:T(2,128)S(1)}, u32[]{:S(2)}, u32[]{:S(2)}) collective-permute-start(f32[2,360,360]{2,0,1:T(2,128)S(1)} %collective-permute-done.10), channel_id=1, source_target_pairs={{0,32},{2,482},{4,36},{6,486},{8,40},{10,490},{12,44},{14,494},{16... | collective-permute-start | bytes 3110408 | tf_op jit(solution)/shard_map/ppermute | solution.py:69
  118.6 18.5 %collective-permute-start.12 = (f32[2,360,360]{2,0,1:T(2,128)S(1)}, f32[2,360,360]{2,0,1:T(2,128)S(1)}, u32[]{:S(2)}, u32[]{:S(2)}) collective-permute-start(f32[2,360,360]{2,0,1:T(2,128)S(1)} %collective-permute-done.11), channel_id=1, source_target_pairs={{0,32},{2,482},{4,36},{6,486},{8,40},{10,490},{12,44},{14,494},{16... | collective-permute-start | bytes 3110408 | tf_op jit(solution)/shard_map/ppermute | solution.py:69
  137.1 18.5 %collective-permute-start.13 = (f32[2,360,360]{2,0,1:T(2,128)S(1)}, f32[2,360,360]{2,0,1:T(2,128)S(1)}, u32[]{:S(2)}, u32[]{:S(2)}) collective-permute-start(f32[2,360,360]{2,0,1:T(2,128)S(1)} %collective-permute-done.12), channel_id=1, source_target_pairs={{0,32},{2,482},{4,36},{6,486},{8,40},{10,490},{12,44},{14,494},{16... | collective-permute-start | bytes 3110408 | tf_op jit(solution)/shard_map/ppermute | solution.py:69
  155.8 17.8 %copy-start.1 = (f32[360,360]{1,0:T(8,128)S(1)}, f32[360,360]{1,0:T(8,128)}, u32[]{:S(2)}) copy-start(f32[360,360]{1,0:T(8,128)} %param.3) | copy-start | bytes 1555204
  155.8 12.7 %collective-permute-start.14 = (f32[2,180,360]{2,0,1:T(2,128)S(1)}, f32[2,180,360]{2,0,1:T(2,128)S(1)}, u32[]{:S(2)}, u32[]{:S(2)}) collective-permute-start(f32[2,180,360]{2,0,1:T(2,128)S(1)} %constant_dynamic-slice_fusion.1), channel_id=1, source_target_pairs={{0,32},{2,482},{4,36},{6,486},{8,40},{10,490},{12,44},{14,494},{16... | collective-permute-start | bytes 1555208 | tf_op jit(solution)/shard_map/ppermute | solution.py:73
  170.1 3.5 %collective-permute-start.15 = (f32[192,360]{1,0:T(8,128)S(1)}, f32[192,360]{1,0:T(8,128)S(1)}, u32[]{:S(2)}, u32[]{:S(2)}) collective-permute-start(f32[192,360]{1,0:T(8,128)S(1)} %get-tuple-element.43), channel_id=1, source_target_pairs={{0,2},{2,0},{4,6},{6,4},{8,10},{10,8},{12,14},{14,12},{16,18},{18,... | collective-permute-start | bytes 829448 | tf_op jit(solution)/shard_map/ppermute | solution.py:97
  175.3 9.3 %collective-permute-start.16 = (f32[96,360]{1,0:T(8,128)S(1)}, f32[96,360]{1,0:T(8,128)S(1)}, u32[]{:S(2)}, u32[]{:S(2)}) collective-permute-start(f32[96,360]{1,0:T(8,128)S(1)} %constant_dynamic-slice_fusion), channel_id=1, source_target_pairs={{0,1},{1,0},{2,3},{3,2},{4,5},{5,4},{6,7},{7,6},{8,9},{9,8},{10,11... | collective-permute-start | bytes 414728 | tf_op jit(solution)/shard_map/ppermute | solution.py:101

commit v10 on v8

--- a/solution.py
+++ b/solution.py
@@ -34,15 +34,13 @@
 
     swap = [(i * n + c, c * n + i) for i in range(n) for c in range(n)]
     moved = lax.ppermute(amplitudes, ("row", "col"), swap)
-    theirs = lax.dynamic_slice_in_dim(moved, (1 - d) * half, half, axis=0)
-    mine = lax.dynamic_slice_in_dim(moved, d * half, half, axis=0)
-    g_theirs = lax.all_gather(theirs, "col", axis=0, tiled=False)
-    g_mine = lax.all_gather(mine, "col", axis=0, tiled=False)
+    gathered = lax.all_gather(moved, "col", axis=0, tiled=False)
+    total = ring_reduce(gathered, integrals, me, n)
 
-    sent = ring_reduce(g_theirs, integrals, me, n)
-    got = lax.ppermute(sent, "depth", [(0, 1), (1, 0)])
-    own = ring_reduce(g_mine, integrals, me, n)
-    return 0.5 * (own + got)
+    mine = lax.dynamic_slice_in_dim(total, d * half, half, axis=0)
+    other = lax.dynamic_slice_in_dim(total, (1 - d) * half, half, axis=0)
+    other = lax.ppermute(other, "depth", [(0, 1), (1, 0)])
+    return 0.5 * (mine + other)
 
 
 def solution(mesh):

time: 288 us -> 215 us (0.75)
  starting transfers between devices: 110 us -> 66.1 us
  waiting for transfers between devices: 138 us -> 114 us
  matrix products: 21.8 us -> 18 us
    all_gather x2 -> x1, waiting for transfers between devices: 85.4 us -> 49.1 us  [local(): gathered = lax.all_gather(moved, 'col', axis=0, tiled=False)]
    ppermute x14 -> x7, starting transfers between devices: 39.1 us -> 13.6 us  [ring_reduce(): acc_f = lax.ppermute(acc_f, 'row', fwd) + part(me + ahead - s)]
    ppermute x16 -> x8, starting transfers between devices: 61.7 us -> 43.5 us  [ring_reduce(): got = lax.ppermute(acc_b, 'row', bwd)]
    ppermute x14 -> x7, waiting for transfers between devices: 0.04 us -> 7.17 us  [ring_reduce(): acc_f = lax.ppermute(acc_f, 'row', fwd) + part(me + ahead - s)]
    ppermute x16 -> x8, waiting for transfers between devices: 0.04 us -> 5.02 us  [ring_reduce(): got = lax.ppermute(acc_b, 'row', bwd)]
    dot_general x32 -> x16, matrix products: 21.8 us -> 18 us  [part(): jnp.dot(block, integrals, precision=lax.Precision.HIGHEST, preferred_elem...]
  transfers between devices with their start and end apart: 34 -> 18, of which waited for: 4 -> 12; matrix products, arithmetic and copies ran while one was open for 3% -> 8% of each run, Pallas kernels for 0% -> 0%
where the time goes in v10:
time: 215 us; the launch traced here: 214 us
  waiting for transfers between devices  114 us (53%)
  starting transfers between devices  66.1 us (31%)
  matrix products  18 us (8%)
  between operations  14.1 us (7%)
    all_gather x1, waiting for transfers between devices, local(): gathered = lax.all_gather(moved, 'col', axis=0, tiled=False)  49.1 us
    ppermute x1, waiting for transfers between devices, local(): moved = lax.ppermute(amplitudes, ('row', 'col'), swap)  47.4 us
    ppermute x8, starting transfers between devices, ring_reduce(): got = lax.ppermute(acc_b, 'row', bwd)  43.5 us
    dot_general x16, matrix products, part(): jnp.dot(block, integrals, precision=lax.Precision.HIGHEST, preferred_elem...  18 us
    ppermute x7, starting transfers between devices, ring_reduce(): acc_f = lax.ppermute(acc_f, 'row', fwd) + part(me + ahead - s)  13.6 us
    ppermute x7, waiting for transfers between devices, ring_reduce(): acc_f = lax.ppermute(acc_f, 'row', fwd) + part(me + ahead - s)  7.17 us
    ppermute x1, starting transfers between devices, local(): moved = lax.ppermute(amplitudes, ('row', 'col'), swap)  5.56 us
    ppermute x1, waiting for transfers between devices, local(): other = lax.ppermute(other, 'depth', [(0, 1), (1, 0)])  5.18 us
  transfers between devices with their start and end apart: 18, of which 12 were waited for; matrix products, arithmetic and copies ran while one was open for 8% of the time, Pallas kernels for 0%

profile of v10, /device:TPU:6, one launch (start us, length us, event | category | flops | bytes accessed | tf_op | source)
XLA Modules:
  0.0 213.8 jit_solution(4924768914770218511)
XLA Ops:
  6.5 5.6 %collective-permute-start = (f32[192,360]{1,0:T(8,128)}, f32[192,360]{1,0:T(8,128)S(1)}, u32[]{:S(2)}, u32[]{:S(2)}) collective-permute-start(f32[192,360]{1,0:T(8,128)} %param.2), channel_id=1, source_target_pairs={{0,0},{2,32},{4,64},{6,96},{8,128},{10,160},{12,192},{14,224},{16,... | collective-permute-start | bytes 829448 | tf_op jit(solution)/shard_map/ppermute | solution.py:36
  12.1 47.4 %collective-permute-done = f32[192,360]{1,0:T(8,128)S(1)} collective-permute-done((f32[192,360]{1,0:T(8,128)}, f32[192,360]{1,0:T(8,128)S(1)}, u32[]{:S(2)}, u32[]{:S(2)}) %collective-permute-start) | collective-permute-done | bytes 276512 | tf_op jit(solution)/shard_map/ppermute | solution.py:36
  60.3 49.1 %all-gather.3.cloned.1.call-done = f32[3072,360]{1,0:T(8,128)} async-done(((f32[192,360]{1,0:T(8,128)}), f32[3072,360]{1,0:T(8,128)}) %all-gather.3.cloned.1.call-update) | async-done | bytes 4423696 | tf_op jit(solution)/shard_map/all_gather | solution.py:37
  109.4 1.7 fusion.13
  111.1 6.0 %collective-permute-start.8 = (f32[192,360]{1,0:T(8,128)S(1)}, f32[192,360]{1,0:T(8,128)S(1)}, u32[]{:S(2)}, u32[]{:S(2)}) collective-permute-start(f32[192,360]{1,0:T(8,128)S(1)} %fusion.13), channel_id=1, source_target_pairs={{0,480},{32,0},{64,32},{96,64},{128,96},{160,128},{192,160},{224,1... | collective-permute-start | bytes 829448 | tf_op jit(solution)/shard_map/ppermute | solution.py:23
  117.3 1.9 fusion.28
  119.2 1.9 collective-permute-start.1
  121.1 2.6 %collective-permute-done.8 = f32[192,360]{1,0:T(8,128)S(1)} collective-permute-done((f32[192,360]{1,0:T(8,128)S(1)}, f32[192,360]{1,0:T(8,128)S(1)}, u32[]{:S(2)}, u32[]{:S(2)}) %collective-permute-start.8) | collective-permute-done | bytes 276512 | tf_op jit(solution)/shard_map/ppermute | solution.py:23
  123.7 1.7 convolution_add_fusion
  125.4 5.6 %collective-permute-start.9 = (f32[192,360]{1,0:T(8,128)S(1)}, f32[192,360]{1,0:T(8,128)S(1)}, u32[]{:S(2)}, u32[]{:S(2)}) collective-permute-start(f32[192,360]{1,0:T(8,128)S(1)} %convolution_add_fusion), channel_id=1, source_target_pairs={{0,480},{32,0},{64,32},{96,64},{128,96},{160,128},{192,160},{224,1... | collective-permute-start | bytes 829448 | tf_op jit(solution)/shard_map/ppermute | solution.py:23
  131.0 1.7 fusion.10
  132.8 1.7 convolution_add_fusion.1
  134.5 1.9 collective-permute-start.2
  136.9 5.6 %collective-permute-start.10 = (f32[192,360]{1,0:T(8,128)S(1)}, f32[192,360]{1,0:T(8,128)S(1)}, u32[]{:S(2)}, u32[]{:S(2)}) collective-permute-start(f32[192,360]{1,0:T(8,128)S(1)} %add.252), channel_id=1, source_target_pairs={{0,480},{32,0},{64,32},{96,64},{128,96},{160,128},{192,160},{224,1... | collective-permute-start | bytes 829448 | tf_op jit(solution)/shard_map/ppermute | solution.py:23
  144.0 1.6 collective-permute-done.2
  145.7 1.9 collective-permute-start.3
  147.7 5.4 %collective-permute-start.11 = (f32[192,360]{1,0:T(8,128)S(1)}, f32[192,360]{1,0:T(8,128)S(1)}, u32[]{:S(2)}, u32[]{:S(2)}) collective-permute-start(f32[192,360]{1,0:T(8,128)S(1)} %add.256), channel_id=1, source_target_pairs={{0,480},{32,0},{64,32},{96,64},{128,96},{160,128},{192,160},{224,1... | collective-permute-start | bytes 829448 | tf_op jit(solution)/shard_map/ppermute | solution.py:23
  154.6 1.3 collective-permute-done.3
  155.9 1.9 collective-permute-start.4
  157.9 5.1 %collective-permute-start.12 = (f32[192,360]{1,0:T(8,128)S(1)}, f32[192,360]{1,0:T(8,128)S(1)}, u32[]{:S(2)}, u32[]{:S(2)}) collective-permute-start(f32[192,360]{1,0:T(8,128)S(1)} %add.260), channel_id=1, source_target_pairs={{0,480},{32,0},{64,32},{96,64},{128,96},{160,128},{192,160},{224,1... | collective-permute-start | bytes 829448 | tf_op jit(solution)/shard_map/ppermute | solution.py:23
  164.6 1.2 collective-permute-done.4
  165.8 1.9 collective-permute-start.5
  167.8 5.1 %collective-permute-start.13 = (f32[192,360]{1,0:T(8,128)S(1)}, f32[192,360]{1,0:T(8,128)S(1)}, u32[]{:S(2)}, u32[]{:S(2)}) collective-permute-start(f32[192,360]{1,0:T(8,128)S(1)} %add.264), channel_id=1, source_target_pairs={{0,480},{32,0},{64,32},{96,64},{128,96},{160,128},{192,160},{224,1... | collective-permute-start | bytes 829448 | tf_op jit(solution)/shard_map/ppermute | solution.py:23
  175.7 2.1 collective-permute-start.6
  177.8 5.1 %collective-permute-start.14 = (f32[192,360]{1,0:T(8,128)S(1)}, f32[192,360]{1,0:T(8,128)S(1)}, u32[]{:S(2)}, u32[]{:S(2)}) collective-permute-start(f32[192,360]{1,0:T(8,128)S(1)} %add.268), channel_id=1, source_target_pairs={{0,480},{32,0},{64,32},{96,64},{128,96},{160,128},{192,160},{224,1... | collective-permute-start | bytes 829448 | tf_op jit(solution)/shard_map/ppermute | solution.py:23
  184.5 1.4 collective-permute-done.6
  185.9 1.9 collective-permute-start.7
  187.9 5.6 %collective-permute-start.15 = (f32[192,360]{1,0:T(8,128)S(1)}, f32[192,360]{1,0:T(8,128)S(1)}, u32[]{:S(2)}, u32[]{:S(2)}) collective-permute-start(f32[192,360]{1,0:T(8,128)S(1)} %add.272), channel_id=1, source_target_pairs={{0,480},{32,0},{64,32},{96,64},{128,96},{160,128},{192,160},{224,1... | collective-permute-start | bytes 829448 | tf_op jit(solution)/shard_map/ppermute | solution.py:23
  193.5 1.7 fusion.15
  195.7 2.0 collective-permute-done.15
  197.8 3.4 %collective-permute-start.16 = (f32[96,360]{1,0:T(8,128)S(1)}, f32[96,360]{1,0:T(8,128)S(1)}, u32[]{:S(2)}, u32[]{:S(2)}) collective-permute-start(f32[96,360]{1,0:T(8,128)S(1)} %constant_dynamic-slice_fusion), channel_id=1, source_target_pairs={{0,1},{1,0},{2,3},{3,2},{4,5},{5,4},{6,7},{7,6},{8,9},{9,8},{10,11... | collective-permute-start | bytes 414728 | tf_op jit(solution)/shard_map/ppermute | solution.py:42
  201.1 5.2 %collective-permute-done.16 = f32[96,360]{1,0:T(8,128)S(1)} collective-permute-done((f32[96,360]{1,0:T(8,128)S(1)}, f32[96,360]{1,0:T(8,128)S(1)}, u32[]{:S(2)}, u32[]{:S(2)}) %collective-permute-start.16) | collective-permute-done | bytes 138272 | tf_op jit(solution)/shard_map/ppermute | solution.py:42
  (41 shorter events, 11.6 us)
Async XLA Ops:
  6.5 102.8 %copy-start = (f32[360,360]{1,0:T(8,128)S(1)}, f32[360,360]{1,0:T(8,128)}, u32[]{:S(2)}) copy-start(f32[360,360]{1,0:T(8,128)} %param.3) | copy-start | bytes 1555204
  6.5 102.8 %all-gather.3.cloned.1.call-start = ((), (), s32[]{:S(2)}) async-start(), calls=%async_computation | async-start | bytes 5013504 | tf_op jit(solution)/shard_map/all_gather | solution.py:37
  6.5 53.0 %collective-permute-start = (f32[192,360]{1,0:T(8,128)}, f32[192,360]{1,0:T(8,128)S(1)}, u32[]{:S(2)}, u32[]{:S(2)}) collective-permute-start(f32[192,360]{1,0:T(8,128)} %param.2), channel_id=1, source_target_pairs={{0,0},{2,32},{4,64},{6,96},{8,128},{10,160},{12,192},{14,224},{16,... | collective-permute-start | bytes 829448 | tf_op jit(solution)/shard_map/ppermute | solution.py:36
  59.5 0.7 copy-start.2
  111.1 12.6 %collective-permute-start.8 = (f32[192,360]{1,0:T(8,128)S(1)}, f32[192,360]{1,0:T(8,128)S(1)}, u32[]{:S(2)}, u32[]{:S(2)}) collective-permute-start(f32[192,360]{1,0:T(8,128)S(1)} %fusion.13), channel_id=1, source_target_pairs={{0,480},{32,0},{64,32},{96,64},{128,96},{160,128},{192,160},{224,1... | collective-permute-start | bytes 829448 | tf_op jit(solution)/shard_map/ppermute | solution.py:23
  117.3 25.2 %copy-start.1 = (f32[3072,360]{1,0:T(8,128)S(1)}, f32[3072,360]{1,0:T(8,128)}, u32[]{:S(2)}) copy-start(f32[3072,360]{1,0:T(8,128)} %all-gather.3.cloned.1.call-done) | copy-start | bytes 13271044
  119.2 13.6 %collective-permute-start.1 = (f32[192,360]{1,0:T(8,128)S(1)}, f32[192,360]{1,0:T(8,128)S(1)}, u32[]{:S(2)}, u32[]{:S(2)}) collective-permute-start(f32[192,360]{1,0:T(8,128)S(1)} %fusion.28), channel_id=1, source_target_pairs={{0,32},{32,64},{64,96},{96,128},{128,160},{160,192},{192,224},{224... | collective-permute-start | bytes 829448 | tf_op jit(solution)/shard_map/ppermute | solution.py:22
  125.4 11.4 %collective-permute-start.9 = (f32[192,360]{1,0:T(8,128)S(1)}, f32[192,360]{1,0:T(8,128)S(1)}, u32[]{:S(2)}, u32[]{:S(2)}) collective-permute-start(f32[192,360]{1,0:T(8,128)S(1)} %convolution_add_fusion), channel_id=1, source_target_pairs={{0,480},{32,0},{64,32},{96,64},{128,96},{160,128},{192,160},{224,1... | collective-permute-start | bytes 829448 | tf_op jit(solution)/shard_map/ppermute | solution.py:23
  134.5 11.2 %collective-permute-start.2 = (f32[192,360]{1,0:T(8,128)S(1)}, f32[192,360]{1,0:T(8,128)S(1)}, u32[]{:S(2)}, u32[]{:S(2)}) collective-permute-start(f32[192,360]{1,0:T(8,128)S(1)} %convolution_add_fusion.1), channel_id=1, source_target_pairs={{0,32},{32,64},{64,96},{96,128},{128,160},{160,192},{192,224},{224... | collective-permute-start | bytes 829448 | tf_op jit(solution)/shard_map/ppermute | solution.py:22
  136.9 10.7 %collective-permute-start.10 = (f32[192,360]{1,0:T(8,128)S(1)}, f32[192,360]{1,0:T(8,128)S(1)}, u32[]{:S(2)}, u32[]{:S(2)}) collective-permute-start(f32[192,360]{1,0:T(8,128)S(1)} %add.252), channel_id=1, source_target_pairs={{0,480},{32,0},{64,32},{96,64},{128,96},{160,128},{192,160},{224,1... | collective-permute-start | bytes 829448 | tf_op jit(solution)/shard_map/ppermute | solution.py:23
  145.7 10.2 %collective-permute-start.3 = (f32[192,360]{1,0:T(8,128)S(1)}, f32[192,360]{1,0:T(8,128)S(1)}, u32[]{:S(2)}, u32[]{:S(2)}) collective-permute-start(f32[192,360]{1,0:T(8,128)S(1)} %add.227), channel_id=1, source_target_pairs={{0,32},{32,64},{64,96},{96,128},{128,160},{160,192},{192,224},{224... | collective-permute-start | bytes 829448 | tf_op jit(solution)/shard_map/ppermute | solution.py:22
  147.7 10.2 %collective-permute-start.11 = (f32[192,360]{1,0:T(8,128)S(1)}, f32[192,360]{1,0:T(8,128)S(1)}, u32[]{:S(2)}, u32[]{:S(2)}) collective-permute-start(f32[192,360]{1,0:T(8,128)S(1)} %add.256), channel_id=1, source_target_pairs={{0,480},{32,0},{64,32},{96,64},{128,96},{160,128},{192,160},{224,1... | collective-permute-start | bytes 829448 | tf_op jit(solution)/shard_map/ppermute | solution.py:23
  155.9 9.8 %collective-permute-start.4 = (f32[192,360]{1,0:T(8,128)S(1)}, f32[192,360]{1,0:T(8,128)S(1)}, u32[]{:S(2)}, u32[]{:S(2)}) collective-permute-start(f32[192,360]{1,0:T(8,128)S(1)} %add.230), channel_id=1, source_target_pairs={{0,32},{32,64},{64,96},{96,128},{128,160},{160,192},{192,224},{224... | collective-permute-start | bytes 829448 | tf_op jit(solution)/shard_map/ppermute | solution.py:22
  157.9 9.8 %collective-permute-start.12 = (f32[192,360]{1,0:T(8,128)S(1)}, f32[192,360]{1,0:T(8,128)S(1)}, u32[]{:S(2)}, u32[]{:S(2)}) collective-permute-start(f32[192,360]{1,0:T(8,128)S(1)} %add.260), channel_id=1, source_target_pairs={{0,480},{32,0},{64,32},{96,64},{128,96},{160,128},{192,160},{224,1... | collective-permute-start | bytes 829448 | tf_op jit(solution)/shard_map/ppermute | solution.py:23
  165.8 9.8 %collective-permute-start.5 = (f32[192,360]{1,0:T(8,128)S(1)}, f32[192,360]{1,0:T(8,128)S(1)}, u32[]{:S(2)}, u32[]{:S(2)}) collective-permute-start(f32[192,360]{1,0:T(8,128)S(1)} %add.233), channel_id=1, source_target_pairs={{0,32},{32,64},{64,96},{96,128},{128,160},{160,192},{192,224},{224... | collective-permute-start | bytes 829448 | tf_op jit(solution)/shard_map/ppermute | solution.py:22
  167.8 10.0 %collective-permute-start.13 = (f32[192,360]{1,0:T(8,128)S(1)}, f32[192,360]{1,0:T(8,128)S(1)}, u32[]{:S(2)}, u32[]{:S(2)}) collective-permute-start(f32[192,360]{1,0:T(8,128)S(1)} %add.264), channel_id=1, source_target_pairs={{0,480},{32,0},{64,32},{96,64},{128,96},{160,128},{192,160},{224,1... | collective-permute-start | bytes 829448 | tf_op jit(solution)/shard_map/ppermute | solution.py:23
  175.7 10.2 %collective-permute-start.6 = (f32[192,360]{1,0:T(8,128)S(1)}, f32[192,360]{1,0:T(8,128)S(1)}, u32[]{:S(2)}, u32[]{:S(2)}) collective-permute-start(f32[192,360]{1,0:T(8,128)S(1)} %add.236), channel_id=1, source_target_pairs={{0,32},{32,64},{64,96},{96,128},{128,160},{160,192},{192,224},{224... | collective-permute-start | bytes 829448 | tf_op jit(solution)/shard_map/ppermute | solution.py:22
  177.8 10.0 %collective-permute-start.14 = (f32[192,360]{1,0:T(8,128)S(1)}, f32[192,360]{1,0:T(8,128)S(1)}, u32[]{:S(2)}, u32[]{:S(2)}) collective-permute-start(f32[192,360]{1,0:T(8,128)S(1)} %add.268), channel_id=1, source_target_pairs={{0,480},{32,0},{64,32},{96,64},{128,96},{160,128},{192,160},{224,1... | collective-permute-start | bytes 829448 | tf_op jit(solution)/shard_map/ppermute | solution.py:23
  185.9 9.8 %collective-permute-start.7 = (f32[192,360]{1,0:T(8,128)S(1)}, f32[192,360]{1,0:T(8,128)S(1)}, u32[]{:S(2)}, u32[]{:S(2)}) collective-permute-start(f32[192,360]{1,0:T(8,128)S(1)} %add.239), channel_id=1, source_target_pairs={{0,32},{32,64},{64,96},{96,128},{128,160},{160,192},{192,224},{224... | collective-permute-start | bytes 829448 | tf_op jit(solution)/shard_map/ppermute | solution.py:22
  187.9 9.8 %collective-permute-start.15 = (f32[192,360]{1,0:T(8,128)S(1)}, f32[192,360]{1,0:T(8,128)S(1)}, u32[]{:S(2)}, u32[]{:S(2)}) collective-permute-start(f32[192,360]{1,0:T(8,128)S(1)} %add.272), channel_id=1, source_target_pairs={{0,480},{32,0},{64,32},{96,64},{128,96},{160,128},{192,160},{224,1... | collective-permute-start | bytes 829448 | tf_op jit(solution)/shard_map/ppermute | solution.py:23
  197.8 8.5 %collective-permute-start.16 = (f32[96,360]{1,0:T(8,128)S(1)}, f32[96,360]{1,0:T(8,128)S(1)}, u32[]{:S(2)}, u32[]{:S(2)}) collective-permute-start(f32[96,360]{1,0:T(8,128)S(1)} %constant_dynamic-slice_fusion), channel_id=1, source_target_pairs={{0,1},{1,0},{2,3},{3,2},{4,5},{5,4},{6,7},{7,6},{8,9},{9,8},{10,11... | collective-permute-start | bytes 414728 | tf_op jit(solution)/shard_map/ppermute | solution.py:42
Sparse Core Ops, SparseCore 0:
  60.4 48.9 all-gather.2

commit v11 on v4

--- a/solution.py
+++ b/solution.py
@@ -3,8 +3,8 @@
 from jax import lax
 from jax.sharding import PartitionSpec as P
 
-FIRST_DOT_STEP = 5
-DOTS_PER_STEP = 5
+FIRST_DOT_STEP = 6
+DOTS_PER_STEP = 6
 
 
 def gather_col(block):

time: 157 us -> 155 us (0.987)
  waiting for transfers between devices: 40.5 us -> 38.5 us
where the time goes in v11:
time: 155 us; the launch traced here: 154 us
  starting transfers between devices  89.5 us (58%)
  waiting for transfers between devices  38.5 us (25%)
  matrix products  18.8 us (12%)
  other arithmetic  3.96 us (3%)
  local copies, waits for them, and re-layouts  1.84 us (1%)
    ppermute x7, starting transfers between devices, local(): behind = lax.ppermute(behind, 'row', bwd)  44.6 us
    ppermute x7, waiting for transfers between devices, local(): ahead = lax.ppermute(ahead, 'row', fwd)  26 us
    dot_general x17, matrix products, product(): jnp.dot(cols[:, lo:hi], block, precision=lax.Precision.HIGHEST, preferred...  18.8 us
    ppermute x7, starting transfers between devices, local(): ahead = lax.ppermute(ahead, 'row', fwd)  15.3 us
    ppermute x1, starting transfers between devices, local(): bottom = lax.ppermute(behind[m:], 'row', bwd)  5.6 us
    ppermute x1, waiting for transfers between devices, local(): other = lax.ppermute(other, 'depth', [(0, 1), (1, 0)])  5.21 us
    ppermute x1, starting transfers between devices, gather_col(): opp_b = lax.ppermute(above[:, h:], 'col', down)  4.84 us
    ppermute x1, starting transfers between devices, gather_col(): above = lax.ppermute(quad, 'col', down)  3.57 us
  transfers between devices with their start and end apart: 23, of which 12 were waited for; matrix products, arithmetic and copies ran while one was open for 14% of the time, Pallas kernels for 0%

profile of v11, /device:TPU:6, one launch (start us, length us, event | category | flops | bytes accessed | tf_op | source)
XLA Modules:
  0.0 154.0 jit_solution(8172530941367187112)
XLA Ops:
  0.0 1.9 %collective-permute-start = (f32[192,360]{1,0:T(8,128)}, f32[192,360]{1,0:T(8,128)S(1)}, u32[]{:S(2)}, u32[]{:S(2)}) collective-permute-start(f32[192,360]{1,0:T(8,128)} %param.2), channel_id=1, source_target_pairs={{0,2},{2,0},{4,6},{6,4},{8,10},{10,8},{12,14},{14,12},{16,18},{18,... | collective-permute-start | bytes 829448 | tf_op jit(solution)/shard_map/ppermute | solution.py:15
  4.8 2.7 %collective-permute-start.1 = (f32[2,192,360]{2,1,0:T(8,128)S(1)}, f32[2,192,360]{2,1,0:T(8,128)S(1)}, u32[]{:S(2)}, u32[]{:S(2)}) collective-permute-start(f32[2,192,360]{2,1,0:T(8,128)S(1)} %maximum_select_fusion.1), channel_id=1, source_target_pairs={{0,4},{2,6},{4,0},{6,2},{8,12},{10,14},{12,8},{14,10},{16,20},{18,... | collective-permute-start | bytes 1658888 | tf_op jit(solution)/shard_map/ppermute | solution.py:17
  7.5 3.8 %collective-permute-start.6 = (f32[360,360]{1,0:T(8,128)}, f32[360,360]{1,0:T(8,128)}, u32[]{:S(2)}, u32[]{:S(2)}) collective-permute-start(f32[360,360]{1,0:T(8,128)} %param.3), channel_id=1, source_target_pairs={{0,32},{32,64},{64,96},{96,128},{128,160},{160,192},{192,224},{224... | collective-permute-start | bytes 1555208 | tf_op jit(solution)/shard_map/ppermute | solution.py:61
  11.4 9.5 %collective-permute-start.7 = (f32[360,360]{1,0:T(8,128)}, f32[360,360]{1,0:T(8,128)}, u32[]{:S(2)}, u32[]{:S(2)}) collective-permute-start(f32[360,360]{1,0:T(8,128)} %param.3), channel_id=1, source_target_pairs={{0,480},{32,0},{64,32},{96,64},{128,96},{160,128},{192,160},{224,1... | collective-permute-start | bytes 1555208 | tf_op jit(solution)/shard_map/ppermute | solution.py:63
  22.1 3.5 %collective-permute-start.3 = (f32[4,192,360]{2,1,0:T(8,128)S(1)}, f32[4,192,360]{2,1,0:T(8,128)S(1)}, u32[]{:S(2)}, u32[]{:S(2)}) collective-permute-start(f32[4,192,360]{2,1,0:T(8,128)S(1)} %maximum_select_fusion), channel_id=1, source_target_pairs={{0,8},{2,10},{4,12},{6,14},{8,16},{10,18},{12,20},{14,22},{16,24},... | collective-permute-start | bytes 3317768 | tf_op jit(solution)/shard_map/ppermute | solution.py:21
  25.6 3.6 %collective-permute-start.2 = (f32[4,192,360]{2,1,0:T(8,128)S(1)}, f32[4,192,360]{2,1,0:T(8,128)S(1)}, u32[]{:S(2)}, u32[]{:S(2)}) collective-permute-start(f32[4,192,360]{2,1,0:T(8,128)S(1)} %maximum_select_fusion), channel_id=1, source_target_pairs={{0,24},{2,26},{4,28},{6,30},{8,0},{10,2},{12,4},{14,6},{16,8},{18,... | collective-permute-start | bytes 3317768 | tf_op jit(solution)/shard_map/ppermute | solution.py:22
  29.2 2.6 %collective-permute-done.6 = f32[360,360]{1,0:T(8,128)} collective-permute-done((f32[360,360]{1,0:T(8,128)}, f32[360,360]{1,0:T(8,128)}, u32[]{:S(2)}, u32[]{:S(2)}) %collective-permute-start.6) | collective-permute-done | bytes 518432 | tf_op jit(solution)/shard_map/ppermute | solution.py:61
  31.8 1.9 %collective-permute-start.8 = (f32[360,360]{1,0:T(8,128)}, f32[360,360]{1,0:T(8,128)S(1)}, u32[]{:S(2)}, u32[]{:S(2)}) collective-permute-start(f32[360,360]{1,0:T(8,128)} %collective-permute-done.6), channel_id=1, source_target_pairs={{0,32},{32,64},{64,96},{96,128},{128,160},{160,192},{192,224},{224... | collective-permute-start | bytes 1555208 | tf_op jit(solution)/shard_map/ppermute | solution.py:61
  33.7 8.8 %collective-permute-start.9 = (f32[360,360]{1,0:T(8,128)}, f32[360,360]{1,0:T(8,128)S(1)}, u32[]{:S(2)}, u32[]{:S(2)}) collective-permute-start(f32[360,360]{1,0:T(8,128)} %collective-permute-done.7), channel_id=1, source_target_pairs={{0,480},{32,0},{64,32},{96,64},{128,96},{160,128},{192,160},{224,1... | collective-permute-start | bytes 1555208 | tf_op jit(solution)/shard_map/ppermute | solution.py:63
  42.6 9.9 %collective-permute-done.8 = f32[360,360]{1,0:T(8,128)S(1)} collective-permute-done((f32[360,360]{1,0:T(8,128)}, f32[360,360]{1,0:T(8,128)S(1)}, u32[]{:S(2)}, u32[]{:S(2)}) %collective-permute-start.8) | collective-permute-done | bytes 518432 | tf_op jit(solution)/shard_map/ppermute | solution.py:61
  52.4 1.9 %collective-permute-start.10 = (f32[360,360]{1,0:T(8,128)S(1)}, f32[360,360]{1,0:T(8,128)}, u32[]{:S(2)}, u32[]{:S(2)}) collective-permute-start(f32[360,360]{1,0:T(8,128)S(1)} %collective-permute-done.8), channel_id=1, source_target_pairs={{0,32},{32,64},{64,96},{96,128},{128,160},{160,192},{192,224},{224... | collective-permute-start | bytes 1555208 | tf_op jit(solution)/shard_map/ppermute | solution.py:61
  54.4 5.1 %collective-permute-start.14 = (f32[360,360]{1,0:T(8,128)S(1)}, f32[360,360]{1,0:T(8,128)}, u32[]{:S(2)}, u32[]{:S(2)}) collective-permute-start(f32[360,360]{1,0:T(8,128)S(1)} %collective-permute-done.9), channel_id=1, source_target_pairs={{0,480},{32,0},{64,32},{96,64},{128,96},{160,128},{192,160},{224,1... | collective-permute-start | bytes 1555208 | tf_op jit(solution)/shard_map/ppermute | solution.py:63
  60.4 2.2 %collective-permute-start.4 = (f32[4,96,360]{2,1,0:T(8,128)}, f32[4,96,360]{2,1,0:T(8,128)}, u32[]{:S(2)}, u32[]{:S(2)}) collective-permute-start(f32[4,96,360]{2,1,0:T(8,128)} %slice.24), channel_id=1, source_target_pairs={{0,8},{2,10},{4,12},{6,14},{8,16},{10,18},{12,20},{14,22},{16,24},... | collective-permute-start | bytes 1658888 | tf_op jit(solution)/shard_map/ppermute | solution.py:24
  63.5 4.8 %collective-permute-start.5 = (f32[4,96,360]{2,1,0:T(8,128)}, f32[4,96,360]{2,1,0:T(8,128)}, u32[]{:S(2)}, u32[]{:S(2)}) collective-permute-start(f32[4,96,360]{2,1,0:T(8,128)} %slice.25), channel_id=1, source_target_pairs={{0,24},{2,26},{4,28},{6,30},{8,0},{10,2},{12,4},{14,6},{16,8},{18,... | collective-permute-start | bytes 1658888 | tf_op jit(solution)/shard_map/ppermute | solution.py:25
  68.4 1.9 %collective-permute-start.11 = (f32[360,360]{1,0:T(8,128)}, f32[360,360]{1,0:T(8,128)}, u32[]{:S(2)}, u32[]{:S(2)}) collective-permute-start(f32[360,360]{1,0:T(8,128)} %collective-permute-done.10), channel_id=1, source_target_pairs={{0,32},{32,64},{64,96},{96,128},{128,160},{160,192},{192,224},{224... | collective-permute-start | bytes 1555208 | tf_op jit(solution)/shard_map/ppermute | solution.py:61
  70.3 5.1 %collective-permute-start.15 = (f32[360,360]{1,0:T(8,128)}, f32[360,360]{1,0:T(8,128)}, u32[]{:S(2)}, u32[]{:S(2)}) collective-permute-start(f32[360,360]{1,0:T(8,128)} %collective-permute-done.14), channel_id=1, source_target_pairs={{0,480},{32,0},{64,32},{96,64},{128,96},{160,128},{192,160},{224,1... | collective-permute-start | bytes 1555208 | tf_op jit(solution)/shard_map/ppermute | solution.py:63
  76.4 7.4 %collective-permute-done.11 = f32[360,360]{1,0:T(8,128)} collective-permute-done((f32[360,360]{1,0:T(8,128)}, f32[360,360]{1,0:T(8,128)}, u32[]{:S(2)}, u32[]{:S(2)}) %collective-permute-start.11) | collective-permute-done | bytes 518432 | tf_op jit(solution)/shard_map/ppermute | solution.py:61
  83.8 1.9 %collective-permute-start.12 = (f32[360,360]{1,0:T(8,128)}, f32[360,360]{1,0:T(8,128)S(1)}, u32[]{:S(2)}, u32[]{:S(2)}) collective-permute-start(f32[360,360]{1,0:T(8,128)} %collective-permute-done.11), channel_id=1, source_target_pairs={{0,32},{32,64},{64,96},{96,128},{128,160},{160,192},{192,224},{224... | collective-permute-start | bytes 1555208 | tf_op jit(solution)/shard_map/ppermute | solution.py:61
  85.7 5.1 %collective-permute-start.16 = (f32[360,360]{1,0:T(8,128)}, f32[360,360]{1,0:T(8,128)S(1)}, u32[]{:S(2)}, u32[]{:S(2)}) collective-permute-start(f32[360,360]{1,0:T(8,128)} %collective-permute-done.15), channel_id=1, source_target_pairs={{0,480},{32,0},{64,32},{96,64},{128,96},{160,128},{192,160},{224,1... | collective-permute-start | bytes 1555208 | tf_op jit(solution)/shard_map/ppermute | solution.py:63
  90.9 2.1 %pad_maximum_fusion = f32[16,192,360]{2,1,0:T(8,128)S(1)} fusion(f32[4,192,360]{2,1,0:T(8,128)S(1)} %collective-permute-done.3, f32[4,96,360]{2,1,0:T(8,128)} %collective-permute-done.5, f32[4,96,360]{2,1,0:T(8,128)} %collective-permute-done.4, f32[4,192,360]{2,1,0:T(8,128)S(1)} %collective-permute-done.2, f32[4,192,360]{2,1,0:T(8,128)S(1)} %maximum_select_fusion), kind=kLoop, calls=%fused_computation | loop fusion | flops 4423680 | bytes 8847360 | tf_op jit(solution)/shard_map/concatenate | solution.py:27
  93.0 1.9 %fusion.18 = f32[192,360]{1,0:T(8,128)S(1)} fusion(f32[360,360]{1,0:T(8,128)} %collective-permute-done.14, f32[16,192,360]{2,1,0:T(8,128)S(1)} %pad_maximum_fusion, s32[]{:T(128)S(6)} %select_n.374), kind=kOutput, calls=%fused_computation.28 | convolution fusion | flops 298598400 | bytes 1089796 | tf_op jit(solution)/shard_map/dot_general | solution.py:48
  102.7 1.9 %collective-permute-start.13 = (f32[360,360]{1,0:T(8,128)S(1)}, f32[360,360]{1,0:T(8,128)S(1)}, u32[]{:S(2)}, u32[]{:S(2)}) collective-permute-start(f32[360,360]{1,0:T(8,128)S(1)} %collective-permute-done.12), channel_id=1, source_target_pairs={{0,32},{32,64},{64,96},{96,128},{128,160},{160,192},{192,224},{224... | collective-permute-start | bytes 1555208 | tf_op jit(solution)/shard_map/ppermute | solution.py:61
  104.6 5.1 %collective-permute-start.17 = (f32[360,360]{1,0:T(8,128)S(1)}, f32[360,360]{1,0:T(8,128)S(1)}, u32[]{:S(2)}, u32[]{:S(2)}) collective-permute-start(f32[360,360]{1,0:T(8,128)S(1)} %collective-permute-done.16), channel_id=1, source_target_pairs={{0,480},{32,0},{64,32},{96,64},{128,96},{160,128},{192,160},{224,1... | collective-permute-start | bytes 1555208 | tf_op jit(solution)/shard_map/ppermute | solution.py:63
  112.4 4.0 %collective-permute-done.13 = f32[360,360]{1,0:T(8,128)S(1)} collective-permute-done((f32[360,360]{1,0:T(8,128)S(1)}, f32[360,360]{1,0:T(8,128)S(1)}, u32[]{:S(2)}, u32[]{:S(2)}) %collective-permute-start.13) | collective-permute-done | bytes 518432 | tf_op jit(solution)/shard_map/ppermute | solution.py:61
  117.6 1.9 %collective-permute-start.18 = (f32[360,360]{1,0:T(8,128)S(1)}, f32[360,360]{1,0:T(8,128)S(1)}, u32[]{:S(2)}, u32[]{:S(2)}) collective-permute-start(f32[360,360]{1,0:T(8,128)S(1)} %collective-permute-done.13), channel_id=1, source_target_pairs={{0,32},{32,64},{64,96},{96,128},{128,160},{160,192},{192,224},{224... | collective-permute-start | bytes 1555208 | tf_op jit(solution)/shard_map/ppermute | solution.py:61
  119.5 5.8 %collective-permute-start.19 = (f32[360,360]{1,0:T(8,128)S(1)}, f32[360,360]{1,0:T(8,128)S(1)}, u32[]{:S(2)}, u32[]{:S(2)}) collective-permute-start(f32[360,360]{1,0:T(8,128)S(1)} %collective-permute-done.17), channel_id=1, source_target_pairs={{0,480},{32,0},{64,32},{96,64},{128,96},{160,128},{192,160},{224,1... | collective-permute-start | bytes 1555208 | tf_op jit(solution)/shard_map/ppermute | solution.py:63
  125.3 1.8 %fusion.2 = f32[192,360]{1,0:T(8,128)S(1)} fusion(f32[192,360]{1,0:T(8,128)S(1)} %fusion.15, f32[360,360]{1,0:T(8,128)} %collective-permute-done.11, f32[16,192,360]{2,1,0:T(8,128)S(1)} %pad_maximum_fusion, s32[]{:T(128)S(6)} %select_n.379, f32[192,360]{1,0:T(8,128)S(1)} %convolution_add_fusion.4, f32[192,360]{1,0:T(8,128)S(1)} %fusion.18), kind=kOutput, calls=%fused_computation.11 | convolution fusion | flops 298805760 | bytes 1974532 | tf_op jit(solution)/shard_map/dot_general | solution.py:48
  128.6 2.1 %collective-permute-done.18 = f32[360,360]{1,0:T(8,128)S(1)} collective-permute-done((f32[360,360]{1,0:T(8,128)S(1)}, f32[360,360]{1,0:T(8,128)S(1)}, u32[]{:S(2)}, u32[]{:S(2)}) %collective-permute-start.18) | collective-permute-done | bytes 518432 | tf_op jit(solution)/shard_map/ppermute | solution.py:61
  132.1 1.9 %collective-permute-start.20 = (f32[180,360]{1,0:T(8,128)S(1)}, f32[180,360]{1,0:T(8,128)S(1)}, u32[]{:S(2)}, u32[]{:S(2)}) collective-permute-start(f32[180,360]{1,0:T(8,128)S(1)} %slice.20), channel_id=1, source_target_pairs={{0,32},{32,64},{64,96},{96,128},{128,160},{160,192},{192,224},{224... | collective-permute-start | bytes 777608 | tf_op jit(solution)/shard_map/ppermute | solution.py:67
  134.1 5.6 %collective-permute-start.21 = (f32[180,360]{1,0:T(8,128)S(1)}, f32[180,360]{1,0:T(8,128)S(1)}, u32[]{:S(2)}, u32[]{:S(2)}) collective-permute-start(f32[180,360]{1,0:T(8,128)S(1)} %slice.21), channel_id=1, source_target_pairs={{0,480},{32,0},{64,32},{96,64},{128,96},{160,128},{192,160},{224,1... | collective-permute-start | bytes 777608 | tf_op jit(solution)/shard_map/ppermute | solution.py:68
  144.8 3.3 %collective-permute-start.22 = (f32[96,360]{1,0:T(8,128)S(1)}, f32[96,360]{1,0:T(8,128)S(1)}, u32[]{:S(2)}, u32[]{:S(2)}) collective-permute-start(f32[96,360]{1,0:T(8,128)S(1)} %constant_dynamic-slice_fusion), channel_id=1, source_target_pairs={{0,1},{1,0},{2,3},{3,2},{4,5},{5,4},{6,7},{7,6},{8,9},{9,8},{10,11... | collective-permute-start | bytes 414728 | tf_op jit(solution)/shard_map/ppermute | solution.py:85
  148.1 5.2 %collective-permute-done.22 = f32[96,360]{1,0:T(8,128)S(1)} collective-permute-done((f32[96,360]{1,0:T(8,128)S(1)}, f32[96,360]{1,0:T(8,128)S(1)}, u32[]{:S(2)}, u32[]{:S(2)}) %collective-permute-start.22) | collective-permute-done | bytes 138272 | tf_op jit(solution)/shard_map/ppermute | solution.py:85
  (51 shorter events, 26.0 us)
Async XLA Ops:
  0.0 3.7 %collective-permute-start = (f32[192,360]{1,0:T(8,128)}, f32[192,360]{1,0:T(8,128)S(1)}, u32[]{:S(2)}, u32[]{:S(2)}) collective-permute-start(f32[192,360]{1,0:T(8,128)} %param.2), channel_id=1, source_target_pairs={{0,2},{2,0},{4,6},{6,4},{8,10},{10,8},{12,14},{14,12},{16,18},{18,... | collective-permute-start | bytes 829448 | tf_op jit(solution)/shard_map/ppermute | solution.py:15
  4.8 17.3 %collective-permute-start.1 = (f32[2,192,360]{2,1,0:T(8,128)S(1)}, f32[2,192,360]{2,1,0:T(8,128)S(1)}, u32[]{:S(2)}, u32[]{:S(2)}) collective-permute-start(f32[2,192,360]{2,1,0:T(8,128)S(1)} %maximum_select_fusion.1), channel_id=1, source_target_pairs={{0,4},{2,6},{4,0},{6,2},{8,12},{10,14},{12,8},{14,10},{16,20},{18,... | collective-permute-start | bytes 1658888 | tf_op jit(solution)/shard_map/ppermute | solution.py:17
  7.5 24.3 %collective-permute-start.6 = (f32[360,360]{1,0:T(8,128)}, f32[360,360]{1,0:T(8,128)}, u32[]{:S(2)}, u32[]{:S(2)}) collective-permute-start(f32[360,360]{1,0:T(8,128)} %param.3), channel_id=1, source_target_pairs={{0,32},{32,64},{64,96},{96,128},{128,160},{160,192},{192,224},{224... | collective-permute-start | bytes 1555208 | tf_op jit(solution)/shard_map/ppermute | solution.py:61
  11.4 22.4 %collective-permute-start.7 = (f32[360,360]{1,0:T(8,128)}, f32[360,360]{1,0:T(8,128)}, u32[]{:S(2)}, u32[]{:S(2)}) collective-permute-start(f32[360,360]{1,0:T(8,128)} %param.3), channel_id=1, source_target_pairs={{0,480},{32,0},{64,32},{96,64},{128,96},{160,128},{192,160},{224,1... | collective-permute-start | bytes 1555208 | tf_op jit(solution)/shard_map/ppermute | solution.py:63
  22.1 37.4 %collective-permute-start.3 = (f32[4,192,360]{2,1,0:T(8,128)S(1)}, f32[4,192,360]{2,1,0:T(8,128)S(1)}, u32[]{:S(2)}, u32[]{:S(2)}) collective-permute-start(f32[4,192,360]{2,1,0:T(8,128)S(1)} %maximum_select_fusion), channel_id=1, source_target_pairs={{0,8},{2,10},{4,12},{6,14},{8,16},{10,18},{12,20},{14,22},{16,24},... | collective-permute-start | bytes 3317768 | tf_op jit(solution)/shard_map/ppermute | solution.py:21
  25.6 37.0 %collective-permute-start.2 = (f32[4,192,360]{2,1,0:T(8,128)S(1)}, f32[4,192,360]{2,1,0:T(8,128)S(1)}, u32[]{:S(2)}, u32[]{:S(2)}) collective-permute-start(f32[4,192,360]{2,1,0:T(8,128)S(1)} %maximum_select_fusion), channel_id=1, source_target_pairs={{0,24},{2,26},{4,28},{6,30},{8,0},{10,2},{12,4},{14,6},{16,8},{18,... | collective-permute-start | bytes 3317768 | tf_op jit(solution)/shard_map/ppermute | solution.py:22
  31.8 20.6 %collective-permute-start.8 = (f32[360,360]{1,0:T(8,128)}, f32[360,360]{1,0:T(8,128)S(1)}, u32[]{:S(2)}, u32[]{:S(2)}) collective-permute-start(f32[360,360]{1,0:T(8,128)} %collective-permute-done.6), channel_id=1, source_target_pairs={{0,32},{32,64},{64,96},{96,128},{128,160},{160,192},{192,224},{224... | collective-permute-start | bytes 1555208 | tf_op jit(solution)/shard_map/ppermute | solution.py:61
  33.7 20.6 %collective-permute-start.9 = (f32[360,360]{1,0:T(8,128)}, f32[360,360]{1,0:T(8,128)S(1)}, u32[]{:S(2)}, u32[]{:S(2)}) collective-permute-start(f32[360,360]{1,0:T(8,128)} %collective-permute-done.7), channel_id=1, source_target_pairs={{0,480},{32,0},{64,32},{96,64},{128,96},{160,128},{192,160},{224,1... | collective-permute-start | bytes 1555208 | tf_op jit(solution)/shard_map/ppermute | solution.py:63
  52.4 10.2 %copy-start.1 = (f32[360,360]{1,0:T(8,128)}, f32[360,360]{1,0:T(8,128)S(1)}, u32[]{:S(2)}) copy-start(f32[360,360]{1,0:T(8,128)S(1)} %collective-permute-done.8) | copy-start | bytes 1555204
  52.4 15.9 %collective-permute-start.10 = (f32[360,360]{1,0:T(8,128)S(1)}, f32[360,360]{1,0:T(8,128)}, u32[]{:S(2)}, u32[]{:S(2)}) collective-permute-start(f32[360,360]{1,0:T(8,128)S(1)} %collective-permute-done.8), channel_id=1, source_target_pairs={{0,32},{32,64},{64,96},{96,128},{128,160},{160,192},{192,224},{224... | collective-permute-start | bytes 1555208 | tf_op jit(solution)/shard_map/ppermute | solution.py:61
  54.4 14.0 %copy-start.3 = (f32[360,360]{1,0:T(8,128)}, f32[360,360]{1,0:T(8,128)S(1)}, u32[]{:S(2)}) copy-start(f32[360,360]{1,0:T(8,128)S(1)} %collective-permute-done.9) | copy-start | bytes 1555204
  54.4 15.9 %collective-permute-start.14 = (f32[360,360]{1,0:T(8,128)S(1)}, f32[360,360]{1,0:T(8,128)}, u32[]{:S(2)}, u32[]{:S(2)}) collective-permute-start(f32[360,360]{1,0:T(8,128)S(1)} %collective-permute-done.9), channel_id=1, source_target_pairs={{0,480},{32,0},{64,32},{96,64},{128,96},{160,128},{192,160},{224,1... | collective-permute-start | bytes 1555208 | tf_op jit(solution)/shard_map/ppermute | solution.py:63
  60.4 30.5 %collective-permute-start.4 = (f32[4,96,360]{2,1,0:T(8,128)}, f32[4,96,360]{2,1,0:T(8,128)}, u32[]{:S(2)}, u32[]{:S(2)}) collective-permute-start(f32[4,96,360]{2,1,0:T(8,128)} %slice.24), channel_id=1, source_target_pairs={{0,8},{2,10},{4,12},{6,14},{8,16},{10,18},{12,20},{14,22},{16,24},... | collective-permute-start | bytes 1658888 | tf_op jit(solution)/shard_map/ppermute | solution.py:24
  63.5 27.4 %collective-permute-start.5 = (f32[4,96,360]{2,1,0:T(8,128)}, f32[4,96,360]{2,1,0:T(8,128)}, u32[]{:S(2)}, u32[]{:S(2)}) collective-permute-start(f32[4,96,360]{2,1,0:T(8,128)} %slice.25), channel_id=1, source_target_pairs={{0,24},{2,26},{4,28},{6,30},{8,0},{10,2},{12,4},{14,6},{16,8},{18,... | collective-permute-start | bytes 1658888 | tf_op jit(solution)/shard_map/ppermute | solution.py:25
  68.4 15.5 %collective-permute-start.11 = (f32[360,360]{1,0:T(8,128)}, f32[360,360]{1,0:T(8,128)}, u32[]{:S(2)}, u32[]{:S(2)}) collective-permute-start(f32[360,360]{1,0:T(8,128)} %collective-permute-done.10), channel_id=1, source_target_pairs={{0,32},{32,64},{64,96},{96,128},{128,160},{160,192},{192,224},{224... | collective-permute-start | bytes 1555208 | tf_op jit(solution)/shard_map/ppermute | solution.py:61
  70.3 15.4 %collective-permute-start.15 = (f32[360,360]{1,0:T(8,128)}, f32[360,360]{1,0:T(8,128)}, u32[]{:S(2)}, u32[]{:S(2)}) collective-permute-start(f32[360,360]{1,0:T(8,128)} %collective-permute-done.14), channel_id=1, source_target_pairs={{0,480},{32,0},{64,32},{96,64},{128,96},{160,128},{192,160},{224,1... | collective-permute-start | bytes 1555208 | tf_op jit(solution)/shard_map/ppermute | solution.py:63
  76.4 24.0 %copy-start.4 = (f32[360,360]{1,0:T(8,128)S(1)}, f32[360,360]{1,0:T(8,128)}, u32[]{:S(2)}) copy-start(f32[360,360]{1,0:T(8,128)} %copy-done.3) | copy-start | bytes 1555204
  83.8 18.9 %collective-permute-start.12 = (f32[360,360]{1,0:T(8,128)}, f32[360,360]{1,0:T(8,128)S(1)}, u32[]{:S(2)}, u32[]{:S(2)}) collective-permute-start(f32[360,360]{1,0:T(8,128)} %collective-permute-done.11), channel_id=1, source_target_pairs={{0,32},{32,64},{64,96},{96,128},{128,160},{160,192},{192,224},{224... | collective-permute-start | bytes 1555208 | tf_op jit(solution)/shard_map/ppermute | solution.py:61
  85.7 18.9 %collective-permute-start.16 = (f32[360,360]{1,0:T(8,128)}, f32[360,360]{1,0:T(8,128)S(1)}, u32[]{:S(2)}, u32[]{:S(2)}) collective-permute-start(f32[360,360]{1,0:T(8,128)} %collective-permute-done.15), channel_id=1, source_target_pairs={{0,480},{32,0},{64,32},{96,64},{128,96},{160,128},{192,160},{224,1... | collective-permute-start | bytes 1555208 | tf_op jit(solution)/shard_map/ppermute | solution.py:63
  93.0 8.1 %copy-start = (f32[360,360]{1,0:T(8,128)S(1)}, f32[360,360]{1,0:T(8,128)}, u32[]{:S(2)}) copy-start(f32[360,360]{1,0:T(8,128)} %param.3) | copy-start | bytes 1555204
  93.0 8.9 %copy-start.2 = (f32[360,360]{1,0:T(8,128)S(1)}, f32[360,360]{1,0:T(8,128)}, u32[]{:S(2)}) copy-start(f32[360,360]{1,0:T(8,128)} %copy-done.1) | copy-start | bytes 1555204
  102.7 13.7 %collective-permute-start.13 = (f32[360,360]{1,0:T(8,128)S(1)}, f32[360,360]{1,0:T(8,128)S(1)}, u32[]{:S(2)}, u32[]{:S(2)}) collective-permute-start(f32[360,360]{1,0:T(8,128)S(1)} %collective-permute-done.12), channel_id=1, source_target_pairs={{0,32},{32,64},{64,96},{96,128},{128,160},{160,192},{192,224},{224... | collective-permute-start | bytes 1555208 | tf_op jit(solution)/shard_map/ppermute | solution.py:61
  104.6 12.9 %collective-permute-start.17 = (f32[360,360]{1,0:T(8,128)S(1)}, f32[360,360]{1,0:T(8,128)S(1)}, u32[]{:S(2)}, u32[]{:S(2)}) collective-permute-start(f32[360,360]{1,0:T(8,128)S(1)} %collective-permute-done.16), channel_id=1, source_target_pairs={{0,480},{32,0},{64,32},{96,64},{128,96},{160,128},{192,160},{224,1... | collective-permute-start | bytes 1555208 | tf_op jit(solution)/shard_map/ppermute | solution.py:63
  117.6 13.2 %collective-permute-start.18 = (f32[360,360]{1,0:T(8,128)S(1)}, f32[360,360]{1,0:T(8,128)S(1)}, u32[]{:S(2)}, u32[]{:S(2)}) collective-permute-start(f32[360,360]{1,0:T(8,128)S(1)} %collective-permute-done.13), channel_id=1, source_target_pairs={{0,32},{32,64},{64,96},{96,128},{128,160},{160,192},{192,224},{224... | collective-permute-start | bytes 1555208 | tf_op jit(solution)/shard_map/ppermute | solution.py:61
  119.5 12.6 %collective-permute-start.19 = (f32[360,360]{1,0:T(8,128)S(1)}, f32[360,360]{1,0:T(8,128)S(1)}, u32[]{:S(2)}, u32[]{:S(2)}) collective-permute-start(f32[360,360]{1,0:T(8,128)S(1)} %collective-permute-done.17), channel_id=1, source_target_pairs={{0,480},{32,0},{64,32},{96,64},{128,96},{160,128},{192,160},{224,1... | collective-permute-start | bytes 1555208 | tf_op jit(solution)/shard_map/ppermute | solution.py:63
  132.1 10.2 %collective-permute-start.20 = (f32[180,360]{1,0:T(8,128)S(1)}, f32[180,360]{1,0:T(8,128)S(1)}, u32[]{:S(2)}, u32[]{:S(2)}) collective-permute-start(f32[180,360]{1,0:T(8,128)S(1)} %slice.20), channel_id=1, source_target_pairs={{0,32},{32,64},{64,96},{96,128},{128,160},{160,192},{192,224},{224... | collective-permute-start | bytes 777608 | tf_op jit(solution)/shard_map/ppermute | solution.py:67
  134.1 9.7 %collective-permute-start.21 = (f32[180,360]{1,0:T(8,128)S(1)}, f32[180,360]{1,0:T(8,128)S(1)}, u32[]{:S(2)}, u32[]{:S(2)}) collective-permute-start(f32[180,360]{1,0:T(8,128)S(1)} %slice.21), channel_id=1, source_target_pairs={{0,480},{32,0},{64,32},{96,64},{128,96},{160,128},{192,160},{224,1... | collective-permute-start | bytes 777608 | tf_op jit(solution)/shard_map/ppermute | solution.py:68
  144.8 8.5 %collective-permute-start.22 = (f32[96,360]{1,0:T(8,128)S(1)}, f32[96,360]{1,0:T(8,128)S(1)}, u32[]{:S(2)}, u32[]{:S(2)}) collective-permute-start(f32[96,360]{1,0:T(8,128)S(1)} %constant_dynamic-slice_fusion), channel_id=1, source_target_pairs={{0,1},{1,0},{2,3},{3,2},{4,5},{5,4},{6,7},{7,6},{8,9},{9,8},{10,11... | collective-permute-start | bytes 414728 | tf_op jit(solution)/shard_map/ppermute | solution.py:85

commit v12 on v11

--- a/solution.py
+++ b/solution.py
@@ -3,8 +3,8 @@
 from jax import lax
 from jax.sharding import PartitionSpec as P
 
-FIRST_DOT_STEP = 6
-DOTS_PER_STEP = 6
+FIRST_DOT_STEP = 7
+DOTS_PER_STEP = 8
 
 
 def gather_col(block):
@@ -40,6 +40,12 @@
     rows = amplitudes.shape[0]
     half = rows // 2
 
+    fwd = [(i, (i + 1) % n) for i in range(n)]
+    bwd = [(i, (i - 1) % n) for i in range(n)]
+    first_ahead = lax.ppermute(integrals, "row", fwd)
+    first_behind = lax.ppermute(integrals, "row", bwd)
+    amplitudes, first_ahead, first_behind = lax.optimization_barrier(
+        (amplitudes, first_ahead, first_behind))
     strip, place = gather_col(amplitudes)
 
     def product(block, owner, lo=0, hi=None):
@@ -48,8 +54,6 @@
         return jnp.dot(cols[:, lo:hi], block, precision=lax.Precision.HIGHEST,
                        preferred_element_type=jnp.float32)
 
-    fwd = [(i, (i + 1) % n) for i in range(n)]
-    bwd = [(i, (i - 1) % n) for i in range(n)]
     total = None
     pending = [(integrals, me, 0, kb)]
     ahead = integrals
@@ -57,7 +61,11 @@
     last = n // 2
     for step in range(1, last + 1):
         arrived = []
-        if step < last:
+        if step == 1:
+            ahead, behind = first_ahead, first_behind
+            arrived.append((ahead, (me - step) % n, 0, kb))
+            arrived.append((behind, (me + step) % n, 0, kb))
+        elif step < last:
             ahead = lax.ppermute(ahead, "row", fwd)
             arrived.append((ahead, (me - step) % n, 0, kb))
             behind = lax.ppermute(behind, "row", bwd)

time: 155 us -> 164 us (1.058)
  waiting for transfers between devices: 38.5 us -> 48.3 us
  starting transfers between devices: 89.5 us -> 86.3 us
  matrix products: 18.8 us -> 20.9 us
    ppermute x0 -> x2, starting transfers between devices: none -> 13.3 us  [the longest x1 9.5 us: local(): first_behind = lax.ppermute(integrals, 'row', bwd)]
    ppermute x7 -> x6, starting transfers between devices: 44.6 us -> 31.9 us  [local(): behind = lax.ppermute(behind, 'row', bwd)]
    ppermute x0 -> x2, waiting for transfers between devices: none -> 12.1 us  [the longest x1 10.9 us: local(): first_ahead = lax.ppermute(integrals, 'row', fwd)]
    ppermute x1, waiting for transfers between devices: 1.14 us -> 6.95 us  [gather_col(): far = lax.ppermute(pair, 'col', [(i, i ^ 2) for i in range(n)])]
    ppermute x7 -> x6, waiting for transfers between devices: 26 us -> 21.1 us  [local(): ahead = lax.ppermute(ahead, 'row', fwd)]
    ppermute x7 -> x6, starting transfers between devices: 15.3 us -> 11.5 us  [local(): ahead = lax.ppermute(ahead, 'row', fwd)]
    dot_general x17, matrix products: 18.8 us -> 20.9 us  [product(): jnp.dot(cols[:, lo:hi], block, precision=lax.Precision.HIGHEST, preferred...]
  transfers between devices with their start and end apart: 23 -> 23, of which waited for: 12 -> 9; matrix products, arithmetic and copies ran while one was open for 14% -> 15% of each run, Pallas kernels for 0% -> 0%
where the time goes in v12:
time: 164 us; the launch traced here: 163 us
  starting transfers between devices  86.3 us (53%)
  waiting for transfers between devices  48.3 us (29%)
  matrix products  20.9 us (13%)
  other arithmetic  3.96 us (2%)
  local copies, waits for them, and re-layouts  1.84 us (1%)
    ppermute x6, starting transfers between devices, local(): behind = lax.ppermute(behind, 'row', bwd)  31.9 us
    ppermute x6, waiting for transfers between devices, local(): ahead = lax.ppermute(ahead, 'row', fwd)  21.1 us
    dot_general x17, matrix products, product(): jnp.dot(cols[:, lo:hi], block, precision=lax.Precision.HIGHEST, preferred...  20.9 us
    ppermute x6, starting transfers between devices, local(): ahead = lax.ppermute(ahead, 'row', fwd)  11.5 us
    ppermute x1, waiting for transfers between devices, local(): first_ahead = lax.ppermute(integrals, 'row', fwd)  10.9 us
    ppermute x1, starting transfers between devices, local(): first_behind = lax.ppermute(integrals, 'row', bwd)  9.5 us
    ppermute x1, waiting for transfers between devices, gather_col(): far = lax.ppermute(pair, 'col', [(i, i ^ 2) for i in range(n)])  6.95 us
    ppermute x1, starting transfers between devices, local(): bottom = lax.ppermute(behind[m:], 'row', bwd)  5.6 us
  transfers between devices with their start and end apart: 23, of which 9 were waited for; matrix products, arithmetic and copies ran while one was open for 15% of the time, Pallas kernels for 0%

profile of v12, /device:TPU:6, one launch (start us, length us, event | category | flops | bytes accessed | tf_op | source)
XLA Modules:
  0.0 162.8 jit_solution(17130209555543366327)
XLA Ops:
  0.0 3.8 %collective-permute-start = (f32[360,360]{1,0:T(8,128)}, f32[360,360]{1,0:T(8,128)}, u32[]{:S(2)}, u32[]{:S(2)}) collective-permute-start(f32[360,360]{1,0:T(8,128)} %param.3), channel_id=1, source_target_pairs={{0,32},{32,64},{64,96},{96,128},{128,160},{160,192},{192,224},{224... | collective-permute-start | bytes 1555208 | tf_op jit(solution)/shard_map/ppermute | solution.py:45
  3.8 9.5 %collective-permute-start.1 = (f32[360,360]{1,0:T(8,128)}, f32[360,360]{1,0:T(8,128)}, u32[]{:S(2)}, u32[]{:S(2)}) collective-permute-start(f32[360,360]{1,0:T(8,128)} %param.3), channel_id=1, source_target_pairs={{0,480},{32,0},{64,32},{96,64},{128,96},{160,128},{192,160},{224,1... | collective-permute-start | bytes 1555208 | tf_op jit(solution)/shard_map/ppermute | solution.py:46
  13.3 10.9 %collective-permute-done = f32[360,360]{1,0:T(8,128)} collective-permute-done((f32[360,360]{1,0:T(8,128)}, f32[360,360]{1,0:T(8,128)}, u32[]{:S(2)}, u32[]{:S(2)}) %collective-permute-start) | collective-permute-done | bytes 518432 | tf_op jit(solution)/shard_map/ppermute | solution.py:45
  25.4 1.9 %collective-permute-start.2 = (f32[192,360]{1,0:T(8,128)}, f32[192,360]{1,0:T(8,128)S(1)}, u32[]{:S(2)}, u32[]{:S(2)}) collective-permute-start(f32[192,360]{1,0:T(8,128)} %param.2), channel_id=1, source_target_pairs={{0,2},{2,0},{4,6},{6,4},{8,10},{10,8},{12,14},{14,12},{16,18},{18,... | collective-permute-start | bytes 829448 | tf_op jit(solution)/shard_map/ppermute | solution.py:15
  30.2 2.7 %collective-permute-start.3 = (f32[2,192,360]{2,1,0:T(8,128)S(1)}, f32[2,192,360]{2,1,0:T(8,128)S(1)}, u32[]{:S(2)}, u32[]{:S(2)}) collective-permute-start(f32[2,192,360]{2,1,0:T(8,128)S(1)} %maximum_select_fusion.1), channel_id=1, source_target_pairs={{0,4},{2,6},{4,0},{6,2},{8,12},{10,14},{12,8},{14,10},{16,20},{18,... | collective-permute-start | bytes 1658888 | tf_op jit(solution)/shard_map/ppermute | solution.py:17
  32.9 1.9 %collective-permute-start.8 = (f32[360,360]{1,0:T(8,128)}, f32[360,360]{1,0:T(8,128)}, u32[]{:S(2)}, u32[]{:S(2)}) collective-permute-start(f32[360,360]{1,0:T(8,128)} %collective-permute-done), channel_id=1, source_target_pairs={{0,32},{32,64},{64,96},{96,128},{128,160},{160,192},{192,224},{224... | collective-permute-start | bytes 1555208 | tf_op jit(solution)/shard_map/ppermute | solution.py:69
  34.9 5.6 %collective-permute-start.9 = (f32[360,360]{1,0:T(8,128)}, f32[360,360]{1,0:T(8,128)}, u32[]{:S(2)}, u32[]{:S(2)}) collective-permute-start(f32[360,360]{1,0:T(8,128)} %collective-permute-done.1), channel_id=1, source_target_pairs={{0,480},{32,0},{64,32},{96,64},{128,96},{160,128},{192,160},{224,1... | collective-permute-start | bytes 1555208 | tf_op jit(solution)/shard_map/ppermute | solution.py:71
  40.5 6.9 %collective-permute-done.3 = f32[2,192,360]{2,1,0:T(8,128)S(1)} collective-permute-done((f32[2,192,360]{2,1,0:T(8,128)S(1)}, f32[2,192,360]{2,1,0:T(8,128)S(1)}, u32[]{:S(2)}, u32[]{:S(2)}) %collective-permute-start.3) | collective-permute-done | bytes 552992 | tf_op jit(solution)/shard_map/ppermute | solution.py:17
  47.6 3.5 %collective-permute-start.5 = (f32[4,192,360]{2,1,0:T(8,128)S(1)}, f32[4,192,360]{2,1,0:T(8,128)S(1)}, u32[]{:S(2)}, u32[]{:S(2)}) collective-permute-start(f32[4,192,360]{2,1,0:T(8,128)S(1)} %maximum_select_fusion), channel_id=1, source_target_pairs={{0,8},{2,10},{4,12},{6,14},{8,16},{10,18},{12,20},{14,22},{16,24},... | collective-permute-start | bytes 3317768 | tf_op jit(solution)/shard_map/ppermute | solution.py:21
  51.0 3.6 %collective-permute-start.4 = (f32[4,192,360]{2,1,0:T(8,128)S(1)}, f32[4,192,360]{2,1,0:T(8,128)S(1)}, u32[]{:S(2)}, u32[]{:S(2)}) collective-permute-start(f32[4,192,360]{2,1,0:T(8,128)S(1)} %maximum_select_fusion), channel_id=1, source_target_pairs={{0,24},{2,26},{4,28},{6,30},{8,0},{10,2},{12,4},{14,6},{16,8},{18,... | collective-permute-start | bytes 3317768 | tf_op jit(solution)/shard_map/ppermute | solution.py:22
  54.6 1.9 %collective-permute-start.10 = (f32[360,360]{1,0:T(8,128)}, f32[360,360]{1,0:T(8,128)S(1)}, u32[]{:S(2)}, u32[]{:S(2)}) collective-permute-start(f32[360,360]{1,0:T(8,128)} %collective-permute-done.8), channel_id=1, source_target_pairs={{0,32},{32,64},{64,96},{96,128},{128,160},{160,192},{192,224},{224... | collective-permute-start | bytes 1555208 | tf_op jit(solution)/shard_map/ppermute | solution.py:69
  56.6 5.6 %collective-permute-start.11 = (f32[360,360]{1,0:T(8,128)}, f32[360,360]{1,0:T(8,128)S(1)}, u32[]{:S(2)}, u32[]{:S(2)}) collective-permute-start(f32[360,360]{1,0:T(8,128)} %collective-permute-done.9), channel_id=1, source_target_pairs={{0,480},{32,0},{64,32},{96,64},{128,96},{160,128},{192,160},{224,1... | collective-permute-start | bytes 1555208 | tf_op jit(solution)/shard_map/ppermute | solution.py:71
  62.2 9.9 %collective-permute-done.10 = f32[360,360]{1,0:T(8,128)S(1)} collective-permute-done((f32[360,360]{1,0:T(8,128)}, f32[360,360]{1,0:T(8,128)S(1)}, u32[]{:S(2)}, u32[]{:S(2)}) %collective-permute-start.10) | collective-permute-done | bytes 518432 | tf_op jit(solution)/shard_map/ppermute | solution.py:69
  72.1 1.9 %collective-permute-start.12 = (f32[360,360]{1,0:T(8,128)S(1)}, f32[360,360]{1,0:T(8,128)}, u32[]{:S(2)}, u32[]{:S(2)}) collective-permute-start(f32[360,360]{1,0:T(8,128)S(1)} %collective-permute-done.10), channel_id=1, source_target_pairs={{0,32},{32,64},{64,96},{96,128},{128,160},{160,192},{192,224},{224... | collective-permute-start | bytes 1555208 | tf_op jit(solution)/shard_map/ppermute | solution.py:69
  74.0 5.1 %collective-permute-start.16 = (f32[360,360]{1,0:T(8,128)S(1)}, f32[360,360]{1,0:T(8,128)}, u32[]{:S(2)}, u32[]{:S(2)}) collective-permute-start(f32[360,360]{1,0:T(8,128)S(1)} %collective-permute-done.11), channel_id=1, source_target_pairs={{0,480},{32,0},{64,32},{96,64},{128,96},{160,128},{192,160},{224,1... | collective-permute-start | bytes 1555208 | tf_op jit(solution)/shard_map/ppermute | solution.py:71
  80.0 2.2 %collective-permute-start.6 = (f32[4,96,360]{2,1,0:T(8,128)}, f32[4,96,360]{2,1,0:T(8,128)}, u32[]{:S(2)}, u32[]{:S(2)}) collective-permute-start(f32[4,96,360]{2,1,0:T(8,128)} %slice.24), channel_id=1, source_target_pairs={{0,8},{2,10},{4,12},{6,14},{8,16},{10,18},{12,20},{14,22},{16,24},... | collective-permute-start | bytes 1658888 | tf_op jit(solution)/shard_map/ppermute | solution.py:24
  83.1 4.8 %collective-permute-start.7 = (f32[4,96,360]{2,1,0:T(8,128)}, f32[4,96,360]{2,1,0:T(8,128)}, u32[]{:S(2)}, u32[]{:S(2)}) collective-permute-start(f32[4,96,360]{2,1,0:T(8,128)} %slice.25), channel_id=1, source_target_pairs={{0,24},{2,26},{4,28},{6,30},{8,0},{10,2},{12,4},{14,6},{16,8},{18,... | collective-permute-start | bytes 1658888 | tf_op jit(solution)/shard_map/ppermute | solution.py:25
  88.0 1.9 %collective-permute-start.13 = (f32[360,360]{1,0:T(8,128)}, f32[360,360]{1,0:T(8,128)}, u32[]{:S(2)}, u32[]{:S(2)}) collective-permute-start(f32[360,360]{1,0:T(8,128)} %collective-permute-done.12), channel_id=1, source_target_pairs={{0,32},{32,64},{64,96},{96,128},{128,160},{160,192},{192,224},{224... | collective-permute-start | bytes 1555208 | tf_op jit(solution)/shard_map/ppermute | solution.py:69
  89.9 5.1 %collective-permute-start.17 = (f32[360,360]{1,0:T(8,128)}, f32[360,360]{1,0:T(8,128)}, u32[]{:S(2)}, u32[]{:S(2)}) collective-permute-start(f32[360,360]{1,0:T(8,128)} %collective-permute-done.16), channel_id=1, source_target_pairs={{0,480},{32,0},{64,32},{96,64},{128,96},{160,128},{192,160},{224,1... | collective-permute-start | bytes 1555208 | tf_op jit(solution)/shard_map/ppermute | solution.py:71
  96.0 7.4 %collective-permute-done.13 = f32[360,360]{1,0:T(8,128)} collective-permute-done((f32[360,360]{1,0:T(8,128)}, f32[360,360]{1,0:T(8,128)}, u32[]{:S(2)}, u32[]{:S(2)}) %collective-permute-start.13) | collective-permute-done | bytes 518432 | tf_op jit(solution)/shard_map/ppermute | solution.py:69
  103.4 1.9 %collective-permute-start.14 = (f32[360,360]{1,0:T(8,128)}, f32[360,360]{1,0:T(8,128)S(1)}, u32[]{:S(2)}, u32[]{:S(2)}) collective-permute-start(f32[360,360]{1,0:T(8,128)} %collective-permute-done.13), channel_id=1, source_target_pairs={{0,32},{32,64},{64,96},{96,128},{128,160},{160,192},{192,224},{224... | collective-permute-start | bytes 1555208 | tf_op jit(solution)/shard_map/ppermute | solution.py:69
  105.4 5.1 %collective-permute-start.18 = (f32[360,360]{1,0:T(8,128)}, f32[360,360]{1,0:T(8,128)S(1)}, u32[]{:S(2)}, u32[]{:S(2)}) collective-permute-start(f32[360,360]{1,0:T(8,128)} %collective-permute-done.17), channel_id=1, source_target_pairs={{0,480},{32,0},{64,32},{96,64},{128,96},{160,128},{192,160},{224,1... | collective-permute-start | bytes 1555208 | tf_op jit(solution)/shard_map/ppermute | solution.py:71
  110.5 2.1 %pad_maximum_fusion = f32[16,192,360]{2,1,0:T(8,128)S(1)} fusion(f32[4,192,360]{2,1,0:T(8,128)S(1)} %collective-permute-done.5, f32[4,96,360]{2,1,0:T(8,128)} %collective-permute-done.7, f32[4,96,360]{2,1,0:T(8,128)} %collective-permute-done.6, f32[4,192,360]{2,1,0:T(8,128)S(1)} %collective-permute-done.4, f32[4,192,360]{2,1,0:T(8,128)S(1)} %maximum_select_fusion), kind=kLoop, calls=%fused_computation | loop fusion | flops 4423680 | bytes 8847360 | tf_op jit(solution)/shard_map/concatenate | solution.py:27
  112.6 1.9 %fusion.28 = f32[192,360]{1,0:T(8,128)S(1)} fusion(f32[360,360]{1,0:T(8,128)} %collective-permute-done, f32[16,192,360]{2,1,0:T(8,128)S(1)} %pad_maximum_fusion, s32[]{:T(128)S(6)} %select_n.349), kind=kOutput, calls=%fused_computation.37 | convolution fusion | flops 298598400 | bytes 1089796 | tf_op jit(solution)/shard_map/dot_general | solution.py:54
  114.5 1.9 %fusion.26 = f32[192,360]{1,0:T(8,128)S(1)} fusion(f32[360,360]{1,0:T(8,128)} %collective-permute-done.1, f32[16,192,360]{2,1,0:T(8,128)S(1)} %pad_maximum_fusion, s32[]{:T(128)S(6)} %select_n.354), kind=kOutput, calls=%fused_computation.35 | convolution fusion | flops 298598400 | bytes 1089796 | tf_op jit(solution)/shard_map/dot_general | solution.py:54
  126.0 1.9 %collective-permute-start.15 = (f32[360,360]{1,0:T(8,128)S(1)}, f32[360,360]{1,0:T(8,128)S(1)}, u32[]{:S(2)}, u32[]{:S(2)}) collective-permute-start(f32[360,360]{1,0:T(8,128)S(1)} %collective-permute-done.14), channel_id=1, source_target_pairs={{0,32},{32,64},{64,96},{96,128},{128,160},{160,192},{192,224},{224... | collective-permute-start | bytes 1555208 | tf_op jit(solution)/shard_map/ppermute | solution.py:69
  127.9 5.3 %collective-permute-start.19 = (f32[360,360]{1,0:T(8,128)S(1)}, f32[360,360]{1,0:T(8,128)S(1)}, u32[]{:S(2)}, u32[]{:S(2)}) collective-permute-start(f32[360,360]{1,0:T(8,128)S(1)} %collective-permute-done.18), channel_id=1, source_target_pairs={{0,480},{32,0},{64,32},{96,64},{128,96},{160,128},{192,160},{224,1... | collective-permute-start | bytes 1555208 | tf_op jit(solution)/shard_map/ppermute | solution.py:71
  135.8 3.8 %collective-permute-done.15 = f32[360,360]{1,0:T(8,128)S(1)} collective-permute-done((f32[360,360]{1,0:T(8,128)S(1)}, f32[360,360]{1,0:T(8,128)S(1)}, u32[]{:S(2)}, u32[]{:S(2)}) %collective-permute-start.15) | collective-permute-done | bytes 518432 | tf_op jit(solution)/shard_map/ppermute | solution.py:69
  140.9 1.9 %collective-permute-start.20 = (f32[180,360]{1,0:T(8,128)S(1)}, f32[180,360]{1,0:T(8,128)S(1)}, u32[]{:S(2)}, u32[]{:S(2)}) collective-permute-start(f32[180,360]{1,0:T(8,128)S(1)} %slice.20), channel_id=1, source_target_pairs={{0,32},{32,64},{64,96},{96,128},{128,160},{160,192},{192,224},{224... | collective-permute-start | bytes 777608 | tf_op jit(solution)/shard_map/ppermute | solution.py:75
  142.8 5.6 %collective-permute-start.21 = (f32[180,360]{1,0:T(8,128)S(1)}, f32[180,360]{1,0:T(8,128)S(1)}, u32[]{:S(2)}, u32[]{:S(2)}) collective-permute-start(f32[180,360]{1,0:T(8,128)S(1)} %slice.21), channel_id=1, source_target_pairs={{0,480},{32,0},{64,32},{96,64},{128,96},{160,128},{192,160},{224,1... | collective-permute-start | bytes 777608 | tf_op jit(solution)/shard_map/ppermute | solution.py:76
  153.6 3.3 %collective-permute-start.22 = (f32[96,360]{1,0:T(8,128)S(1)}, f32[96,360]{1,0:T(8,128)S(1)}, u32[]{:S(2)}, u32[]{:S(2)}) collective-permute-start(f32[96,360]{1,0:T(8,128)S(1)} %constant_dynamic-slice_fusion), channel_id=1, source_target_pairs={{0,1},{1,0},{2,3},{3,2},{4,5},{5,4},{6,7},{7,6},{8,9},{9,8},{10,11... | collective-permute-start | bytes 414728 | tf_op jit(solution)/shard_map/ppermute | solution.py:93
  156.9 5.2 %collective-permute-done.22 = f32[96,360]{1,0:T(8,128)S(1)} collective-permute-done((f32[96,360]{1,0:T(8,128)S(1)}, f32[96,360]{1,0:T(8,128)S(1)}, u32[]{:S(2)}, u32[]{:S(2)}) %collective-permute-start.22) | collective-permute-done | bytes 138272 | tf_op jit(solution)/shard_map/ppermute | solution.py:93
  (51 shorter events, 25.1 us)
Async XLA Ops:
  0.0 24.2 %collective-permute-start = (f32[360,360]{1,0:T(8,128)}, f32[360,360]{1,0:T(8,128)}, u32[]{:S(2)}, u32[]{:S(2)}) collective-permute-start(f32[360,360]{1,0:T(8,128)} %param.3), channel_id=1, source_target_pairs={{0,32},{32,64},{64,96},{96,128},{128,160},{160,192},{192,224},{224... | collective-permute-start | bytes 1555208 | tf_op jit(solution)/shard_map/ppermute | solution.py:45
  3.8 21.6 %collective-permute-start.1 = (f32[360,360]{1,0:T(8,128)}, f32[360,360]{1,0:T(8,128)}, u32[]{:S(2)}, u32[]{:S(2)}) collective-permute-start(f32[360,360]{1,0:T(8,128)} %param.3), channel_id=1, source_target_pairs={{0,480},{32,0},{64,32},{96,64},{128,96},{160,128},{192,160},{224,1... | collective-permute-start | bytes 1555208 | tf_op jit(solution)/shard_map/ppermute | solution.py:46
  25.4 3.7 %collective-permute-start.2 = (f32[192,360]{1,0:T(8,128)}, f32[192,360]{1,0:T(8,128)S(1)}, u32[]{:S(2)}, u32[]{:S(2)}) collective-permute-start(f32[192,360]{1,0:T(8,128)} %param.2), channel_id=1, source_target_pairs={{0,2},{2,0},{4,6},{6,4},{8,10},{10,8},{12,14},{14,12},{16,18},{18,... | collective-permute-start | bytes 829448 | tf_op jit(solution)/shard_map/ppermute | solution.py:15
  30.2 17.3 %collective-permute-start.3 = (f32[2,192,360]{2,1,0:T(8,128)S(1)}, f32[2,192,360]{2,1,0:T(8,128)S(1)}, u32[]{:S(2)}, u32[]{:S(2)}) collective-permute-start(f32[2,192,360]{2,1,0:T(8,128)S(1)} %maximum_select_fusion.1), channel_id=1, source_target_pairs={{0,4},{2,6},{4,0},{6,2},{8,12},{10,14},{12,8},{14,10},{16,20},{18,... | collective-permute-start | bytes 1658888 | tf_op jit(solution)/shard_map/ppermute | solution.py:17
  32.9 21.7 %collective-permute-start.8 = (f32[360,360]{1,0:T(8,128)}, f32[360,360]{1,0:T(8,128)}, u32[]{:S(2)}, u32[]{:S(2)}) collective-permute-start(f32[360,360]{1,0:T(8,128)} %collective-permute-done), channel_id=1, source_target_pairs={{0,32},{32,64},{64,96},{96,128},{128,160},{160,192},{192,224},{224... | collective-permute-start | bytes 1555208 | tf_op jit(solution)/shard_map/ppermute | solution.py:69
  34.9 21.7 %collective-permute-start.9 = (f32[360,360]{1,0:T(8,128)}, f32[360,360]{1,0:T(8,128)}, u32[]{:S(2)}, u32[]{:S(2)}) collective-permute-start(f32[360,360]{1,0:T(8,128)} %collective-permute-done.1), channel_id=1, source_target_pairs={{0,480},{32,0},{64,32},{96,64},{128,96},{160,128},{192,160},{224,1... | collective-permute-start | bytes 1555208 | tf_op jit(solution)/shard_map/ppermute | solution.py:71
  47.6 31.6 %collective-permute-start.5 = (f32[4,192,360]{2,1,0:T(8,128)S(1)}, f32[4,192,360]{2,1,0:T(8,128)S(1)}, u32[]{:S(2)}, u32[]{:S(2)}) collective-permute-start(f32[4,192,360]{2,1,0:T(8,128)S(1)} %maximum_select_fusion), channel_id=1, source_target_pairs={{0,8},{2,10},{4,12},{6,14},{8,16},{10,18},{12,20},{14,22},{16,24},... | collective-permute-start | bytes 3317768 | tf_op jit(solution)/shard_map/ppermute | solution.py:21
  51.0 31.2 %collective-permute-start.4 = (f32[4,192,360]{2,1,0:T(8,128)S(1)}, f32[4,192,360]{2,1,0:T(8,128)S(1)}, u32[]{:S(2)}, u32[]{:S(2)}) collective-permute-start(f32[4,192,360]{2,1,0:T(8,128)S(1)} %maximum_select_fusion), channel_id=1, source_target_pairs={{0,24},{2,26},{4,28},{6,30},{8,0},{10,2},{12,4},{14,6},{16,8},{18,... | collective-permute-start | bytes 3317768 | tf_op jit(solution)/shard_map/ppermute | solution.py:22
  54.6 17.4 %collective-permute-start.10 = (f32[360,360]{1,0:T(8,128)}, f32[360,360]{1,0:T(8,128)S(1)}, u32[]{:S(2)}, u32[]{:S(2)}) collective-permute-start(f32[360,360]{1,0:T(8,128)} %collective-permute-done.8), channel_id=1, source_target_pairs={{0,32},{32,64},{64,96},{96,128},{128,160},{160,192},{192,224},{224... | collective-permute-start | bytes 1555208 | tf_op jit(solution)/shard_map/ppermute | solution.py:69
  56.6 17.4 %collective-permute-start.11 = (f32[360,360]{1,0:T(8,128)}, f32[360,360]{1,0:T(8,128)S(1)}, u32[]{:S(2)}, u32[]{:S(2)}) collective-permute-start(f32[360,360]{1,0:T(8,128)} %collective-permute-done.9), channel_id=1, source_target_pairs={{0,480},{32,0},{64,32},{96,64},{128,96},{160,128},{192,160},{224,1... | collective-permute-start | bytes 1555208 | tf_op jit(solution)/shard_map/ppermute | solution.py:71
  72.1 10.2 %copy-start.1 = (f32[360,360]{1,0:T(8,128)}, f32[360,360]{1,0:T(8,128)S(1)}, u32[]{:S(2)}) copy-start(f32[360,360]{1,0:T(8,128)S(1)} %collective-permute-done.10) | copy-start | bytes 1555204
  72.1 15.9 %collective-permute-start.12 = (f32[360,360]{1,0:T(8,128)S(1)}, f32[360,360]{1,0:T(8,128)}, u32[]{:S(2)}, u32[]{:S(2)}) collective-permute-start(f32[360,360]{1,0:T(8,128)S(1)} %collective-permute-done.10), channel_id=1, source_target_pairs={{0,32},{32,64},{64,96},{96,128},{128,160},{160,192},{192,224},{224... | collective-permute-start | bytes 1555208 | tf_op jit(solution)/shard_map/ppermute | solution.py:69
  74.0 14.0 %copy-start.3 = (f32[360,360]{1,0:T(8,128)}, f32[360,360]{1,0:T(8,128)S(1)}, u32[]{:S(2)}) copy-start(f32[360,360]{1,0:T(8,128)S(1)} %collective-permute-done.11) | copy-start | bytes 1555204
  74.0 15.9 %collective-permute-start.16 = (f32[360,360]{1,0:T(8,128)S(1)}, f32[360,360]{1,0:T(8,128)}, u32[]{:S(2)}, u32[]{:S(2)}) collective-permute-start(f32[360,360]{1,0:T(8,128)S(1)} %collective-permute-done.11), channel_id=1, source_target_pairs={{0,480},{32,0},{64,32},{96,64},{128,96},{160,128},{192,160},{224,1... | collective-permute-start | bytes 1555208 | tf_op jit(solution)/shard_map/ppermute | solution.py:71
  80.0 30.5 %collective-permute-start.6 = (f32[4,96,360]{2,1,0:T(8,128)}, f32[4,96,360]{2,1,0:T(8,128)}, u32[]{:S(2)}, u32[]{:S(2)}) collective-permute-start(f32[4,96,360]{2,1,0:T(8,128)} %slice.24), channel_id=1, source_target_pairs={{0,8},{2,10},{4,12},{6,14},{8,16},{10,18},{12,20},{14,22},{16,24},... | collective-permute-start | bytes 1658888 | tf_op jit(solution)/shard_map/ppermute | solution.py:24
  83.1 27.4 %collective-permute-start.7 = (f32[4,96,360]{2,1,0:T(8,128)}, f32[4,96,360]{2,1,0:T(8,128)}, u32[]{:S(2)}, u32[]{:S(2)}) collective-permute-start(f32[4,96,360]{2,1,0:T(8,128)} %slice.25), channel_id=1, source_target_pairs={{0,24},{2,26},{4,28},{6,30},{8,0},{10,2},{12,4},{14,6},{16,8},{18,... | collective-permute-start | bytes 1658888 | tf_op jit(solution)/shard_map/ppermute | solution.py:25
  88.0 15.5 %collective-permute-start.13 = (f32[360,360]{1,0:T(8,128)}, f32[360,360]{1,0:T(8,128)}, u32[]{:S(2)}, u32[]{:S(2)}) collective-permute-start(f32[360,360]{1,0:T(8,128)} %collective-permute-done.12), channel_id=1, source_target_pairs={{0,32},{32,64},{64,96},{96,128},{128,160},{160,192},{192,224},{224... | collective-permute-start | bytes 1555208 | tf_op jit(solution)/shard_map/ppermute | solution.py:69
  89.9 15.4 %collective-permute-start.17 = (f32[360,360]{1,0:T(8,128)}, f32[360,360]{1,0:T(8,128)}, u32[]{:S(2)}, u32[]{:S(2)}) collective-permute-start(f32[360,360]{1,0:T(8,128)} %collective-permute-done.16), channel_id=1, source_target_pairs={{0,480},{32,0},{64,32},{96,64},{128,96},{160,128},{192,160},{224,1... | collective-permute-start | bytes 1555208 | tf_op jit(solution)/shard_map/ppermute | solution.py:71
  96.0 24.0 %copy-start = (f32[360,360]{1,0:T(8,128)S(1)}, f32[360,360]{1,0:T(8,128)}, u32[]{:S(2)}) copy-start(f32[360,360]{1,0:T(8,128)} %param.3) | copy-start | bytes 1555204
  103.4 22.5 %collective-permute-start.14 = (f32[360,360]{1,0:T(8,128)}, f32[360,360]{1,0:T(8,128)S(1)}, u32[]{:S(2)}, u32[]{:S(2)}) collective-permute-start(f32[360,360]{1,0:T(8,128)} %collective-permute-done.13), channel_id=1, source_target_pairs={{0,32},{32,64},{64,96},{96,128},{128,160},{160,192},{192,224},{224... | collective-permute-start | bytes 1555208 | tf_op jit(solution)/shard_map/ppermute | solution.py:69
  105.4 22.5 %collective-permute-start.18 = (f32[360,360]{1,0:T(8,128)}, f32[360,360]{1,0:T(8,128)S(1)}, u32[]{:S(2)}, u32[]{:S(2)}) collective-permute-start(f32[360,360]{1,0:T(8,128)} %collective-permute-done.17), channel_id=1, source_target_pairs={{0,480},{32,0},{64,32},{96,64},{128,96},{160,128},{192,160},{224,1... | collective-permute-start | bytes 1555208 | tf_op jit(solution)/shard_map/ppermute | solution.py:71
  112.6 8.2 %copy-start.4 = (f32[360,360]{1,0:T(8,128)S(1)}, f32[360,360]{1,0:T(8,128)}, u32[]{:S(2)}) copy-start(f32[360,360]{1,0:T(8,128)} %copy-done.3) | copy-start | bytes 1555204
  114.5 10.7 %copy-start.2 = (f32[360,360]{1,0:T(8,128)S(1)}, f32[360,360]{1,0:T(8,128)}, u32[]{:S(2)}) copy-start(f32[360,360]{1,0:T(8,128)} %copy-done.1) | copy-start | bytes 1555204
  126.0 13.7 %collective-permute-start.15 = (f32[360,360]{1,0:T(8,128)S(1)}, f32[360,360]{1,0:T(8,128)S(1)}, u32[]{:S(2)}, u32[]{:S(2)}) collective-permute-start(f32[360,360]{1,0:T(8,128)S(1)} %collective-permute-done.14), channel_id=1, source_target_pairs={{0,32},{32,64},{64,96},{96,128},{128,160},{160,192},{192,224},{224... | collective-permute-start | bytes 1555208 | tf_op jit(solution)/shard_map/ppermute | solution.py:69
  127.9 12.9 %collective-permute-start.19 = (f32[360,360]{1,0:T(8,128)S(1)}, f32[360,360]{1,0:T(8,128)S(1)}, u32[]{:S(2)}, u32[]{:S(2)}) collective-permute-start(f32[360,360]{1,0:T(8,128)S(1)} %collective-permute-done.18), channel_id=1, source_target_pairs={{0,480},{32,0},{64,32},{96,64},{128,96},{160,128},{192,160},{224,1... | collective-permute-start | bytes 1555208 | tf_op jit(solution)/shard_map/ppermute | solution.py:71
  140.9 11.7 %collective-permute-start.20 = (f32[180,360]{1,0:T(8,128)S(1)}, f32[180,360]{1,0:T(8,128)S(1)}, u32[]{:S(2)}, u32[]{:S(2)}) collective-permute-start(f32[180,360]{1,0:T(8,128)S(1)} %slice.20), channel_id=1, source_target_pairs={{0,32},{32,64},{64,96},{96,128},{128,160},{160,192},{192,224},{224... | collective-permute-start | bytes 777608 | tf_op jit(solution)/shard_map/ppermute | solution.py:75
  142.8 9.7 %collective-permute-start.21 = (f32[180,360]{1,0:T(8,128)S(1)}, f32[180,360]{1,0:T(8,128)S(1)}, u32[]{:S(2)}, u32[]{:S(2)}) collective-permute-start(f32[180,360]{1,0:T(8,128)S(1)} %slice.21), channel_id=1, source_target_pairs={{0,480},{32,0},{64,32},{96,64},{128,96},{160,128},{192,160},{224,1... | collective-permute-start | bytes 777608 | tf_op jit(solution)/shard_map/ppermute | solution.py:76
  153.6 8.5 %collective-permute-start.22 = (f32[96,360]{1,0:T(8,128)S(1)}, f32[96,360]{1,0:T(8,128)S(1)}, u32[]{:S(2)}, u32[]{:S(2)}) collective-permute-start(f32[96,360]{1,0:T(8,128)S(1)} %constant_dynamic-slice_fusion), channel_id=1, source_target_pairs={{0,1},{1,0},{2,3},{3,2},{4,5},{5,4},{6,7},{7,6},{8,9},{9,8},{10,11... | collective-permute-start | bytes 414728 | tf_op jit(solution)/shard_map/ppermute | solution.py:93

commit v13 on v11

--- a/solution.py
+++ b/solution.py
@@ -40,7 +40,10 @@
     rows = amplitudes.shape[0]
     half = rows // 2
 
-    strip, place = gather_col(amplitudes)
+    strip = lax.all_gather(amplitudes, "col", axis=0, tiled=False)
+
+    def place(owner):
+        return owner
 
     def product(block, owner, lo=0, hi=None):
         hi = kb if hi is None else hi

time: 155 us -> 159 us (1.026)
  starting transfers between devices: 89.5 us -> 68.9 us
  waiting for transfers between devices: 38.5 us -> 55.1 us
  between operations: 1.5 us -> 14.1 us
  other arithmetic: 3.96 us -> 0.68 us
  local copies, waits for them, and re-layouts: 1.84 us -> 0.12 us
    ppermute x7, waiting for transfers between devices: 2.52 us -> 42.2 us  [local(): behind = lax.ppermute(behind, 'row', bwd)]
    ppermute x7, waiting for transfers between devices: 26 us -> 1.65 us  [local(): ahead = lax.ppermute(ahead, 'row', fwd)]
    ppermute x6 -> x0, starting transfers between devices: 18.7 us -> none  [the longest x1 4.84 us: gather_col(): opp_b = lax.ppermute(above[:, h:], 'col', down)]
    ppermute x1, waiting for transfers between devices: 0.29 us -> 5.26 us  [local(): top = lax.ppermute(ahead[:m], 'row', fwd)]
    ppermute x6 -> x0, waiting for transfers between devices: 2.9 us -> none  [the longest x1 1.74 us: gather_col(): other = lax.ppermute(block, 'col', [(i, i ^ 1) for i in range(n)])]
    concatenate x1 -> x0, other arithmetic: 2.1 us -> none  [gather_col(): stack = jnp.concatenate([quad, above, opposite, below])]
    ppermute x7, starting transfers between devices: 15.3 us -> 13.4 us  [local(): ahead = lax.ppermute(ahead, 'row', fwd)]
    slice x2 -> x0, local copies, waits for them, and re-layouts: 1.73 us -> none  [the longest x1 0.86 us: gather_col(): opp_a = lax.ppermute(below[:, :h], 'col', up)]
  transfers between devices with their start and end apart: 23 -> 18, of which waited for: 12 -> 9; matrix products, arithmetic and copies ran while one was open for 14% -> 11% of each run, Pallas kernels for 0% -> 0%
where the time goes in v13:
time: 159 us; the launch traced here: 158 us
  starting transfers between devices  68.9 us (43%)
  waiting for transfers between devices  55.1 us (35%)
  matrix products  19 us (12%)
  between operations  14.1 us (9%)
    ppermute x7, starting transfers between devices, local(): behind = lax.ppermute(behind, 'row', bwd)  44.5 us
    ppermute x7, waiting for transfers between devices, local(): behind = lax.ppermute(behind, 'row', bwd)  42.2 us
    dot_general x17, matrix products, product(): jnp.dot(cols[:, lo:hi], block, precision=lax.Precision.HIGHEST, preferred...  19 us
    ppermute x7, starting transfers between devices, local(): ahead = lax.ppermute(ahead, 'row', fwd)  13.4 us
    ppermute x1, starting transfers between devices, local(): bottom = lax.ppermute(behind[m:], 'row', bwd)  5.6 us
    ppermute x1, waiting for transfers between devices, local(): top = lax.ppermute(ahead[:m], 'row', fwd)  5.26 us
    ppermute x1, waiting for transfers between devices, local(): other = lax.ppermute(other, 'depth', [(0, 1), (1, 0)])  5.22 us
    ppermute x1, starting transfers between devices, local(): other = lax.ppermute(other, 'depth', [(0, 1), (1, 0)])  3.31 us
  transfers between devices with their start and end apart: 18, of which 9 were waited for; matrix products, arithmetic and copies ran while one was open for 11% of the time, Pallas kernels for 0%

profile of v13, /device:TPU:6, one launch (start us, length us, event | category | flops | bytes accessed | tf_op | source)
XLA Modules:
  0.0 158.0 jit_solution(16129631947287756196)
XLA Ops:
  7.3 11.4 %collective-permute-start.1 = (f32[360,360]{1,0:T(8,128)}, f32[360,360]{1,0:T(8,128)S(1)}, u32[]{:S(2)}, u32[]{:S(2)}) collective-permute-start(f32[360,360]{1,0:T(8,128)} %param.3), channel_id=1, source_target_pairs={{0,480},{32,0},{64,32},{96,64},{128,96},{160,128},{192,160},{224,1... | collective-permute-start | bytes 1555208 | tf_op jit(solution)/shard_map/ppermute | solution.py:66
  18.7 1.9 %collective-permute-start = (f32[360,360]{1,0:T(8,128)}, f32[360,360]{1,0:T(8,128)S(1)}, u32[]{:S(2)}, u32[]{:S(2)}) collective-permute-start(f32[360,360]{1,0:T(8,128)} %param.3), channel_id=1, source_target_pairs={{0,32},{32,64},{64,96},{96,128},{128,160},{160,192},{192,224},{224... | collective-permute-start | bytes 1555208 | tf_op jit(solution)/shard_map/ppermute | solution.py:64
  20.6 10.2 %collective-permute-done.1 = f32[360,360]{1,0:T(8,128)S(1)} collective-permute-done((f32[360,360]{1,0:T(8,128)}, f32[360,360]{1,0:T(8,128)S(1)}, u32[]{:S(2)}, u32[]{:S(2)}) %collective-permute-start.1) | collective-permute-done | bytes 518432 | tf_op jit(solution)/shard_map/ppermute | solution.py:66
  30.8 5.5 %collective-permute-start.3 = (f32[360,360]{1,0:T(8,128)S(1)}, f32[360,360]{1,0:T(8,128)S(1)}, u32[]{:S(2)}, u32[]{:S(2)}) collective-permute-start(f32[360,360]{1,0:T(8,128)S(1)} %collective-permute-done.1), channel_id=1, source_target_pairs={{0,480},{32,0},{64,32},{96,64},{128,96},{160,128},{192,160},{224,1... | collective-permute-start | bytes 1555208 | tf_op jit(solution)/shard_map/ppermute | solution.py:66
  36.3 1.9 %collective-permute-start.2 = (f32[360,360]{1,0:T(8,128)S(1)}, f32[360,360]{1,0:T(8,128)S(1)}, u32[]{:S(2)}, u32[]{:S(2)}) collective-permute-start(f32[360,360]{1,0:T(8,128)S(1)} %collective-permute-done), channel_id=1, source_target_pairs={{0,32},{32,64},{64,96},{96,128},{128,160},{160,192},{192,224},{224... | collective-permute-start | bytes 1555208 | tf_op jit(solution)/shard_map/ppermute | solution.py:64
  38.2 9.0 %collective-permute-done.3 = f32[360,360]{1,0:T(8,128)S(1)} collective-permute-done((f32[360,360]{1,0:T(8,128)S(1)}, f32[360,360]{1,0:T(8,128)S(1)}, u32[]{:S(2)}, u32[]{:S(2)}) %collective-permute-start.3) | collective-permute-done | bytes 518432 | tf_op jit(solution)/shard_map/ppermute | solution.py:66
  47.2 5.6 %collective-permute-start.8 = (f32[360,360]{1,0:T(8,128)S(1)}, f32[360,360]{1,0:T(8,128)S(1)}, u32[]{:S(2)}, u32[]{:S(2)}) collective-permute-start(f32[360,360]{1,0:T(8,128)S(1)} %collective-permute-done.3), channel_id=1, source_target_pairs={{0,480},{32,0},{64,32},{96,64},{128,96},{160,128},{192,160},{224,1... | collective-permute-start | bytes 1555208 | tf_op jit(solution)/shard_map/ppermute | solution.py:66
  52.8 1.9 %collective-permute-start.4 = (f32[360,360]{1,0:T(8,128)S(1)}, f32[360,360]{1,0:T(8,128)S(1)}, u32[]{:S(2)}, u32[]{:S(2)}) collective-permute-start(f32[360,360]{1,0:T(8,128)S(1)} %collective-permute-done.2), channel_id=1, source_target_pairs={{0,32},{32,64},{64,96},{96,128},{128,160},{160,192},{192,224},{224... | collective-permute-start | bytes 1555208 | tf_op jit(solution)/shard_map/ppermute | solution.py:64
  54.7 8.0 %collective-permute-done.8 = f32[360,360]{1,0:T(8,128)S(1)} collective-permute-done((f32[360,360]{1,0:T(8,128)S(1)}, f32[360,360]{1,0:T(8,128)S(1)}, u32[]{:S(2)}, u32[]{:S(2)}) %collective-permute-start.8) | collective-permute-done | bytes 518432 | tf_op jit(solution)/shard_map/ppermute | solution.py:66
  62.7 5.6 %collective-permute-start.9 = (f32[360,360]{1,0:T(8,128)S(1)}, f32[360,360]{1,0:T(8,128)S(1)}, u32[]{:S(2)}, u32[]{:S(2)}) collective-permute-start(f32[360,360]{1,0:T(8,128)S(1)} %collective-permute-done.8), channel_id=1, source_target_pairs={{0,480},{32,0},{64,32},{96,64},{128,96},{160,128},{192,160},{224,1... | collective-permute-start | bytes 1555208 | tf_op jit(solution)/shard_map/ppermute | solution.py:66
  68.4 1.9 %collective-permute-start.5 = (f32[360,360]{1,0:T(8,128)S(1)}, f32[360,360]{1,0:T(8,128)S(1)}, u32[]{:S(2)}, u32[]{:S(2)}) collective-permute-start(f32[360,360]{1,0:T(8,128)S(1)} %collective-permute-done.4), channel_id=1, source_target_pairs={{0,32},{32,64},{64,96},{96,128},{128,160},{160,192},{192,224},{224... | collective-permute-start | bytes 1555208 | tf_op jit(solution)/shard_map/ppermute | solution.py:64
  70.3 7.1 %collective-permute-done.9 = f32[360,360]{1,0:T(8,128)S(1)} collective-permute-done((f32[360,360]{1,0:T(8,128)S(1)}, f32[360,360]{1,0:T(8,128)S(1)}, u32[]{:S(2)}, u32[]{:S(2)}) %collective-permute-start.9) | collective-permute-done | bytes 518432 | tf_op jit(solution)/shard_map/ppermute | solution.py:66
  77.4 5.6 %collective-permute-start.10 = (f32[360,360]{1,0:T(8,128)S(1)}, f32[360,360]{1,0:T(8,128)}, u32[]{:S(2)}, u32[]{:S(2)}) collective-permute-start(f32[360,360]{1,0:T(8,128)S(1)} %collective-permute-done.9), channel_id=1, source_target_pairs={{0,480},{32,0},{64,32},{96,64},{128,96},{160,128},{192,160},{224,1... | collective-permute-start | bytes 1555208 | tf_op jit(solution)/shard_map/ppermute | solution.py:66
  83.0 1.9 %collective-permute-start.6 = (f32[360,360]{1,0:T(8,128)S(1)}, f32[360,360]{1,0:T(8,128)S(1)}, u32[]{:S(2)}, u32[]{:S(2)}) collective-permute-start(f32[360,360]{1,0:T(8,128)S(1)} %collective-permute-done.5), channel_id=1, source_target_pairs={{0,32},{32,64},{64,96},{96,128},{128,160},{160,192},{192,224},{224... | collective-permute-start | bytes 1555208 | tf_op jit(solution)/shard_map/ppermute | solution.py:64
  85.2 5.9 %collective-permute-done.10 = f32[360,360]{1,0:T(8,128)} collective-permute-done((f32[360,360]{1,0:T(8,128)S(1)}, f32[360,360]{1,0:T(8,128)}, u32[]{:S(2)}, u32[]{:S(2)}) %collective-permute-start.10) | collective-permute-done | bytes 518432 | tf_op jit(solution)/shard_map/ppermute | solution.py:66
  91.1 5.7 %collective-permute-start.11 = (f32[360,360]{1,0:T(8,128)}, f32[360,360]{1,0:T(8,128)S(1)}, u32[]{:S(2)}, u32[]{:S(2)}) collective-permute-start(f32[360,360]{1,0:T(8,128)} %collective-permute-done.10), channel_id=1, source_target_pairs={{0,480},{32,0},{64,32},{96,64},{128,96},{160,128},{192,160},{224,1... | collective-permute-start | bytes 1555208 | tf_op jit(solution)/shard_map/ppermute | solution.py:66
  96.8 1.9 %collective-permute-start.7 = (f32[360,360]{1,0:T(8,128)S(1)}, f32[360,360]{1,0:T(8,128)}, u32[]{:S(2)}, u32[]{:S(2)}) collective-permute-start(f32[360,360]{1,0:T(8,128)S(1)} %collective-permute-done.6), channel_id=1, source_target_pairs={{0,32},{32,64},{64,96},{96,128},{128,160},{160,192},{192,224},{224... | collective-permute-start | bytes 1555208 | tf_op jit(solution)/shard_map/ppermute | solution.py:64
  98.8 2.0 %fusion.25 = f32[192,360]{1,0:T(8,128)S(1)} fusion(f32[360,360]{1,0:T(8,128)} %param.3, f32[16,192,360]{2,1,0:T(8,128)} %bitcast.65, s32[]{:T(128)S(6)} %select_n.121), kind=kOutput, calls=%fused_computation.33 | convolution fusion | flops 298598400 | bytes 1124356 | tf_op jit(solution)/shard_map/dot_general | solution.py:51
  100.9 1.9 %convolution_add_fusion.7 = f32[192,360]{1,0:T(8,128)S(1)} fusion(f32[192,360]{1,0:T(8,128)S(1)} %fusion.25, f32[360,360]{1,0:T(8,128)} %copy-done.4, f32[16,192,360]{2,1,0:T(8,128)} %bitcast.66, s32[]{:T(128)S(6)} %select_n.123), kind=kOutput, calls=%fused_computation.7 | convolution fusion | flops 298667520 | bytes 1400836 | tf_op jit(solution)/shard_map/dot_general | solution.py:51
  102.8 1.7 %convolution_add_fusion.6 = f32[192,360]{1,0:T(8,128)S(1)} fusion(f32[192,360]{1,0:T(8,128)S(1)} %convolution_add_fusion.7, f32[360,360]{1,0:T(8,128)S(1)} %collective-permute-done.1, f32[16,192,360]{2,1,0:T(8,128)} %bitcast.67, s32[]{:T(128)S(6)} %select_n.125), kind=kOutput, calls=%fused_computation.6 | convolution fusion | flops 298667520 | bytes 1366276 | tf_op jit(solution)/shard_map/dot_general | solution.py:51
  104.5 1.9 %fusion.20 = f32[192,360]{1,0:T(8,128)S(1)} fusion(f32[360,360]{1,0:T(8,128)} %copy-done.3, f32[16,192,360]{2,1,0:T(8,128)} %bitcast.68, s32[]{:T(128)S(6)} %select_n.129), kind=kOutput, calls=%fused_computation.28 | convolution fusion | flops 298598400 | bytes 1124356 | tf_op jit(solution)/shard_map/dot_general | solution.py:51
  108.0 1.6 %collective-permute-done.7 = f32[360,360]{1,0:T(8,128)} collective-permute-done((f32[360,360]{1,0:T(8,128)S(1)}, f32[360,360]{1,0:T(8,128)}, u32[]{:S(2)}, u32[]{:S(2)}) %collective-permute-start.7) | collective-permute-done | bytes 518432 | tf_op jit(solution)/shard_map/ppermute | solution.py:64
  109.6 1.9 %collective-permute-start.12 = (f32[360,360]{1,0:T(8,128)}, f32[360,360]{1,0:T(8,128)S(1)}, u32[]{:S(2)}, u32[]{:S(2)}) collective-permute-start(f32[360,360]{1,0:T(8,128)} %collective-permute-done.7), channel_id=1, source_target_pairs={{0,32},{32,64},{64,96},{96,128},{128,160},{160,192},{192,224},{224... | collective-permute-start | bytes 1555208 | tf_op jit(solution)/shard_map/ppermute | solution.py:64
  111.5 5.1 %collective-permute-start.13 = (f32[360,360]{1,0:T(8,128)S(1)}, f32[360,360]{1,0:T(8,128)S(1)}, u32[]{:S(2)}, u32[]{:S(2)}) collective-permute-start(f32[360,360]{1,0:T(8,128)S(1)} %collective-permute-done.11), channel_id=1, source_target_pairs={{0,480},{32,0},{64,32},{96,64},{128,96},{160,128},{192,160},{224,1... | collective-permute-start | bytes 1555208 | tf_op jit(solution)/shard_map/ppermute | solution.py:66
  118.2 1.8 %fusion.11 = f32[192,360]{1,0:T(8,128)S(1)} fusion(f32[360,360]{1,0:T(8,128)} %collective-permute-done.10, f32[16,192,360]{2,1,0:T(8,128)S(1)} %bitcast.73, s32[]{:T(128)S(6)} %select_n.141), kind=kOutput, calls=%fused_computation.19 | convolution fusion | flops 298598400 | bytes 1089796 | tf_op jit(solution)/shard_map/dot_general | solution.py:51
  121.6 1.8 %convolution_add_fusion.1 = f32[192,360]{1,0:T(8,128)S(1)} fusion(f32[192,360]{1,0:T(8,128)S(1)} %fusion.2, f32[360,360]{1,0:T(8,128)} %collective-permute-done.7, f32[16,192,360]{2,1,0:T(8,128)S(1)} %bitcast.77, s32[]{:T(128)S(6)} %select_n.143), kind=kOutput, calls=%fused_computation.1 | convolution fusion | flops 298667520 | bytes 1384708 | tf_op jit(solution)/shard_map/dot_general | solution.py:51
  123.4 2.1 %collective-permute-done.13 = f32[360,360]{1,0:T(8,128)S(1)} collective-permute-done((f32[360,360]{1,0:T(8,128)S(1)}, f32[360,360]{1,0:T(8,128)S(1)}, u32[]{:S(2)}, u32[]{:S(2)}) %collective-permute-start.13) | collective-permute-done | bytes 518432 | tf_op jit(solution)/shard_map/ppermute | solution.py:66
  125.6 5.6 %collective-permute-start.15 = (f32[180,360]{1,0:T(8,128)S(1)}, f32[180,360]{1,0:T(8,128)S(1)}, u32[]{:S(2)}, u32[]{:S(2)}) collective-permute-start(f32[180,360]{1,0:T(8,128)S(1)} %slice.13), channel_id=1, source_target_pairs={{0,480},{32,0},{64,32},{96,64},{128,96},{160,128},{192,160},{224,1... | collective-permute-start | bytes 777608 | tf_op jit(solution)/shard_map/ppermute | solution.py:71
  131.2 2.1 %collective-permute-start.14 = (f32[180,360]{1,0:T(8,128)S(1)}, f32[180,360]{1,0:T(8,128)S(1)}, u32[]{:S(2)}, u32[]{:S(2)}) collective-permute-start(f32[180,360]{1,0:T(8,128)S(1)} %slice.12), channel_id=1, source_target_pairs={{0,32},{32,64},{64,96},{96,128},{128,160},{160,192},{192,224},{224... | collective-permute-start | bytes 777608 | tf_op jit(solution)/shard_map/ppermute | solution.py:70
  135.6 5.3 %collective-permute-done.14 = f32[180,360]{1,0:T(8,128)S(1)} collective-permute-done((f32[180,360]{1,0:T(8,128)S(1)}, f32[180,360]{1,0:T(8,128)S(1)}, u32[]{:S(2)}, u32[]{:S(2)}) %collective-permute-start.14) | collective-permute-done | bytes 259232 | tf_op jit(solution)/shard_map/ppermute | solution.py:70
  141.9 3.3 %collective-permute-start.16 = (f32[96,360]{1,0:T(8,128)S(1)}, f32[96,360]{1,0:T(8,128)S(1)}, u32[]{:S(2)}, u32[]{:S(2)}) collective-permute-start(f32[96,360]{1,0:T(8,128)S(1)} %constant_dynamic-slice_fusion), channel_id=1, source_target_pairs={{0,1},{1,0},{2,3},{3,2},{4,5},{5,4},{6,7},{7,6},{8,9},{9,8},{10,11... | collective-permute-start | bytes 414728 | tf_op jit(solution)/shard_map/ppermute | solution.py:88
  145.2 5.2 %collective-permute-done.16 = f32[96,360]{1,0:T(8,128)S(1)} collective-permute-done((f32[96,360]{1,0:T(8,128)S(1)}, f32[96,360]{1,0:T(8,128)S(1)}, u32[]{:S(2)}, u32[]{:S(2)}) %collective-permute-start.16) | collective-permute-done | bytes 138272 | tf_op jit(solution)/shard_map/ppermute | solution.py:88
  (41 shorter events, 9.4 us)
Async XLA Ops:
  6.5 92.3 %all-gather.3.cloned.1.call-start = ((), (), s32[]{:S(2)}) async-start(), calls=%async_computation | async-start | bytes 5013504 | tf_op jit(solution)/shard_map/all_gather | solution.py:43
  7.3 23.5 %collective-permute-start.1 = (f32[360,360]{1,0:T(8,128)}, f32[360,360]{1,0:T(8,128)S(1)}, u32[]{:S(2)}, u32[]{:S(2)}) collective-permute-start(f32[360,360]{1,0:T(8,128)} %param.3), channel_id=1, source_target_pairs={{0,480},{32,0},{64,32},{96,64},{128,96},{160,128},{192,160},{224,1... | collective-permute-start | bytes 1555208 | tf_op jit(solution)/shard_map/ppermute | solution.py:66
  18.7 17.6 %collective-permute-start = (f32[360,360]{1,0:T(8,128)}, f32[360,360]{1,0:T(8,128)S(1)}, u32[]{:S(2)}, u32[]{:S(2)}) collective-permute-start(f32[360,360]{1,0:T(8,128)} %param.3), channel_id=1, source_target_pairs={{0,32},{32,64},{64,96},{96,128},{128,160},{160,192},{192,224},{224... | collective-permute-start | bytes 1555208 | tf_op jit(solution)/shard_map/ppermute | solution.py:64
  30.8 16.4 %collective-permute-start.3 = (f32[360,360]{1,0:T(8,128)S(1)}, f32[360,360]{1,0:T(8,128)S(1)}, u32[]{:S(2)}, u32[]{:S(2)}) collective-permute-start(f32[360,360]{1,0:T(8,128)S(1)} %collective-permute-done.1), channel_id=1, source_target_pairs={{0,480},{32,0},{64,32},{96,64},{128,96},{160,128},{192,160},{224,1... | collective-permute-start | bytes 1555208 | tf_op jit(solution)/shard_map/ppermute | solution.py:66
  36.3 46.7 %copy-start.4 = (f32[360,360]{1,0:T(8,128)}, f32[360,360]{1,0:T(8,128)S(1)}, u32[]{:S(2)}) copy-start(f32[360,360]{1,0:T(8,128)S(1)} %collective-permute-done) | copy-start | bytes 1555204
  36.3 16.5 %collective-permute-start.2 = (f32[360,360]{1,0:T(8,128)S(1)}, f32[360,360]{1,0:T(8,128)S(1)}, u32[]{:S(2)}, u32[]{:S(2)}) collective-permute-start(f32[360,360]{1,0:T(8,128)S(1)} %collective-permute-done), channel_id=1, source_target_pairs={{0,32},{32,64},{64,96},{96,128},{128,160},{160,192},{192,224},{224... | collective-permute-start | bytes 1555208 | tf_op jit(solution)/shard_map/ppermute | solution.py:64
  47.2 21.2 %copy-start.3 = (f32[360,360]{1,0:T(8,128)}, f32[360,360]{1,0:T(8,128)S(1)}, u32[]{:S(2)}) copy-start(f32[360,360]{1,0:T(8,128)S(1)} %collective-permute-done.3) | copy-start | bytes 1555204
  47.2 15.6 %collective-permute-start.8 = (f32[360,360]{1,0:T(8,128)S(1)}, f32[360,360]{1,0:T(8,128)S(1)}, u32[]{:S(2)}, u32[]{:S(2)}) collective-permute-start(f32[360,360]{1,0:T(8,128)S(1)} %collective-permute-done.3), channel_id=1, source_target_pairs={{0,480},{32,0},{64,32},{96,64},{128,96},{160,128},{192,160},{224,1... | collective-permute-start | bytes 1555208 | tf_op jit(solution)/shard_map/ppermute | solution.py:66
  52.8 15.6 %collective-permute-start.4 = (f32[360,360]{1,0:T(8,128)S(1)}, f32[360,360]{1,0:T(8,128)S(1)}, u32[]{:S(2)}, u32[]{:S(2)}) collective-permute-start(f32[360,360]{1,0:T(8,128)S(1)} %collective-permute-done.2), channel_id=1, source_target_pairs={{0,32},{32,64},{64,96},{96,128},{128,160},{160,192},{192,224},{224... | collective-permute-start | bytes 1555208 | tf_op jit(solution)/shard_map/ppermute | solution.py:64
  62.7 14.7 %collective-permute-start.9 = (f32[360,360]{1,0:T(8,128)S(1)}, f32[360,360]{1,0:T(8,128)S(1)}, u32[]{:S(2)}, u32[]{:S(2)}) collective-permute-start(f32[360,360]{1,0:T(8,128)S(1)} %collective-permute-done.8), channel_id=1, source_target_pairs={{0,480},{32,0},{64,32},{96,64},{128,96},{160,128},{192,160},{224,1... | collective-permute-start | bytes 1555208 | tf_op jit(solution)/shard_map/ppermute | solution.py:66
  68.3 14.7 %copy-start.5 = (f32[360,360]{1,0:T(8,128)}, f32[360,360]{1,0:T(8,128)S(1)}, u32[]{:S(2)}) copy-start(f32[360,360]{1,0:T(8,128)S(1)} %collective-permute-done.4) | copy-start | bytes 1555204
  68.4 14.6 %collective-permute-start.5 = (f32[360,360]{1,0:T(8,128)S(1)}, f32[360,360]{1,0:T(8,128)S(1)}, u32[]{:S(2)}, u32[]{:S(2)}) collective-permute-start(f32[360,360]{1,0:T(8,128)S(1)} %collective-permute-done.4), channel_id=1, source_target_pairs={{0,32},{32,64},{64,96},{96,128},{128,160},{160,192},{192,224},{224... | collective-permute-start | bytes 1555208 | tf_op jit(solution)/shard_map/ppermute | solution.py:64
  77.4 7.8 %copy-start.1 = (f32[360,360]{1,0:T(8,128)}, f32[360,360]{1,0:T(8,128)S(1)}, u32[]{:S(2)}) copy-start(f32[360,360]{1,0:T(8,128)S(1)} %collective-permute-done.9) | copy-start | bytes 1555204
  77.4 13.7 %collective-permute-start.10 = (f32[360,360]{1,0:T(8,128)S(1)}, f32[360,360]{1,0:T(8,128)}, u32[]{:S(2)}, u32[]{:S(2)}) collective-permute-start(f32[360,360]{1,0:T(8,128)S(1)} %collective-permute-done.9), channel_id=1, source_target_pairs={{0,480},{32,0},{64,32},{96,64},{128,96},{160,128},{192,160},{224,1... | collective-permute-start | bytes 1555208 | tf_op jit(solution)/shard_map/ppermute | solution.py:66
  83.0 13.8 %collective-permute-start.6 = (f32[360,360]{1,0:T(8,128)S(1)}, f32[360,360]{1,0:T(8,128)S(1)}, u32[]{:S(2)}, u32[]{:S(2)}) collective-permute-start(f32[360,360]{1,0:T(8,128)S(1)} %collective-permute-done.5), channel_id=1, source_target_pairs={{0,32},{32,64},{64,96},{96,128},{128,160},{160,192},{192,224},{224... | collective-permute-start | bytes 1555208 | tf_op jit(solution)/shard_map/ppermute | solution.py:64
  91.1 16.9 %collective-permute-start.11 = (f32[360,360]{1,0:T(8,128)}, f32[360,360]{1,0:T(8,128)S(1)}, u32[]{:S(2)}, u32[]{:S(2)}) collective-permute-start(f32[360,360]{1,0:T(8,128)} %collective-permute-done.10), channel_id=1, source_target_pairs={{0,480},{32,0},{64,32},{96,64},{128,96},{160,128},{192,160},{224,1... | collective-permute-start | bytes 1555208 | tf_op jit(solution)/shard_map/ppermute | solution.py:66
  96.8 12.8 %collective-permute-start.7 = (f32[360,360]{1,0:T(8,128)S(1)}, f32[360,360]{1,0:T(8,128)}, u32[]{:S(2)}, u32[]{:S(2)}) collective-permute-start(f32[360,360]{1,0:T(8,128)S(1)} %collective-permute-done.6), channel_id=1, source_target_pairs={{0,32},{32,64},{64,96},{96,128},{128,160},{160,192},{192,224},{224... | collective-permute-start | bytes 1555208 | tf_op jit(solution)/shard_map/ppermute | solution.py:64
  98.8 7.6 %copy-start = (f32[3072,360]{1,0:T(8,128)S(1)}, f32[3072,360]{1,0:T(8,128)}, u32[]{:S(2)}) copy-start(f32[3072,360]{1,0:T(8,128)} %all-gather.3.cloned.1.call-done) | copy-start | bytes 13271044
  98.8 8.4 %copy-start.6 = (f32[360,360]{1,0:T(8,128)S(1)}, f32[360,360]{1,0:T(8,128)}, u32[]{:S(2)}) copy-start(f32[360,360]{1,0:T(8,128)} %copy-done.5) | copy-start | bytes 1555204
  98.8 18.6 %copy-start.2 = (f32[360,360]{1,0:T(8,128)S(1)}, f32[360,360]{1,0:T(8,128)}, u32[]{:S(2)}) copy-start(f32[360,360]{1,0:T(8,128)} %copy-done.1) | copy-start | bytes 1555204
  109.6 13.8 %collective-permute-start.12 = (f32[360,360]{1,0:T(8,128)}, f32[360,360]{1,0:T(8,128)S(1)}, u32[]{:S(2)}, u32[]{:S(2)}) collective-permute-start(f32[360,360]{1,0:T(8,128)} %collective-permute-done.7), channel_id=1, source_target_pairs={{0,32},{32,64},{64,96},{96,128},{128,160},{160,192},{192,224},{224... | collective-permute-start | bytes 1555208 | tf_op jit(solution)/shard_map/ppermute | solution.py:64
  111.5 14.0 %collective-permute-start.13 = (f32[360,360]{1,0:T(8,128)S(1)}, f32[360,360]{1,0:T(8,128)S(1)}, u32[]{:S(2)}, u32[]{:S(2)}) collective-permute-start(f32[360,360]{1,0:T(8,128)S(1)} %collective-permute-done.11), channel_id=1, source_target_pairs={{0,480},{32,0},{64,32},{96,64},{128,96},{160,128},{192,160},{224,1... | collective-permute-start | bytes 1555208 | tf_op jit(solution)/shard_map/ppermute | solution.py:66
  125.6 10.0 %collective-permute-start.15 = (f32[180,360]{1,0:T(8,128)S(1)}, f32[180,360]{1,0:T(8,128)S(1)}, u32[]{:S(2)}, u32[]{:S(2)}) collective-permute-start(f32[180,360]{1,0:T(8,128)S(1)} %slice.13), channel_id=1, source_target_pairs={{0,480},{32,0},{64,32},{96,64},{128,96},{160,128},{192,160},{224,1... | collective-permute-start | bytes 777608 | tf_op jit(solution)/shard_map/ppermute | solution.py:71
  131.2 9.7 %collective-permute-start.14 = (f32[180,360]{1,0:T(8,128)S(1)}, f32[180,360]{1,0:T(8,128)S(1)}, u32[]{:S(2)}, u32[]{:S(2)}) collective-permute-start(f32[180,360]{1,0:T(8,128)S(1)} %slice.12), channel_id=1, source_target_pairs={{0,32},{32,64},{64,96},{96,128},{128,160},{160,192},{192,224},{224... | collective-permute-start | bytes 777608 | tf_op jit(solution)/shard_map/ppermute | solution.py:70
  141.9 8.5 %collective-permute-start.16 = (f32[96,360]{1,0:T(8,128)S(1)}, f32[96,360]{1,0:T(8,128)S(1)}, u32[]{:S(2)}, u32[]{:S(2)}) collective-permute-start(f32[96,360]{1,0:T(8,128)S(1)} %constant_dynamic-slice_fusion), channel_id=1, source_target_pairs={{0,1},{1,0},{2,3},{3,2},{4,5},{5,4},{6,7},{7,6},{8,9},{9,8},{10,11... | collective-permute-start | bytes 414728 | tf_op jit(solution)/shard_map/ppermute | solution.py:88
Sparse Core Ops, SparseCore 0:
  9.5 50.0 all-gather.2

commit v14 on v11

--- a/solution.py
+++ b/solution.py
@@ -12,19 +12,20 @@
     c = lax.axis_index("col")
     core, xlo, y = c % 2, (c // 2) % 2, c // 4
     ny = n // 4
-    other = lax.ppermute(block, "col", [(i, i ^ 1) for i in range(n)])
-    pair = jnp.where(core == 0, jnp.stack([block, other]), jnp.stack([other, block]))
-    far = lax.ppermute(pair, "col", [(i, i ^ 2) for i in range(n)])
-    quad = jnp.where(xlo == 0, jnp.concatenate([pair, far]), jnp.concatenate([far, pair]))
     up = [(i, (i + 4) % n) for i in range(n)]
     down = [(i, (i - 4) % n) for i in range(n)]
-    below = lax.ppermute(quad, "col", up)
-    above = lax.ppermute(quad, "col", down)
-    h = quad.shape[1] // 2
-    opp_a = lax.ppermute(below[:, :h], "col", up)
-    opp_b = lax.ppermute(above[:, h:], "col", down)
-    opposite = jnp.concatenate([opp_a, opp_b], axis=1)
-    stack = jnp.concatenate([quad, above, opposite, below])
+    below = lax.ppermute(block, "col", up)
+    above = lax.ppermute(block, "col", down)
+    h = block.shape[0] // 2
+    opp_a = lax.ppermute(below[:h], "col", up)
+    opp_b = lax.ppermute(above[h:], "col", down)
+    opposite = jnp.concatenate([opp_a, opp_b], axis=0)
+    ring = jnp.stack([block, above, opposite, below])
+    far = lax.ppermute(ring, "col", [(i, i ^ 2) for i in range(n)])
+    pair = jnp.where(xlo == 0, jnp.stack([ring, far]), jnp.stack([far, ring]))
+    other = lax.ppermute(pair, "col", [(i, i ^ 1) for i in range(n)])
+    quad = jnp.where(core == 0, jnp.stack([pair, other]), jnp.stack([other, pair]))
+    stack = jnp.reshape(jnp.transpose(quad, (2, 1, 0, 3, 4)), (n,) + block.shape)
 
     def place(owner):
         return ((owner // 4 - y) % ny) * 4 + owner % 4

time: 155 us -> 188 us (1.21)
  waiting for transfers between devices: 38.5 us -> 66.4 us
  other arithmetic: 3.96 us -> 8.36 us
  starting transfers between devices: 89.5 us -> 91.6 us
    ppermute x6, waiting for transfers between devices: 2.9 us -> 19.5 us  [the longest x1 11.8 us: gather_col(): far = lax.ppermute(ring, 'col', [(i, i ^ 2) for i in range(n)])]
    ppermute x7, waiting for transfers between devices: 26 us -> 38.7 us  [local(): ahead = lax.ppermute(ahead, 'row', fwd)]
    select_n x2 -> x3, other arithmetic: 1.18 us -> 4.83 us  [the longest x1 2.95 us: gather_col(): jnp.where(core == 0, jnp.stack([pair, other]), jnp.stack([other, pair]))]
    another operation x0 -> x3, other arithmetic: none -> 2.85 us  [the longest x2 2.83 us: gather_col(): pair = jnp.where(xlo == 0, jnp.stack([ring, far]), jnp.stack([far, ring]))]
    concatenate x1 -> x0, other arithmetic: 2.1 us -> none  [gather_col(): stack = jnp.concatenate([quad, above, opposite, below])]
    ppermute x7, starting transfers between devices: 15.3 us -> 17.2 us  [local(): ahead = lax.ppermute(ahead, 'row', fwd)]
  transfers between devices with their start and end apart: 23 -> 23, of which waited for: 12 -> 13; matrix products, arithmetic and copies ran while one was open for 14% -> 12% of each run, Pallas kernels for 0% -> 0%
where the time goes in v14:
time: 188 us; the launch traced here: 187 us
  starting transfers between devices  91.6 us (49%)
  waiting for transfers between devices  66.4 us (35%)
  matrix products  18.8 us (10%)
  other arithmetic  8.36 us (4%)
    ppermute x7, starting transfers between devices, local(): behind = lax.ppermute(behind, 'row', bwd)  44.8 us
    ppermute x7, waiting for transfers between devices, local(): ahead = lax.ppermute(ahead, 'row', fwd)  38.7 us
    dot_general x17, matrix products, product(): jnp.dot(cols[:, lo:hi], block, precision=lax.Precision.HIGHEST, preferred...  18.8 us
    ppermute x7, starting transfers between devices, local(): ahead = lax.ppermute(ahead, 'row', fwd)  17.2 us
    ppermute x1, waiting for transfers between devices, gather_col(): far = lax.ppermute(ring, 'col', [(i, i ^ 2) for i in range(n)])  11.8 us
    ppermute x1, starting transfers between devices, local(): bottom = lax.ppermute(behind[m:], 'row', bwd)  5.6 us
    ppermute x1, waiting for transfers between devices, local(): other = lax.ppermute(other, 'depth', [(0, 1), (1, 0)])  5.23 us
    ppermute x1, waiting for transfers between devices, gather_col(): below = lax.ppermute(block, 'col', up)  5.06 us
  transfers between devices with their start and end apart: 23, of which 13 were waited for; matrix products, arithmetic and copies ran while one was open for 12% of the time, Pallas kernels for 0%

profile of v14, /device:TPU:6, one launch (start us, length us, event | category | flops | bytes accessed | tf_op | source)
XLA Modules:
  0.0 186.8 jit_solution(4886469841462867050)
XLA Ops:
  0.0 3.5 %collective-permute-start.1 = (f32[192,360]{1,0:T(8,128)}, f32[192,360]{1,0:T(8,128)S(1)}, u32[]{:S(2)}, u32[]{:S(2)}) collective-permute-start(f32[192,360]{1,0:T(8,128)} %param.2), channel_id=1, source_target_pairs={{0,8},{2,10},{4,12},{6,14},{8,16},{10,18},{12,20},{14,22},{16,24},... | collective-permute-start | bytes 829448 | tf_op jit(solution)/shard_map/ppermute | solution.py:17
  3.5 3.6 %collective-permute-start = (f32[192,360]{1,0:T(8,128)}, f32[192,360]{1,0:T(8,128)S(1)}, u32[]{:S(2)}, u32[]{:S(2)}) collective-permute-start(f32[192,360]{1,0:T(8,128)} %param.2), channel_id=1, source_target_pairs={{0,24},{2,26},{4,28},{6,30},{8,0},{10,2},{12,4},{14,6},{16,8},{18,... | collective-permute-start | bytes 829448 | tf_op jit(solution)/shard_map/ppermute | solution.py:18
  7.1 5.1 %collective-permute-done.1 = f32[192,360]{1,0:T(8,128)S(1)} collective-permute-done((f32[192,360]{1,0:T(8,128)}, f32[192,360]{1,0:T(8,128)S(1)}, u32[]{:S(2)}, u32[]{:S(2)}) %collective-permute-start.1) | collective-permute-done | bytes 276512 | tf_op jit(solution)/shard_map/ppermute | solution.py:17
  12.1 2.2 %collective-permute-start.2 = (f32[96,360]{1,0:T(8,128)S(1)}, f32[96,360]{1,0:T(8,128)S(1)}, u32[]{:S(2)}, u32[]{:S(2)}) collective-permute-start(f32[96,360]{1,0:T(8,128)S(1)} %slice.24), channel_id=1, source_target_pairs={{0,8},{2,10},{4,12},{6,14},{8,16},{10,18},{12,20},{14,22},{16,24},... | collective-permute-start | bytes 414728 | tf_op jit(solution)/shard_map/ppermute | solution.py:20
  14.4 4.8 %collective-permute-start.3 = (f32[96,360]{1,0:T(8,128)S(1)}, f32[96,360]{1,0:T(8,128)S(1)}, u32[]{:S(2)}, u32[]{:S(2)}) collective-permute-start(f32[96,360]{1,0:T(8,128)S(1)} %slice.25), channel_id=1, source_target_pairs={{0,24},{2,26},{4,28},{6,30},{8,0},{10,2},{12,4},{14,6},{16,8},{18,... | collective-permute-start | bytes 414728 | tf_op jit(solution)/shard_map/ppermute | solution.py:21
  21.9 2.3 %fusion.64 = (f32[1,1,4,192,360]{4,3,2,1,0:T(8,128)S(1)}, f32[1,4,192,360]{3,2,0,1:T(8,128)S(1)}, f32[4,192,360]{2,1,0:T(8,128)}) fusion(f32[1,192,360]{2,1,0:T(8,128)S(1)} %bitcast.97, f32[1,192,360]{2,1,0:T(8,128)S(1)} %maximum_bitcast_fusion, f32[1,192,360]{2,1,0:T(8,128)S(1)} %bitcast.98, f32[1,192,360]{2,1,0:T(8,128)} %bitcast.99), kind=kLoop, calls=%fused_computation.81 | loop fusion | flops 829440 | bytes 4423680 | tf_op jit(solution)/shard_map/stack | solution.py:25
  24.2 2.7 %collective-permute-start.4 = (f32[4,192,360]{2,1,0:T(8,128)}, f32[4,192,360]{2,1,0:T(8,128)S(1)}, u32[]{:S(2)}, u32[]{:S(2)}) collective-permute-start(f32[4,192,360]{2,1,0:T(8,128)} %get-tuple-element.23), channel_id=1, source_target_pairs={{0,4},{2,6},{4,0},{6,2},{8,12},{10,14},{12,8},{14,10},{16,20},{18,... | collective-permute-start | bytes 3317768 | tf_op jit(solution)/shard_map/ppermute | solution.py:24
  27.0 3.8 %collective-permute-start.6 = (f32[360,360]{1,0:T(8,128)}, f32[360,360]{1,0:T(8,128)}, u32[]{:S(2)}, u32[]{:S(2)}) collective-permute-start(f32[360,360]{1,0:T(8,128)} %param.3), channel_id=1, source_target_pairs={{0,32},{32,64},{64,96},{96,128},{128,160},{160,192},{192,224},{224... | collective-permute-start | bytes 1555208 | tf_op jit(solution)/shard_map/ppermute | solution.py:62
  30.8 9.5 %collective-permute-start.7 = (f32[360,360]{1,0:T(8,128)}, f32[360,360]{1,0:T(8,128)}, u32[]{:S(2)}, u32[]{:S(2)}) collective-permute-start(f32[360,360]{1,0:T(8,128)} %param.3), channel_id=1, source_target_pairs={{0,480},{32,0},{64,32},{96,64},{128,96},{160,128},{192,160},{224,1... | collective-permute-start | bytes 1555208 | tf_op jit(solution)/shard_map/ppermute | solution.py:64
  40.4 11.8 %collective-permute-done.4 = f32[4,192,360]{2,1,0:T(8,128)S(1)} collective-permute-done((f32[4,192,360]{2,1,0:T(8,128)}, f32[4,192,360]{2,1,0:T(8,128)S(1)}, u32[]{:S(2)}, u32[]{:S(2)}) %collective-permute-start.4) | collective-permute-done | bytes 1105952 | tf_op jit(solution)/shard_map/ppermute | solution.py:24
  53.8 1.9 %collective-permute-start.5 = (f32[2,4,192,360]{3,2,0,1:T(8,128)}, f32[2,4,192,360]{3,2,0,1:T(8,128)}, u32[]{:S(2)}, u32[]{:S(2)}) collective-permute-start(f32[2,4,192,360]{3,2,0,1:T(8,128)} %maximum_select_fusion.1), channel_id=1, source_target_pairs={{0,2},{2,0},{4,6},{6,4},{8,10},{10,8},{12,14},{14,12},{16,18},{18,... | collective-permute-start | bytes 6635528 | tf_op jit(solution)/shard_map/ppermute | solution.py:26
  55.7 3.8 %collective-permute-start.8 = (f32[360,360]{1,0:T(8,128)}, f32[360,360]{1,0:T(8,128)S(1)}, u32[]{:S(2)}, u32[]{:S(2)}) collective-permute-start(f32[360,360]{1,0:T(8,128)} %collective-permute-done.6), channel_id=1, source_target_pairs={{0,32},{32,64},{64,96},{96,128},{128,160},{160,192},{192,224},{224... | collective-permute-start | bytes 1555208 | tf_op jit(solution)/shard_map/ppermute | solution.py:62
  59.5 9.5 %collective-permute-start.9 = (f32[360,360]{1,0:T(8,128)}, f32[360,360]{1,0:T(8,128)S(1)}, u32[]{:S(2)}, u32[]{:S(2)}) collective-permute-start(f32[360,360]{1,0:T(8,128)} %collective-permute-done.7), channel_id=1, source_target_pairs={{0,480},{32,0},{64,32},{96,64},{128,96},{160,128},{192,160},{224,1... | collective-permute-start | bytes 1555208 | tf_op jit(solution)/shard_map/ppermute | solution.py:64
  69.0 11.5 %collective-permute-done.8 = f32[360,360]{1,0:T(8,128)S(1)} collective-permute-done((f32[360,360]{1,0:T(8,128)}, f32[360,360]{1,0:T(8,128)S(1)}, u32[]{:S(2)}, u32[]{:S(2)}) %collective-permute-start.8) | collective-permute-done | bytes 518432 | tf_op jit(solution)/shard_map/ppermute | solution.py:62
  80.5 1.9 %collective-permute-start.10 = (f32[360,360]{1,0:T(8,128)S(1)}, f32[360,360]{1,0:T(8,128)}, u32[]{:S(2)}, u32[]{:S(2)}) collective-permute-start(f32[360,360]{1,0:T(8,128)S(1)} %collective-permute-done.8), channel_id=1, source_target_pairs={{0,32},{32,64},{64,96},{96,128},{128,160},{160,192},{192,224},{224... | collective-permute-start | bytes 1555208 | tf_op jit(solution)/shard_map/ppermute | solution.py:62
  82.4 5.1 %collective-permute-start.14 = (f32[360,360]{1,0:T(8,128)S(1)}, f32[360,360]{1,0:T(8,128)}, u32[]{:S(2)}, u32[]{:S(2)}) collective-permute-start(f32[360,360]{1,0:T(8,128)S(1)} %collective-permute-done.9), channel_id=1, source_target_pairs={{0,480},{32,0},{64,32},{96,64},{128,96},{160,128},{192,160},{224,1... | collective-permute-start | bytes 1555208 | tf_op jit(solution)/shard_map/ppermute | solution.py:64
  87.6 10.5 %collective-permute-done.10 = f32[360,360]{1,0:T(8,128)} collective-permute-done((f32[360,360]{1,0:T(8,128)S(1)}, f32[360,360]{1,0:T(8,128)}, u32[]{:S(2)}, u32[]{:S(2)}) %collective-permute-start.10) | collective-permute-done | bytes 518432 | tf_op jit(solution)/shard_map/ppermute | solution.py:62
  98.0 1.9 %collective-permute-start.11 = (f32[360,360]{1,0:T(8,128)}, f32[360,360]{1,0:T(8,128)S(1)}, u32[]{:S(2)}, u32[]{:S(2)}) collective-permute-start(f32[360,360]{1,0:T(8,128)} %collective-permute-done.10), channel_id=1, source_target_pairs={{0,32},{32,64},{64,96},{96,128},{128,160},{160,192},{192,224},{224... | collective-permute-start | bytes 1555208 | tf_op jit(solution)/shard_map/ppermute | solution.py:62
  100.0 5.1 %collective-permute-start.15 = (f32[360,360]{1,0:T(8,128)}, f32[360,360]{1,0:T(8,128)}, u32[]{:S(2)}, u32[]{:S(2)}) collective-permute-start(f32[360,360]{1,0:T(8,128)} %collective-permute-done.14), channel_id=1, source_target_pairs={{0,480},{32,0},{64,32},{96,64},{128,96},{160,128},{192,160},{224,1... | collective-permute-start | bytes 1555208 | tf_op jit(solution)/shard_map/ppermute | solution.py:64
  106.1 8.7 %collective-permute-done.11 = f32[360,360]{1,0:T(8,128)S(1)} collective-permute-done((f32[360,360]{1,0:T(8,128)}, f32[360,360]{1,0:T(8,128)S(1)}, u32[]{:S(2)}, u32[]{:S(2)}) %collective-permute-start.11) | collective-permute-done | bytes 518432 | tf_op jit(solution)/shard_map/ppermute | solution.py:62
  114.9 1.9 %collective-permute-start.12 = (f32[360,360]{1,0:T(8,128)S(1)}, f32[360,360]{1,0:T(8,128)S(1)}, u32[]{:S(2)}, u32[]{:S(2)}) collective-permute-start(f32[360,360]{1,0:T(8,128)S(1)} %collective-permute-done.11), channel_id=1, source_target_pairs={{0,32},{32,64},{64,96},{96,128},{128,160},{160,192},{192,224},{224... | collective-permute-start | bytes 1555208 | tf_op jit(solution)/shard_map/ppermute | solution.py:62
  116.8 5.1 %collective-permute-start.16 = (f32[360,360]{1,0:T(8,128)}, f32[360,360]{1,0:T(8,128)S(1)}, u32[]{:S(2)}, u32[]{:S(2)}) collective-permute-start(f32[360,360]{1,0:T(8,128)} %collective-permute-done.15), channel_id=1, source_target_pairs={{0,480},{32,0},{64,32},{96,64},{128,96},{160,128},{192,160},{224,1... | collective-permute-start | bytes 1555208 | tf_op jit(solution)/shard_map/ppermute | solution.py:64
  122.7 7.8 %collective-permute-done.12 = f32[360,360]{1,0:T(8,128)S(1)} collective-permute-done((f32[360,360]{1,0:T(8,128)S(1)}, f32[360,360]{1,0:T(8,128)S(1)}, u32[]{:S(2)}, u32[]{:S(2)}) %collective-permute-start.12) | collective-permute-done | bytes 518432 | tf_op jit(solution)/shard_map/ppermute | solution.py:62
  130.5 1.9 %collective-permute-start.13 = (f32[360,360]{1,0:T(8,128)S(1)}, f32[360,360]{1,0:T(8,128)S(1)}, u32[]{:S(2)}, u32[]{:S(2)}) collective-permute-start(f32[360,360]{1,0:T(8,128)S(1)} %collective-permute-done.12), channel_id=1, source_target_pairs={{0,32},{32,64},{64,96},{96,128},{128,160},{160,192},{192,224},{224... | collective-permute-start | bytes 1555208 | tf_op jit(solution)/shard_map/ppermute | solution.py:62
  132.5 5.1 %collective-permute-start.17 = (f32[360,360]{1,0:T(8,128)S(1)}, f32[360,360]{1,0:T(8,128)S(1)}, u32[]{:S(2)}, u32[]{:S(2)}) collective-permute-start(f32[360,360]{1,0:T(8,128)S(1)} %collective-permute-done.16), channel_id=1, source_target_pairs={{0,480},{32,0},{64,32},{96,64},{128,96},{160,128},{192,160},{224,1... | collective-permute-start | bytes 1555208 | tf_op jit(solution)/shard_map/ppermute | solution.py:64
  137.6 2.9 %maximum_select_fusion = f32[2,2,4,192,360]{4,3,0,1,2:T(8,128)S(1)} fusion(f32[1,2,4,192,360]{4,3,0,1,2:T(8,128)} %bitcast.8, f32[1,2,4,192,360]{4,3,0,1,2:T(8,128)S(1)} %copy_select_fusion, pred[]{:T(512)S(6)} %eq.59), kind=kLoop, calls=%fused_computation | loop fusion | flops 3317760 | bytes 8847361 | tf_op jit(solution)/shard_map/jit(_where)/select_n | solution.py:27
  149.5 1.9 %collective-permute-start.18 = (f32[360,360]{1,0:T(8,128)S(1)}, f32[360,360]{1,0:T(8,128)S(1)}, u32[]{:S(2)}, u32[]{:S(2)}) collective-permute-start(f32[360,360]{1,0:T(8,128)S(1)} %collective-permute-done.13), channel_id=1, source_target_pairs={{0,32},{32,64},{64,96},{96,128},{128,160},{160,192},{192,224},{224... | collective-permute-start | bytes 1555208 | tf_op jit(solution)/shard_map/ppermute | solution.py:62
  151.4 5.3 %collective-permute-start.19 = (f32[360,360]{1,0:T(8,128)S(1)}, f32[360,360]{1,0:T(8,128)S(1)}, u32[]{:S(2)}, u32[]{:S(2)}) collective-permute-start(f32[360,360]{1,0:T(8,128)S(1)} %collective-permute-done.17), channel_id=1, source_target_pairs={{0,480},{32,0},{64,32},{96,64},{128,96},{160,128},{192,160},{224,1... | collective-permute-start | bytes 1555208 | tf_op jit(solution)/shard_map/ppermute | solution.py:64
  164.9 1.9 %collective-permute-start.20 = (f32[180,360]{1,0:T(8,128)S(1)}, f32[180,360]{1,0:T(8,128)S(1)}, u32[]{:S(2)}, u32[]{:S(2)}) collective-permute-start(f32[180,360]{1,0:T(8,128)S(1)} %slice.20), channel_id=1, source_target_pairs={{0,32},{32,64},{64,96},{96,128},{128,160},{160,192},{192,224},{224... | collective-permute-start | bytes 777608 | tf_op jit(solution)/shard_map/ppermute | solution.py:68
  166.8 5.6 %collective-permute-start.21 = (f32[180,360]{1,0:T(8,128)S(1)}, f32[180,360]{1,0:T(8,128)S(1)}, u32[]{:S(2)}, u32[]{:S(2)}) collective-permute-start(f32[180,360]{1,0:T(8,128)S(1)} %slice.21), channel_id=1, source_target_pairs={{0,480},{32,0},{64,32},{96,64},{128,96},{160,128},{192,160},{224,1... | collective-permute-start | bytes 777608 | tf_op jit(solution)/shard_map/ppermute | solution.py:69
  177.6 3.3 %collective-permute-start.22 = (f32[96,360]{1,0:T(8,128)S(1)}, f32[96,360]{1,0:T(8,128)S(1)}, u32[]{:S(2)}, u32[]{:S(2)}) collective-permute-start(f32[96,360]{1,0:T(8,128)S(1)} %constant_dynamic-slice_fusion), channel_id=1, source_target_pairs={{0,1},{1,0},{2,3},{3,2},{4,5},{5,4},{6,7},{7,6},{8,9},{9,8},{10,11... | collective-permute-start | bytes 414728 | tf_op jit(solution)/shard_map/ppermute | solution.py:86
  180.9 5.2 %collective-permute-done.22 = f32[96,360]{1,0:T(8,128)S(1)} collective-permute-done((f32[96,360]{1,0:T(8,128)S(1)}, f32[96,360]{1,0:T(8,128)S(1)}, u32[]{:S(2)}, u32[]{:S(2)}) %collective-permute-start.22) | collective-permute-done | bytes 138272 | tf_op jit(solution)/shard_map/ppermute | solution.py:86
  (48 shorter events, 27.8 us)
Async XLA Ops:
  0.0 12.1 %collective-permute-start.1 = (f32[192,360]{1,0:T(8,128)}, f32[192,360]{1,0:T(8,128)S(1)}, u32[]{:S(2)}, u32[]{:S(2)}) collective-permute-start(f32[192,360]{1,0:T(8,128)} %param.2), channel_id=1, source_target_pairs={{0,8},{2,10},{4,12},{6,14},{8,16},{10,18},{12,20},{14,22},{16,24},... | collective-permute-start | bytes 829448 | tf_op jit(solution)/shard_map/ppermute | solution.py:17
  3.5 10.9 %collective-permute-start = (f32[192,360]{1,0:T(8,128)}, f32[192,360]{1,0:T(8,128)S(1)}, u32[]{:S(2)}, u32[]{:S(2)}) collective-permute-start(f32[192,360]{1,0:T(8,128)} %param.2), channel_id=1, source_target_pairs={{0,24},{2,26},{4,28},{6,30},{8,0},{10,2},{12,4},{14,6},{16,8},{18,... | collective-permute-start | bytes 829448 | tf_op jit(solution)/shard_map/ppermute | solution.py:18
  12.1 8.2 %collective-permute-start.2 = (f32[96,360]{1,0:T(8,128)S(1)}, f32[96,360]{1,0:T(8,128)S(1)}, u32[]{:S(2)}, u32[]{:S(2)}) collective-permute-start(f32[96,360]{1,0:T(8,128)S(1)} %slice.24), channel_id=1, source_target_pairs={{0,8},{2,10},{4,12},{6,14},{8,16},{10,18},{12,20},{14,22},{16,24},... | collective-permute-start | bytes 414728 | tf_op jit(solution)/shard_map/ppermute | solution.py:20
  14.4 7.5 %collective-permute-start.3 = (f32[96,360]{1,0:T(8,128)S(1)}, f32[96,360]{1,0:T(8,128)S(1)}, u32[]{:S(2)}, u32[]{:S(2)}) collective-permute-start(f32[96,360]{1,0:T(8,128)S(1)} %slice.25), channel_id=1, source_target_pairs={{0,24},{2,26},{4,28},{6,30},{8,0},{10,2},{12,4},{14,6},{16,8},{18,... | collective-permute-start | bytes 414728 | tf_op jit(solution)/shard_map/ppermute | solution.py:21
  24.2 27.9 %collective-permute-start.4 = (f32[4,192,360]{2,1,0:T(8,128)}, f32[4,192,360]{2,1,0:T(8,128)S(1)}, u32[]{:S(2)}, u32[]{:S(2)}) collective-permute-start(f32[4,192,360]{2,1,0:T(8,128)} %get-tuple-element.23), channel_id=1, source_target_pairs={{0,4},{2,6},{4,0},{6,2},{8,12},{10,14},{12,8},{14,10},{16,20},{18,... | collective-permute-start | bytes 3317768 | tf_op jit(solution)/shard_map/ppermute | solution.py:24
  27.0 28.7 %collective-permute-start.6 = (f32[360,360]{1,0:T(8,128)}, f32[360,360]{1,0:T(8,128)}, u32[]{:S(2)}, u32[]{:S(2)}) collective-permute-start(f32[360,360]{1,0:T(8,128)} %param.3), channel_id=1, source_target_pairs={{0,32},{32,64},{64,96},{96,128},{128,160},{160,192},{192,224},{224... | collective-permute-start | bytes 1555208 | tf_op jit(solution)/shard_map/ppermute | solution.py:62
  30.8 28.7 %collective-permute-start.7 = (f32[360,360]{1,0:T(8,128)}, f32[360,360]{1,0:T(8,128)}, u32[]{:S(2)}, u32[]{:S(2)}) collective-permute-start(f32[360,360]{1,0:T(8,128)} %param.3), channel_id=1, source_target_pairs={{0,480},{32,0},{64,32},{96,64},{128,96},{160,128},{192,160},{224,1... | collective-permute-start | bytes 1555208 | tf_op jit(solution)/shard_map/ppermute | solution.py:64
  53.8 83.8 %collective-permute-start.5 = (f32[2,4,192,360]{3,2,0,1:T(8,128)}, f32[2,4,192,360]{3,2,0,1:T(8,128)}, u32[]{:S(2)}, u32[]{:S(2)}) collective-permute-start(f32[2,4,192,360]{3,2,0,1:T(8,128)} %maximum_select_fusion.1), channel_id=1, source_target_pairs={{0,2},{2,0},{4,6},{6,4},{8,10},{10,8},{12,14},{14,12},{16,18},{18,... | collective-permute-start | bytes 6635528 | tf_op jit(solution)/shard_map/ppermute | solution.py:26
  55.7 24.8 %collective-permute-start.8 = (f32[360,360]{1,0:T(8,128)}, f32[360,360]{1,0:T(8,128)S(1)}, u32[]{:S(2)}, u32[]{:S(2)}) collective-permute-start(f32[360,360]{1,0:T(8,128)} %collective-permute-done.6), channel_id=1, source_target_pairs={{0,32},{32,64},{64,96},{96,128},{128,160},{160,192},{192,224},{224... | collective-permute-start | bytes 1555208 | tf_op jit(solution)/shard_map/ppermute | solution.py:62
  59.5 22.9 %collective-permute-start.9 = (f32[360,360]{1,0:T(8,128)}, f32[360,360]{1,0:T(8,128)S(1)}, u32[]{:S(2)}, u32[]{:S(2)}) collective-permute-start(f32[360,360]{1,0:T(8,128)} %collective-permute-done.7), channel_id=1, source_target_pairs={{0,480},{32,0},{64,32},{96,64},{128,96},{160,128},{192,160},{224,1... | collective-permute-start | bytes 1555208 | tf_op jit(solution)/shard_map/ppermute | solution.py:64
  80.5 17.6 %collective-permute-start.10 = (f32[360,360]{1,0:T(8,128)S(1)}, f32[360,360]{1,0:T(8,128)}, u32[]{:S(2)}, u32[]{:S(2)}) collective-permute-start(f32[360,360]{1,0:T(8,128)S(1)} %collective-permute-done.8), channel_id=1, source_target_pairs={{0,32},{32,64},{64,96},{96,128},{128,160},{160,192},{192,224},{224... | collective-permute-start | bytes 1555208 | tf_op jit(solution)/shard_map/ppermute | solution.py:62
  82.4 15.6 %copy-start = (f32[360,360]{1,0:T(8,128)}, f32[360,360]{1,0:T(8,128)S(1)}, u32[]{:S(2)}) copy-start(f32[360,360]{1,0:T(8,128)S(1)} %collective-permute-done.9) | copy-start | bytes 1555204
  82.4 17.5 %collective-permute-start.14 = (f32[360,360]{1,0:T(8,128)S(1)}, f32[360,360]{1,0:T(8,128)}, u32[]{:S(2)}, u32[]{:S(2)}) collective-permute-start(f32[360,360]{1,0:T(8,128)S(1)} %collective-permute-done.9), channel_id=1, source_target_pairs={{0,480},{32,0},{64,32},{96,64},{128,96},{160,128},{192,160},{224,1... | collective-permute-start | bytes 1555208 | tf_op jit(solution)/shard_map/ppermute | solution.py:64
  98.0 16.8 %collective-permute-start.11 = (f32[360,360]{1,0:T(8,128)}, f32[360,360]{1,0:T(8,128)S(1)}, u32[]{:S(2)}, u32[]{:S(2)}) collective-permute-start(f32[360,360]{1,0:T(8,128)} %collective-permute-done.10), channel_id=1, source_target_pairs={{0,32},{32,64},{64,96},{96,128},{128,160},{160,192},{192,224},{224... | collective-permute-start | bytes 1555208 | tf_op jit(solution)/shard_map/ppermute | solution.py:62
  100.0 16.8 %collective-permute-start.15 = (f32[360,360]{1,0:T(8,128)}, f32[360,360]{1,0:T(8,128)}, u32[]{:S(2)}, u32[]{:S(2)}) collective-permute-start(f32[360,360]{1,0:T(8,128)} %collective-permute-done.14), channel_id=1, source_target_pairs={{0,480},{32,0},{64,32},{96,64},{128,96},{160,128},{192,160},{224,1... | collective-permute-start | bytes 1555208 | tf_op jit(solution)/shard_map/ppermute | solution.py:64
  114.9 15.7 %collective-permute-start.12 = (f32[360,360]{1,0:T(8,128)S(1)}, f32[360,360]{1,0:T(8,128)S(1)}, u32[]{:S(2)}, u32[]{:S(2)}) collective-permute-start(f32[360,360]{1,0:T(8,128)S(1)} %collective-permute-done.11), channel_id=1, source_target_pairs={{0,32},{32,64},{64,96},{96,128},{128,160},{160,192},{192,224},{224... | collective-permute-start | bytes 1555208 | tf_op jit(solution)/shard_map/ppermute | solution.py:62
  116.8 15.7 %collective-permute-start.16 = (f32[360,360]{1,0:T(8,128)}, f32[360,360]{1,0:T(8,128)S(1)}, u32[]{:S(2)}, u32[]{:S(2)}) collective-permute-start(f32[360,360]{1,0:T(8,128)} %collective-permute-done.15), channel_id=1, source_target_pairs={{0,480},{32,0},{64,32},{96,64},{128,96},{160,128},{192,160},{224,1... | collective-permute-start | bytes 1555208 | tf_op jit(solution)/shard_map/ppermute | solution.py:64
  130.5 18.9 %collective-permute-start.13 = (f32[360,360]{1,0:T(8,128)S(1)}, f32[360,360]{1,0:T(8,128)S(1)}, u32[]{:S(2)}, u32[]{:S(2)}) collective-permute-start(f32[360,360]{1,0:T(8,128)S(1)} %collective-permute-done.12), channel_id=1, source_target_pairs={{0,32},{32,64},{64,96},{96,128},{128,160},{160,192},{192,224},{224... | collective-permute-start | bytes 1555208 | tf_op jit(solution)/shard_map/ppermute | solution.py:62
  132.5 17.0 %collective-permute-start.17 = (f32[360,360]{1,0:T(8,128)S(1)}, f32[360,360]{1,0:T(8,128)S(1)}, u32[]{:S(2)}, u32[]{:S(2)}) collective-permute-start(f32[360,360]{1,0:T(8,128)S(1)} %collective-permute-done.16), channel_id=1, source_target_pairs={{0,480},{32,0},{64,32},{96,64},{128,96},{160,128},{192,160},{224,1... | collective-permute-start | bytes 1555208 | tf_op jit(solution)/shard_map/ppermute | solution.py:64
  140.6 5.5 %copy-start.1 = (f32[360,360]{1,0:T(8,128)S(1)}, f32[360,360]{1,0:T(8,128)}, u32[]{:S(2)}) copy-start(f32[360,360]{1,0:T(8,128)} %copy-done) | copy-start | bytes 1555204
  149.5 14.2 %collective-permute-start.18 = (f32[360,360]{1,0:T(8,128)S(1)}, f32[360,360]{1,0:T(8,128)S(1)}, u32[]{:S(2)}, u32[]{:S(2)}) collective-permute-start(f32[360,360]{1,0:T(8,128)S(1)} %collective-permute-done.13), channel_id=1, source_target_pairs={{0,32},{32,64},{64,96},{96,128},{128,160},{160,192},{192,224},{224... | collective-permute-start | bytes 1555208 | tf_op jit(solution)/shard_map/ppermute | solution.py:62
  151.4 13.5 %collective-permute-start.19 = (f32[360,360]{1,0:T(8,128)S(1)}, f32[360,360]{1,0:T(8,128)S(1)}, u32[]{:S(2)}, u32[]{:S(2)}) collective-permute-start(f32[360,360]{1,0:T(8,128)S(1)} %collective-permute-done.17), channel_id=1, source_target_pairs={{0,480},{32,0},{64,32},{96,64},{128,96},{160,128},{192,160},{224,1... | collective-permute-start | bytes 1555208 | tf_op jit(solution)/shard_map/ppermute | solution.py:64
  164.9 10.2 %collective-permute-start.20 = (f32[180,360]{1,0:T(8,128)S(1)}, f32[180,360]{1,0:T(8,128)S(1)}, u32[]{:S(2)}, u32[]{:S(2)}) collective-permute-start(f32[180,360]{1,0:T(8,128)S(1)} %slice.20), channel_id=1, source_target_pairs={{0,32},{32,64},{64,96},{96,128},{128,160},{160,192},{192,224},{224... | collective-permute-start | bytes 777608 | tf_op jit(solution)/shard_map/ppermute | solution.py:68
  166.8 9.7 %collective-permute-start.21 = (f32[180,360]{1,0:T(8,128)S(1)}, f32[180,360]{1,0:T(8,128)S(1)}, u32[]{:S(2)}, u32[]{:S(2)}) collective-permute-start(f32[180,360]{1,0:T(8,128)S(1)} %slice.21), channel_id=1, source_target_pairs={{0,480},{32,0},{64,32},{96,64},{128,96},{160,128},{192,160},{224,1... | collective-permute-start | bytes 777608 | tf_op jit(solution)/shard_map/ppermute | solution.py:69
  177.6 8.5 %collective-permute-start.22 = (f32[96,360]{1,0:T(8,128)S(1)}, f32[96,360]{1,0:T(8,128)S(1)}, u32[]{:S(2)}, u32[]{:S(2)}) collective-permute-start(f32[96,360]{1,0:T(8,128)S(1)} %constant_dynamic-slice_fusion), channel_id=1, source_target_pairs={{0,1},{1,0},{2,3},{3,2},{4,5},{5,4},{6,7},{7,6},{8,9},{9,8},{10,11... | collective-permute-start | bytes 414728 | tf_op jit(solution)/shard_map/ppermute | solution.py:86

commit v15 on v11

--- a/solution.py
+++ b/solution.py
@@ -3,8 +3,8 @@
 from jax import lax
 from jax.sharding import PartitionSpec as P
 
-FIRST_DOT_STEP = 6
-DOTS_PER_STEP = 6
+FIRST_DOT_STEP = 4
+DOTS_PER_STEP = 4
 
 
 def gather_col(block):

time: 155 us -> 168 us (1.084)
  waiting for transfers between devices: 38.5 us -> 55.7 us
  starting transfers between devices: 89.5 us -> 86.6 us
  matrix products: 18.8 us -> 16.6 us
    ppermute x1, waiting for transfers between devices: 1.14 us -> 14.5 us  [gather_col(): far = lax.ppermute(pair, 'col', [(i, i ^ 2) for i in range(n)])]
    ppermute x7, starting transfers between devices: 44.6 us -> 41.7 us  [local(): behind = lax.ppermute(behind, 'row', bwd)]
    ppermute x7, waiting for transfers between devices: 2.52 us -> 5.42 us  [local(): behind = lax.ppermute(behind, 'row', bwd)]
    ppermute x1, starting transfers between devices: 5.6 us -> 3.19 us  [local(): bottom = lax.ppermute(behind[m:], 'row', bwd)]
    ppermute x1, starting transfers between devices: 1.92 us -> 4.33 us  [local(): top = lax.ppermute(ahead[:m], 'row', fwd)]
    dot_general x17, matrix products: 18.8 us -> 16.6 us  [product(): jnp.dot(cols[:, lo:hi], block, precision=lax.Precision.HIGHEST, preferred...]
  transfers between devices with their start and end apart: 23 -> 23, of which waited for: 12 -> 14; matrix products, arithmetic and copies ran while one was open for 14% -> 12% of each run, Pallas kernels for 0% -> 0%
where the time goes in v15:
time: 168 us; the launch traced here: 166 us
  starting transfers between devices  86.6 us (52%)
  waiting for transfers between devices  55.7 us (33%)
  matrix products  16.6 us (10%)
  other arithmetic  3.96 us (2%)
  local copies, waits for them, and re-layouts  1.84 us (1%)
    ppermute x7, starting transfers between devices, local(): behind = lax.ppermute(behind, 'row', bwd)  41.7 us
    ppermute x7, waiting for transfers between devices, local(): ahead = lax.ppermute(ahead, 'row', fwd)  25.1 us
    dot_general x17, matrix products, product(): jnp.dot(cols[:, lo:hi], block, precision=lax.Precision.HIGHEST, preferred...  16.6 us
    ppermute x7, starting transfers between devices, local(): ahead = lax.ppermute(ahead, 'row', fwd)  15.3 us
    ppermute x1, waiting for transfers between devices, gather_col(): far = lax.ppermute(pair, 'col', [(i, i ^ 2) for i in range(n)])  14.5 us
    ppermute x7, waiting for transfers between devices, local(): behind = lax.ppermute(behind, 'row', bwd)  5.42 us
    ppermute x1, waiting for transfers between devices, local(): other = lax.ppermute(other, 'depth', [(0, 1), (1, 0)])  5.22 us
    ppermute x1, starting transfers between devices, gather_col(): opp_b = lax.ppermute(above[:, h:], 'col', down)  4.84 us
  transfers between devices with their start and end apart: 23, of which 14 were waited for; matrix products, arithmetic and copies ran while one was open for 12% of the time, Pallas kernels for 0%

profile of v15, /device:TPU:6, one launch (start us, length us, event | category | flops | bytes accessed | tf_op | source)
XLA Modules:
  0.0 166.2 jit_solution(18098296986154021257)
XLA Ops:
  0.0 1.9 %collective-permute-start = (f32[192,360]{1,0:T(8,128)}, f32[192,360]{1,0:T(8,128)S(1)}, u32[]{:S(2)}, u32[]{:S(2)}) collective-permute-start(f32[192,360]{1,0:T(8,128)} %param.2), channel_id=1, source_target_pairs={{0,2},{2,0},{4,6},{6,4},{8,10},{10,8},{12,14},{14,12},{16,18},{18,... | collective-permute-start | bytes 829448 | tf_op jit(solution)/shard_map/ppermute | solution.py:15
  4.8 2.7 %collective-permute-start.1 = (f32[2,192,360]{2,1,0:T(8,128)S(1)}, f32[2,192,360]{2,1,0:T(8,128)S(1)}, u32[]{:S(2)}, u32[]{:S(2)}) collective-permute-start(f32[2,192,360]{2,1,0:T(8,128)S(1)} %maximum_select_fusion.1), channel_id=1, source_target_pairs={{0,4},{2,6},{4,0},{6,2},{8,12},{10,14},{12,8},{14,10},{16,20},{18,... | collective-permute-start | bytes 1658888 | tf_op jit(solution)/shard_map/ppermute | solution.py:17
  7.6 14.5 %collective-permute-done.1 = f32[2,192,360]{2,1,0:T(8,128)S(1)} collective-permute-done((f32[2,192,360]{2,1,0:T(8,128)S(1)}, f32[2,192,360]{2,1,0:T(8,128)S(1)}, u32[]{:S(2)}, u32[]{:S(2)}) %collective-permute-start.1) | collective-permute-done | bytes 552992 | tf_op jit(solution)/shard_map/ppermute | solution.py:17
  22.1 3.5 %collective-permute-start.3 = (f32[4,192,360]{2,1,0:T(8,128)S(1)}, f32[4,192,360]{2,1,0:T(8,128)S(1)}, u32[]{:S(2)}, u32[]{:S(2)}) collective-permute-start(f32[4,192,360]{2,1,0:T(8,128)S(1)} %maximum_select_fusion), channel_id=1, source_target_pairs={{0,8},{2,10},{4,12},{6,14},{8,16},{10,18},{12,20},{14,22},{16,24},... | collective-permute-start | bytes 3317768 | tf_op jit(solution)/shard_map/ppermute | solution.py:21
  25.6 3.6 %collective-permute-start.2 = (f32[4,192,360]{2,1,0:T(8,128)S(1)}, f32[4,192,360]{2,1,0:T(8,128)S(1)}, u32[]{:S(2)}, u32[]{:S(2)}) collective-permute-start(f32[4,192,360]{2,1,0:T(8,128)S(1)} %maximum_select_fusion), channel_id=1, source_target_pairs={{0,24},{2,26},{4,28},{6,30},{8,0},{10,2},{12,4},{14,6},{16,8},{18,... | collective-permute-start | bytes 3317768 | tf_op jit(solution)/shard_map/ppermute | solution.py:22
  29.2 3.8 %collective-permute-start.6 = (f32[360,360]{1,0:T(8,128)}, f32[360,360]{1,0:T(8,128)S(1)}, u32[]{:S(2)}, u32[]{:S(2)}) collective-permute-start(f32[360,360]{1,0:T(8,128)} %param.3), channel_id=1, source_target_pairs={{0,32},{32,64},{64,96},{96,128},{128,160},{160,192},{192,224},{224... | collective-permute-start | bytes 1555208 | tf_op jit(solution)/shard_map/ppermute | solution.py:61
  33.0 9.5 %collective-permute-start.7 = (f32[360,360]{1,0:T(8,128)}, f32[360,360]{1,0:T(8,128)S(1)}, u32[]{:S(2)}, u32[]{:S(2)}) collective-permute-start(f32[360,360]{1,0:T(8,128)} %param.3), channel_id=1, source_target_pairs={{0,480},{32,0},{64,32},{96,64},{128,96},{160,128},{192,160},{224,1... | collective-permute-start | bytes 1555208 | tf_op jit(solution)/shard_map/ppermute | solution.py:63
  42.5 9.8 %collective-permute-done.6 = f32[360,360]{1,0:T(8,128)S(1)} collective-permute-done((f32[360,360]{1,0:T(8,128)}, f32[360,360]{1,0:T(8,128)S(1)}, u32[]{:S(2)}, u32[]{:S(2)}) %collective-permute-start.6) | collective-permute-done | bytes 518432 | tf_op jit(solution)/shard_map/ppermute | solution.py:61
  52.3 1.9 %collective-permute-start.8 = (f32[360,360]{1,0:T(8,128)S(1)}, f32[360,360]{1,0:T(8,128)}, u32[]{:S(2)}, u32[]{:S(2)}) collective-permute-start(f32[360,360]{1,0:T(8,128)S(1)} %collective-permute-done.6), channel_id=1, source_target_pairs={{0,32},{32,64},{64,96},{96,128},{128,160},{160,192},{192,224},{224... | collective-permute-start | bytes 1555208 | tf_op jit(solution)/shard_map/ppermute | solution.py:61
  54.3 5.1 %collective-permute-start.11 = (f32[360,360]{1,0:T(8,128)S(1)}, f32[360,360]{1,0:T(8,128)}, u32[]{:S(2)}, u32[]{:S(2)}) collective-permute-start(f32[360,360]{1,0:T(8,128)S(1)} %collective-permute-done.7), channel_id=1, source_target_pairs={{0,480},{32,0},{64,32},{96,64},{128,96},{160,128},{192,160},{224,1... | collective-permute-start | bytes 1555208 | tf_op jit(solution)/shard_map/ppermute | solution.py:63
  60.3 2.2 %collective-permute-start.4 = (f32[4,96,360]{2,1,0:T(8,128)}, f32[4,96,360]{2,1,0:T(8,128)}, u32[]{:S(2)}, u32[]{:S(2)}) collective-permute-start(f32[4,96,360]{2,1,0:T(8,128)} %slice.24), channel_id=1, source_target_pairs={{0,8},{2,10},{4,12},{6,14},{8,16},{10,18},{12,20},{14,22},{16,24},... | collective-permute-start | bytes 1658888 | tf_op jit(solution)/shard_map/ppermute | solution.py:24
  63.4 4.8 %collective-permute-start.5 = (f32[4,96,360]{2,1,0:T(8,128)}, f32[4,96,360]{2,1,0:T(8,128)}, u32[]{:S(2)}, u32[]{:S(2)}) collective-permute-start(f32[4,96,360]{2,1,0:T(8,128)} %slice.25), channel_id=1, source_target_pairs={{0,24},{2,26},{4,28},{6,30},{8,0},{10,2},{12,4},{14,6},{16,8},{18,... | collective-permute-start | bytes 1658888 | tf_op jit(solution)/shard_map/ppermute | solution.py:25
  68.2 1.9 %collective-permute-start.9 = (f32[360,360]{1,0:T(8,128)}, f32[360,360]{1,0:T(8,128)}, u32[]{:S(2)}, u32[]{:S(2)}) collective-permute-start(f32[360,360]{1,0:T(8,128)} %collective-permute-done.8), channel_id=1, source_target_pairs={{0,32},{32,64},{64,96},{96,128},{128,160},{160,192},{192,224},{224... | collective-permute-start | bytes 1555208 | tf_op jit(solution)/shard_map/ppermute | solution.py:61
  70.2 5.1 %collective-permute-start.12 = (f32[360,360]{1,0:T(8,128)}, f32[360,360]{1,0:T(8,128)}, u32[]{:S(2)}, u32[]{:S(2)}) collective-permute-start(f32[360,360]{1,0:T(8,128)} %collective-permute-done.11), channel_id=1, source_target_pairs={{0,480},{32,0},{64,32},{96,64},{128,96},{160,128},{192,160},{224,1... | collective-permute-start | bytes 1555208 | tf_op jit(solution)/shard_map/ppermute | solution.py:63
  76.3 7.3 %collective-permute-done.9 = f32[360,360]{1,0:T(8,128)} collective-permute-done((f32[360,360]{1,0:T(8,128)}, f32[360,360]{1,0:T(8,128)}, u32[]{:S(2)}, u32[]{:S(2)}) %collective-permute-start.9) | collective-permute-done | bytes 518432 | tf_op jit(solution)/shard_map/ppermute | solution.py:61
  83.6 1.9 %collective-permute-start.10 = (f32[360,360]{1,0:T(8,128)}, f32[360,360]{1,0:T(8,128)S(1)}, u32[]{:S(2)}, u32[]{:S(2)}) collective-permute-start(f32[360,360]{1,0:T(8,128)} %collective-permute-done.9), channel_id=1, source_target_pairs={{0,32},{32,64},{64,96},{96,128},{128,160},{160,192},{192,224},{224... | collective-permute-start | bytes 1555208 | tf_op jit(solution)/shard_map/ppermute | solution.py:61
  85.5 5.1 %collective-permute-start.13 = (f32[360,360]{1,0:T(8,128)}, f32[360,360]{1,0:T(8,128)S(1)}, u32[]{:S(2)}, u32[]{:S(2)}) collective-permute-start(f32[360,360]{1,0:T(8,128)} %collective-permute-done.12), channel_id=1, source_target_pairs={{0,480},{32,0},{64,32},{96,64},{128,96},{160,128},{192,160},{224,1... | collective-permute-start | bytes 1555208 | tf_op jit(solution)/shard_map/ppermute | solution.py:63
  90.7 2.1 %pad_maximum_fusion = f32[16,192,360]{2,1,0:T(8,128)S(1)} fusion(f32[4,192,360]{2,1,0:T(8,128)S(1)} %collective-permute-done.3, f32[4,96,360]{2,1,0:T(8,128)} %collective-permute-done.5, f32[4,96,360]{2,1,0:T(8,128)} %collective-permute-done.4, f32[4,192,360]{2,1,0:T(8,128)S(1)} %collective-permute-done.2, f32[4,192,360]{2,1,0:T(8,128)S(1)} %maximum_select_fusion), kind=kLoop, calls=%fused_computation | loop fusion | flops 4423680 | bytes 8847360 | tf_op jit(solution)/shard_map/concatenate | solution.py:27
  99.2 1.9 %collective-permute-start.14 = (f32[360,360]{1,0:T(8,128)S(1)}, f32[360,360]{1,0:T(8,128)S(1)}, u32[]{:S(2)}, u32[]{:S(2)}) collective-permute-start(f32[360,360]{1,0:T(8,128)S(1)} %collective-permute-done.10), channel_id=1, source_target_pairs={{0,32},{32,64},{64,96},{96,128},{128,160},{160,192},{192,224},{224... | collective-permute-start | bytes 1555208 | tf_op jit(solution)/shard_map/ppermute | solution.py:61
  101.1 5.5 %collective-permute-start.15 = (f32[360,360]{1,0:T(8,128)S(1)}, f32[360,360]{1,0:T(8,128)S(1)}, u32[]{:S(2)}, u32[]{:S(2)}) collective-permute-start(f32[360,360]{1,0:T(8,128)S(1)} %collective-permute-done.13), channel_id=1, source_target_pairs={{0,480},{32,0},{64,32},{96,64},{128,96},{160,128},{192,160},{224,1... | collective-permute-start | bytes 1555208 | tf_op jit(solution)/shard_map/ppermute | solution.py:63
  110.3 1.8 %fusion.1 = f32[192,360]{1,0:T(8,128)S(1)} fusion(f32[192,360]{1,0:T(8,128)S(1)} %fusion.18, f32[360,360]{1,0:T(8,128)} %collective-permute-done.9, f32[16,192,360]{2,1,0:T(8,128)S(1)} %pad_maximum_fusion, s32[]{:T(128)S(6)} %select_n.369, f32[192,360]{1,0:T(8,128)S(1)} %convolution_add_fusion.3, f32[192,360]{1,0:T(8,128)S(1)} %fusion.21), kind=kOutput, calls=%fused_computation.8 | convolution fusion | flops 298805760 | bytes 1974532 | tf_op jit(solution)/shard_map/dot_general | solution.py:48
  114.0 1.9 %collective-permute-start.16 = (f32[360,360]{1,0:T(8,128)S(1)}, f32[360,360]{1,0:T(8,128)S(1)}, u32[]{:S(2)}, u32[]{:S(2)}) collective-permute-start(f32[360,360]{1,0:T(8,128)S(1)} %collective-permute-done.14), channel_id=1, source_target_pairs={{0,32},{32,64},{64,96},{96,128},{128,160},{160,192},{192,224},{224... | collective-permute-start | bytes 1555208 | tf_op jit(solution)/shard_map/ppermute | solution.py:61
  115.9 5.8 %collective-permute-start.17 = (f32[360,360]{1,0:T(8,128)S(1)}, f32[360,360]{1,0:T(8,128)S(1)}, u32[]{:S(2)}, u32[]{:S(2)}) collective-permute-start(f32[360,360]{1,0:T(8,128)S(1)} %collective-permute-done.15), channel_id=1, source_target_pairs={{0,480},{32,0},{64,32},{96,64},{128,96},{160,128},{192,160},{224,1... | collective-permute-start | bytes 1555208 | tf_op jit(solution)/shard_map/ppermute | solution.py:63
  124.0 3.1 %collective-permute-done.16 = f32[360,360]{1,0:T(8,128)S(1)} collective-permute-done((f32[360,360]{1,0:T(8,128)S(1)}, f32[360,360]{1,0:T(8,128)S(1)}, u32[]{:S(2)}, u32[]{:S(2)}) %collective-permute-start.16) | collective-permute-done | bytes 518432 | tf_op jit(solution)/shard_map/ppermute | solution.py:61
  128.5 2.0 %collective-permute-start.18 = (f32[360,360]{1,0:T(8,128)S(1)}, f32[360,360]{1,0:T(8,128)S(1)}, u32[]{:S(2)}, u32[]{:S(2)}) collective-permute-start(f32[360,360]{1,0:T(8,128)S(1)} %collective-permute-done.16), channel_id=1, source_target_pairs={{0,32},{32,64},{64,96},{96,128},{128,160},{160,192},{192,224},{224... | collective-permute-start | bytes 1555208 | tf_op jit(solution)/shard_map/ppermute | solution.py:61
  130.4 5.6 %collective-permute-start.19 = (f32[360,360]{1,0:T(8,128)S(1)}, f32[360,360]{1,0:T(8,128)S(1)}, u32[]{:S(2)}, u32[]{:S(2)}) collective-permute-start(f32[360,360]{1,0:T(8,128)S(1)} %collective-permute-done.17), channel_id=1, source_target_pairs={{0,480},{32,0},{64,32},{96,64},{128,96},{160,128},{192,160},{224,1... | collective-permute-start | bytes 1555208 | tf_op jit(solution)/shard_map/ppermute | solution.py:63
  137.6 4.0 %collective-permute-done.18 = f32[360,360]{1,0:T(8,128)S(1)} collective-permute-done((f32[360,360]{1,0:T(8,128)S(1)}, f32[360,360]{1,0:T(8,128)S(1)}, u32[]{:S(2)}, u32[]{:S(2)}) %collective-permute-start.18) | collective-permute-done | bytes 518432 | tf_op jit(solution)/shard_map/ppermute | solution.py:61
  143.1 4.3 %collective-permute-start.20 = (f32[180,360]{1,0:T(8,128)S(1)}, f32[180,360]{1,0:T(8,128)S(1)}, u32[]{:S(2)}, u32[]{:S(2)}) collective-permute-start(f32[180,360]{1,0:T(8,128)S(1)} %slice.20), channel_id=1, source_target_pairs={{0,32},{32,64},{64,96},{96,128},{128,160},{160,192},{192,224},{224... | collective-permute-start | bytes 777608 | tf_op jit(solution)/shard_map/ppermute | solution.py:67
  147.5 3.2 %collective-permute-start.21 = (f32[180,360]{1,0:T(8,128)S(1)}, f32[180,360]{1,0:T(8,128)S(1)}, u32[]{:S(2)}, u32[]{:S(2)}) collective-permute-start(f32[180,360]{1,0:T(8,128)S(1)} %slice.21), channel_id=1, source_target_pairs={{0,480},{32,0},{64,32},{96,64},{128,96},{160,128},{192,160},{224,1... | collective-permute-start | bytes 777608 | tf_op jit(solution)/shard_map/ppermute | solution.py:68
  153.3 2.7 %collective-permute-done.21 = f32[180,360]{1,0:T(8,128)S(1)} collective-permute-done((f32[180,360]{1,0:T(8,128)S(1)}, f32[180,360]{1,0:T(8,128)S(1)}, u32[]{:S(2)}, u32[]{:S(2)}) %collective-permute-start.21) | collective-permute-done | bytes 259232 | tf_op jit(solution)/shard_map/ppermute | solution.py:68
  157.0 3.3 %collective-permute-start.22 = (f32[96,360]{1,0:T(8,128)S(1)}, f32[96,360]{1,0:T(8,128)S(1)}, u32[]{:S(2)}, u32[]{:S(2)}) collective-permute-start(f32[96,360]{1,0:T(8,128)S(1)} %constant_dynamic-slice_fusion), channel_id=1, source_target_pairs={{0,1},{1,0},{2,3},{3,2},{4,5},{5,4},{6,7},{7,6},{8,9},{9,8},{10,11... | collective-permute-start | bytes 414728 | tf_op jit(solution)/shard_map/ppermute | solution.py:85
  160.3 5.2 %collective-permute-done.22 = f32[96,360]{1,0:T(8,128)S(1)} collective-permute-done((f32[96,360]{1,0:T(8,128)S(1)}, f32[96,360]{1,0:T(8,128)S(1)}, u32[]{:S(2)}, u32[]{:S(2)}) %collective-permute-start.22) | collective-permute-done | bytes 138272 | tf_op jit(solution)/shard_map/ppermute | solution.py:85
  (51 shorter events, 27.7 us)
Async XLA Ops:
  0.0 3.7 %collective-permute-start = (f32[192,360]{1,0:T(8,128)}, f32[192,360]{1,0:T(8,128)S(1)}, u32[]{:S(2)}, u32[]{:S(2)}) collective-permute-start(f32[192,360]{1,0:T(8,128)} %param.2), channel_id=1, source_target_pairs={{0,2},{2,0},{4,6},{6,4},{8,10},{10,8},{12,14},{14,12},{16,18},{18,... | collective-permute-start | bytes 829448 | tf_op jit(solution)/shard_map/ppermute | solution.py:15
  4.8 17.3 %collective-permute-start.1 = (f32[2,192,360]{2,1,0:T(8,128)S(1)}, f32[2,192,360]{2,1,0:T(8,128)S(1)}, u32[]{:S(2)}, u32[]{:S(2)}) collective-permute-start(f32[2,192,360]{2,1,0:T(8,128)S(1)} %maximum_select_fusion.1), channel_id=1, source_target_pairs={{0,4},{2,6},{4,0},{6,2},{8,12},{10,14},{12,8},{14,10},{16,20},{18,... | collective-permute-start | bytes 1658888 | tf_op jit(solution)/shard_map/ppermute | solution.py:17
  22.1 37.3 %collective-permute-start.3 = (f32[4,192,360]{2,1,0:T(8,128)S(1)}, f32[4,192,360]{2,1,0:T(8,128)S(1)}, u32[]{:S(2)}, u32[]{:S(2)}) collective-permute-start(f32[4,192,360]{2,1,0:T(8,128)S(1)} %maximum_select_fusion), channel_id=1, source_target_pairs={{0,8},{2,10},{4,12},{6,14},{8,16},{10,18},{12,20},{14,22},{16,24},... | collective-permute-start | bytes 3317768 | tf_op jit(solution)/shard_map/ppermute | solution.py:21
  25.6 36.9 %collective-permute-start.2 = (f32[4,192,360]{2,1,0:T(8,128)S(1)}, f32[4,192,360]{2,1,0:T(8,128)S(1)}, u32[]{:S(2)}, u32[]{:S(2)}) collective-permute-start(f32[4,192,360]{2,1,0:T(8,128)S(1)} %maximum_select_fusion), channel_id=1, source_target_pairs={{0,24},{2,26},{4,28},{6,30},{8,0},{10,2},{12,4},{14,6},{16,8},{18,... | collective-permute-start | bytes 3317768 | tf_op jit(solution)/shard_map/ppermute | solution.py:22
  29.2 23.1 %collective-permute-start.6 = (f32[360,360]{1,0:T(8,128)}, f32[360,360]{1,0:T(8,128)S(1)}, u32[]{:S(2)}, u32[]{:S(2)}) collective-permute-start(f32[360,360]{1,0:T(8,128)} %param.3), channel_id=1, source_target_pairs={{0,32},{32,64},{64,96},{96,128},{128,160},{160,192},{192,224},{224... | collective-permute-start | bytes 1555208 | tf_op jit(solution)/shard_map/ppermute | solution.py:61
  33.0 21.2 %collective-permute-start.7 = (f32[360,360]{1,0:T(8,128)}, f32[360,360]{1,0:T(8,128)S(1)}, u32[]{:S(2)}, u32[]{:S(2)}) collective-permute-start(f32[360,360]{1,0:T(8,128)} %param.3), channel_id=1, source_target_pairs={{0,480},{32,0},{64,32},{96,64},{128,96},{160,128},{192,160},{224,1... | collective-permute-start | bytes 1555208 | tf_op jit(solution)/shard_map/ppermute | solution.py:63
  52.3 10.2 %copy-start.1 = (f32[360,360]{1,0:T(8,128)}, f32[360,360]{1,0:T(8,128)S(1)}, u32[]{:S(2)}) copy-start(f32[360,360]{1,0:T(8,128)S(1)} %collective-permute-done.6) | copy-start | bytes 1555204
  52.3 15.9 %collective-permute-start.8 = (f32[360,360]{1,0:T(8,128)S(1)}, f32[360,360]{1,0:T(8,128)}, u32[]{:S(2)}, u32[]{:S(2)}) collective-permute-start(f32[360,360]{1,0:T(8,128)S(1)} %collective-permute-done.6), channel_id=1, source_target_pairs={{0,32},{32,64},{64,96},{96,128},{128,160},{160,192},{192,224},{224... | collective-permute-start | bytes 1555208 | tf_op jit(solution)/shard_map/ppermute | solution.py:61
  54.3 14.0 %copy-start.3 = (f32[360,360]{1,0:T(8,128)}, f32[360,360]{1,0:T(8,128)S(1)}, u32[]{:S(2)}) copy-start(f32[360,360]{1,0:T(8,128)S(1)} %collective-permute-done.7) | copy-start | bytes 1555204
  54.3 15.9 %collective-permute-start.11 = (f32[360,360]{1,0:T(8,128)S(1)}, f32[360,360]{1,0:T(8,128)}, u32[]{:S(2)}, u32[]{:S(2)}) collective-permute-start(f32[360,360]{1,0:T(8,128)S(1)} %collective-permute-done.7), channel_id=1, source_target_pairs={{0,480},{32,0},{64,32},{96,64},{128,96},{160,128},{192,160},{224,1... | collective-permute-start | bytes 1555208 | tf_op jit(solution)/shard_map/ppermute | solution.py:63
  60.3 30.4 %collective-permute-start.4 = (f32[4,96,360]{2,1,0:T(8,128)}, f32[4,96,360]{2,1,0:T(8,128)}, u32[]{:S(2)}, u32[]{:S(2)}) collective-permute-start(f32[4,96,360]{2,1,0:T(8,128)} %slice.24), channel_id=1, source_target_pairs={{0,8},{2,10},{4,12},{6,14},{8,16},{10,18},{12,20},{14,22},{16,24},... | collective-permute-start | bytes 1658888 | tf_op jit(solution)/shard_map/ppermute | solution.py:24
  63.4 27.3 %collective-permute-start.5 = (f32[4,96,360]{2,1,0:T(8,128)}, f32[4,96,360]{2,1,0:T(8,128)}, u32[]{:S(2)}, u32[]{:S(2)}) collective-permute-start(f32[4,96,360]{2,1,0:T(8,128)} %slice.25), channel_id=1, source_target_pairs={{0,24},{2,26},{4,28},{6,30},{8,0},{10,2},{12,4},{14,6},{16,8},{18,... | collective-permute-start | bytes 1658888 | tf_op jit(solution)/shard_map/ppermute | solution.py:25
  68.2 15.4 %collective-permute-start.9 = (f32[360,360]{1,0:T(8,128)}, f32[360,360]{1,0:T(8,128)}, u32[]{:S(2)}, u32[]{:S(2)}) collective-permute-start(f32[360,360]{1,0:T(8,128)} %collective-permute-done.8), channel_id=1, source_target_pairs={{0,32},{32,64},{64,96},{96,128},{128,160},{160,192},{192,224},{224... | collective-permute-start | bytes 1555208 | tf_op jit(solution)/shard_map/ppermute | solution.py:61
  70.2 15.4 %collective-permute-start.12 = (f32[360,360]{1,0:T(8,128)}, f32[360,360]{1,0:T(8,128)}, u32[]{:S(2)}, u32[]{:S(2)}) collective-permute-start(f32[360,360]{1,0:T(8,128)} %collective-permute-done.11), channel_id=1, source_target_pairs={{0,480},{32,0},{64,32},{96,64},{128,96},{160,128},{192,160},{224,1... | collective-permute-start | bytes 1555208 | tf_op jit(solution)/shard_map/ppermute | solution.py:63
  76.3 16.5 %copy-start.2 = (f32[360,360]{1,0:T(8,128)S(1)}, f32[360,360]{1,0:T(8,128)}, u32[]{:S(2)}) copy-start(f32[360,360]{1,0:T(8,128)} %copy-done.1) | copy-start | bytes 1555204
  76.3 17.3 %copy-start.4 = (f32[360,360]{1,0:T(8,128)S(1)}, f32[360,360]{1,0:T(8,128)}, u32[]{:S(2)}) copy-start(f32[360,360]{1,0:T(8,128)} %copy-done.3) | copy-start | bytes 1555204
  76.3 18.0 %copy-start = (f32[360,360]{1,0:T(8,128)S(1)}, f32[360,360]{1,0:T(8,128)}, u32[]{:S(2)}) copy-start(f32[360,360]{1,0:T(8,128)} %param.3) | copy-start | bytes 1555204
  83.6 14.3 %collective-permute-start.10 = (f32[360,360]{1,0:T(8,128)}, f32[360,360]{1,0:T(8,128)S(1)}, u32[]{:S(2)}, u32[]{:S(2)}) collective-permute-start(f32[360,360]{1,0:T(8,128)} %collective-permute-done.9), channel_id=1, source_target_pairs={{0,32},{32,64},{64,96},{96,128},{128,160},{160,192},{192,224},{224... | collective-permute-start | bytes 1555208 | tf_op jit(solution)/shard_map/ppermute | solution.py:61
  85.5 13.7 %collective-permute-start.13 = (f32[360,360]{1,0:T(8,128)}, f32[360,360]{1,0:T(8,128)S(1)}, u32[]{:S(2)}, u32[]{:S(2)}) collective-permute-start(f32[360,360]{1,0:T(8,128)} %collective-permute-done.12), channel_id=1, source_target_pairs={{0,480},{32,0},{64,32},{96,64},{128,96},{160,128},{192,160},{224,1... | collective-permute-start | bytes 1555208 | tf_op jit(solution)/shard_map/ppermute | solution.py:63
  99.2 13.6 %collective-permute-start.14 = (f32[360,360]{1,0:T(8,128)S(1)}, f32[360,360]{1,0:T(8,128)S(1)}, u32[]{:S(2)}, u32[]{:S(2)}) collective-permute-start(f32[360,360]{1,0:T(8,128)S(1)} %collective-permute-done.10), channel_id=1, source_target_pairs={{0,32},{32,64},{64,96},{96,128},{128,160},{160,192},{192,224},{224... | collective-permute-start | bytes 1555208 | tf_op jit(solution)/shard_map/ppermute | solution.py:61
  101.1 12.8 %collective-permute-start.15 = (f32[360,360]{1,0:T(8,128)S(1)}, f32[360,360]{1,0:T(8,128)S(1)}, u32[]{:S(2)}, u32[]{:S(2)}) collective-permute-start(f32[360,360]{1,0:T(8,128)S(1)} %collective-permute-done.13), channel_id=1, source_target_pairs={{0,480},{32,0},{64,32},{96,64},{128,96},{160,128},{192,160},{224,1... | collective-permute-start | bytes 1555208 | tf_op jit(solution)/shard_map/ppermute | solution.py:63
  114.0 13.0 %collective-permute-start.16 = (f32[360,360]{1,0:T(8,128)S(1)}, f32[360,360]{1,0:T(8,128)S(1)}, u32[]{:S(2)}, u32[]{:S(2)}) collective-permute-start(f32[360,360]{1,0:T(8,128)S(1)} %collective-permute-done.14), channel_id=1, source_target_pairs={{0,32},{32,64},{64,96},{96,128},{128,160},{160,192},{192,224},{224... | collective-permute-start | bytes 1555208 | tf_op jit(solution)/shard_map/ppermute | solution.py:61
  115.9 12.6 %collective-permute-start.17 = (f32[360,360]{1,0:T(8,128)S(1)}, f32[360,360]{1,0:T(8,128)S(1)}, u32[]{:S(2)}, u32[]{:S(2)}) collective-permute-start(f32[360,360]{1,0:T(8,128)S(1)} %collective-permute-done.15), channel_id=1, source_target_pairs={{0,480},{32,0},{64,32},{96,64},{128,96},{160,128},{192,160},{224,1... | collective-permute-start | bytes 1555208 | tf_op jit(solution)/shard_map/ppermute | solution.py:63
  128.5 13.0 %collective-permute-start.18 = (f32[360,360]{1,0:T(8,128)S(1)}, f32[360,360]{1,0:T(8,128)S(1)}, u32[]{:S(2)}, u32[]{:S(2)}) collective-permute-start(f32[360,360]{1,0:T(8,128)S(1)} %collective-permute-done.16), channel_id=1, source_target_pairs={{0,32},{32,64},{64,96},{96,128},{128,160},{160,192},{192,224},{224... | collective-permute-start | bytes 1555208 | tf_op jit(solution)/shard_map/ppermute | solution.py:61
  130.4 12.6 %collective-permute-start.19 = (f32[360,360]{1,0:T(8,128)S(1)}, f32[360,360]{1,0:T(8,128)S(1)}, u32[]{:S(2)}, u32[]{:S(2)}) collective-permute-start(f32[360,360]{1,0:T(8,128)S(1)} %collective-permute-done.17), channel_id=1, source_target_pairs={{0,480},{32,0},{64,32},{96,64},{128,96},{160,128},{192,160},{224,1... | collective-permute-start | bytes 1555208 | tf_op jit(solution)/shard_map/ppermute | solution.py:63
  143.1 10.2 %collective-permute-start.20 = (f32[180,360]{1,0:T(8,128)S(1)}, f32[180,360]{1,0:T(8,128)S(1)}, u32[]{:S(2)}, u32[]{:S(2)}) collective-permute-start(f32[180,360]{1,0:T(8,128)S(1)} %slice.20), channel_id=1, source_target_pairs={{0,32},{32,64},{64,96},{96,128},{128,160},{160,192},{192,224},{224... | collective-permute-start | bytes 777608 | tf_op jit(solution)/shard_map/ppermute | solution.py:67
  147.5 8.5 %collective-permute-start.21 = (f32[180,360]{1,0:T(8,128)S(1)}, f32[180,360]{1,0:T(8,128)S(1)}, u32[]{:S(2)}, u32[]{:S(2)}) collective-permute-start(f32[180,360]{1,0:T(8,128)S(1)} %slice.21), channel_id=1, source_target_pairs={{0,480},{32,0},{64,32},{96,64},{128,96},{160,128},{192,160},{224,1... | collective-permute-start | bytes 777608 | tf_op jit(solution)/shard_map/ppermute | solution.py:68
  157.0 8.5 %collective-permute-start.22 = (f32[96,360]{1,0:T(8,128)S(1)}, f32[96,360]{1,0:T(8,128)S(1)}, u32[]{:S(2)}, u32[]{:S(2)}) collective-permute-start(f32[96,360]{1,0:T(8,128)S(1)} %constant_dynamic-slice_fusion), channel_id=1, source_target_pairs={{0,1},{1,0},{2,3},{3,2},{4,5},{5,4},{6,7},{7,6},{8,9},{9,8},{10,11... | collective-permute-start | bytes 414728 | tf_op jit(solution)/shard_map/ppermute | solution.py:85

commit v16 on v11

--- a/solution.py
+++ b/solution.py
@@ -42,9 +42,11 @@
 
     strip, place = gather_col(amplitudes)
 
-    def product(block, owner, lo=0, hi=None):
+    def product(block, owner, lo=0, hi=None, start=None):
         hi = kb if hi is None else hi
         cols = lax.dynamic_index_in_dim(strip, place(owner), axis=0, keepdims=False)
+        if start is not None:
+            cols = lax.dynamic_slice_in_dim(cols, start, half, axis=0)
         return jnp.dot(cols[:, lo:hi], block, precision=lax.Precision.HIGHEST,
                        preferred_element_type=jnp.float32)
 
@@ -76,13 +78,13 @@
             pending = pending[DOTS_PER_STEP:]
             total, ahead, behind = lax.optimization_barrier((total, ahead, behind))
         pending = pending + arrived
-    for block, owner, lo, hi in pending:
-        part = product(block, owner, lo, hi)
-        total = part if total is None else total + part
-
     mine = lax.dynamic_slice_in_dim(total, d * half, half, axis=0)
     other = lax.dynamic_slice_in_dim(total, (1 - d) * half, half, axis=0)
+    for block, owner, lo, hi in pending:
+        other = other + product(block, owner, lo, hi, (1 - d) * half)
     other = lax.ppermute(other, "depth", [(0, 1), (1, 0)])
+    for block, owner, lo, hi in pending:
+        mine = mine + product(block, owner, lo, hi, d * half)
     return 0.5 * (mine + other)
 
 

time: 155 us -> 155 us (level)
    dot_general x17 -> x19, matrix products: 18.8 us -> 19.2 us  [product(): jnp.dot(cols[:, lo:hi], block, precision=lax.Precision.HIGHEST, preferred...]
  transfers between devices with their start and end apart: 23 -> 23, of which waited for: 12 -> 12; matrix products, arithmetic and copies ran while one was open for 14% -> 15% of each run, Pallas kernels for 0% -> 0%
where the time goes in v16:
time: 155 us; the launch traced here: 154 us
  starting transfers between devices  89.5 us (58%)
  waiting for transfers between devices  37.7 us (24%)
  matrix products  19.2 us (12%)
  other arithmetic  3.97 us (3%)
  local copies, waits for them, and re-layouts  1.82 us (1%)
    ppermute x7, starting transfers between devices, local(): behind = lax.ppermute(behind, 'row', bwd)  44.6 us
    ppermute x7, waiting for transfers between devices, local(): ahead = lax.ppermute(ahead, 'row', fwd)  26 us
    dot_general x19, matrix products, product(): jnp.dot(cols[:, lo:hi], block, precision=lax.Precision.HIGHEST, preferred...  19.2 us
    ppermute x7, starting transfers between devices, local(): ahead = lax.ppermute(ahead, 'row', fwd)  15.3 us
    ppermute x1, starting transfers between devices, local(): bottom = lax.ppermute(behind[m:], 'row', bwd)  5.6 us
    ppermute x1, starting transfers between devices, gather_col(): opp_b = lax.ppermute(above[:, h:], 'col', down)  4.84 us
    ppermute x1, waiting for transfers between devices, local(): other = lax.ppermute(other, 'depth', [(0, 1), (1, 0)])  4.51 us
    ppermute x1, starting transfers between devices, gather_col(): above = lax.ppermute(quad, 'col', down)  3.57 us
  transfers between devices with their start and end apart: 23, of which 12 were waited for; matrix products, arithmetic and copies ran while one was open for 15% of the time, Pallas kernels for 0%

profile of v16, /device:TPU:6, one launch (start us, length us, event | category | flops | bytes accessed | tf_op | source)
XLA Modules:
  0.0 153.7 jit_solution(4113778637408580220)
XLA Ops:
  0.0 1.9 %collective-permute-start = (f32[192,360]{1,0:T(8,128)}, f32[192,360]{1,0:T(8,128)S(1)}, u32[]{:S(2)}, u32[]{:S(2)}) collective-permute-start(f32[192,360]{1,0:T(8,128)} %param.2), channel_id=1, source_target_pairs={{0,2},{2,0},{4,6},{6,4},{8,10},{10,8},{12,14},{14,12},{16,18},{18,... | collective-permute-start | bytes 829448 | tf_op jit(solution)/shard_map/ppermute | solution.py:15
  4.8 2.7 %collective-permute-start.1 = (f32[2,192,360]{2,1,0:T(8,128)S(1)}, f32[2,192,360]{2,1,0:T(8,128)S(1)}, u32[]{:S(2)}, u32[]{:S(2)}) collective-permute-start(f32[2,192,360]{2,1,0:T(8,128)S(1)} %maximum_select_fusion.1), channel_id=1, source_target_pairs={{0,4},{2,6},{4,0},{6,2},{8,12},{10,14},{12,8},{14,10},{16,20},{18,... | collective-permute-start | bytes 1658888 | tf_op jit(solution)/shard_map/ppermute | solution.py:17
  7.5 3.8 %collective-permute-start.6 = (f32[360,360]{1,0:T(8,128)}, f32[360,360]{1,0:T(8,128)}, u32[]{:S(2)}, u32[]{:S(2)}) collective-permute-start(f32[360,360]{1,0:T(8,128)} %param.3), channel_id=1, source_target_pairs={{0,32},{32,64},{64,96},{96,128},{128,160},{160,192},{192,224},{224... | collective-permute-start | bytes 1555208 | tf_op jit(solution)/shard_map/ppermute | solution.py:63
  11.4 9.5 %collective-permute-start.7 = (f32[360,360]{1,0:T(8,128)}, f32[360,360]{1,0:T(8,128)}, u32[]{:S(2)}, u32[]{:S(2)}) collective-permute-start(f32[360,360]{1,0:T(8,128)} %param.3), channel_id=1, source_target_pairs={{0,480},{32,0},{64,32},{96,64},{128,96},{160,128},{192,160},{224,1... | collective-permute-start | bytes 1555208 | tf_op jit(solution)/shard_map/ppermute | solution.py:65
  22.1 3.5 %collective-permute-start.3 = (f32[4,192,360]{2,1,0:T(8,128)S(1)}, f32[4,192,360]{2,1,0:T(8,128)S(1)}, u32[]{:S(2)}, u32[]{:S(2)}) collective-permute-start(f32[4,192,360]{2,1,0:T(8,128)S(1)} %maximum_select_fusion), channel_id=1, source_target_pairs={{0,8},{2,10},{4,12},{6,14},{8,16},{10,18},{12,20},{14,22},{16,24},... | collective-permute-start | bytes 3317768 | tf_op jit(solution)/shard_map/ppermute | solution.py:21
  25.6 3.6 %collective-permute-start.2 = (f32[4,192,360]{2,1,0:T(8,128)S(1)}, f32[4,192,360]{2,1,0:T(8,128)S(1)}, u32[]{:S(2)}, u32[]{:S(2)}) collective-permute-start(f32[4,192,360]{2,1,0:T(8,128)S(1)} %maximum_select_fusion), channel_id=1, source_target_pairs={{0,24},{2,26},{4,28},{6,30},{8,0},{10,2},{12,4},{14,6},{16,8},{18,... | collective-permute-start | bytes 3317768 | tf_op jit(solution)/shard_map/ppermute | solution.py:22
  29.2 2.6 %collective-permute-done.6 = f32[360,360]{1,0:T(8,128)} collective-permute-done((f32[360,360]{1,0:T(8,128)}, f32[360,360]{1,0:T(8,128)}, u32[]{:S(2)}, u32[]{:S(2)}) %collective-permute-start.6) | collective-permute-done | bytes 518432 | tf_op jit(solution)/shard_map/ppermute | solution.py:63
  31.8 1.9 %collective-permute-start.8 = (f32[360,360]{1,0:T(8,128)}, f32[360,360]{1,0:T(8,128)S(1)}, u32[]{:S(2)}, u32[]{:S(2)}) collective-permute-start(f32[360,360]{1,0:T(8,128)} %collective-permute-done.6), channel_id=1, source_target_pairs={{0,32},{32,64},{64,96},{96,128},{128,160},{160,192},{192,224},{224... | collective-permute-start | bytes 1555208 | tf_op jit(solution)/shard_map/ppermute | solution.py:63
  33.7 8.8 %collective-permute-start.9 = (f32[360,360]{1,0:T(8,128)}, f32[360,360]{1,0:T(8,128)S(1)}, u32[]{:S(2)}, u32[]{:S(2)}) collective-permute-start(f32[360,360]{1,0:T(8,128)} %collective-permute-done.7), channel_id=1, source_target_pairs={{0,480},{32,0},{64,32},{96,64},{128,96},{160,128},{192,160},{224,1... | collective-permute-start | bytes 1555208 | tf_op jit(solution)/shard_map/ppermute | solution.py:65
  42.6 9.9 %collective-permute-done.8 = f32[360,360]{1,0:T(8,128)S(1)} collective-permute-done((f32[360,360]{1,0:T(8,128)}, f32[360,360]{1,0:T(8,128)S(1)}, u32[]{:S(2)}, u32[]{:S(2)}) %collective-permute-start.8) | collective-permute-done | bytes 518432 | tf_op jit(solution)/shard_map/ppermute | solution.py:63
  52.4 1.9 %collective-permute-start.10 = (f32[360,360]{1,0:T(8,128)S(1)}, f32[360,360]{1,0:T(8,128)}, u32[]{:S(2)}, u32[]{:S(2)}) collective-permute-start(f32[360,360]{1,0:T(8,128)S(1)} %collective-permute-done.8), channel_id=1, source_target_pairs={{0,32},{32,64},{64,96},{96,128},{128,160},{160,192},{192,224},{224... | collective-permute-start | bytes 1555208 | tf_op jit(solution)/shard_map/ppermute | solution.py:63
  54.4 5.1 %collective-permute-start.14 = (f32[360,360]{1,0:T(8,128)S(1)}, f32[360,360]{1,0:T(8,128)}, u32[]{:S(2)}, u32[]{:S(2)}) collective-permute-start(f32[360,360]{1,0:T(8,128)S(1)} %collective-permute-done.9), channel_id=1, source_target_pairs={{0,480},{32,0},{64,32},{96,64},{128,96},{160,128},{192,160},{224,1... | collective-permute-start | bytes 1555208 | tf_op jit(solution)/shard_map/ppermute | solution.py:65
  60.4 2.2 %collective-permute-start.4 = (f32[4,96,360]{2,1,0:T(8,128)}, f32[4,96,360]{2,1,0:T(8,128)}, u32[]{:S(2)}, u32[]{:S(2)}) collective-permute-start(f32[4,96,360]{2,1,0:T(8,128)} %slice.32), channel_id=1, source_target_pairs={{0,8},{2,10},{4,12},{6,14},{8,16},{10,18},{12,20},{14,22},{16,24},... | collective-permute-start | bytes 1658888 | tf_op jit(solution)/shard_map/ppermute | solution.py:24
  63.5 4.8 %collective-permute-start.5 = (f32[4,96,360]{2,1,0:T(8,128)}, f32[4,96,360]{2,1,0:T(8,128)}, u32[]{:S(2)}, u32[]{:S(2)}) collective-permute-start(f32[4,96,360]{2,1,0:T(8,128)} %slice.33), channel_id=1, source_target_pairs={{0,24},{2,26},{4,28},{6,30},{8,0},{10,2},{12,4},{14,6},{16,8},{18,... | collective-permute-start | bytes 1658888 | tf_op jit(solution)/shard_map/ppermute | solution.py:25
  68.4 1.9 %collective-permute-start.11 = (f32[360,360]{1,0:T(8,128)}, f32[360,360]{1,0:T(8,128)}, u32[]{:S(2)}, u32[]{:S(2)}) collective-permute-start(f32[360,360]{1,0:T(8,128)} %collective-permute-done.10), channel_id=1, source_target_pairs={{0,32},{32,64},{64,96},{96,128},{128,160},{160,192},{192,224},{224... | collective-permute-start | bytes 1555208 | tf_op jit(solution)/shard_map/ppermute | solution.py:63
  70.3 5.1 %collective-permute-start.15 = (f32[360,360]{1,0:T(8,128)}, f32[360,360]{1,0:T(8,128)}, u32[]{:S(2)}, u32[]{:S(2)}) collective-permute-start(f32[360,360]{1,0:T(8,128)} %collective-permute-done.14), channel_id=1, source_target_pairs={{0,480},{32,0},{64,32},{96,64},{128,96},{160,128},{192,160},{224,1... | collective-permute-start | bytes 1555208 | tf_op jit(solution)/shard_map/ppermute | solution.py:65
  76.4 7.4 %collective-permute-done.11 = f32[360,360]{1,0:T(8,128)} collective-permute-done((f32[360,360]{1,0:T(8,128)}, f32[360,360]{1,0:T(8,128)}, u32[]{:S(2)}, u32[]{:S(2)}) %collective-permute-start.11) | collective-permute-done | bytes 518432 | tf_op jit(solution)/shard_map/ppermute | solution.py:63
  83.8 1.9 %collective-permute-start.12 = (f32[360,360]{1,0:T(8,128)}, f32[360,360]{1,0:T(8,128)S(1)}, u32[]{:S(2)}, u32[]{:S(2)}) collective-permute-start(f32[360,360]{1,0:T(8,128)} %collective-permute-done.11), channel_id=1, source_target_pairs={{0,32},{32,64},{64,96},{96,128},{128,160},{160,192},{192,224},{224... | collective-permute-start | bytes 1555208 | tf_op jit(solution)/shard_map/ppermute | solution.py:63
  85.7 5.1 %collective-permute-start.16 = (f32[360,360]{1,0:T(8,128)}, f32[360,360]{1,0:T(8,128)S(1)}, u32[]{:S(2)}, u32[]{:S(2)}) collective-permute-start(f32[360,360]{1,0:T(8,128)} %collective-permute-done.15), channel_id=1, source_target_pairs={{0,480},{32,0},{64,32},{96,64},{128,96},{160,128},{192,160},{224,1... | collective-permute-start | bytes 1555208 | tf_op jit(solution)/shard_map/ppermute | solution.py:65
  90.9 2.1 %pad_maximum_fusion = f32[16,192,360]{2,1,0:T(8,128)S(1)} fusion(f32[4,192,360]{2,1,0:T(8,128)S(1)} %collective-permute-done.3, f32[4,96,360]{2,1,0:T(8,128)} %collective-permute-done.5, f32[4,96,360]{2,1,0:T(8,128)} %collective-permute-done.4, f32[4,192,360]{2,1,0:T(8,128)S(1)} %collective-permute-done.2, f32[4,192,360]{2,1,0:T(8,128)S(1)} %maximum_select_fusion), kind=kLoop, calls=%fused_computation | loop fusion | flops 4423680 | bytes 8847360 | tf_op jit(solution)/shard_map/concatenate | solution.py:27
  93.0 1.9 %fusion.18 = f32[192,360]{1,0:T(8,128)S(1)} fusion(f32[360,360]{1,0:T(8,128)} %collective-permute-done.14, f32[16,192,360]{2,1,0:T(8,128)S(1)} %pad_maximum_fusion, s32[]{:T(128)S(6)} %select_n.396), kind=kOutput, calls=%fused_computation.28 | convolution fusion | flops 298598400 | bytes 1089796 | tf_op jit(solution)/shard_map/dot_general | solution.py:50
  102.7 1.9 %collective-permute-start.13 = (f32[360,360]{1,0:T(8,128)S(1)}, f32[360,360]{1,0:T(8,128)S(1)}, u32[]{:S(2)}, u32[]{:S(2)}) collective-permute-start(f32[360,360]{1,0:T(8,128)S(1)} %collective-permute-done.12), channel_id=1, source_target_pairs={{0,32},{32,64},{64,96},{96,128},{128,160},{160,192},{192,224},{224... | collective-permute-start | bytes 1555208 | tf_op jit(solution)/shard_map/ppermute | solution.py:63
  104.6 5.1 %collective-permute-start.17 = (f32[360,360]{1,0:T(8,128)S(1)}, f32[360,360]{1,0:T(8,128)S(1)}, u32[]{:S(2)}, u32[]{:S(2)}) collective-permute-start(f32[360,360]{1,0:T(8,128)S(1)} %collective-permute-done.16), channel_id=1, source_target_pairs={{0,480},{32,0},{64,32},{96,64},{128,96},{160,128},{192,160},{224,1... | collective-permute-start | bytes 1555208 | tf_op jit(solution)/shard_map/ppermute | solution.py:65
  112.4 4.0 %collective-permute-done.13 = f32[360,360]{1,0:T(8,128)S(1)} collective-permute-done((f32[360,360]{1,0:T(8,128)S(1)}, f32[360,360]{1,0:T(8,128)S(1)}, u32[]{:S(2)}, u32[]{:S(2)}) %collective-permute-start.13) | collective-permute-done | bytes 518432 | tf_op jit(solution)/shard_map/ppermute | solution.py:63
  117.6 1.9 %collective-permute-start.18 = (f32[360,360]{1,0:T(8,128)S(1)}, f32[360,360]{1,0:T(8,128)S(1)}, u32[]{:S(2)}, u32[]{:S(2)}) collective-permute-start(f32[360,360]{1,0:T(8,128)S(1)} %collective-permute-done.13), channel_id=1, source_target_pairs={{0,32},{32,64},{64,96},{96,128},{128,160},{160,192},{192,224},{224... | collective-permute-start | bytes 1555208 | tf_op jit(solution)/shard_map/ppermute | solution.py:63
  119.5 5.8 %collective-permute-start.19 = (f32[360,360]{1,0:T(8,128)S(1)}, f32[360,360]{1,0:T(8,128)S(1)}, u32[]{:S(2)}, u32[]{:S(2)}) collective-permute-start(f32[360,360]{1,0:T(8,128)S(1)} %collective-permute-done.17), channel_id=1, source_target_pairs={{0,480},{32,0},{64,32},{96,64},{128,96},{160,128},{192,160},{224,1... | collective-permute-start | bytes 1555208 | tf_op jit(solution)/shard_map/ppermute | solution.py:65
  125.3 1.8 %fusion.2 = f32[192,360]{1,0:T(8,128)S(1)} fusion(f32[192,360]{1,0:T(8,128)S(1)} %fusion.15, f32[360,360]{1,0:T(8,128)} %collective-permute-done.11, f32[16,192,360]{2,1,0:T(8,128)S(1)} %pad_maximum_fusion, s32[]{:T(128)S(6)} %select_n.401, f32[192,360]{1,0:T(8,128)S(1)} %convolution_add_fusion.4, f32[192,360]{1,0:T(8,128)S(1)} %fusion.18), kind=kOutput, calls=%fused_computation.11 | convolution fusion | flops 298805760 | bytes 1974532 | tf_op jit(solution)/shard_map/dot_general | solution.py:50
  128.6 2.1 %collective-permute-done.18 = f32[360,360]{1,0:T(8,128)S(1)} collective-permute-done((f32[360,360]{1,0:T(8,128)S(1)}, f32[360,360]{1,0:T(8,128)S(1)}, u32[]{:S(2)}, u32[]{:S(2)}) %collective-permute-start.18) | collective-permute-done | bytes 518432 | tf_op jit(solution)/shard_map/ppermute | solution.py:63
  132.1 1.9 %collective-permute-start.20 = (f32[180,360]{1,0:T(8,128)S(1)}, f32[180,360]{1,0:T(8,128)S(1)}, u32[]{:S(2)}, u32[]{:S(2)}) collective-permute-start(f32[180,360]{1,0:T(8,128)S(1)} %slice.26), channel_id=1, source_target_pairs={{0,32},{32,64},{64,96},{96,128},{128,160},{160,192},{192,224},{224... | collective-permute-start | bytes 777608 | tf_op jit(solution)/shard_map/ppermute | solution.py:69
  134.0 5.6 %collective-permute-start.21 = (f32[180,360]{1,0:T(8,128)S(1)}, f32[180,360]{1,0:T(8,128)S(1)}, u32[]{:S(2)}, u32[]{:S(2)}) collective-permute-start(f32[180,360]{1,0:T(8,128)S(1)} %slice.27), channel_id=1, source_target_pairs={{0,480},{32,0},{64,32},{96,64},{128,96},{160,128},{192,160},{224,1... | collective-permute-start | bytes 777608 | tf_op jit(solution)/shard_map/ppermute | solution.py:70
  144.5 3.3 %collective-permute-start.22 = (f32[96,360]{1,0:T(8,128)S(1)}, f32[96,360]{1,0:T(8,128)S(1)}, u32[]{:S(2)}, u32[]{:S(2)}) collective-permute-start(f32[96,360]{1,0:T(8,128)S(1)} %add_add_fusion), channel_id=1, source_target_pairs={{0,1},{1,0},{2,3},{3,2},{4,5},{5,4},{6,7},{7,6},{8,9},{9,8},{10,11... | collective-permute-start | bytes 414728 | tf_op jit(solution)/shard_map/ppermute | solution.py:85
  148.5 4.5 %collective-permute-done.22 = f32[96,360]{1,0:T(8,128)S(1)} collective-permute-done((f32[96,360]{1,0:T(8,128)S(1)}, f32[96,360]{1,0:T(8,128)S(1)}, u32[]{:S(2)}, u32[]{:S(2)}) %collective-permute-start.22) | collective-permute-done | bytes 138272 | tf_op jit(solution)/shard_map/ppermute | solution.py:85
  (52 shorter events, 26.4 us)
Async XLA Ops:
  0.0 3.7 %collective-permute-start = (f32[192,360]{1,0:T(8,128)}, f32[192,360]{1,0:T(8,128)S(1)}, u32[]{:S(2)}, u32[]{:S(2)}) collective-permute-start(f32[192,360]{1,0:T(8,128)} %param.2), channel_id=1, source_target_pairs={{0,2},{2,0},{4,6},{6,4},{8,10},{10,8},{12,14},{14,12},{16,18},{18,... | collective-permute-start | bytes 829448 | tf_op jit(solution)/shard_map/ppermute | solution.py:15
  4.8 17.3 %collective-permute-start.1 = (f32[2,192,360]{2,1,0:T(8,128)S(1)}, f32[2,192,360]{2,1,0:T(8,128)S(1)}, u32[]{:S(2)}, u32[]{:S(2)}) collective-permute-start(f32[2,192,360]{2,1,0:T(8,128)S(1)} %maximum_select_fusion.1), channel_id=1, source_target_pairs={{0,4},{2,6},{4,0},{6,2},{8,12},{10,14},{12,8},{14,10},{16,20},{18,... | collective-permute-start | bytes 1658888 | tf_op jit(solution)/shard_map/ppermute | solution.py:17
  7.5 24.3 %collective-permute-start.6 = (f32[360,360]{1,0:T(8,128)}, f32[360,360]{1,0:T(8,128)}, u32[]{:S(2)}, u32[]{:S(2)}) collective-permute-start(f32[360,360]{1,0:T(8,128)} %param.3), channel_id=1, source_target_pairs={{0,32},{32,64},{64,96},{96,128},{128,160},{160,192},{192,224},{224... | collective-permute-start | bytes 1555208 | tf_op jit(solution)/shard_map/ppermute | solution.py:63
  11.4 22.4 %collective-permute-start.7 = (f32[360,360]{1,0:T(8,128)}, f32[360,360]{1,0:T(8,128)}, u32[]{:S(2)}, u32[]{:S(2)}) collective-permute-start(f32[360,360]{1,0:T(8,128)} %param.3), channel_id=1, source_target_pairs={{0,480},{32,0},{64,32},{96,64},{128,96},{160,128},{192,160},{224,1... | collective-permute-start | bytes 1555208 | tf_op jit(solution)/shard_map/ppermute | solution.py:65
  22.1 37.4 %collective-permute-start.3 = (f32[4,192,360]{2,1,0:T(8,128)S(1)}, f32[4,192,360]{2,1,0:T(8,128)S(1)}, u32[]{:S(2)}, u32[]{:S(2)}) collective-permute-start(f32[4,192,360]{2,1,0:T(8,128)S(1)} %maximum_select_fusion), channel_id=1, source_target_pairs={{0,8},{2,10},{4,12},{6,14},{8,16},{10,18},{12,20},{14,22},{16,24},... | collective-permute-start | bytes 3317768 | tf_op jit(solution)/shard_map/ppermute | solution.py:21
  25.6 37.0 %collective-permute-start.2 = (f32[4,192,360]{2,1,0:T(8,128)S(1)}, f32[4,192,360]{2,1,0:T(8,128)S(1)}, u32[]{:S(2)}, u32[]{:S(2)}) collective-permute-start(f32[4,192,360]{2,1,0:T(8,128)S(1)} %maximum_select_fusion), channel_id=1, source_target_pairs={{0,24},{2,26},{4,28},{6,30},{8,0},{10,2},{12,4},{14,6},{16,8},{18,... | collective-permute-start | bytes 3317768 | tf_op jit(solution)/shard_map/ppermute | solution.py:22
  31.8 20.6 %collective-permute-start.8 = (f32[360,360]{1,0:T(8,128)}, f32[360,360]{1,0:T(8,128)S(1)}, u32[]{:S(2)}, u32[]{:S(2)}) collective-permute-start(f32[360,360]{1,0:T(8,128)} %collective-permute-done.6), channel_id=1, source_target_pairs={{0,32},{32,64},{64,96},{96,128},{128,160},{160,192},{192,224},{224... | collective-permute-start | bytes 1555208 | tf_op jit(solution)/shard_map/ppermute | solution.py:63
  33.7 20.6 %collective-permute-start.9 = (f32[360,360]{1,0:T(8,128)}, f32[360,360]{1,0:T(8,128)S(1)}, u32[]{:S(2)}, u32[]{:S(2)}) collective-permute-start(f32[360,360]{1,0:T(8,128)} %collective-permute-done.7), channel_id=1, source_target_pairs={{0,480},{32,0},{64,32},{96,64},{128,96},{160,128},{192,160},{224,1... | collective-permute-start | bytes 1555208 | tf_op jit(solution)/shard_map/ppermute | solution.py:65
  52.4 10.2 %copy-start.1 = (f32[360,360]{1,0:T(8,128)}, f32[360,360]{1,0:T(8,128)S(1)}, u32[]{:S(2)}) copy-start(f32[360,360]{1,0:T(8,128)S(1)} %collective-permute-done.8) | copy-start | bytes 1555204
  52.4 15.9 %collective-permute-start.10 = (f32[360,360]{1,0:T(8,128)S(1)}, f32[360,360]{1,0:T(8,128)}, u32[]{:S(2)}, u32[]{:S(2)}) collective-permute-start(f32[360,360]{1,0:T(8,128)S(1)} %collective-permute-done.8), channel_id=1, source_target_pairs={{0,32},{32,64},{64,96},{96,128},{128,160},{160,192},{192,224},{224... | collective-permute-start | bytes 1555208 | tf_op jit(solution)/shard_map/ppermute | solution.py:63
  54.4 14.0 %copy-start.3 = (f32[360,360]{1,0:T(8,128)}, f32[360,360]{1,0:T(8,128)S(1)}, u32[]{:S(2)}) copy-start(f32[360,360]{1,0:T(8,128)S(1)} %collective-permute-done.9) | copy-start | bytes 1555204
  54.4 15.9 %collective-permute-start.14 = (f32[360,360]{1,0:T(8,128)S(1)}, f32[360,360]{1,0:T(8,128)}, u32[]{:S(2)}, u32[]{:S(2)}) collective-permute-start(f32[360,360]{1,0:T(8,128)S(1)} %collective-permute-done.9), channel_id=1, source_target_pairs={{0,480},{32,0},{64,32},{96,64},{128,96},{160,128},{192,160},{224,1... | collective-permute-start | bytes 1555208 | tf_op jit(solution)/shard_map/ppermute | solution.py:65
  60.4 30.5 %collective-permute-start.4 = (f32[4,96,360]{2,1,0:T(8,128)}, f32[4,96,360]{2,1,0:T(8,128)}, u32[]{:S(2)}, u32[]{:S(2)}) collective-permute-start(f32[4,96,360]{2,1,0:T(8,128)} %slice.32), channel_id=1, source_target_pairs={{0,8},{2,10},{4,12},{6,14},{8,16},{10,18},{12,20},{14,22},{16,24},... | collective-permute-start | bytes 1658888 | tf_op jit(solution)/shard_map/ppermute | solution.py:24
  63.5 27.4 %collective-permute-start.5 = (f32[4,96,360]{2,1,0:T(8,128)}, f32[4,96,360]{2,1,0:T(8,128)}, u32[]{:S(2)}, u32[]{:S(2)}) collective-permute-start(f32[4,96,360]{2,1,0:T(8,128)} %slice.33), channel_id=1, source_target_pairs={{0,24},{2,26},{4,28},{6,30},{8,0},{10,2},{12,4},{14,6},{16,8},{18,... | collective-permute-start | bytes 1658888 | tf_op jit(solution)/shard_map/ppermute | solution.py:25
  68.4 15.4 %collective-permute-start.11 = (f32[360,360]{1,0:T(8,128)}, f32[360,360]{1,0:T(8,128)}, u32[]{:S(2)}, u32[]{:S(2)}) collective-permute-start(f32[360,360]{1,0:T(8,128)} %collective-permute-done.10), channel_id=1, source_target_pairs={{0,32},{32,64},{64,96},{96,128},{128,160},{160,192},{192,224},{224... | collective-permute-start | bytes 1555208 | tf_op jit(solution)/shard_map/ppermute | solution.py:63
  70.3 15.4 %collective-permute-start.15 = (f32[360,360]{1,0:T(8,128)}, f32[360,360]{1,0:T(8,128)}, u32[]{:S(2)}, u32[]{:S(2)}) collective-permute-start(f32[360,360]{1,0:T(8,128)} %collective-permute-done.14), channel_id=1, source_target_pairs={{0,480},{32,0},{64,32},{96,64},{128,96},{160,128},{192,160},{224,1... | collective-permute-start | bytes 1555208 | tf_op jit(solution)/shard_map/ppermute | solution.py:65
  76.4 22.1 %copy-start.4 = (f32[360,360]{1,0:T(8,128)S(1)}, f32[360,360]{1,0:T(8,128)}, u32[]{:S(2)}) copy-start(f32[360,360]{1,0:T(8,128)} %copy-done.3) | copy-start | bytes 1555204
  83.8 18.9 %collective-permute-start.12 = (f32[360,360]{1,0:T(8,128)}, f32[360,360]{1,0:T(8,128)S(1)}, u32[]{:S(2)}, u32[]{:S(2)}) collective-permute-start(f32[360,360]{1,0:T(8,128)} %collective-permute-done.11), channel_id=1, source_target_pairs={{0,32},{32,64},{64,96},{96,128},{128,160},{160,192},{192,224},{224... | collective-permute-start | bytes 1555208 | tf_op jit(solution)/shard_map/ppermute | solution.py:63
  85.7 18.9 %collective-permute-start.16 = (f32[360,360]{1,0:T(8,128)}, f32[360,360]{1,0:T(8,128)S(1)}, u32[]{:S(2)}, u32[]{:S(2)}) collective-permute-start(f32[360,360]{1,0:T(8,128)} %collective-permute-done.15), channel_id=1, source_target_pairs={{0,480},{32,0},{64,32},{96,64},{128,96},{160,128},{192,160},{224,1... | collective-permute-start | bytes 1555208 | tf_op jit(solution)/shard_map/ppermute | solution.py:65
  93.0 8.1 %copy-start = (f32[360,360]{1,0:T(8,128)S(1)}, f32[360,360]{1,0:T(8,128)}, u32[]{:S(2)}) copy-start(f32[360,360]{1,0:T(8,128)} %param.3) | copy-start | bytes 1555204
  93.0 8.9 %copy-start.2 = (f32[360,360]{1,0:T(8,128)S(1)}, f32[360,360]{1,0:T(8,128)}, u32[]{:S(2)}) copy-start(f32[360,360]{1,0:T(8,128)} %copy-done.1) | copy-start | bytes 1555204
  102.7 13.7 %collective-permute-start.13 = (f32[360,360]{1,0:T(8,128)S(1)}, f32[360,360]{1,0:T(8,128)S(1)}, u32[]{:S(2)}, u32[]{:S(2)}) collective-permute-start(f32[360,360]{1,0:T(8,128)S(1)} %collective-permute-done.12), channel_id=1, source_target_pairs={{0,32},{32,64},{64,96},{96,128},{128,160},{160,192},{192,224},{224... | collective-permute-start | bytes 1555208 | tf_op jit(solution)/shard_map/ppermute | solution.py:63
  104.6 12.9 %collective-permute-start.17 = (f32[360,360]{1,0:T(8,128)S(1)}, f32[360,360]{1,0:T(8,128)S(1)}, u32[]{:S(2)}, u32[]{:S(2)}) collective-permute-start(f32[360,360]{1,0:T(8,128)S(1)} %collective-permute-done.16), channel_id=1, source_target_pairs={{0,480},{32,0},{64,32},{96,64},{128,96},{160,128},{192,160},{224,1... | collective-permute-start | bytes 1555208 | tf_op jit(solution)/shard_map/ppermute | solution.py:65
  117.6 13.2 %collective-permute-start.18 = (f32[360,360]{1,0:T(8,128)S(1)}, f32[360,360]{1,0:T(8,128)S(1)}, u32[]{:S(2)}, u32[]{:S(2)}) collective-permute-start(f32[360,360]{1,0:T(8,128)S(1)} %collective-permute-done.13), channel_id=1, source_target_pairs={{0,32},{32,64},{64,96},{96,128},{128,160},{160,192},{192,224},{224... | collective-permute-start | bytes 1555208 | tf_op jit(solution)/shard_map/ppermute | solution.py:63
  119.5 12.6 %collective-permute-start.19 = (f32[360,360]{1,0:T(8,128)S(1)}, f32[360,360]{1,0:T(8,128)S(1)}, u32[]{:S(2)}, u32[]{:S(2)}) collective-permute-start(f32[360,360]{1,0:T(8,128)S(1)} %collective-permute-done.17), channel_id=1, source_target_pairs={{0,480},{32,0},{64,32},{96,64},{128,96},{160,128},{192,160},{224,1... | collective-permute-start | bytes 1555208 | tf_op jit(solution)/shard_map/ppermute | solution.py:65
  132.1 10.2 %collective-permute-start.20 = (f32[180,360]{1,0:T(8,128)S(1)}, f32[180,360]{1,0:T(8,128)S(1)}, u32[]{:S(2)}, u32[]{:S(2)}) collective-permute-start(f32[180,360]{1,0:T(8,128)S(1)} %slice.26), channel_id=1, source_target_pairs={{0,32},{32,64},{64,96},{96,128},{128,160},{160,192},{192,224},{224... | collective-permute-start | bytes 777608 | tf_op jit(solution)/shard_map/ppermute | solution.py:69
  134.0 9.7 %collective-permute-start.21 = (f32[180,360]{1,0:T(8,128)S(1)}, f32[180,360]{1,0:T(8,128)S(1)}, u32[]{:S(2)}, u32[]{:S(2)}) collective-permute-start(f32[180,360]{1,0:T(8,128)S(1)} %slice.27), channel_id=1, source_target_pairs={{0,480},{32,0},{64,32},{96,64},{128,96},{160,128},{192,160},{224,1... | collective-permute-start | bytes 777608 | tf_op jit(solution)/shard_map/ppermute | solution.py:70
  144.5 8.5 %collective-permute-start.22 = (f32[96,360]{1,0:T(8,128)S(1)}, f32[96,360]{1,0:T(8,128)S(1)}, u32[]{:S(2)}, u32[]{:S(2)}) collective-permute-start(f32[96,360]{1,0:T(8,128)S(1)} %add_add_fusion), channel_id=1, source_target_pairs={{0,1},{1,0},{2,3},{3,2},{4,5},{5,4},{6,7},{7,6},{8,9},{9,8},{10,11... | collective-permute-start | bytes 414728 | tf_op jit(solution)/shard_map/ppermute | solution.py:85

commit v17 on v16

--- a/solution.py
+++ b/solution.py
@@ -4,7 +4,7 @@
 from jax.sharding import PartitionSpec as P
 
 FIRST_DOT_STEP = 6
-DOTS_PER_STEP = 6
+DOTS_PER_STEP = 5
 
 
 def gather_col(block):

time: 155 us -> 155 us (level)
  transfers between devices with their start and end apart: 23 -> 23, of which waited for: 12 -> 11; matrix products, arithmetic and copies ran while one was open for 15% -> 15% of each run, Pallas kernels for 0% -> 0%
where the time goes in v17:
time: 155 us; the launch traced here: 154 us
  starting transfers between devices  89.5 us (58%)
  waiting for transfers between devices  38 us (25%)
  matrix products  19.2 us (12%)
  other arithmetic  3.97 us (3%)
  local copies, waits for them, and re-layouts  1.82 us (1%)
    ppermute x7, starting transfers between devices, local(): behind = lax.ppermute(behind, 'row', bwd)  44.6 us
    ppermute x7, waiting for transfers between devices, local(): ahead = lax.ppermute(ahead, 'row', fwd)  27.1 us
    dot_general x19, matrix products, product(): jnp.dot(cols[:, lo:hi], block, precision=lax.Precision.HIGHEST, preferred...  19.2 us
    ppermute x7, starting transfers between devices, local(): ahead = lax.ppermute(ahead, 'row', fwd)  15.3 us
    ppermute x1, starting transfers between devices, local(): bottom = lax.ppermute(behind[m:], 'row', bwd)  5.6 us
    ppermute x1, starting transfers between devices, gather_col(): opp_b = lax.ppermute(above[:, h:], 'col', down)  4.84 us
    ppermute x1, waiting for transfers between devices, local(): other = lax.ppermute(other, 'depth', [(0, 1), (1, 0)])  4.5 us
    ppermute x1, starting transfers between devices, gather_col(): above = lax.ppermute(quad, 'col', down)  3.57 us
  transfers between devices with their start and end apart: 23, of which 11 were waited for; matrix products, arithmetic and copies ran while one was open for 15% of the time, Pallas kernels for 0%

profile of v17, /device:TPU:6, one launch (start us, length us, event | category | flops | bytes accessed | tf_op | source)
XLA Modules:
  0.0 154.0 jit_solution(6789909178372279314)
XLA Ops:
  0.0 1.9 %collective-permute-start = (f32[192,360]{1,0:T(8,128)}, f32[192,360]{1,0:T(8,128)S(1)}, u32[]{:S(2)}, u32[]{:S(2)}) collective-permute-start(f32[192,360]{1,0:T(8,128)} %param.2), channel_id=1, source_target_pairs={{0,2},{2,0},{4,6},{6,4},{8,10},{10,8},{12,14},{14,12},{16,18},{18,... | collective-permute-start | bytes 829448 | tf_op jit(solution)/shard_map/ppermute | solution.py:15
  4.8 2.7 %collective-permute-start.1 = (f32[2,192,360]{2,1,0:T(8,128)S(1)}, f32[2,192,360]{2,1,0:T(8,128)S(1)}, u32[]{:S(2)}, u32[]{:S(2)}) collective-permute-start(f32[2,192,360]{2,1,0:T(8,128)S(1)} %maximum_select_fusion.1), channel_id=1, source_target_pairs={{0,4},{2,6},{4,0},{6,2},{8,12},{10,14},{12,8},{14,10},{16,20},{18,... | collective-permute-start | bytes 1658888 | tf_op jit(solution)/shard_map/ppermute | solution.py:17
  7.5 3.8 %collective-permute-start.6 = (f32[360,360]{1,0:T(8,128)}, f32[360,360]{1,0:T(8,128)}, u32[]{:S(2)}, u32[]{:S(2)}) collective-permute-start(f32[360,360]{1,0:T(8,128)} %param.3), channel_id=1, source_target_pairs={{0,32},{32,64},{64,96},{96,128},{128,160},{160,192},{192,224},{224... | collective-permute-start | bytes 1555208 | tf_op jit(solution)/shard_map/ppermute | solution.py:63
  11.4 9.5 %collective-permute-start.7 = (f32[360,360]{1,0:T(8,128)}, f32[360,360]{1,0:T(8,128)}, u32[]{:S(2)}, u32[]{:S(2)}) collective-permute-start(f32[360,360]{1,0:T(8,128)} %param.3), channel_id=1, source_target_pairs={{0,480},{32,0},{64,32},{96,64},{128,96},{160,128},{192,160},{224,1... | collective-permute-start | bytes 1555208 | tf_op jit(solution)/shard_map/ppermute | solution.py:65
  22.1 3.5 %collective-permute-start.3 = (f32[4,192,360]{2,1,0:T(8,128)S(1)}, f32[4,192,360]{2,1,0:T(8,128)S(1)}, u32[]{:S(2)}, u32[]{:S(2)}) collective-permute-start(f32[4,192,360]{2,1,0:T(8,128)S(1)} %maximum_select_fusion), channel_id=1, source_target_pairs={{0,8},{2,10},{4,12},{6,14},{8,16},{10,18},{12,20},{14,22},{16,24},... | collective-permute-start | bytes 3317768 | tf_op jit(solution)/shard_map/ppermute | solution.py:21
  25.6 3.6 %collective-permute-start.2 = (f32[4,192,360]{2,1,0:T(8,128)S(1)}, f32[4,192,360]{2,1,0:T(8,128)S(1)}, u32[]{:S(2)}, u32[]{:S(2)}) collective-permute-start(f32[4,192,360]{2,1,0:T(8,128)S(1)} %maximum_select_fusion), channel_id=1, source_target_pairs={{0,24},{2,26},{4,28},{6,30},{8,0},{10,2},{12,4},{14,6},{16,8},{18,... | collective-permute-start | bytes 3317768 | tf_op jit(solution)/shard_map/ppermute | solution.py:22
  29.2 2.6 %collective-permute-done.6 = f32[360,360]{1,0:T(8,128)} collective-permute-done((f32[360,360]{1,0:T(8,128)}, f32[360,360]{1,0:T(8,128)}, u32[]{:S(2)}, u32[]{:S(2)}) %collective-permute-start.6) | collective-permute-done | bytes 518432 | tf_op jit(solution)/shard_map/ppermute | solution.py:63
  31.8 1.9 %collective-permute-start.8 = (f32[360,360]{1,0:T(8,128)}, f32[360,360]{1,0:T(8,128)S(1)}, u32[]{:S(2)}, u32[]{:S(2)}) collective-permute-start(f32[360,360]{1,0:T(8,128)} %collective-permute-done.6), channel_id=1, source_target_pairs={{0,32},{32,64},{64,96},{96,128},{128,160},{160,192},{192,224},{224... | collective-permute-start | bytes 1555208 | tf_op jit(solution)/shard_map/ppermute | solution.py:63
  33.7 8.8 %collective-permute-start.9 = (f32[360,360]{1,0:T(8,128)}, f32[360,360]{1,0:T(8,128)S(1)}, u32[]{:S(2)}, u32[]{:S(2)}) collective-permute-start(f32[360,360]{1,0:T(8,128)} %collective-permute-done.7), channel_id=1, source_target_pairs={{0,480},{32,0},{64,32},{96,64},{128,96},{160,128},{192,160},{224,1... | collective-permute-start | bytes 1555208 | tf_op jit(solution)/shard_map/ppermute | solution.py:65
  42.6 9.9 %collective-permute-done.8 = f32[360,360]{1,0:T(8,128)S(1)} collective-permute-done((f32[360,360]{1,0:T(8,128)}, f32[360,360]{1,0:T(8,128)S(1)}, u32[]{:S(2)}, u32[]{:S(2)}) %collective-permute-start.8) | collective-permute-done | bytes 518432 | tf_op jit(solution)/shard_map/ppermute | solution.py:63
  52.4 1.9 %collective-permute-start.10 = (f32[360,360]{1,0:T(8,128)S(1)}, f32[360,360]{1,0:T(8,128)}, u32[]{:S(2)}, u32[]{:S(2)}) collective-permute-start(f32[360,360]{1,0:T(8,128)S(1)} %collective-permute-done.8), channel_id=1, source_target_pairs={{0,32},{32,64},{64,96},{96,128},{128,160},{160,192},{192,224},{224... | collective-permute-start | bytes 1555208 | tf_op jit(solution)/shard_map/ppermute | solution.py:63
  54.4 5.1 %collective-permute-start.14 = (f32[360,360]{1,0:T(8,128)S(1)}, f32[360,360]{1,0:T(8,128)}, u32[]{:S(2)}, u32[]{:S(2)}) collective-permute-start(f32[360,360]{1,0:T(8,128)S(1)} %collective-permute-done.9), channel_id=1, source_target_pairs={{0,480},{32,0},{64,32},{96,64},{128,96},{160,128},{192,160},{224,1... | collective-permute-start | bytes 1555208 | tf_op jit(solution)/shard_map/ppermute | solution.py:65
  60.4 2.2 %collective-permute-start.4 = (f32[4,96,360]{2,1,0:T(8,128)}, f32[4,96,360]{2,1,0:T(8,128)}, u32[]{:S(2)}, u32[]{:S(2)}) collective-permute-start(f32[4,96,360]{2,1,0:T(8,128)} %slice.32), channel_id=1, source_target_pairs={{0,8},{2,10},{4,12},{6,14},{8,16},{10,18},{12,20},{14,22},{16,24},... | collective-permute-start | bytes 1658888 | tf_op jit(solution)/shard_map/ppermute | solution.py:24
  63.5 4.8 %collective-permute-start.5 = (f32[4,96,360]{2,1,0:T(8,128)}, f32[4,96,360]{2,1,0:T(8,128)}, u32[]{:S(2)}, u32[]{:S(2)}) collective-permute-start(f32[4,96,360]{2,1,0:T(8,128)} %slice.33), channel_id=1, source_target_pairs={{0,24},{2,26},{4,28},{6,30},{8,0},{10,2},{12,4},{14,6},{16,8},{18,... | collective-permute-start | bytes 1658888 | tf_op jit(solution)/shard_map/ppermute | solution.py:25
  68.4 1.9 %collective-permute-start.11 = (f32[360,360]{1,0:T(8,128)}, f32[360,360]{1,0:T(8,128)}, u32[]{:S(2)}, u32[]{:S(2)}) collective-permute-start(f32[360,360]{1,0:T(8,128)} %collective-permute-done.10), channel_id=1, source_target_pairs={{0,32},{32,64},{64,96},{96,128},{128,160},{160,192},{192,224},{224... | collective-permute-start | bytes 1555208 | tf_op jit(solution)/shard_map/ppermute | solution.py:63
  70.3 5.1 %collective-permute-start.15 = (f32[360,360]{1,0:T(8,128)}, f32[360,360]{1,0:T(8,128)}, u32[]{:S(2)}, u32[]{:S(2)}) collective-permute-start(f32[360,360]{1,0:T(8,128)} %collective-permute-done.14), channel_id=1, source_target_pairs={{0,480},{32,0},{64,32},{96,64},{128,96},{160,128},{192,160},{224,1... | collective-permute-start | bytes 1555208 | tf_op jit(solution)/shard_map/ppermute | solution.py:65
  76.4 7.4 %collective-permute-done.11 = f32[360,360]{1,0:T(8,128)} collective-permute-done((f32[360,360]{1,0:T(8,128)}, f32[360,360]{1,0:T(8,128)}, u32[]{:S(2)}, u32[]{:S(2)}) %collective-permute-start.11) | collective-permute-done | bytes 518432 | tf_op jit(solution)/shard_map/ppermute | solution.py:63
  83.8 1.9 %collective-permute-start.12 = (f32[360,360]{1,0:T(8,128)}, f32[360,360]{1,0:T(8,128)S(1)}, u32[]{:S(2)}, u32[]{:S(2)}) collective-permute-start(f32[360,360]{1,0:T(8,128)} %collective-permute-done.11), channel_id=1, source_target_pairs={{0,32},{32,64},{64,96},{96,128},{128,160},{160,192},{192,224},{224... | collective-permute-start | bytes 1555208 | tf_op jit(solution)/shard_map/ppermute | solution.py:63
  85.7 5.1 %collective-permute-start.16 = (f32[360,360]{1,0:T(8,128)}, f32[360,360]{1,0:T(8,128)S(1)}, u32[]{:S(2)}, u32[]{:S(2)}) collective-permute-start(f32[360,360]{1,0:T(8,128)} %collective-permute-done.15), channel_id=1, source_target_pairs={{0,480},{32,0},{64,32},{96,64},{128,96},{160,128},{192,160},{224,1... | collective-permute-start | bytes 1555208 | tf_op jit(solution)/shard_map/ppermute | solution.py:65
  90.9 2.1 %pad_maximum_fusion = f32[16,192,360]{2,1,0:T(8,128)S(1)} fusion(f32[4,192,360]{2,1,0:T(8,128)S(1)} %collective-permute-done.3, f32[4,96,360]{2,1,0:T(8,128)} %collective-permute-done.5, f32[4,96,360]{2,1,0:T(8,128)} %collective-permute-done.4, f32[4,192,360]{2,1,0:T(8,128)S(1)} %collective-permute-done.2, f32[4,192,360]{2,1,0:T(8,128)S(1)} %maximum_select_fusion), kind=kLoop, calls=%fused_computation | loop fusion | flops 4423680 | bytes 8847360 | tf_op jit(solution)/shard_map/concatenate | solution.py:27
  93.0 1.9 %fusion.20 = f32[192,360]{1,0:T(8,128)S(1)} fusion(f32[360,360]{1,0:T(8,128)} %collective-permute-done.10, f32[16,192,360]{2,1,0:T(8,128)S(1)} %pad_maximum_fusion, s32[]{:T(128)S(6)} %select_n.391), kind=kOutput, calls=%fused_computation.29 | convolution fusion | flops 298598400 | bytes 1089796 | tf_op jit(solution)/shard_map/dot_general | solution.py:50
  94.9 1.8 %fusion.27 = f32[192,360]{1,0:T(8,128)S(1)} fusion(f32[360,360]{1,0:T(8,128)} %collective-permute-done.6, f32[16,192,360]{2,1,0:T(8,128)S(1)} %pad_maximum_fusion, s32[]{:T(128)S(6)} %select_n.371), kind=kOutput, calls=%fused_computation.36 | convolution fusion | flops 298598400 | bytes 1089796 | tf_op jit(solution)/shard_map/dot_general | solution.py:50
  103.0 1.9 %collective-permute-start.13 = (f32[360,360]{1,0:T(8,128)S(1)}, f32[360,360]{1,0:T(8,128)S(1)}, u32[]{:S(2)}, u32[]{:S(2)}) collective-permute-start(f32[360,360]{1,0:T(8,128)S(1)} %collective-permute-done.12), channel_id=1, source_target_pairs={{0,32},{32,64},{64,96},{96,128},{128,160},{160,192},{192,224},{224... | collective-permute-start | bytes 1555208 | tf_op jit(solution)/shard_map/ppermute | solution.py:63
  104.9 5.1 %collective-permute-start.17 = (f32[360,360]{1,0:T(8,128)S(1)}, f32[360,360]{1,0:T(8,128)S(1)}, u32[]{:S(2)}, u32[]{:S(2)}) collective-permute-start(f32[360,360]{1,0:T(8,128)S(1)} %collective-permute-done.16), channel_id=1, source_target_pairs={{0,480},{32,0},{64,32},{96,64},{128,96},{160,128},{192,160},{224,1... | collective-permute-start | bytes 1555208 | tf_op jit(solution)/shard_map/ppermute | solution.py:65
  111.6 5.0 %collective-permute-done.13 = f32[360,360]{1,0:T(8,128)S(1)} collective-permute-done((f32[360,360]{1,0:T(8,128)S(1)}, f32[360,360]{1,0:T(8,128)S(1)}, u32[]{:S(2)}, u32[]{:S(2)}) %collective-permute-start.13) | collective-permute-done | bytes 518432 | tf_op jit(solution)/shard_map/ppermute | solution.py:63
  117.9 1.9 %collective-permute-start.18 = (f32[360,360]{1,0:T(8,128)S(1)}, f32[360,360]{1,0:T(8,128)S(1)}, u32[]{:S(2)}, u32[]{:S(2)}) collective-permute-start(f32[360,360]{1,0:T(8,128)S(1)} %collective-permute-done.13), channel_id=1, source_target_pairs={{0,32},{32,64},{64,96},{96,128},{128,160},{160,192},{192,224},{224... | collective-permute-start | bytes 1555208 | tf_op jit(solution)/shard_map/ppermute | solution.py:63
  119.8 5.8 %collective-permute-start.19 = (f32[360,360]{1,0:T(8,128)S(1)}, f32[360,360]{1,0:T(8,128)S(1)}, u32[]{:S(2)}, u32[]{:S(2)}) collective-permute-start(f32[360,360]{1,0:T(8,128)S(1)} %collective-permute-done.17), channel_id=1, source_target_pairs={{0,480},{32,0},{64,32},{96,64},{128,96},{160,128},{192,160},{224,1... | collective-permute-start | bytes 1555208 | tf_op jit(solution)/shard_map/ppermute | solution.py:65
  128.9 2.2 %collective-permute-done.18 = f32[360,360]{1,0:T(8,128)S(1)} collective-permute-done((f32[360,360]{1,0:T(8,128)S(1)}, f32[360,360]{1,0:T(8,128)S(1)}, u32[]{:S(2)}, u32[]{:S(2)}) %collective-permute-start.18) | collective-permute-done | bytes 518432 | tf_op jit(solution)/shard_map/ppermute | solution.py:63
  132.4 1.9 %collective-permute-start.20 = (f32[180,360]{1,0:T(8,128)S(1)}, f32[180,360]{1,0:T(8,128)S(1)}, u32[]{:S(2)}, u32[]{:S(2)}) collective-permute-start(f32[180,360]{1,0:T(8,128)S(1)} %slice.26), channel_id=1, source_target_pairs={{0,32},{32,64},{64,96},{96,128},{128,160},{160,192},{192,224},{224... | collective-permute-start | bytes 777608 | tf_op jit(solution)/shard_map/ppermute | solution.py:69
  134.3 5.6 %collective-permute-start.21 = (f32[180,360]{1,0:T(8,128)S(1)}, f32[180,360]{1,0:T(8,128)S(1)}, u32[]{:S(2)}, u32[]{:S(2)}) collective-permute-start(f32[180,360]{1,0:T(8,128)S(1)} %slice.27), channel_id=1, source_target_pairs={{0,480},{32,0},{64,32},{96,64},{128,96},{160,128},{192,160},{224,1... | collective-permute-start | bytes 777608 | tf_op jit(solution)/shard_map/ppermute | solution.py:70
  144.8 3.3 %collective-permute-start.22 = (f32[96,360]{1,0:T(8,128)S(1)}, f32[96,360]{1,0:T(8,128)S(1)}, u32[]{:S(2)}, u32[]{:S(2)}) collective-permute-start(f32[96,360]{1,0:T(8,128)S(1)} %add_add_fusion), channel_id=1, source_target_pairs={{0,1},{1,0},{2,3},{3,2},{4,5},{5,4},{6,7},{7,6},{8,9},{9,8},{10,11... | collective-permute-start | bytes 414728 | tf_op jit(solution)/shard_map/ppermute | solution.py:85
  148.8 4.5 %collective-permute-done.22 = f32[96,360]{1,0:T(8,128)S(1)} collective-permute-done((f32[96,360]{1,0:T(8,128)S(1)}, f32[96,360]{1,0:T(8,128)S(1)}, u32[]{:S(2)}, u32[]{:S(2)}) %collective-permute-start.22) | collective-permute-done | bytes 138272 | tf_op jit(solution)/shard_map/ppermute | solution.py:85
  (52 shorter events, 25.6 us)
Async XLA Ops:
  0.0 3.7 %collective-permute-start = (f32[192,360]{1,0:T(8,128)}, f32[192,360]{1,0:T(8,128)S(1)}, u32[]{:S(2)}, u32[]{:S(2)}) collective-permute-start(f32[192,360]{1,0:T(8,128)} %param.2), channel_id=1, source_target_pairs={{0,2},{2,0},{4,6},{6,4},{8,10},{10,8},{12,14},{14,12},{16,18},{18,... | collective-permute-start | bytes 829448 | tf_op jit(solution)/shard_map/ppermute | solution.py:15
  4.8 17.3 %collective-permute-start.1 = (f32[2,192,360]{2,1,0:T(8,128)S(1)}, f32[2,192,360]{2,1,0:T(8,128)S(1)}, u32[]{:S(2)}, u32[]{:S(2)}) collective-permute-start(f32[2,192,360]{2,1,0:T(8,128)S(1)} %maximum_select_fusion.1), channel_id=1, source_target_pairs={{0,4},{2,6},{4,0},{6,2},{8,12},{10,14},{12,8},{14,10},{16,20},{18,... | collective-permute-start | bytes 1658888 | tf_op jit(solution)/shard_map/ppermute | solution.py:17
  7.5 24.3 %collective-permute-start.6 = (f32[360,360]{1,0:T(8,128)}, f32[360,360]{1,0:T(8,128)}, u32[]{:S(2)}, u32[]{:S(2)}) collective-permute-start(f32[360,360]{1,0:T(8,128)} %param.3), channel_id=1, source_target_pairs={{0,32},{32,64},{64,96},{96,128},{128,160},{160,192},{192,224},{224... | collective-permute-start | bytes 1555208 | tf_op jit(solution)/shard_map/ppermute | solution.py:63
  11.4 22.4 %collective-permute-start.7 = (f32[360,360]{1,0:T(8,128)}, f32[360,360]{1,0:T(8,128)}, u32[]{:S(2)}, u32[]{:S(2)}) collective-permute-start(f32[360,360]{1,0:T(8,128)} %param.3), channel_id=1, source_target_pairs={{0,480},{32,0},{64,32},{96,64},{128,96},{160,128},{192,160},{224,1... | collective-permute-start | bytes 1555208 | tf_op jit(solution)/shard_map/ppermute | solution.py:65
  22.1 37.4 %collective-permute-start.3 = (f32[4,192,360]{2,1,0:T(8,128)S(1)}, f32[4,192,360]{2,1,0:T(8,128)S(1)}, u32[]{:S(2)}, u32[]{:S(2)}) collective-permute-start(f32[4,192,360]{2,1,0:T(8,128)S(1)} %maximum_select_fusion), channel_id=1, source_target_pairs={{0,8},{2,10},{4,12},{6,14},{8,16},{10,18},{12,20},{14,22},{16,24},... | collective-permute-start | bytes 3317768 | tf_op jit(solution)/shard_map/ppermute | solution.py:21
  25.6 37.0 %collective-permute-start.2 = (f32[4,192,360]{2,1,0:T(8,128)S(1)}, f32[4,192,360]{2,1,0:T(8,128)S(1)}, u32[]{:S(2)}, u32[]{:S(2)}) collective-permute-start(f32[4,192,360]{2,1,0:T(8,128)S(1)} %maximum_select_fusion), channel_id=1, source_target_pairs={{0,24},{2,26},{4,28},{6,30},{8,0},{10,2},{12,4},{14,6},{16,8},{18,... | collective-permute-start | bytes 3317768 | tf_op jit(solution)/shard_map/ppermute | solution.py:22
  31.8 20.6 %collective-permute-start.8 = (f32[360,360]{1,0:T(8,128)}, f32[360,360]{1,0:T(8,128)S(1)}, u32[]{:S(2)}, u32[]{:S(2)}) collective-permute-start(f32[360,360]{1,0:T(8,128)} %collective-permute-done.6), channel_id=1, source_target_pairs={{0,32},{32,64},{64,96},{96,128},{128,160},{160,192},{192,224},{224... | collective-permute-start | bytes 1555208 | tf_op jit(solution)/shard_map/ppermute | solution.py:63
  33.7 20.6 %collective-permute-start.9 = (f32[360,360]{1,0:T(8,128)}, f32[360,360]{1,0:T(8,128)S(1)}, u32[]{:S(2)}, u32[]{:S(2)}) collective-permute-start(f32[360,360]{1,0:T(8,128)} %collective-permute-done.7), channel_id=1, source_target_pairs={{0,480},{32,0},{64,32},{96,64},{128,96},{160,128},{192,160},{224,1... | collective-permute-start | bytes 1555208 | tf_op jit(solution)/shard_map/ppermute | solution.py:65
  52.4 10.2 %copy-start.1 = (f32[360,360]{1,0:T(8,128)}, f32[360,360]{1,0:T(8,128)S(1)}, u32[]{:S(2)}) copy-start(f32[360,360]{1,0:T(8,128)S(1)} %collective-permute-done.8) | copy-start | bytes 1555204
  52.4 15.9 %collective-permute-start.10 = (f32[360,360]{1,0:T(8,128)S(1)}, f32[360,360]{1,0:T(8,128)}, u32[]{:S(2)}, u32[]{:S(2)}) collective-permute-start(f32[360,360]{1,0:T(8,128)S(1)} %collective-permute-done.8), channel_id=1, source_target_pairs={{0,32},{32,64},{64,96},{96,128},{128,160},{160,192},{192,224},{224... | collective-permute-start | bytes 1555208 | tf_op jit(solution)/shard_map/ppermute | solution.py:63
  54.4 14.0 %copy-start.3 = (f32[360,360]{1,0:T(8,128)}, f32[360,360]{1,0:T(8,128)S(1)}, u32[]{:S(2)}) copy-start(f32[360,360]{1,0:T(8,128)S(1)} %collective-permute-done.9) | copy-start | bytes 1555204
  54.4 15.9 %collective-permute-start.14 = (f32[360,360]{1,0:T(8,128)S(1)}, f32[360,360]{1,0:T(8,128)}, u32[]{:S(2)}, u32[]{:S(2)}) collective-permute-start(f32[360,360]{1,0:T(8,128)S(1)} %collective-permute-done.9), channel_id=1, source_target_pairs={{0,480},{32,0},{64,32},{96,64},{128,96},{160,128},{192,160},{224,1... | collective-permute-start | bytes 1555208 | tf_op jit(solution)/shard_map/ppermute | solution.py:65
  60.4 30.5 %collective-permute-start.4 = (f32[4,96,360]{2,1,0:T(8,128)}, f32[4,96,360]{2,1,0:T(8,128)}, u32[]{:S(2)}, u32[]{:S(2)}) collective-permute-start(f32[4,96,360]{2,1,0:T(8,128)} %slice.32), channel_id=1, source_target_pairs={{0,8},{2,10},{4,12},{6,14},{8,16},{10,18},{12,20},{14,22},{16,24},... | collective-permute-start | bytes 1658888 | tf_op jit(solution)/shard_map/ppermute | solution.py:24
  63.5 27.4 %collective-permute-start.5 = (f32[4,96,360]{2,1,0:T(8,128)}, f32[4,96,360]{2,1,0:T(8,128)}, u32[]{:S(2)}, u32[]{:S(2)}) collective-permute-start(f32[4,96,360]{2,1,0:T(8,128)} %slice.33), channel_id=1, source_target_pairs={{0,24},{2,26},{4,28},{6,30},{8,0},{10,2},{12,4},{14,6},{16,8},{18,... | collective-permute-start | bytes 1658888 | tf_op jit(solution)/shard_map/ppermute | solution.py:25
  68.4 15.4 %collective-permute-start.11 = (f32[360,360]{1,0:T(8,128)}, f32[360,360]{1,0:T(8,128)}, u32[]{:S(2)}, u32[]{:S(2)}) collective-permute-start(f32[360,360]{1,0:T(8,128)} %collective-permute-done.10), channel_id=1, source_target_pairs={{0,32},{32,64},{64,96},{96,128},{128,160},{160,192},{192,224},{224... | collective-permute-start | bytes 1555208 | tf_op jit(solution)/shard_map/ppermute | solution.py:63
  70.3 15.4 %collective-permute-start.15 = (f32[360,360]{1,0:T(8,128)}, f32[360,360]{1,0:T(8,128)}, u32[]{:S(2)}, u32[]{:S(2)}) collective-permute-start(f32[360,360]{1,0:T(8,128)} %collective-permute-done.14), channel_id=1, source_target_pairs={{0,480},{32,0},{64,32},{96,64},{128,96},{160,128},{192,160},{224,1... | collective-permute-start | bytes 1555208 | tf_op jit(solution)/shard_map/ppermute | solution.py:65
  76.4 22.1 %copy-start.4 = (f32[360,360]{1,0:T(8,128)S(1)}, f32[360,360]{1,0:T(8,128)}, u32[]{:S(2)}) copy-start(f32[360,360]{1,0:T(8,128)} %copy-done.3) | copy-start | bytes 1555204
  83.8 19.2 %collective-permute-start.12 = (f32[360,360]{1,0:T(8,128)}, f32[360,360]{1,0:T(8,128)S(1)}, u32[]{:S(2)}, u32[]{:S(2)}) collective-permute-start(f32[360,360]{1,0:T(8,128)} %collective-permute-done.11), channel_id=1, source_target_pairs={{0,32},{32,64},{64,96},{96,128},{128,160},{160,192},{192,224},{224... | collective-permute-start | bytes 1555208 | tf_op jit(solution)/shard_map/ppermute | solution.py:63
  85.7 19.2 %collective-permute-start.16 = (f32[360,360]{1,0:T(8,128)}, f32[360,360]{1,0:T(8,128)S(1)}, u32[]{:S(2)}, u32[]{:S(2)}) collective-permute-start(f32[360,360]{1,0:T(8,128)} %collective-permute-done.15), channel_id=1, source_target_pairs={{0,480},{32,0},{64,32},{96,64},{128,96},{160,128},{192,160},{224,1... | collective-permute-start | bytes 1555208 | tf_op jit(solution)/shard_map/ppermute | solution.py:65
  93.0 17.1 %copy-start = (f32[360,360]{1,0:T(8,128)S(1)}, f32[360,360]{1,0:T(8,128)}, u32[]{:S(2)}) copy-start(f32[360,360]{1,0:T(8,128)} %param.3) | copy-start | bytes 1555204
  93.0 17.8 %copy-start.2 = (f32[360,360]{1,0:T(8,128)S(1)}, f32[360,360]{1,0:T(8,128)}, u32[]{:S(2)}) copy-start(f32[360,360]{1,0:T(8,128)} %copy-done.1) | copy-start | bytes 1555204
  103.0 13.7 %collective-permute-start.13 = (f32[360,360]{1,0:T(8,128)S(1)}, f32[360,360]{1,0:T(8,128)S(1)}, u32[]{:S(2)}, u32[]{:S(2)}) collective-permute-start(f32[360,360]{1,0:T(8,128)S(1)} %collective-permute-done.12), channel_id=1, source_target_pairs={{0,32},{32,64},{64,96},{96,128},{128,160},{160,192},{192,224},{224... | collective-permute-start | bytes 1555208 | tf_op jit(solution)/shard_map/ppermute | solution.py:63
  104.9 12.9 %collective-permute-start.17 = (f32[360,360]{1,0:T(8,128)S(1)}, f32[360,360]{1,0:T(8,128)S(1)}, u32[]{:S(2)}, u32[]{:S(2)}) collective-permute-start(f32[360,360]{1,0:T(8,128)S(1)} %collective-permute-done.16), channel_id=1, source_target_pairs={{0,480},{32,0},{64,32},{96,64},{128,96},{160,128},{192,160},{224,1... | collective-permute-start | bytes 1555208 | tf_op jit(solution)/shard_map/ppermute | solution.py:65
  117.9 13.2 %collective-permute-start.18 = (f32[360,360]{1,0:T(8,128)S(1)}, f32[360,360]{1,0:T(8,128)S(1)}, u32[]{:S(2)}, u32[]{:S(2)}) collective-permute-start(f32[360,360]{1,0:T(8,128)S(1)} %collective-permute-done.13), channel_id=1, source_target_pairs={{0,32},{32,64},{64,96},{96,128},{128,160},{160,192},{192,224},{224... | collective-permute-start | bytes 1555208 | tf_op jit(solution)/shard_map/ppermute | solution.py:63
  119.8 12.6 %collective-permute-start.19 = (f32[360,360]{1,0:T(8,128)S(1)}, f32[360,360]{1,0:T(8,128)S(1)}, u32[]{:S(2)}, u32[]{:S(2)}) collective-permute-start(f32[360,360]{1,0:T(8,128)S(1)} %collective-permute-done.17), channel_id=1, source_target_pairs={{0,480},{32,0},{64,32},{96,64},{128,96},{160,128},{192,160},{224,1... | collective-permute-start | bytes 1555208 | tf_op jit(solution)/shard_map/ppermute | solution.py:65
  132.4 10.6 %collective-permute-start.20 = (f32[180,360]{1,0:T(8,128)S(1)}, f32[180,360]{1,0:T(8,128)S(1)}, u32[]{:S(2)}, u32[]{:S(2)}) collective-permute-start(f32[180,360]{1,0:T(8,128)S(1)} %slice.26), channel_id=1, source_target_pairs={{0,32},{32,64},{64,96},{96,128},{128,160},{160,192},{192,224},{224... | collective-permute-start | bytes 777608 | tf_op jit(solution)/shard_map/ppermute | solution.py:69
  134.3 9.7 %collective-permute-start.21 = (f32[180,360]{1,0:T(8,128)S(1)}, f32[180,360]{1,0:T(8,128)S(1)}, u32[]{:S(2)}, u32[]{:S(2)}) collective-permute-start(f32[180,360]{1,0:T(8,128)S(1)} %slice.27), channel_id=1, source_target_pairs={{0,480},{32,0},{64,32},{96,64},{128,96},{160,128},{192,160},{224,1... | collective-permute-start | bytes 777608 | tf_op jit(solution)/shard_map/ppermute | solution.py:70
  144.8 8.5 %collective-permute-start.22 = (f32[96,360]{1,0:T(8,128)S(1)}, f32[96,360]{1,0:T(8,128)S(1)}, u32[]{:S(2)}, u32[]{:S(2)}) collective-permute-start(f32[96,360]{1,0:T(8,128)S(1)} %add_add_fusion), channel_id=1, source_target_pairs={{0,1},{1,0},{2,3},{3,2},{4,5},{5,4},{6,7},{7,6},{8,9},{9,8},{10,11... | collective-permute-start | bytes 414728 | tf_op jit(solution)/shard_map/ppermute | solution.py:85

commit v18 on v16

--- a/solution.py
+++ b/solution.py
@@ -71,6 +71,8 @@
             arrived.append((top, (me - step) % n, 0, m))
             arrived.append((bottom, (me - step) % n, m, kb))
             ahead, behind = top, bottom
+        if step == FIRST_DOT_STEP - 1:
+            strip, ahead, behind = lax.optimization_barrier((strip, ahead, behind))
         if step >= FIRST_DOT_STEP:
             for block, owner, lo, hi in pending[:DOTS_PER_STEP]:
                 part = product(block, owner, lo, hi)

time: 155 us -> 154 us (level)
  starting transfers between devices: 89.5 us -> 85.5 us
  matrix products: 19.2 us -> 21.2 us
    ppermute x7, starting transfers between devices: 44.6 us -> 40.9 us  [local(): behind = lax.ppermute(behind, 'row', bwd)]
    ppermute x1, waiting for transfers between devices: 0.01 us -> 2.38 us  [gather_col(): opp_b = lax.ppermute(above[:, h:], 'col', down)]
    dot_general x19, matrix products: 19.2 us -> 21.2 us  [product(): jnp.dot(cols[:, lo:hi], block, precision=lax.Precision.HIGHEST, preferred...]
  transfers between devices with their start and end apart: 23 -> 23, of which waited for: 12 -> 11; matrix products, arithmetic and copies ran while one was open for 15% -> 16% of each run, Pallas kernels for 0% -> 0%
where the time goes in v18:
time: 154 us; the launch traced here: 152 us
  starting transfers between devices  85.5 us (56%)
  waiting for transfers between devices  38.2 us (25%)
  matrix products  21.2 us (14%)
  other arithmetic  3.91 us (3%)
  local copies, waits for them, and re-layouts  1.82 us (1%)
  between operations  1.55 us (1%)
    ppermute x7, starting transfers between devices, local(): behind = lax.ppermute(behind, 'row', bwd)  40.9 us
    ppermute x7, waiting for transfers between devices, local(): ahead = lax.ppermute(ahead, 'row', fwd)  24.6 us
    dot_general x19, matrix products, product(): jnp.dot(cols[:, lo:hi], block, precision=lax.Precision.HIGHEST, preferred...  21.2 us
    ppermute x7, starting transfers between devices, local(): ahead = lax.ppermute(ahead, 'row', fwd)  15.3 us
    ppermute x1, starting transfers between devices, local(): bottom = lax.ppermute(behind[m:], 'row', bwd)  5.6 us
    ppermute x1, waiting for transfers between devices, local(): other = lax.ppermute(other, 'depth', [(0, 1), (1, 0)])  4.8 us
    ppermute x1, starting transfers between devices, gather_col(): above = lax.ppermute(quad, 'col', down)  3.57 us
    ppermute x1, starting transfers between devices, gather_col(): opp_b = lax.ppermute(above[:, h:], 'col', down)  3.56 us
  transfers between devices with their start and end apart: 23, of which 11 were waited for; matrix products, arithmetic and copies ran while one was open for 16% of the time, Pallas kernels for 0%

profile of v18, /device:TPU:6, one launch (start us, length us, event | category | flops | bytes accessed | tf_op | source)
XLA Modules:
  0.0 152.2 jit_solution(5247189861867463763)
XLA Ops:
  0.0 1.9 %collective-permute-start = (f32[192,360]{1,0:T(8,128)}, f32[192,360]{1,0:T(8,128)S(1)}, u32[]{:S(2)}, u32[]{:S(2)}) collective-permute-start(f32[192,360]{1,0:T(8,128)} %param.2), channel_id=1, source_target_pairs={{0,2},{2,0},{4,6},{6,4},{8,10},{10,8},{12,14},{14,12},{16,18},{18,... | collective-permute-start | bytes 829448 | tf_op jit(solution)/shard_map/ppermute | solution.py:15
  4.8 2.7 %collective-permute-start.1 = (f32[2,192,360]{2,1,0:T(8,128)S(1)}, f32[2,192,360]{2,1,0:T(8,128)S(1)}, u32[]{:S(2)}, u32[]{:S(2)}) collective-permute-start(f32[2,192,360]{2,1,0:T(8,128)S(1)} %maximum_select_fusion.1), channel_id=1, source_target_pairs={{0,4},{2,6},{4,0},{6,2},{8,12},{10,14},{12,8},{14,10},{16,20},{18,... | collective-permute-start | bytes 1658888 | tf_op jit(solution)/shard_map/ppermute | solution.py:17
  7.5 3.8 %collective-permute-start.6 = (f32[360,360]{1,0:T(8,128)}, f32[360,360]{1,0:T(8,128)}, u32[]{:S(2)}, u32[]{:S(2)}) collective-permute-start(f32[360,360]{1,0:T(8,128)} %param.3), channel_id=1, source_target_pairs={{0,32},{32,64},{64,96},{96,128},{128,160},{160,192},{192,224},{224... | collective-permute-start | bytes 1555208 | tf_op jit(solution)/shard_map/ppermute | solution.py:63
  11.4 9.5 %collective-permute-start.11 = (f32[360,360]{1,0:T(8,128)}, f32[360,360]{1,0:T(8,128)}, u32[]{:S(2)}, u32[]{:S(2)}) collective-permute-start(f32[360,360]{1,0:T(8,128)} %param.3), channel_id=1, source_target_pairs={{0,480},{32,0},{64,32},{96,64},{128,96},{160,128},{192,160},{224,1... | collective-permute-start | bytes 1555208 | tf_op jit(solution)/shard_map/ppermute | solution.py:65
  20.9 10.9 %collective-permute-done.6 = f32[360,360]{1,0:T(8,128)} collective-permute-done((f32[360,360]{1,0:T(8,128)}, f32[360,360]{1,0:T(8,128)}, u32[]{:S(2)}, u32[]{:S(2)}) %collective-permute-start.6) | collective-permute-done | bytes 518432 | tf_op jit(solution)/shard_map/ppermute | solution.py:63
  31.8 1.9 %collective-permute-start.7 = (f32[360,360]{1,0:T(8,128)}, f32[360,360]{1,0:T(8,128)}, u32[]{:S(2)}, u32[]{:S(2)}) collective-permute-start(f32[360,360]{1,0:T(8,128)} %collective-permute-done.6), channel_id=1, source_target_pairs={{0,32},{32,64},{64,96},{96,128},{128,160},{160,192},{192,224},{224... | collective-permute-start | bytes 1555208 | tf_op jit(solution)/shard_map/ppermute | solution.py:63
  33.7 5.1 %collective-permute-start.12 = (f32[360,360]{1,0:T(8,128)}, f32[360,360]{1,0:T(8,128)}, u32[]{:S(2)}, u32[]{:S(2)}) collective-permute-start(f32[360,360]{1,0:T(8,128)} %collective-permute-done.11), channel_id=1, source_target_pairs={{0,480},{32,0},{64,32},{96,64},{128,96},{160,128},{192,160},{224,1... | collective-permute-start | bytes 1555208 | tf_op jit(solution)/shard_map/ppermute | solution.py:65
  39.0 3.5 %collective-permute-start.3 = (f32[4,192,360]{2,1,0:T(8,128)S(1)}, f32[4,192,360]{2,1,0:T(8,128)S(1)}, u32[]{:S(2)}, u32[]{:S(2)}) collective-permute-start(f32[4,192,360]{2,1,0:T(8,128)S(1)} %maximum_select_fusion), channel_id=1, source_target_pairs={{0,8},{2,10},{4,12},{6,14},{8,16},{10,18},{12,20},{14,22},{16,24},... | collective-permute-start | bytes 3317768 | tf_op jit(solution)/shard_map/ppermute | solution.py:21
  42.5 3.6 %collective-permute-start.2 = (f32[4,192,360]{2,1,0:T(8,128)S(1)}, f32[4,192,360]{2,1,0:T(8,128)S(1)}, u32[]{:S(2)}, u32[]{:S(2)}) collective-permute-start(f32[4,192,360]{2,1,0:T(8,128)S(1)} %maximum_select_fusion), channel_id=1, source_target_pairs={{0,24},{2,26},{4,28},{6,30},{8,0},{10,2},{12,4},{14,6},{16,8},{18,... | collective-permute-start | bytes 3317768 | tf_op jit(solution)/shard_map/ppermute | solution.py:22
  46.1 2.9 %collective-permute-done.7 = f32[360,360]{1,0:T(8,128)} collective-permute-done((f32[360,360]{1,0:T(8,128)}, f32[360,360]{1,0:T(8,128)}, u32[]{:S(2)}, u32[]{:S(2)}) %collective-permute-start.7) | collective-permute-done | bytes 518432 | tf_op jit(solution)/shard_map/ppermute | solution.py:63
  49.0 1.9 %collective-permute-start.8 = (f32[360,360]{1,0:T(8,128)}, f32[360,360]{1,0:T(8,128)S(1)}, u32[]{:S(2)}, u32[]{:S(2)}) collective-permute-start(f32[360,360]{1,0:T(8,128)} %collective-permute-done.7), channel_id=1, source_target_pairs={{0,32},{32,64},{64,96},{96,128},{128,160},{160,192},{192,224},{224... | collective-permute-start | bytes 1555208 | tf_op jit(solution)/shard_map/ppermute | solution.py:63
  50.9 5.1 %collective-permute-start.13 = (f32[360,360]{1,0:T(8,128)}, f32[360,360]{1,0:T(8,128)S(1)}, u32[]{:S(2)}, u32[]{:S(2)}) collective-permute-start(f32[360,360]{1,0:T(8,128)} %collective-permute-done.12), channel_id=1, source_target_pairs={{0,480},{32,0},{64,32},{96,64},{128,96},{160,128},{192,160},{224,1... | collective-permute-start | bytes 1555208 | tf_op jit(solution)/shard_map/ppermute | solution.py:65
  56.0 9.1 %collective-permute-done.8 = f32[360,360]{1,0:T(8,128)S(1)} collective-permute-done((f32[360,360]{1,0:T(8,128)}, f32[360,360]{1,0:T(8,128)S(1)}, u32[]{:S(2)}, u32[]{:S(2)}) %collective-permute-start.8) | collective-permute-done | bytes 518432 | tf_op jit(solution)/shard_map/ppermute | solution.py:63
  65.1 1.9 %collective-permute-start.9 = (f32[360,360]{1,0:T(8,128)S(1)}, f32[360,360]{1,0:T(8,128)}, u32[]{:S(2)}, u32[]{:S(2)}) collective-permute-start(f32[360,360]{1,0:T(8,128)S(1)} %collective-permute-done.8), channel_id=1, source_target_pairs={{0,32},{32,64},{64,96},{96,128},{128,160},{160,192},{192,224},{224... | collective-permute-start | bytes 1555208 | tf_op jit(solution)/shard_map/ppermute | solution.py:63
  67.0 5.1 %collective-permute-start.14 = (f32[360,360]{1,0:T(8,128)S(1)}, f32[360,360]{1,0:T(8,128)}, u32[]{:S(2)}, u32[]{:S(2)}) collective-permute-start(f32[360,360]{1,0:T(8,128)S(1)} %collective-permute-done.13), channel_id=1, source_target_pairs={{0,480},{32,0},{64,32},{96,64},{128,96},{160,128},{192,160},{224,1... | collective-permute-start | bytes 1555208 | tf_op jit(solution)/shard_map/ppermute | solution.py:65
  73.0 3.5 %collective-permute-start.4 = (f32[4,96,360]{2,1,0:T(8,128)}, f32[4,96,360]{2,1,0:T(8,128)}, u32[]{:S(2)}, u32[]{:S(2)}) collective-permute-start(f32[4,96,360]{2,1,0:T(8,128)} %slice.32), channel_id=1, source_target_pairs={{0,8},{2,10},{4,12},{6,14},{8,16},{10,18},{12,20},{14,22},{16,24},... | collective-permute-start | bytes 1658888 | tf_op jit(solution)/shard_map/ppermute | solution.py:24
  77.4 3.6 %collective-permute-start.5 = (f32[4,96,360]{2,1,0:T(8,128)}, f32[4,96,360]{2,1,0:T(8,128)}, u32[]{:S(2)}, u32[]{:S(2)}) collective-permute-start(f32[4,96,360]{2,1,0:T(8,128)} %slice.33), channel_id=1, source_target_pairs={{0,24},{2,26},{4,28},{6,30},{8,0},{10,2},{12,4},{14,6},{16,8},{18,... | collective-permute-start | bytes 1658888 | tf_op jit(solution)/shard_map/ppermute | solution.py:25
  81.0 1.9 %collective-permute-start.10 = (f32[360,360]{1,0:T(8,128)}, f32[360,360]{1,0:T(8,128)}, u32[]{:S(2)}, u32[]{:S(2)}) collective-permute-start(f32[360,360]{1,0:T(8,128)} %collective-permute-done.9), channel_id=1, source_target_pairs={{0,32},{32,64},{64,96},{96,128},{128,160},{160,192},{192,224},{224... | collective-permute-start | bytes 1555208 | tf_op jit(solution)/shard_map/ppermute | solution.py:63
  82.9 5.1 %collective-permute-start.15 = (f32[360,360]{1,0:T(8,128)}, f32[360,360]{1,0:T(8,128)}, u32[]{:S(2)}, u32[]{:S(2)}) collective-permute-start(f32[360,360]{1,0:T(8,128)} %collective-permute-done.14), channel_id=1, source_target_pairs={{0,480},{32,0},{64,32},{96,64},{128,96},{160,128},{192,160},{224,1... | collective-permute-start | bytes 1555208 | tf_op jit(solution)/shard_map/ppermute | solution.py:65
  89.1 2.4 %collective-permute-done.5 = f32[4,96,360]{2,1,0:T(8,128)} collective-permute-done((f32[4,96,360]{2,1,0:T(8,128)}, f32[4,96,360]{2,1,0:T(8,128)}, u32[]{:S(2)}, u32[]{:S(2)}) %collective-permute-start.5) | collective-permute-done | bytes 552992 | tf_op jit(solution)/shard_map/ppermute | solution.py:25
  91.5 2.0 %pad_maximum_fusion = f32[16,192,360]{2,1,0:T(8,128)S(1)} fusion(f32[4,192,360]{2,1,0:T(8,128)S(1)} %collective-permute-done.3, f32[4,96,360]{2,1,0:T(8,128)} %collective-permute-done.5, f32[4,96,360]{2,1,0:T(8,128)} %collective-permute-done.4, f32[4,192,360]{2,1,0:T(8,128)S(1)} %collective-permute-done.2, f32[4,192,360]{2,1,0:T(8,128)S(1)} %maximum_select_fusion), kind=kLoop, calls=%fused_computation | loop fusion | flops 4423680 | bytes 8847360 | tf_op jit(solution)/shard_map/concatenate | solution.py:27
  96.5 1.9 %collective-permute-start.16 = (f32[360,360]{1,0:T(8,128)}, f32[360,360]{1,0:T(8,128)S(1)}, u32[]{:S(2)}, u32[]{:S(2)}) collective-permute-start(f32[360,360]{1,0:T(8,128)} %collective-permute-done.10), channel_id=1, source_target_pairs={{0,32},{32,64},{64,96},{96,128},{128,160},{160,192},{192,224},{224... | collective-permute-start | bytes 1555208 | tf_op jit(solution)/shard_map/ppermute | solution.py:63
  98.4 5.6 %collective-permute-start.17 = (f32[360,360]{1,0:T(8,128)}, f32[360,360]{1,0:T(8,128)S(1)}, u32[]{:S(2)}, u32[]{:S(2)}) collective-permute-start(f32[360,360]{1,0:T(8,128)} %collective-permute-done.15), channel_id=1, source_target_pairs={{0,480},{32,0},{64,32},{96,64},{128,96},{160,128},{192,160},{224,1... | collective-permute-start | bytes 1555208 | tf_op jit(solution)/shard_map/ppermute | solution.py:65
  106.6 1.9 %fusion.15 = f32[192,360]{1,0:T(8,128)S(1)} fusion(f32[360,360]{1,0:T(8,128)} %collective-permute-done.14, f32[16,192,360]{2,1,0:T(8,128)S(1)} %pad_maximum_fusion, s32[]{:T(128)S(6)} %select_n.406), kind=kOutput, calls=%fused_computation.25 | convolution fusion | flops 298598400 | bytes 1089796 | tf_op jit(solution)/shard_map/dot_general | solution.py:50
  113.9 1.8 %fusion = f32[192,360]{1,0:T(8,128)S(1)} fusion(f32[192,360]{1,0:T(8,128)S(1)} %fusion.20, f32[192,360]{1,0:T(8,128)S(1)} %convolution_add_fusion.5, f32[360,360]{1,0:T(8,128)} %collective-permute-done.7, f32[16,192,360]{2,1,0:T(8,128)S(1)} %pad_maximum_fusion, s32[]{:T(128)S(6)} %select_n.381), kind=kOutput, calls=%fused_computation.9 | convolution fusion | flops 298736640 | bytes 1679620 | tf_op jit(solution)/shard_map/dot_general | solution.py:50
  116.6 1.9 %collective-permute-start.18 = (f32[360,360]{1,0:T(8,128)S(1)}, f32[360,360]{1,0:T(8,128)S(1)}, u32[]{:S(2)}, u32[]{:S(2)}) collective-permute-start(f32[360,360]{1,0:T(8,128)S(1)} %collective-permute-done.16), channel_id=1, source_target_pairs={{0,32},{32,64},{64,96},{96,128},{128,160},{160,192},{192,224},{224... | collective-permute-start | bytes 1555208 | tf_op jit(solution)/shard_map/ppermute | solution.py:63
  118.5 5.3 %collective-permute-start.19 = (f32[360,360]{1,0:T(8,128)S(1)}, f32[360,360]{1,0:T(8,128)S(1)}, u32[]{:S(2)}, u32[]{:S(2)}) collective-permute-start(f32[360,360]{1,0:T(8,128)S(1)} %collective-permute-done.17), channel_id=1, source_target_pairs={{0,480},{32,0},{64,32},{96,64},{128,96},{160,128},{192,160},{224,1... | collective-permute-start | bytes 1555208 | tf_op jit(solution)/shard_map/ppermute | solution.py:65
  124.6 1.8 %fusion.1 = f32[192,360]{1,0:T(8,128)S(1)} fusion(f32[192,360]{1,0:T(8,128)S(1)} %fusion.15, f32[192,360]{1,0:T(8,128)S(1)} %convolution_add_fusion.2, f32[360,360]{1,0:T(8,128)} %collective-permute-done.9, f32[16,192,360]{2,1,0:T(8,128)S(1)} %pad_maximum_fusion, s32[]{:T(128)S(6)} %select_n.401), kind=kOutput, calls=%fused_computation.10 | convolution fusion | flops 298736640 | bytes 1679620 | tf_op jit(solution)/shard_map/dot_general | solution.py:50
  130.6 1.9 %collective-permute-start.20 = (f32[180,360]{1,0:T(8,128)S(1)}, f32[180,360]{1,0:T(8,128)S(1)}, u32[]{:S(2)}, u32[]{:S(2)}) collective-permute-start(f32[180,360]{1,0:T(8,128)S(1)} %slice.26), channel_id=1, source_target_pairs={{0,32},{32,64},{64,96},{96,128},{128,160},{160,192},{192,224},{224... | collective-permute-start | bytes 777608 | tf_op jit(solution)/shard_map/ppermute | solution.py:69
  132.6 5.6 %collective-permute-start.21 = (f32[180,360]{1,0:T(8,128)S(1)}, f32[180,360]{1,0:T(8,128)S(1)}, u32[]{:S(2)}, u32[]{:S(2)}) collective-permute-start(f32[180,360]{1,0:T(8,128)S(1)} %slice.27), channel_id=1, source_target_pairs={{0,480},{32,0},{64,32},{96,64},{128,96},{160,128},{192,160},{224,1... | collective-permute-start | bytes 777608 | tf_op jit(solution)/shard_map/ppermute | solution.py:70
  143.0 3.0 %collective-permute-start.22 = (f32[96,360]{1,0:T(8,128)S(1)}, f32[96,360]{1,0:T(8,128)S(1)}, u32[]{:S(2)}, u32[]{:S(2)}) collective-permute-start(f32[96,360]{1,0:T(8,128)S(1)} %add_add_fusion.1), channel_id=1, source_target_pairs={{0,1},{1,0},{2,3},{3,2},{4,5},{5,4},{6,7},{7,6},{8,9},{9,8},{10,11... | collective-permute-start | bytes 414728 | tf_op jit(solution)/shard_map/ppermute | solution.py:87
  146.7 4.8 %collective-permute-done.22 = f32[96,360]{1,0:T(8,128)S(1)} collective-permute-done((f32[96,360]{1,0:T(8,128)S(1)}, f32[96,360]{1,0:T(8,128)S(1)}, u32[]{:S(2)}, u32[]{:S(2)}) %collective-permute-start.22) | collective-permute-done | bytes 138272 | tf_op jit(solution)/shard_map/ppermute | solution.py:87
  (52 shorter events, 27.6 us)
Async XLA Ops:
  0.0 3.7 %collective-permute-start = (f32[192,360]{1,0:T(8,128)}, f32[192,360]{1,0:T(8,128)S(1)}, u32[]{:S(2)}, u32[]{:S(2)}) collective-permute-start(f32[192,360]{1,0:T(8,128)} %param.2), channel_id=1, source_target_pairs={{0,2},{2,0},{4,6},{6,4},{8,10},{10,8},{12,14},{14,12},{16,18},{18,... | collective-permute-start | bytes 829448 | tf_op jit(solution)/shard_map/ppermute | solution.py:15
  4.8 34.1 %collective-permute-start.1 = (f32[2,192,360]{2,1,0:T(8,128)S(1)}, f32[2,192,360]{2,1,0:T(8,128)S(1)}, u32[]{:S(2)}, u32[]{:S(2)}) collective-permute-start(f32[2,192,360]{2,1,0:T(8,128)S(1)} %maximum_select_fusion.1), channel_id=1, source_target_pairs={{0,4},{2,6},{4,0},{6,2},{8,12},{10,14},{12,8},{14,10},{16,20},{18,... | collective-permute-start | bytes 1658888 | tf_op jit(solution)/shard_map/ppermute | solution.py:17
  7.5 24.3 %collective-permute-start.6 = (f32[360,360]{1,0:T(8,128)}, f32[360,360]{1,0:T(8,128)}, u32[]{:S(2)}, u32[]{:S(2)}) collective-permute-start(f32[360,360]{1,0:T(8,128)} %param.3), channel_id=1, source_target_pairs={{0,32},{32,64},{64,96},{96,128},{128,160},{160,192},{192,224},{224... | collective-permute-start | bytes 1555208 | tf_op jit(solution)/shard_map/ppermute | solution.py:63
  11.4 22.4 %collective-permute-start.11 = (f32[360,360]{1,0:T(8,128)}, f32[360,360]{1,0:T(8,128)}, u32[]{:S(2)}, u32[]{:S(2)}) collective-permute-start(f32[360,360]{1,0:T(8,128)} %param.3), channel_id=1, source_target_pairs={{0,480},{32,0},{64,32},{96,64},{128,96},{160,128},{192,160},{224,1... | collective-permute-start | bytes 1555208 | tf_op jit(solution)/shard_map/ppermute | solution.py:65
  31.8 17.2 %collective-permute-start.7 = (f32[360,360]{1,0:T(8,128)}, f32[360,360]{1,0:T(8,128)}, u32[]{:S(2)}, u32[]{:S(2)}) collective-permute-start(f32[360,360]{1,0:T(8,128)} %collective-permute-done.6), channel_id=1, source_target_pairs={{0,32},{32,64},{64,96},{96,128},{128,160},{160,192},{192,224},{224... | collective-permute-start | bytes 1555208 | tf_op jit(solution)/shard_map/ppermute | solution.py:63
  33.7 17.2 %collective-permute-start.12 = (f32[360,360]{1,0:T(8,128)}, f32[360,360]{1,0:T(8,128)}, u32[]{:S(2)}, u32[]{:S(2)}) collective-permute-start(f32[360,360]{1,0:T(8,128)} %collective-permute-done.11), channel_id=1, source_target_pairs={{0,480},{32,0},{64,32},{96,64},{128,96},{160,128},{192,160},{224,1... | collective-permute-start | bytes 1555208 | tf_op jit(solution)/shard_map/ppermute | solution.py:65
  39.0 33.2 %collective-permute-start.3 = (f32[4,192,360]{2,1,0:T(8,128)S(1)}, f32[4,192,360]{2,1,0:T(8,128)S(1)}, u32[]{:S(2)}, u32[]{:S(2)}) collective-permute-start(f32[4,192,360]{2,1,0:T(8,128)S(1)} %maximum_select_fusion), channel_id=1, source_target_pairs={{0,8},{2,10},{4,12},{6,14},{8,16},{10,18},{12,20},{14,22},{16,24},... | collective-permute-start | bytes 3317768 | tf_op jit(solution)/shard_map/ppermute | solution.py:21
  42.5 34.0 %collective-permute-start.2 = (f32[4,192,360]{2,1,0:T(8,128)S(1)}, f32[4,192,360]{2,1,0:T(8,128)S(1)}, u32[]{:S(2)}, u32[]{:S(2)}) collective-permute-start(f32[4,192,360]{2,1,0:T(8,128)S(1)} %maximum_select_fusion), channel_id=1, source_target_pairs={{0,24},{2,26},{4,28},{6,30},{8,0},{10,2},{12,4},{14,6},{16,8},{18,... | collective-permute-start | bytes 3317768 | tf_op jit(solution)/shard_map/ppermute | solution.py:22
  49.0 16.1 %collective-permute-start.8 = (f32[360,360]{1,0:T(8,128)}, f32[360,360]{1,0:T(8,128)S(1)}, u32[]{:S(2)}, u32[]{:S(2)}) collective-permute-start(f32[360,360]{1,0:T(8,128)} %collective-permute-done.7), channel_id=1, source_target_pairs={{0,32},{32,64},{64,96},{96,128},{128,160},{160,192},{192,224},{224... | collective-permute-start | bytes 1555208 | tf_op jit(solution)/shard_map/ppermute | solution.py:63
  50.9 16.1 %collective-permute-start.13 = (f32[360,360]{1,0:T(8,128)}, f32[360,360]{1,0:T(8,128)S(1)}, u32[]{:S(2)}, u32[]{:S(2)}) collective-permute-start(f32[360,360]{1,0:T(8,128)} %collective-permute-done.12), channel_id=1, source_target_pairs={{0,480},{32,0},{64,32},{96,64},{128,96},{160,128},{192,160},{224,1... | collective-permute-start | bytes 1555208 | tf_op jit(solution)/shard_map/ppermute | solution.py:65
  65.1 17.8 %copy-start.3 = (f32[360,360]{1,0:T(8,128)}, f32[360,360]{1,0:T(8,128)S(1)}, u32[]{:S(2)}) copy-start(f32[360,360]{1,0:T(8,128)S(1)} %collective-permute-done.8) | copy-start | bytes 1555204
  65.1 15.9 %collective-permute-start.9 = (f32[360,360]{1,0:T(8,128)S(1)}, f32[360,360]{1,0:T(8,128)}, u32[]{:S(2)}, u32[]{:S(2)}) collective-permute-start(f32[360,360]{1,0:T(8,128)S(1)} %collective-permute-done.8), channel_id=1, source_target_pairs={{0,32},{32,64},{64,96},{96,128},{128,160},{160,192},{192,224},{224... | collective-permute-start | bytes 1555208 | tf_op jit(solution)/shard_map/ppermute | solution.py:63
  67.0 9.5 %copy-start.1 = (f32[360,360]{1,0:T(8,128)}, f32[360,360]{1,0:T(8,128)S(1)}, u32[]{:S(2)}) copy-start(f32[360,360]{1,0:T(8,128)S(1)} %collective-permute-done.13) | copy-start | bytes 1555204
  67.0 15.9 %collective-permute-start.14 = (f32[360,360]{1,0:T(8,128)S(1)}, f32[360,360]{1,0:T(8,128)}, u32[]{:S(2)}, u32[]{:S(2)}) collective-permute-start(f32[360,360]{1,0:T(8,128)S(1)} %collective-permute-done.13), channel_id=1, source_target_pairs={{0,480},{32,0},{64,32},{96,64},{128,96},{160,128},{192,160},{224,1... | collective-permute-start | bytes 1555208 | tf_op jit(solution)/shard_map/ppermute | solution.py:65
  73.0 16.0 %collective-permute-start.4 = (f32[4,96,360]{2,1,0:T(8,128)}, f32[4,96,360]{2,1,0:T(8,128)}, u32[]{:S(2)}, u32[]{:S(2)}) collective-permute-start(f32[4,96,360]{2,1,0:T(8,128)} %slice.32), channel_id=1, source_target_pairs={{0,8},{2,10},{4,12},{6,14},{8,16},{10,18},{12,20},{14,22},{16,24},... | collective-permute-start | bytes 1658888 | tf_op jit(solution)/shard_map/ppermute | solution.py:24
  77.4 14.1 %collective-permute-start.5 = (f32[4,96,360]{2,1,0:T(8,128)}, f32[4,96,360]{2,1,0:T(8,128)}, u32[]{:S(2)}, u32[]{:S(2)}) collective-permute-start(f32[4,96,360]{2,1,0:T(8,128)} %slice.33), channel_id=1, source_target_pairs={{0,24},{2,26},{4,28},{6,30},{8,0},{10,2},{12,4},{14,6},{16,8},{18,... | collective-permute-start | bytes 1658888 | tf_op jit(solution)/shard_map/ppermute | solution.py:25
  81.0 14.3 %collective-permute-start.10 = (f32[360,360]{1,0:T(8,128)}, f32[360,360]{1,0:T(8,128)}, u32[]{:S(2)}, u32[]{:S(2)}) collective-permute-start(f32[360,360]{1,0:T(8,128)} %collective-permute-done.9), channel_id=1, source_target_pairs={{0,32},{32,64},{64,96},{96,128},{128,160},{160,192},{192,224},{224... | collective-permute-start | bytes 1555208 | tf_op jit(solution)/shard_map/ppermute | solution.py:63
  82.9 13.5 %collective-permute-start.15 = (f32[360,360]{1,0:T(8,128)}, f32[360,360]{1,0:T(8,128)}, u32[]{:S(2)}, u32[]{:S(2)}) collective-permute-start(f32[360,360]{1,0:T(8,128)} %collective-permute-done.14), channel_id=1, source_target_pairs={{0,480},{32,0},{64,32},{96,64},{128,96},{160,128},{192,160},{224,1... | collective-permute-start | bytes 1555208 | tf_op jit(solution)/shard_map/ppermute | solution.py:65
  89.1 14.9 %copy-start = (f32[360,360]{1,0:T(8,128)S(1)}, f32[360,360]{1,0:T(8,128)}, u32[]{:S(2)}) copy-start(f32[360,360]{1,0:T(8,128)} %param.3) | copy-start | bytes 1555204
  93.5 22.2 %copy-start.4 = (f32[360,360]{1,0:T(8,128)S(1)}, f32[360,360]{1,0:T(8,128)}, u32[]{:S(2)}) copy-start(f32[360,360]{1,0:T(8,128)} %copy-done.3) | copy-start | bytes 1555204
  96.5 20.1 %collective-permute-start.16 = (f32[360,360]{1,0:T(8,128)}, f32[360,360]{1,0:T(8,128)S(1)}, u32[]{:S(2)}, u32[]{:S(2)}) collective-permute-start(f32[360,360]{1,0:T(8,128)} %collective-permute-done.10), channel_id=1, source_target_pairs={{0,32},{32,64},{64,96},{96,128},{128,160},{160,192},{192,224},{224... | collective-permute-start | bytes 1555208 | tf_op jit(solution)/shard_map/ppermute | solution.py:63
  98.4 18.2 %collective-permute-start.17 = (f32[360,360]{1,0:T(8,128)}, f32[360,360]{1,0:T(8,128)S(1)}, u32[]{:S(2)}, u32[]{:S(2)}) collective-permute-start(f32[360,360]{1,0:T(8,128)} %collective-permute-done.15), channel_id=1, source_target_pairs={{0,480},{32,0},{64,32},{96,64},{128,96},{160,128},{192,160},{224,1... | collective-permute-start | bytes 1555208 | tf_op jit(solution)/shard_map/ppermute | solution.py:65
  106.6 17.2 %copy-start.2 = (f32[360,360]{1,0:T(8,128)S(1)}, f32[360,360]{1,0:T(8,128)}, u32[]{:S(2)}) copy-start(f32[360,360]{1,0:T(8,128)} %copy-done.1) | copy-start | bytes 1555204
  116.6 13.2 %collective-permute-start.18 = (f32[360,360]{1,0:T(8,128)S(1)}, f32[360,360]{1,0:T(8,128)S(1)}, u32[]{:S(2)}, u32[]{:S(2)}) collective-permute-start(f32[360,360]{1,0:T(8,128)S(1)} %collective-permute-done.16), channel_id=1, source_target_pairs={{0,32},{32,64},{64,96},{96,128},{128,160},{160,192},{192,224},{224... | collective-permute-start | bytes 1555208 | tf_op jit(solution)/shard_map/ppermute | solution.py:63
  118.5 12.1 %collective-permute-start.19 = (f32[360,360]{1,0:T(8,128)S(1)}, f32[360,360]{1,0:T(8,128)S(1)}, u32[]{:S(2)}, u32[]{:S(2)}) collective-permute-start(f32[360,360]{1,0:T(8,128)S(1)} %collective-permute-done.17), channel_id=1, source_target_pairs={{0,480},{32,0},{64,32},{96,64},{128,96},{160,128},{192,160},{224,1... | collective-permute-start | bytes 1555208 | tf_op jit(solution)/shard_map/ppermute | solution.py:65
  130.6 10.2 %collective-permute-start.20 = (f32[180,360]{1,0:T(8,128)S(1)}, f32[180,360]{1,0:T(8,128)S(1)}, u32[]{:S(2)}, u32[]{:S(2)}) collective-permute-start(f32[180,360]{1,0:T(8,128)S(1)} %slice.26), channel_id=1, source_target_pairs={{0,32},{32,64},{64,96},{96,128},{128,160},{160,192},{192,224},{224... | collective-permute-start | bytes 777608 | tf_op jit(solution)/shard_map/ppermute | solution.py:69
  132.6 9.7 %collective-permute-start.21 = (f32[180,360]{1,0:T(8,128)S(1)}, f32[180,360]{1,0:T(8,128)S(1)}, u32[]{:S(2)}, u32[]{:S(2)}) collective-permute-start(f32[180,360]{1,0:T(8,128)S(1)} %slice.27), channel_id=1, source_target_pairs={{0,480},{32,0},{64,32},{96,64},{128,96},{160,128},{192,160},{224,1... | collective-permute-start | bytes 777608 | tf_op jit(solution)/shard_map/ppermute | solution.py:70
  143.0 8.5 %collective-permute-start.22 = (f32[96,360]{1,0:T(8,128)S(1)}, f32[96,360]{1,0:T(8,128)S(1)}, u32[]{:S(2)}, u32[]{:S(2)}) collective-permute-start(f32[96,360]{1,0:T(8,128)S(1)} %add_add_fusion.1), channel_id=1, source_target_pairs={{0,1},{1,0},{2,3},{3,2},{4,5},{5,4},{6,7},{7,6},{8,9},{9,8},{10,11... | collective-permute-start | bytes 414728 | tf_op jit(solution)/shard_map/ppermute | solution.py:87

commit v19 on v18

--- a/solution.py
+++ b/solution.py
@@ -4,7 +4,7 @@
 from jax.sharding import PartitionSpec as P
 
 FIRST_DOT_STEP = 6
-DOTS_PER_STEP = 6
+DOTS_PER_STEP = 7
 
 
 def gather_col(block):

time: 154 us -> 155 us (level)
  transfers between devices with their start and end apart: 23 -> 23, of which waited for: 11 -> 12; matrix products, arithmetic and copies ran while one was open for 16% -> 16% of each run, Pallas kernels for 0% -> 0%
where the time goes in v19:
time: 155 us; the launch traced here: 153 us
  starting transfers between devices  85.5 us (55%)
  waiting for transfers between devices  39 us (25%)
  matrix products  21.2 us (14%)
  other arithmetic  3.93 us (3%)
  local copies, waits for them, and re-layouts  1.82 us (1%)
    ppermute x7, starting transfers between devices, local(): behind = lax.ppermute(behind, 'row', bwd)  40.9 us
    ppermute x7, waiting for transfers between devices, local(): ahead = lax.ppermute(ahead, 'row', fwd)  24.8 us
    dot_general x19, matrix products, product(): jnp.dot(cols[:, lo:hi], block, precision=lax.Precision.HIGHEST, preferred...  21.2 us
    ppermute x7, starting transfers between devices, local(): ahead = lax.ppermute(ahead, 'row', fwd)  15.3 us
    ppermute x1, starting transfers between devices, local(): bottom = lax.ppermute(behind[m:], 'row', bwd)  5.6 us
    ppermute x1, waiting for transfers between devices, local(): other = lax.ppermute(other, 'depth', [(0, 1), (1, 0)])  4.79 us
    ppermute x1, starting transfers between devices, gather_col(): above = lax.ppermute(quad, 'col', down)  3.57 us
    ppermute x1, starting transfers between devices, gather_col(): opp_b = lax.ppermute(above[:, h:], 'col', down)  3.56 us
  transfers between devices with their start and end apart: 23, of which 12 were waited for; matrix products, arithmetic and copies ran while one was open for 16% of the time, Pallas kernels for 0%

profile of v19, /device:TPU:6, one launch (start us, length us, event | category | flops | bytes accessed | tf_op | source)
XLA Modules:
  0.0 153.0 jit_solution(916221938777139980)
XLA Ops:
  0.0 1.9 %collective-permute-start = (f32[192,360]{1,0:T(8,128)}, f32[192,360]{1,0:T(8,128)S(1)}, u32[]{:S(2)}, u32[]{:S(2)}) collective-permute-start(f32[192,360]{1,0:T(8,128)} %param.2), channel_id=1, source_target_pairs={{0,2},{2,0},{4,6},{6,4},{8,10},{10,8},{12,14},{14,12},{16,18},{18,... | collective-permute-start | bytes 829448 | tf_op jit(solution)/shard_map/ppermute | solution.py:15
  4.8 2.7 %collective-permute-start.1 = (f32[2,192,360]{2,1,0:T(8,128)S(1)}, f32[2,192,360]{2,1,0:T(8,128)S(1)}, u32[]{:S(2)}, u32[]{:S(2)}) collective-permute-start(f32[2,192,360]{2,1,0:T(8,128)S(1)} %maximum_select_fusion.1), channel_id=1, source_target_pairs={{0,4},{2,6},{4,0},{6,2},{8,12},{10,14},{12,8},{14,10},{16,20},{18,... | collective-permute-start | bytes 1658888 | tf_op jit(solution)/shard_map/ppermute | solution.py:17
  7.5 3.8 %collective-permute-start.6 = (f32[360,360]{1,0:T(8,128)}, f32[360,360]{1,0:T(8,128)}, u32[]{:S(2)}, u32[]{:S(2)}) collective-permute-start(f32[360,360]{1,0:T(8,128)} %param.3), channel_id=1, source_target_pairs={{0,32},{32,64},{64,96},{96,128},{128,160},{160,192},{192,224},{224... | collective-permute-start | bytes 1555208 | tf_op jit(solution)/shard_map/ppermute | solution.py:63
  11.4 9.5 %collective-permute-start.11 = (f32[360,360]{1,0:T(8,128)}, f32[360,360]{1,0:T(8,128)}, u32[]{:S(2)}, u32[]{:S(2)}) collective-permute-start(f32[360,360]{1,0:T(8,128)} %param.3), channel_id=1, source_target_pairs={{0,480},{32,0},{64,32},{96,64},{128,96},{160,128},{192,160},{224,1... | collective-permute-start | bytes 1555208 | tf_op jit(solution)/shard_map/ppermute | solution.py:65
  20.9 10.9 %collective-permute-done.6 = f32[360,360]{1,0:T(8,128)} collective-permute-done((f32[360,360]{1,0:T(8,128)}, f32[360,360]{1,0:T(8,128)}, u32[]{:S(2)}, u32[]{:S(2)}) %collective-permute-start.6) | collective-permute-done | bytes 518432 | tf_op jit(solution)/shard_map/ppermute | solution.py:63
  31.8 1.9 %collective-permute-start.7 = (f32[360,360]{1,0:T(8,128)}, f32[360,360]{1,0:T(8,128)}, u32[]{:S(2)}, u32[]{:S(2)}) collective-permute-start(f32[360,360]{1,0:T(8,128)} %collective-permute-done.6), channel_id=1, source_target_pairs={{0,32},{32,64},{64,96},{96,128},{128,160},{160,192},{192,224},{224... | collective-permute-start | bytes 1555208 | tf_op jit(solution)/shard_map/ppermute | solution.py:63
  33.7 5.1 %collective-permute-start.12 = (f32[360,360]{1,0:T(8,128)}, f32[360,360]{1,0:T(8,128)}, u32[]{:S(2)}, u32[]{:S(2)}) collective-permute-start(f32[360,360]{1,0:T(8,128)} %collective-permute-done.11), channel_id=1, source_target_pairs={{0,480},{32,0},{64,32},{96,64},{128,96},{160,128},{192,160},{224,1... | collective-permute-start | bytes 1555208 | tf_op jit(solution)/shard_map/ppermute | solution.py:65
  39.0 3.5 %collective-permute-start.3 = (f32[4,192,360]{2,1,0:T(8,128)S(1)}, f32[4,192,360]{2,1,0:T(8,128)S(1)}, u32[]{:S(2)}, u32[]{:S(2)}) collective-permute-start(f32[4,192,360]{2,1,0:T(8,128)S(1)} %maximum_select_fusion), channel_id=1, source_target_pairs={{0,8},{2,10},{4,12},{6,14},{8,16},{10,18},{12,20},{14,22},{16,24},... | collective-permute-start | bytes 3317768 | tf_op jit(solution)/shard_map/ppermute | solution.py:21
  42.5 3.6 %collective-permute-start.2 = (f32[4,192,360]{2,1,0:T(8,128)S(1)}, f32[4,192,360]{2,1,0:T(8,128)S(1)}, u32[]{:S(2)}, u32[]{:S(2)}) collective-permute-start(f32[4,192,360]{2,1,0:T(8,128)S(1)} %maximum_select_fusion), channel_id=1, source_target_pairs={{0,24},{2,26},{4,28},{6,30},{8,0},{10,2},{12,4},{14,6},{16,8},{18,... | collective-permute-start | bytes 3317768 | tf_op jit(solution)/shard_map/ppermute | solution.py:22
  46.1 2.9 %collective-permute-done.7 = f32[360,360]{1,0:T(8,128)} collective-permute-done((f32[360,360]{1,0:T(8,128)}, f32[360,360]{1,0:T(8,128)}, u32[]{:S(2)}, u32[]{:S(2)}) %collective-permute-start.7) | collective-permute-done | bytes 518432 | tf_op jit(solution)/shard_map/ppermute | solution.py:63
  49.0 1.9 %collective-permute-start.8 = (f32[360,360]{1,0:T(8,128)}, f32[360,360]{1,0:T(8,128)S(1)}, u32[]{:S(2)}, u32[]{:S(2)}) collective-permute-start(f32[360,360]{1,0:T(8,128)} %collective-permute-done.7), channel_id=1, source_target_pairs={{0,32},{32,64},{64,96},{96,128},{128,160},{160,192},{192,224},{224... | collective-permute-start | bytes 1555208 | tf_op jit(solution)/shard_map/ppermute | solution.py:63
  50.9 5.1 %collective-permute-start.13 = (f32[360,360]{1,0:T(8,128)}, f32[360,360]{1,0:T(8,128)S(1)}, u32[]{:S(2)}, u32[]{:S(2)}) collective-permute-start(f32[360,360]{1,0:T(8,128)} %collective-permute-done.12), channel_id=1, source_target_pairs={{0,480},{32,0},{64,32},{96,64},{128,96},{160,128},{192,160},{224,1... | collective-permute-start | bytes 1555208 | tf_op jit(solution)/shard_map/ppermute | solution.py:65
  56.0 9.1 %collective-permute-done.8 = f32[360,360]{1,0:T(8,128)S(1)} collective-permute-done((f32[360,360]{1,0:T(8,128)}, f32[360,360]{1,0:T(8,128)S(1)}, u32[]{:S(2)}, u32[]{:S(2)}) %collective-permute-start.8) | collective-permute-done | bytes 518432 | tf_op jit(solution)/shard_map/ppermute | solution.py:63
  65.1 1.9 %collective-permute-start.9 = (f32[360,360]{1,0:T(8,128)S(1)}, f32[360,360]{1,0:T(8,128)}, u32[]{:S(2)}, u32[]{:S(2)}) collective-permute-start(f32[360,360]{1,0:T(8,128)S(1)} %collective-permute-done.8), channel_id=1, source_target_pairs={{0,32},{32,64},{64,96},{96,128},{128,160},{160,192},{192,224},{224... | collective-permute-start | bytes 1555208 | tf_op jit(solution)/shard_map/ppermute | solution.py:63
  67.0 5.1 %collective-permute-start.14 = (f32[360,360]{1,0:T(8,128)S(1)}, f32[360,360]{1,0:T(8,128)}, u32[]{:S(2)}, u32[]{:S(2)}) collective-permute-start(f32[360,360]{1,0:T(8,128)S(1)} %collective-permute-done.13), channel_id=1, source_target_pairs={{0,480},{32,0},{64,32},{96,64},{128,96},{160,128},{192,160},{224,1... | collective-permute-start | bytes 1555208 | tf_op jit(solution)/shard_map/ppermute | solution.py:65
  73.0 3.5 %collective-permute-start.4 = (f32[4,96,360]{2,1,0:T(8,128)}, f32[4,96,360]{2,1,0:T(8,128)}, u32[]{:S(2)}, u32[]{:S(2)}) collective-permute-start(f32[4,96,360]{2,1,0:T(8,128)} %slice.32), channel_id=1, source_target_pairs={{0,8},{2,10},{4,12},{6,14},{8,16},{10,18},{12,20},{14,22},{16,24},... | collective-permute-start | bytes 1658888 | tf_op jit(solution)/shard_map/ppermute | solution.py:24
  77.4 3.6 %collective-permute-start.5 = (f32[4,96,360]{2,1,0:T(8,128)}, f32[4,96,360]{2,1,0:T(8,128)}, u32[]{:S(2)}, u32[]{:S(2)}) collective-permute-start(f32[4,96,360]{2,1,0:T(8,128)} %slice.33), channel_id=1, source_target_pairs={{0,24},{2,26},{4,28},{6,30},{8,0},{10,2},{12,4},{14,6},{16,8},{18,... | collective-permute-start | bytes 1658888 | tf_op jit(solution)/shard_map/ppermute | solution.py:25
  81.0 1.9 %collective-permute-start.10 = (f32[360,360]{1,0:T(8,128)}, f32[360,360]{1,0:T(8,128)}, u32[]{:S(2)}, u32[]{:S(2)}) collective-permute-start(f32[360,360]{1,0:T(8,128)} %collective-permute-done.9), channel_id=1, source_target_pairs={{0,32},{32,64},{64,96},{96,128},{128,160},{160,192},{192,224},{224... | collective-permute-start | bytes 1555208 | tf_op jit(solution)/shard_map/ppermute | solution.py:63
  82.9 5.1 %collective-permute-start.15 = (f32[360,360]{1,0:T(8,128)}, f32[360,360]{1,0:T(8,128)}, u32[]{:S(2)}, u32[]{:S(2)}) collective-permute-start(f32[360,360]{1,0:T(8,128)} %collective-permute-done.14), channel_id=1, source_target_pairs={{0,480},{32,0},{64,32},{96,64},{128,96},{160,128},{192,160},{224,1... | collective-permute-start | bytes 1555208 | tf_op jit(solution)/shard_map/ppermute | solution.py:65
  89.1 2.4 %collective-permute-done.5 = f32[4,96,360]{2,1,0:T(8,128)} collective-permute-done((f32[4,96,360]{2,1,0:T(8,128)}, f32[4,96,360]{2,1,0:T(8,128)}, u32[]{:S(2)}, u32[]{:S(2)}) %collective-permute-start.5) | collective-permute-done | bytes 552992 | tf_op jit(solution)/shard_map/ppermute | solution.py:25
  91.5 2.0 %pad_maximum_fusion = f32[16,192,360]{2,1,0:T(8,128)S(1)} fusion(f32[4,192,360]{2,1,0:T(8,128)S(1)} %collective-permute-done.3, f32[4,96,360]{2,1,0:T(8,128)} %collective-permute-done.5, f32[4,96,360]{2,1,0:T(8,128)} %collective-permute-done.4, f32[4,192,360]{2,1,0:T(8,128)S(1)} %collective-permute-done.2, f32[4,192,360]{2,1,0:T(8,128)S(1)} %maximum_select_fusion), kind=kLoop, calls=%fused_computation | loop fusion | flops 4423680 | bytes 8847360 | tf_op jit(solution)/shard_map/concatenate | solution.py:27
  96.5 1.9 %collective-permute-start.16 = (f32[360,360]{1,0:T(8,128)}, f32[360,360]{1,0:T(8,128)S(1)}, u32[]{:S(2)}, u32[]{:S(2)}) collective-permute-start(f32[360,360]{1,0:T(8,128)} %collective-permute-done.10), channel_id=1, source_target_pairs={{0,32},{32,64},{64,96},{96,128},{128,160},{160,192},{192,224},{224... | collective-permute-start | bytes 1555208 | tf_op jit(solution)/shard_map/ppermute | solution.py:63
  98.4 5.6 %collective-permute-start.17 = (f32[360,360]{1,0:T(8,128)}, f32[360,360]{1,0:T(8,128)S(1)}, u32[]{:S(2)}, u32[]{:S(2)}) collective-permute-start(f32[360,360]{1,0:T(8,128)} %collective-permute-done.15), channel_id=1, source_target_pairs={{0,480},{32,0},{64,32},{96,64},{128,96},{160,128},{192,160},{224,1... | collective-permute-start | bytes 1555208 | tf_op jit(solution)/shard_map/ppermute | solution.py:65
  104.8 1.9 %fusion.23 = f32[192,360]{1,0:T(8,128)S(1)} fusion(f32[360,360]{1,0:T(8,128)} %collective-permute-done.12, f32[16,192,360]{2,1,0:T(8,128)S(1)} %pad_maximum_fusion, s32[]{:T(128)S(6)} %select_n.386), kind=kOutput, calls=%fused_computation.32 | convolution fusion | flops 298598400 | bytes 1089796 | tf_op jit(solution)/shard_map/dot_general | solution.py:50
  117.3 1.9 %collective-permute-start.18 = (f32[360,360]{1,0:T(8,128)S(1)}, f32[360,360]{1,0:T(8,128)S(1)}, u32[]{:S(2)}, u32[]{:S(2)}) collective-permute-start(f32[360,360]{1,0:T(8,128)S(1)} %collective-permute-done.16), channel_id=1, source_target_pairs={{0,32},{32,64},{64,96},{96,128},{128,160},{160,192},{192,224},{224... | collective-permute-start | bytes 1555208 | tf_op jit(solution)/shard_map/ppermute | solution.py:63
  119.2 5.3 %collective-permute-start.19 = (f32[360,360]{1,0:T(8,128)S(1)}, f32[360,360]{1,0:T(8,128)S(1)}, u32[]{:S(2)}, u32[]{:S(2)}) collective-permute-start(f32[360,360]{1,0:T(8,128)S(1)} %collective-permute-done.17), channel_id=1, source_target_pairs={{0,480},{32,0},{64,32},{96,64},{128,96},{160,128},{192,160},{224,1... | collective-permute-start | bytes 1555208 | tf_op jit(solution)/shard_map/ppermute | solution.py:65
  125.3 1.8 %fusion.2 = f32[192,360]{1,0:T(8,128)S(1)} fusion(f32[192,360]{1,0:T(8,128)S(1)} %fusion.17, f32[192,360]{1,0:T(8,128)S(1)} %fusion.1, f32[360,360]{1,0:T(8,128)} %collective-permute-done.9, f32[16,192,360]{2,1,0:T(8,128)S(1)} %pad_maximum_fusion, s32[]{:T(128)S(6)} %select_n.401), kind=kOutput, calls=%fused_computation.10 | convolution fusion | flops 298736640 | bytes 1679620 | tf_op jit(solution)/shard_map/dot_general | solution.py:50
  127.9 1.8 %fusion.5 = f32[192,360]{1,0:T(8,128)S(1)} fusion(f32[192,360]{1,0:T(8,128)S(1)} %fusion.10, f32[192,360]{1,0:T(8,128)S(1)} %fusion.12, f32[192,360]{1,0:T(8,128)S(1)} %fusion.14, f32[192,360]{1,0:T(8,128)S(1)} %fusion.2, f32[360,360]{1,0:T(8,128)} %collective-permute-done.10, f32[16,192,360]{2,1,0:T(8,128)S(1)} %pad_maximum_fusion, s32[]{:T(128)S(6)} %select_n.411), kind=kOutput, calls=%fused_computation.13 | convolution fusion | flops 298874880 | bytes 2269444 | tf_op jit(solution)/shard_map/dot_general | solution.py:50
  131.4 1.9 %collective-permute-start.20 = (f32[180,360]{1,0:T(8,128)S(1)}, f32[180,360]{1,0:T(8,128)S(1)}, u32[]{:S(2)}, u32[]{:S(2)}) collective-permute-start(f32[180,360]{1,0:T(8,128)S(1)} %slice.26), channel_id=1, source_target_pairs={{0,32},{32,64},{64,96},{96,128},{128,160},{160,192},{192,224},{224... | collective-permute-start | bytes 777608 | tf_op jit(solution)/shard_map/ppermute | solution.py:69
  133.4 5.6 %collective-permute-start.21 = (f32[180,360]{1,0:T(8,128)S(1)}, f32[180,360]{1,0:T(8,128)S(1)}, u32[]{:S(2)}, u32[]{:S(2)}) collective-permute-start(f32[180,360]{1,0:T(8,128)S(1)} %slice.27), channel_id=1, source_target_pairs={{0,480},{32,0},{64,32},{96,64},{128,96},{160,128},{192,160},{224,1... | collective-permute-start | bytes 777608 | tf_op jit(solution)/shard_map/ppermute | solution.py:70
  143.8 3.0 %collective-permute-start.22 = (f32[96,360]{1,0:T(8,128)S(1)}, f32[96,360]{1,0:T(8,128)S(1)}, u32[]{:S(2)}, u32[]{:S(2)}) collective-permute-start(f32[96,360]{1,0:T(8,128)S(1)} %add_add_fusion.1), channel_id=1, source_target_pairs={{0,1},{1,0},{2,3},{3,2},{4,5},{5,4},{6,7},{7,6},{8,9},{9,8},{10,11... | collective-permute-start | bytes 414728 | tf_op jit(solution)/shard_map/ppermute | solution.py:87
  147.5 4.8 %collective-permute-done.22 = f32[96,360]{1,0:T(8,128)S(1)} collective-permute-done((f32[96,360]{1,0:T(8,128)S(1)}, f32[96,360]{1,0:T(8,128)S(1)}, u32[]{:S(2)}, u32[]{:S(2)}) %collective-permute-start.22) | collective-permute-done | bytes 138272 | tf_op jit(solution)/shard_map/ppermute | solution.py:87
  (52 shorter events, 28.4 us)
Async XLA Ops:
  0.0 3.7 %collective-permute-start = (f32[192,360]{1,0:T(8,128)}, f32[192,360]{1,0:T(8,128)S(1)}, u32[]{:S(2)}, u32[]{:S(2)}) collective-permute-start(f32[192,360]{1,0:T(8,128)} %param.2), channel_id=1, source_target_pairs={{0,2},{2,0},{4,6},{6,4},{8,10},{10,8},{12,14},{14,12},{16,18},{18,... | collective-permute-start | bytes 829448 | tf_op jit(solution)/shard_map/ppermute | solution.py:15
  4.8 34.1 %collective-permute-start.1 = (f32[2,192,360]{2,1,0:T(8,128)S(1)}, f32[2,192,360]{2,1,0:T(8,128)S(1)}, u32[]{:S(2)}, u32[]{:S(2)}) collective-permute-start(f32[2,192,360]{2,1,0:T(8,128)S(1)} %maximum_select_fusion.1), channel_id=1, source_target_pairs={{0,4},{2,6},{4,0},{6,2},{8,12},{10,14},{12,8},{14,10},{16,20},{18,... | collective-permute-start | bytes 1658888 | tf_op jit(solution)/shard_map/ppermute | solution.py:17
  7.5 24.3 %collective-permute-start.6 = (f32[360,360]{1,0:T(8,128)}, f32[360,360]{1,0:T(8,128)}, u32[]{:S(2)}, u32[]{:S(2)}) collective-permute-start(f32[360,360]{1,0:T(8,128)} %param.3), channel_id=1, source_target_pairs={{0,32},{32,64},{64,96},{96,128},{128,160},{160,192},{192,224},{224... | collective-permute-start | bytes 1555208 | tf_op jit(solution)/shard_map/ppermute | solution.py:63
  11.4 22.4 %collective-permute-start.11 = (f32[360,360]{1,0:T(8,128)}, f32[360,360]{1,0:T(8,128)}, u32[]{:S(2)}, u32[]{:S(2)}) collective-permute-start(f32[360,360]{1,0:T(8,128)} %param.3), channel_id=1, source_target_pairs={{0,480},{32,0},{64,32},{96,64},{128,96},{160,128},{192,160},{224,1... | collective-permute-start | bytes 1555208 | tf_op jit(solution)/shard_map/ppermute | solution.py:65
  31.8 17.2 %collective-permute-start.7 = (f32[360,360]{1,0:T(8,128)}, f32[360,360]{1,0:T(8,128)}, u32[]{:S(2)}, u32[]{:S(2)}) collective-permute-start(f32[360,360]{1,0:T(8,128)} %collective-permute-done.6), channel_id=1, source_target_pairs={{0,32},{32,64},{64,96},{96,128},{128,160},{160,192},{192,224},{224... | collective-permute-start | bytes 1555208 | tf_op jit(solution)/shard_map/ppermute | solution.py:63
  33.7 17.2 %collective-permute-start.12 = (f32[360,360]{1,0:T(8,128)}, f32[360,360]{1,0:T(8,128)}, u32[]{:S(2)}, u32[]{:S(2)}) collective-permute-start(f32[360,360]{1,0:T(8,128)} %collective-permute-done.11), channel_id=1, source_target_pairs={{0,480},{32,0},{64,32},{96,64},{128,96},{160,128},{192,160},{224,1... | collective-permute-start | bytes 1555208 | tf_op jit(solution)/shard_map/ppermute | solution.py:65
  39.0 33.2 %collective-permute-start.3 = (f32[4,192,360]{2,1,0:T(8,128)S(1)}, f32[4,192,360]{2,1,0:T(8,128)S(1)}, u32[]{:S(2)}, u32[]{:S(2)}) collective-permute-start(f32[4,192,360]{2,1,0:T(8,128)S(1)} %maximum_select_fusion), channel_id=1, source_target_pairs={{0,8},{2,10},{4,12},{6,14},{8,16},{10,18},{12,20},{14,22},{16,24},... | collective-permute-start | bytes 3317768 | tf_op jit(solution)/shard_map/ppermute | solution.py:21
  42.5 34.0 %collective-permute-start.2 = (f32[4,192,360]{2,1,0:T(8,128)S(1)}, f32[4,192,360]{2,1,0:T(8,128)S(1)}, u32[]{:S(2)}, u32[]{:S(2)}) collective-permute-start(f32[4,192,360]{2,1,0:T(8,128)S(1)} %maximum_select_fusion), channel_id=1, source_target_pairs={{0,24},{2,26},{4,28},{6,30},{8,0},{10,2},{12,4},{14,6},{16,8},{18,... | collective-permute-start | bytes 3317768 | tf_op jit(solution)/shard_map/ppermute | solution.py:22
  49.0 16.1 %collective-permute-start.8 = (f32[360,360]{1,0:T(8,128)}, f32[360,360]{1,0:T(8,128)S(1)}, u32[]{:S(2)}, u32[]{:S(2)}) collective-permute-start(f32[360,360]{1,0:T(8,128)} %collective-permute-done.7), channel_id=1, source_target_pairs={{0,32},{32,64},{64,96},{96,128},{128,160},{160,192},{192,224},{224... | collective-permute-start | bytes 1555208 | tf_op jit(solution)/shard_map/ppermute | solution.py:63
  50.9 16.1 %collective-permute-start.13 = (f32[360,360]{1,0:T(8,128)}, f32[360,360]{1,0:T(8,128)S(1)}, u32[]{:S(2)}, u32[]{:S(2)}) collective-permute-start(f32[360,360]{1,0:T(8,128)} %collective-permute-done.12), channel_id=1, source_target_pairs={{0,480},{32,0},{64,32},{96,64},{128,96},{160,128},{192,160},{224,1... | collective-permute-start | bytes 1555208 | tf_op jit(solution)/shard_map/ppermute | solution.py:65
  65.1 11.4 %copy-start = (f32[360,360]{1,0:T(8,128)}, f32[360,360]{1,0:T(8,128)S(1)}, u32[]{:S(2)}) copy-start(f32[360,360]{1,0:T(8,128)S(1)} %collective-permute-done.8) | copy-start | bytes 1555204
  65.1 15.9 %collective-permute-start.9 = (f32[360,360]{1,0:T(8,128)S(1)}, f32[360,360]{1,0:T(8,128)}, u32[]{:S(2)}, u32[]{:S(2)}) collective-permute-start(f32[360,360]{1,0:T(8,128)S(1)} %collective-permute-done.8), channel_id=1, source_target_pairs={{0,32},{32,64},{64,96},{96,128},{128,160},{160,192},{192,224},{224... | collective-permute-start | bytes 1555208 | tf_op jit(solution)/shard_map/ppermute | solution.py:63
  67.0 14.0 %copy-start.3 = (f32[360,360]{1,0:T(8,128)}, f32[360,360]{1,0:T(8,128)S(1)}, u32[]{:S(2)}) copy-start(f32[360,360]{1,0:T(8,128)S(1)} %collective-permute-done.13) | copy-start | bytes 1555204
  67.0 15.9 %collective-permute-start.14 = (f32[360,360]{1,0:T(8,128)S(1)}, f32[360,360]{1,0:T(8,128)}, u32[]{:S(2)}, u32[]{:S(2)}) collective-permute-start(f32[360,360]{1,0:T(8,128)S(1)} %collective-permute-done.13), channel_id=1, source_target_pairs={{0,480},{32,0},{64,32},{96,64},{128,96},{160,128},{192,160},{224,1... | collective-permute-start | bytes 1555208 | tf_op jit(solution)/shard_map/ppermute | solution.py:65
  73.0 16.0 %collective-permute-start.4 = (f32[4,96,360]{2,1,0:T(8,128)}, f32[4,96,360]{2,1,0:T(8,128)}, u32[]{:S(2)}, u32[]{:S(2)}) collective-permute-start(f32[4,96,360]{2,1,0:T(8,128)} %slice.32), channel_id=1, source_target_pairs={{0,8},{2,10},{4,12},{6,14},{8,16},{10,18},{12,20},{14,22},{16,24},... | collective-permute-start | bytes 1658888 | tf_op jit(solution)/shard_map/ppermute | solution.py:24
  77.4 14.1 %collective-permute-start.5 = (f32[4,96,360]{2,1,0:T(8,128)}, f32[4,96,360]{2,1,0:T(8,128)}, u32[]{:S(2)}, u32[]{:S(2)}) collective-permute-start(f32[4,96,360]{2,1,0:T(8,128)} %slice.33), channel_id=1, source_target_pairs={{0,24},{2,26},{4,28},{6,30},{8,0},{10,2},{12,4},{14,6},{16,8},{18,... | collective-permute-start | bytes 1658888 | tf_op jit(solution)/shard_map/ppermute | solution.py:25
  81.0 14.3 %collective-permute-start.10 = (f32[360,360]{1,0:T(8,128)}, f32[360,360]{1,0:T(8,128)}, u32[]{:S(2)}, u32[]{:S(2)}) collective-permute-start(f32[360,360]{1,0:T(8,128)} %collective-permute-done.9), channel_id=1, source_target_pairs={{0,32},{32,64},{64,96},{96,128},{128,160},{160,192},{192,224},{224... | collective-permute-start | bytes 1555208 | tf_op jit(solution)/shard_map/ppermute | solution.py:63
  82.9 13.5 %collective-permute-start.15 = (f32[360,360]{1,0:T(8,128)}, f32[360,360]{1,0:T(8,128)}, u32[]{:S(2)}, u32[]{:S(2)}) collective-permute-start(f32[360,360]{1,0:T(8,128)} %collective-permute-done.14), channel_id=1, source_target_pairs={{0,480},{32,0},{64,32},{96,64},{128,96},{160,128},{192,160},{224,1... | collective-permute-start | bytes 1555208 | tf_op jit(solution)/shard_map/ppermute | solution.py:65
  89.1 14.9 %copy-start.2 = (f32[360,360]{1,0:T(8,128)S(1)}, f32[360,360]{1,0:T(8,128)}, u32[]{:S(2)}) copy-start(f32[360,360]{1,0:T(8,128)} %param.3) | copy-start | bytes 1555204
  89.1 17.6 %copy-start.4 = (f32[360,360]{1,0:T(8,128)S(1)}, f32[360,360]{1,0:T(8,128)}, u32[]{:S(2)}) copy-start(f32[360,360]{1,0:T(8,128)} %copy-done.3) | copy-start | bytes 1555204
  96.5 20.8 %collective-permute-start.16 = (f32[360,360]{1,0:T(8,128)}, f32[360,360]{1,0:T(8,128)S(1)}, u32[]{:S(2)}, u32[]{:S(2)}) collective-permute-start(f32[360,360]{1,0:T(8,128)} %collective-permute-done.10), channel_id=1, source_target_pairs={{0,32},{32,64},{64,96},{96,128},{128,160},{160,192},{192,224},{224... | collective-permute-start | bytes 1555208 | tf_op jit(solution)/shard_map/ppermute | solution.py:63
  98.4 18.9 %collective-permute-start.17 = (f32[360,360]{1,0:T(8,128)}, f32[360,360]{1,0:T(8,128)S(1)}, u32[]{:S(2)}, u32[]{:S(2)}) collective-permute-start(f32[360,360]{1,0:T(8,128)} %collective-permute-done.15), channel_id=1, source_target_pairs={{0,480},{32,0},{64,32},{96,64},{128,96},{160,128},{192,160},{224,1... | collective-permute-start | bytes 1555208 | tf_op jit(solution)/shard_map/ppermute | solution.py:65
  104.8 11.7 %copy-start.1 = (f32[360,360]{1,0:T(8,128)S(1)}, f32[360,360]{1,0:T(8,128)}, u32[]{:S(2)}) copy-start(f32[360,360]{1,0:T(8,128)} %copy-done) | copy-start | bytes 1555204
  117.3 12.6 %collective-permute-start.18 = (f32[360,360]{1,0:T(8,128)S(1)}, f32[360,360]{1,0:T(8,128)S(1)}, u32[]{:S(2)}, u32[]{:S(2)}) collective-permute-start(f32[360,360]{1,0:T(8,128)S(1)} %collective-permute-done.16), channel_id=1, source_target_pairs={{0,32},{32,64},{64,96},{96,128},{128,160},{160,192},{192,224},{224... | collective-permute-start | bytes 1555208 | tf_op jit(solution)/shard_map/ppermute | solution.py:63
  119.2 12.1 %collective-permute-start.19 = (f32[360,360]{1,0:T(8,128)S(1)}, f32[360,360]{1,0:T(8,128)S(1)}, u32[]{:S(2)}, u32[]{:S(2)}) collective-permute-start(f32[360,360]{1,0:T(8,128)S(1)} %collective-permute-done.17), channel_id=1, source_target_pairs={{0,480},{32,0},{64,32},{96,64},{128,96},{160,128},{192,160},{224,1... | collective-permute-start | bytes 1555208 | tf_op jit(solution)/shard_map/ppermute | solution.py:65
  131.4 10.2 %collective-permute-start.20 = (f32[180,360]{1,0:T(8,128)S(1)}, f32[180,360]{1,0:T(8,128)S(1)}, u32[]{:S(2)}, u32[]{:S(2)}) collective-permute-start(f32[180,360]{1,0:T(8,128)S(1)} %slice.26), channel_id=1, source_target_pairs={{0,32},{32,64},{64,96},{96,128},{128,160},{160,192},{192,224},{224... | collective-permute-start | bytes 777608 | tf_op jit(solution)/shard_map/ppermute | solution.py:69
  133.4 9.7 %collective-permute-start.21 = (f32[180,360]{1,0:T(8,128)S(1)}, f32[180,360]{1,0:T(8,128)S(1)}, u32[]{:S(2)}, u32[]{:S(2)}) collective-permute-start(f32[180,360]{1,0:T(8,128)S(1)} %slice.27), channel_id=1, source_target_pairs={{0,480},{32,0},{64,32},{96,64},{128,96},{160,128},{192,160},{224,1... | collective-permute-start | bytes 777608 | tf_op jit(solution)/shard_map/ppermute | solution.py:70
  143.8 8.5 %collective-permute-start.22 = (f32[96,360]{1,0:T(8,128)S(1)}, f32[96,360]{1,0:T(8,128)S(1)}, u32[]{:S(2)}, u32[]{:S(2)}) collective-permute-start(f32[96,360]{1,0:T(8,128)S(1)} %add_add_fusion.1), channel_id=1, source_target_pairs={{0,1},{1,0},{2,3},{3,2},{4,5},{5,4},{6,7},{7,6},{8,9},{9,8},{10,11... | collective-permute-start | bytes 414728 | tf_op jit(solution)/shard_map/ppermute | solution.py:87

commit v20 on v17

--- a/solution.py
+++ b/solution.py
@@ -3,8 +3,8 @@
 from jax import lax
 from jax.sharding import PartitionSpec as P
 
-FIRST_DOT_STEP = 6
-DOTS_PER_STEP = 5
+FIRST_DOT_STEP = 5
+DOTS_AT_STEP = {5: 2, 6: 5, 7: 5, 8: 3}
 
 
 def gather_col(block):
@@ -72,10 +72,11 @@
             arrived.append((bottom, (me - step) % n, m, kb))
             ahead, behind = top, bottom
         if step >= FIRST_DOT_STEP:
-            for block, owner, lo, hi in pending[:DOTS_PER_STEP]:
+            count = DOTS_AT_STEP[step]
+            for block, owner, lo, hi in pending[:count]:
                 part = product(block, owner, lo, hi)
                 total = part if total is None else total + part
-            pending = pending[DOTS_PER_STEP:]
+            pending = pending[count:]
             total, ahead, behind = lax.optimization_barrier((total, ahead, behind))
         pending = pending + arrived
     mine = lax.dynamic_slice_in_dim(total, d * half, half, axis=0)

time: 155 us -> 154 us (level)
    ppermute x7, waiting for transfers between devices: 27.1 us -> 24.5 us  [local(): ahead = lax.ppermute(ahead, 'row', fwd)]
  transfers between devices with their start and end apart: 23 -> 23, of which waited for: 11 -> 12; matrix products, arithmetic and copies ran while one was open for 15% -> 15% of each run, Pallas kernels for 0% -> 0%
where the time goes in v20:
time: 154 us; the launch traced here: 153 us
  starting transfers between devices  89.5 us (58%)
  waiting for transfers between devices  37 us (24%)
  matrix products  19.2 us (12%)
  other arithmetic  3.97 us (3%)
  local copies, waits for them, and re-layouts  1.82 us (1%)
    ppermute x7, starting transfers between devices, local(): behind = lax.ppermute(behind, 'row', bwd)  44.6 us
    ppermute x7, waiting for transfers between devices, local(): ahead = lax.ppermute(ahead, 'row', fwd)  24.5 us
    dot_general x19, matrix products, product(): jnp.dot(cols[:, lo:hi], block, precision=lax.Precision.HIGHEST, preferred...  19.2 us
    ppermute x7, starting transfers between devices, local(): ahead = lax.ppermute(ahead, 'row', fwd)  15.3 us
    ppermute x1, starting transfers between devices, local(): bottom = lax.ppermute(behind[m:], 'row', bwd)  5.6 us
    ppermute x1, starting transfers between devices, gather_col(): opp_b = lax.ppermute(above[:, h:], 'col', down)  4.84 us
    ppermute x1, waiting for transfers between devices, local(): other = lax.ppermute(other, 'depth', [(0, 1), (1, 0)])  4.51 us
    ppermute x1, starting transfers between devices, gather_col(): above = lax.ppermute(quad, 'col', down)  3.57 us
  transfers between devices with their start and end apart: 23, of which 12 were waited for; matrix products, arithmetic and copies ran while one was open for 15% of the time, Pallas kernels for 0%

profile of v20, /device:TPU:6, one launch (start us, length us, event | category | flops | bytes accessed | tf_op | source)
XLA Modules:
  0.0 153.0 jit_solution(17013728060530585788)
XLA Ops:
  0.0 1.9 %collective-permute-start = (f32[192,360]{1,0:T(8,128)}, f32[192,360]{1,0:T(8,128)S(1)}, u32[]{:S(2)}, u32[]{:S(2)}) collective-permute-start(f32[192,360]{1,0:T(8,128)} %param.2), channel_id=1, source_target_pairs={{0,2},{2,0},{4,6},{6,4},{8,10},{10,8},{12,14},{14,12},{16,18},{18,... | collective-permute-start | bytes 829448 | tf_op jit(solution)/shard_map/ppermute | solution.py:15
  4.8 2.7 %collective-permute-start.1 = (f32[2,192,360]{2,1,0:T(8,128)S(1)}, f32[2,192,360]{2,1,0:T(8,128)S(1)}, u32[]{:S(2)}, u32[]{:S(2)}) collective-permute-start(f32[2,192,360]{2,1,0:T(8,128)S(1)} %maximum_select_fusion.1), channel_id=1, source_target_pairs={{0,4},{2,6},{4,0},{6,2},{8,12},{10,14},{12,8},{14,10},{16,20},{18,... | collective-permute-start | bytes 1658888 | tf_op jit(solution)/shard_map/ppermute | solution.py:17
  7.5 3.8 %collective-permute-start.6 = (f32[360,360]{1,0:T(8,128)}, f32[360,360]{1,0:T(8,128)}, u32[]{:S(2)}, u32[]{:S(2)}) collective-permute-start(f32[360,360]{1,0:T(8,128)} %param.3), channel_id=1, source_target_pairs={{0,32},{32,64},{64,96},{96,128},{128,160},{160,192},{192,224},{224... | collective-permute-start | bytes 1555208 | tf_op jit(solution)/shard_map/ppermute | solution.py:63
  11.4 9.5 %collective-permute-start.11 = (f32[360,360]{1,0:T(8,128)}, f32[360,360]{1,0:T(8,128)}, u32[]{:S(2)}, u32[]{:S(2)}) collective-permute-start(f32[360,360]{1,0:T(8,128)} %param.3), channel_id=1, source_target_pairs={{0,480},{32,0},{64,32},{96,64},{128,96},{160,128},{192,160},{224,1... | collective-permute-start | bytes 1555208 | tf_op jit(solution)/shard_map/ppermute | solution.py:65
  22.1 3.5 %collective-permute-start.3 = (f32[4,192,360]{2,1,0:T(8,128)S(1)}, f32[4,192,360]{2,1,0:T(8,128)S(1)}, u32[]{:S(2)}, u32[]{:S(2)}) collective-permute-start(f32[4,192,360]{2,1,0:T(8,128)S(1)} %maximum_select_fusion), channel_id=1, source_target_pairs={{0,8},{2,10},{4,12},{6,14},{8,16},{10,18},{12,20},{14,22},{16,24},... | collective-permute-start | bytes 3317768 | tf_op jit(solution)/shard_map/ppermute | solution.py:21
  25.6 3.6 %collective-permute-start.2 = (f32[4,192,360]{2,1,0:T(8,128)S(1)}, f32[4,192,360]{2,1,0:T(8,128)S(1)}, u32[]{:S(2)}, u32[]{:S(2)}) collective-permute-start(f32[4,192,360]{2,1,0:T(8,128)S(1)} %maximum_select_fusion), channel_id=1, source_target_pairs={{0,24},{2,26},{4,28},{6,30},{8,0},{10,2},{12,4},{14,6},{16,8},{18,... | collective-permute-start | bytes 3317768 | tf_op jit(solution)/shard_map/ppermute | solution.py:22
  29.2 2.6 %collective-permute-done.6 = f32[360,360]{1,0:T(8,128)} collective-permute-done((f32[360,360]{1,0:T(8,128)}, f32[360,360]{1,0:T(8,128)}, u32[]{:S(2)}, u32[]{:S(2)}) %collective-permute-start.6) | collective-permute-done | bytes 518432 | tf_op jit(solution)/shard_map/ppermute | solution.py:63
  31.8 1.9 %collective-permute-start.7 = (f32[360,360]{1,0:T(8,128)}, f32[360,360]{1,0:T(8,128)S(1)}, u32[]{:S(2)}, u32[]{:S(2)}) collective-permute-start(f32[360,360]{1,0:T(8,128)} %collective-permute-done.6), channel_id=1, source_target_pairs={{0,32},{32,64},{64,96},{96,128},{128,160},{160,192},{192,224},{224... | collective-permute-start | bytes 1555208 | tf_op jit(solution)/shard_map/ppermute | solution.py:63
  33.7 8.8 %collective-permute-start.12 = (f32[360,360]{1,0:T(8,128)}, f32[360,360]{1,0:T(8,128)S(1)}, u32[]{:S(2)}, u32[]{:S(2)}) collective-permute-start(f32[360,360]{1,0:T(8,128)} %collective-permute-done.11), channel_id=1, source_target_pairs={{0,480},{32,0},{64,32},{96,64},{128,96},{160,128},{192,160},{224,1... | collective-permute-start | bytes 1555208 | tf_op jit(solution)/shard_map/ppermute | solution.py:65
  42.6 9.9 %collective-permute-done.7 = f32[360,360]{1,0:T(8,128)S(1)} collective-permute-done((f32[360,360]{1,0:T(8,128)}, f32[360,360]{1,0:T(8,128)S(1)}, u32[]{:S(2)}, u32[]{:S(2)}) %collective-permute-start.7) | collective-permute-done | bytes 518432 | tf_op jit(solution)/shard_map/ppermute | solution.py:63
  52.4 1.9 %collective-permute-start.8 = (f32[360,360]{1,0:T(8,128)S(1)}, f32[360,360]{1,0:T(8,128)}, u32[]{:S(2)}, u32[]{:S(2)}) collective-permute-start(f32[360,360]{1,0:T(8,128)S(1)} %collective-permute-done.7), channel_id=1, source_target_pairs={{0,32},{32,64},{64,96},{96,128},{128,160},{160,192},{192,224},{224... | collective-permute-start | bytes 1555208 | tf_op jit(solution)/shard_map/ppermute | solution.py:63
  54.4 5.1 %collective-permute-start.13 = (f32[360,360]{1,0:T(8,128)S(1)}, f32[360,360]{1,0:T(8,128)}, u32[]{:S(2)}, u32[]{:S(2)}) collective-permute-start(f32[360,360]{1,0:T(8,128)S(1)} %collective-permute-done.12), channel_id=1, source_target_pairs={{0,480},{32,0},{64,32},{96,64},{128,96},{160,128},{192,160},{224,1... | collective-permute-start | bytes 1555208 | tf_op jit(solution)/shard_map/ppermute | solution.py:65
  60.4 2.2 %collective-permute-start.4 = (f32[4,96,360]{2,1,0:T(8,128)}, f32[4,96,360]{2,1,0:T(8,128)}, u32[]{:S(2)}, u32[]{:S(2)}) collective-permute-start(f32[4,96,360]{2,1,0:T(8,128)} %slice.32), channel_id=1, source_target_pairs={{0,8},{2,10},{4,12},{6,14},{8,16},{10,18},{12,20},{14,22},{16,24},... | collective-permute-start | bytes 1658888 | tf_op jit(solution)/shard_map/ppermute | solution.py:24
  63.5 4.8 %collective-permute-start.5 = (f32[4,96,360]{2,1,0:T(8,128)}, f32[4,96,360]{2,1,0:T(8,128)}, u32[]{:S(2)}, u32[]{:S(2)}) collective-permute-start(f32[4,96,360]{2,1,0:T(8,128)} %slice.33), channel_id=1, source_target_pairs={{0,24},{2,26},{4,28},{6,30},{8,0},{10,2},{12,4},{14,6},{16,8},{18,... | collective-permute-start | bytes 1658888 | tf_op jit(solution)/shard_map/ppermute | solution.py:25
  68.4 1.9 %collective-permute-start.9 = (f32[360,360]{1,0:T(8,128)}, f32[360,360]{1,0:T(8,128)}, u32[]{:S(2)}, u32[]{:S(2)}) collective-permute-start(f32[360,360]{1,0:T(8,128)} %collective-permute-done.8), channel_id=1, source_target_pairs={{0,32},{32,64},{64,96},{96,128},{128,160},{160,192},{192,224},{224... | collective-permute-start | bytes 1555208 | tf_op jit(solution)/shard_map/ppermute | solution.py:63
  70.3 5.1 %collective-permute-start.14 = (f32[360,360]{1,0:T(8,128)}, f32[360,360]{1,0:T(8,128)}, u32[]{:S(2)}, u32[]{:S(2)}) collective-permute-start(f32[360,360]{1,0:T(8,128)} %collective-permute-done.13), channel_id=1, source_target_pairs={{0,480},{32,0},{64,32},{96,64},{128,96},{160,128},{192,160},{224,1... | collective-permute-start | bytes 1555208 | tf_op jit(solution)/shard_map/ppermute | solution.py:65
  76.4 7.4 %collective-permute-done.9 = f32[360,360]{1,0:T(8,128)} collective-permute-done((f32[360,360]{1,0:T(8,128)}, f32[360,360]{1,0:T(8,128)}, u32[]{:S(2)}, u32[]{:S(2)}) %collective-permute-start.9) | collective-permute-done | bytes 518432 | tf_op jit(solution)/shard_map/ppermute | solution.py:63
  83.8 1.9 %collective-permute-start.10 = (f32[360,360]{1,0:T(8,128)}, f32[360,360]{1,0:T(8,128)S(1)}, u32[]{:S(2)}, u32[]{:S(2)}) collective-permute-start(f32[360,360]{1,0:T(8,128)} %collective-permute-done.9), channel_id=1, source_target_pairs={{0,32},{32,64},{64,96},{96,128},{128,160},{160,192},{192,224},{224... | collective-permute-start | bytes 1555208 | tf_op jit(solution)/shard_map/ppermute | solution.py:63
  85.7 5.1 %collective-permute-start.15 = (f32[360,360]{1,0:T(8,128)}, f32[360,360]{1,0:T(8,128)S(1)}, u32[]{:S(2)}, u32[]{:S(2)}) collective-permute-start(f32[360,360]{1,0:T(8,128)} %collective-permute-done.14), channel_id=1, source_target_pairs={{0,480},{32,0},{64,32},{96,64},{128,96},{160,128},{192,160},{224,1... | collective-permute-start | bytes 1555208 | tf_op jit(solution)/shard_map/ppermute | solution.py:65
  90.9 2.1 %pad_maximum_fusion = f32[16,192,360]{2,1,0:T(8,128)S(1)} fusion(f32[4,192,360]{2,1,0:T(8,128)S(1)} %collective-permute-done.3, f32[4,96,360]{2,1,0:T(8,128)} %collective-permute-done.5, f32[4,96,360]{2,1,0:T(8,128)} %collective-permute-done.4, f32[4,192,360]{2,1,0:T(8,128)S(1)} %collective-permute-done.2, f32[4,192,360]{2,1,0:T(8,128)S(1)} %maximum_select_fusion), kind=kLoop, calls=%fused_computation | loop fusion | flops 4423680 | bytes 8847360 | tf_op jit(solution)/shard_map/concatenate | solution.py:27
  93.0 1.9 %fusion.25 = f32[192,360]{1,0:T(8,128)S(1)} fusion(f32[360,360]{1,0:T(8,128)} %collective-permute-done.11, f32[16,192,360]{2,1,0:T(8,128)S(1)} %pad_maximum_fusion, s32[]{:T(128)S(6)} %select_n.376), kind=kOutput, calls=%fused_computation.33 | convolution fusion | flops 298598400 | bytes 1089796 | tf_op jit(solution)/shard_map/dot_general | solution.py:50
  95.7 1.8 %fusion.27 = f32[192,360]{1,0:T(8,128)S(1)} fusion(f32[360,360]{1,0:T(8,128)} %collective-permute-done.6, f32[16,192,360]{2,1,0:T(8,128)S(1)} %pad_maximum_fusion, s32[]{:T(128)S(6)} %select_n.371), kind=kOutput, calls=%fused_computation.35 | convolution fusion | flops 298598400 | bytes 1089796 | tf_op jit(solution)/shard_map/dot_general | solution.py:50
  102.0 1.9 %collective-permute-start.16 = (f32[360,360]{1,0:T(8,128)S(1)}, f32[360,360]{1,0:T(8,128)S(1)}, u32[]{:S(2)}, u32[]{:S(2)}) collective-permute-start(f32[360,360]{1,0:T(8,128)S(1)} %collective-permute-done.10), channel_id=1, source_target_pairs={{0,32},{32,64},{64,96},{96,128},{128,160},{160,192},{192,224},{224... | collective-permute-start | bytes 1555208 | tf_op jit(solution)/shard_map/ppermute | solution.py:63
  103.9 5.1 %collective-permute-start.17 = (f32[360,360]{1,0:T(8,128)S(1)}, f32[360,360]{1,0:T(8,128)S(1)}, u32[]{:S(2)}, u32[]{:S(2)}) collective-permute-start(f32[360,360]{1,0:T(8,128)S(1)} %collective-permute-done.15), channel_id=1, source_target_pairs={{0,480},{32,0},{64,32},{96,64},{128,96},{160,128},{192,160},{224,1... | collective-permute-start | bytes 1555208 | tf_op jit(solution)/shard_map/ppermute | solution.py:65
  110.6 1.8 %fusion.1 = f32[192,360]{1,0:T(8,128)S(1)} fusion(f32[192,360]{1,0:T(8,128)S(1)} %fusion.19, f32[192,360]{1,0:T(8,128)S(1)} %fusion, f32[360,360]{1,0:T(8,128)} %collective-permute-done.8, f32[16,192,360]{2,1,0:T(8,128)S(1)} %pad_maximum_fusion, s32[]{:T(128)S(6)} %select_n.391), kind=kOutput, calls=%fused_computation.8 | convolution fusion | flops 298736640 | bytes 1679620 | tf_op jit(solution)/shard_map/dot_general | solution.py:50
  112.4 3.2 %collective-permute-done.16 = f32[360,360]{1,0:T(8,128)S(1)} collective-permute-done((f32[360,360]{1,0:T(8,128)S(1)}, f32[360,360]{1,0:T(8,128)S(1)}, u32[]{:S(2)}, u32[]{:S(2)}) %collective-permute-start.16) | collective-permute-done | bytes 518432 | tf_op jit(solution)/shard_map/ppermute | solution.py:63
  116.8 1.9 %collective-permute-start.18 = (f32[360,360]{1,0:T(8,128)S(1)}, f32[360,360]{1,0:T(8,128)S(1)}, u32[]{:S(2)}, u32[]{:S(2)}) collective-permute-start(f32[360,360]{1,0:T(8,128)S(1)} %collective-permute-done.16), channel_id=1, source_target_pairs={{0,32},{32,64},{64,96},{96,128},{128,160},{160,192},{192,224},{224... | collective-permute-start | bytes 1555208 | tf_op jit(solution)/shard_map/ppermute | solution.py:63
  118.7 5.8 %collective-permute-start.19 = (f32[360,360]{1,0:T(8,128)S(1)}, f32[360,360]{1,0:T(8,128)S(1)}, u32[]{:S(2)}, u32[]{:S(2)}) collective-permute-start(f32[360,360]{1,0:T(8,128)S(1)} %collective-permute-done.17), channel_id=1, source_target_pairs={{0,480},{32,0},{64,32},{96,64},{128,96},{160,128},{192,160},{224,1... | collective-permute-start | bytes 1555208 | tf_op jit(solution)/shard_map/ppermute | solution.py:65
  131.4 1.9 %collective-permute-start.20 = (f32[180,360]{1,0:T(8,128)S(1)}, f32[180,360]{1,0:T(8,128)S(1)}, u32[]{:S(2)}, u32[]{:S(2)}) collective-permute-start(f32[180,360]{1,0:T(8,128)S(1)} %slice.26), channel_id=1, source_target_pairs={{0,32},{32,64},{64,96},{96,128},{128,160},{160,192},{192,224},{224... | collective-permute-start | bytes 777608 | tf_op jit(solution)/shard_map/ppermute | solution.py:69
  133.3 5.6 %collective-permute-start.21 = (f32[180,360]{1,0:T(8,128)S(1)}, f32[180,360]{1,0:T(8,128)S(1)}, u32[]{:S(2)}, u32[]{:S(2)}) collective-permute-start(f32[180,360]{1,0:T(8,128)S(1)} %slice.27), channel_id=1, source_target_pairs={{0,480},{32,0},{64,32},{96,64},{128,96},{160,128},{192,160},{224,1... | collective-permute-start | bytes 777608 | tf_op jit(solution)/shard_map/ppermute | solution.py:70
  143.7 3.3 %collective-permute-start.22 = (f32[96,360]{1,0:T(8,128)S(1)}, f32[96,360]{1,0:T(8,128)S(1)}, u32[]{:S(2)}, u32[]{:S(2)}) collective-permute-start(f32[96,360]{1,0:T(8,128)S(1)} %add_add_fusion.1), channel_id=1, source_target_pairs={{0,1},{1,0},{2,3},{3,2},{4,5},{5,4},{6,7},{7,6},{8,9},{9,8},{10,11... | collective-permute-start | bytes 414728 | tf_op jit(solution)/shard_map/ppermute | solution.py:86
  147.8 4.5 %collective-permute-done.22 = f32[96,360]{1,0:T(8,128)S(1)} collective-permute-done((f32[96,360]{1,0:T(8,128)S(1)}, f32[96,360]{1,0:T(8,128)S(1)}, u32[]{:S(2)}, u32[]{:S(2)}) %collective-permute-start.22) | collective-permute-done | bytes 138272 | tf_op jit(solution)/shard_map/ppermute | solution.py:86
  (52 shorter events, 26.8 us)
Async XLA Ops:
  0.0 3.7 %collective-permute-start = (f32[192,360]{1,0:T(8,128)}, f32[192,360]{1,0:T(8,128)S(1)}, u32[]{:S(2)}, u32[]{:S(2)}) collective-permute-start(f32[192,360]{1,0:T(8,128)} %param.2), channel_id=1, source_target_pairs={{0,2},{2,0},{4,6},{6,4},{8,10},{10,8},{12,14},{14,12},{16,18},{18,... | collective-permute-start | bytes 829448 | tf_op jit(solution)/shard_map/ppermute | solution.py:15
  4.8 17.3 %collective-permute-start.1 = (f32[2,192,360]{2,1,0:T(8,128)S(1)}, f32[2,192,360]{2,1,0:T(8,128)S(1)}, u32[]{:S(2)}, u32[]{:S(2)}) collective-permute-start(f32[2,192,360]{2,1,0:T(8,128)S(1)} %maximum_select_fusion.1), channel_id=1, source_target_pairs={{0,4},{2,6},{4,0},{6,2},{8,12},{10,14},{12,8},{14,10},{16,20},{18,... | collective-permute-start | bytes 1658888 | tf_op jit(solution)/shard_map/ppermute | solution.py:17
  7.5 24.3 %collective-permute-start.6 = (f32[360,360]{1,0:T(8,128)}, f32[360,360]{1,0:T(8,128)}, u32[]{:S(2)}, u32[]{:S(2)}) collective-permute-start(f32[360,360]{1,0:T(8,128)} %param.3), channel_id=1, source_target_pairs={{0,32},{32,64},{64,96},{96,128},{128,160},{160,192},{192,224},{224... | collective-permute-start | bytes 1555208 | tf_op jit(solution)/shard_map/ppermute | solution.py:63
  11.4 22.4 %collective-permute-start.11 = (f32[360,360]{1,0:T(8,128)}, f32[360,360]{1,0:T(8,128)}, u32[]{:S(2)}, u32[]{:S(2)}) collective-permute-start(f32[360,360]{1,0:T(8,128)} %param.3), channel_id=1, source_target_pairs={{0,480},{32,0},{64,32},{96,64},{128,96},{160,128},{192,160},{224,1... | collective-permute-start | bytes 1555208 | tf_op jit(solution)/shard_map/ppermute | solution.py:65
  22.1 37.4 %collective-permute-start.3 = (f32[4,192,360]{2,1,0:T(8,128)S(1)}, f32[4,192,360]{2,1,0:T(8,128)S(1)}, u32[]{:S(2)}, u32[]{:S(2)}) collective-permute-start(f32[4,192,360]{2,1,0:T(8,128)S(1)} %maximum_select_fusion), channel_id=1, source_target_pairs={{0,8},{2,10},{4,12},{6,14},{8,16},{10,18},{12,20},{14,22},{16,24},... | collective-permute-start | bytes 3317768 | tf_op jit(solution)/shard_map/ppermute | solution.py:21
  25.6 37.0 %collective-permute-start.2 = (f32[4,192,360]{2,1,0:T(8,128)S(1)}, f32[4,192,360]{2,1,0:T(8,128)S(1)}, u32[]{:S(2)}, u32[]{:S(2)}) collective-permute-start(f32[4,192,360]{2,1,0:T(8,128)S(1)} %maximum_select_fusion), channel_id=1, source_target_pairs={{0,24},{2,26},{4,28},{6,30},{8,0},{10,2},{12,4},{14,6},{16,8},{18,... | collective-permute-start | bytes 3317768 | tf_op jit(solution)/shard_map/ppermute | solution.py:22
  31.8 20.6 %collective-permute-start.7 = (f32[360,360]{1,0:T(8,128)}, f32[360,360]{1,0:T(8,128)S(1)}, u32[]{:S(2)}, u32[]{:S(2)}) collective-permute-start(f32[360,360]{1,0:T(8,128)} %collective-permute-done.6), channel_id=1, source_target_pairs={{0,32},{32,64},{64,96},{96,128},{128,160},{160,192},{192,224},{224... | collective-permute-start | bytes 1555208 | tf_op jit(solution)/shard_map/ppermute | solution.py:63
  33.7 20.6 %collective-permute-start.12 = (f32[360,360]{1,0:T(8,128)}, f32[360,360]{1,0:T(8,128)S(1)}, u32[]{:S(2)}, u32[]{:S(2)}) collective-permute-start(f32[360,360]{1,0:T(8,128)} %collective-permute-done.11), channel_id=1, source_target_pairs={{0,480},{32,0},{64,32},{96,64},{128,96},{160,128},{192,160},{224,1... | collective-permute-start | bytes 1555208 | tf_op jit(solution)/shard_map/ppermute | solution.py:65
  52.4 10.2 %copy-start = (f32[360,360]{1,0:T(8,128)}, f32[360,360]{1,0:T(8,128)S(1)}, u32[]{:S(2)}) copy-start(f32[360,360]{1,0:T(8,128)S(1)} %collective-permute-done.7) | copy-start | bytes 1555204
  52.4 15.9 %collective-permute-start.8 = (f32[360,360]{1,0:T(8,128)S(1)}, f32[360,360]{1,0:T(8,128)}, u32[]{:S(2)}, u32[]{:S(2)}) collective-permute-start(f32[360,360]{1,0:T(8,128)S(1)} %collective-permute-done.7), channel_id=1, source_target_pairs={{0,32},{32,64},{64,96},{96,128},{128,160},{160,192},{192,224},{224... | collective-permute-start | bytes 1555208 | tf_op jit(solution)/shard_map/ppermute | solution.py:63
  54.4 14.0 %copy-start.3 = (f32[360,360]{1,0:T(8,128)}, f32[360,360]{1,0:T(8,128)S(1)}, u32[]{:S(2)}) copy-start(f32[360,360]{1,0:T(8,128)S(1)} %collective-permute-done.12) | copy-start | bytes 1555204
  54.4 15.9 %collective-permute-start.13 = (f32[360,360]{1,0:T(8,128)S(1)}, f32[360,360]{1,0:T(8,128)}, u32[]{:S(2)}, u32[]{:S(2)}) collective-permute-start(f32[360,360]{1,0:T(8,128)S(1)} %collective-permute-done.12), channel_id=1, source_target_pairs={{0,480},{32,0},{64,32},{96,64},{128,96},{160,128},{192,160},{224,1... | collective-permute-start | bytes 1555208 | tf_op jit(solution)/shard_map/ppermute | solution.py:65
  60.4 30.5 %collective-permute-start.4 = (f32[4,96,360]{2,1,0:T(8,128)}, f32[4,96,360]{2,1,0:T(8,128)}, u32[]{:S(2)}, u32[]{:S(2)}) collective-permute-start(f32[4,96,360]{2,1,0:T(8,128)} %slice.32), channel_id=1, source_target_pairs={{0,8},{2,10},{4,12},{6,14},{8,16},{10,18},{12,20},{14,22},{16,24},... | collective-permute-start | bytes 1658888 | tf_op jit(solution)/shard_map/ppermute | solution.py:24
  63.5 27.4 %collective-permute-start.5 = (f32[4,96,360]{2,1,0:T(8,128)}, f32[4,96,360]{2,1,0:T(8,128)}, u32[]{:S(2)}, u32[]{:S(2)}) collective-permute-start(f32[4,96,360]{2,1,0:T(8,128)} %slice.33), channel_id=1, source_target_pairs={{0,24},{2,26},{4,28},{6,30},{8,0},{10,2},{12,4},{14,6},{16,8},{18,... | collective-permute-start | bytes 1658888 | tf_op jit(solution)/shard_map/ppermute | solution.py:25
  68.4 15.4 %collective-permute-start.9 = (f32[360,360]{1,0:T(8,128)}, f32[360,360]{1,0:T(8,128)}, u32[]{:S(2)}, u32[]{:S(2)}) collective-permute-start(f32[360,360]{1,0:T(8,128)} %collective-permute-done.8), channel_id=1, source_target_pairs={{0,32},{32,64},{64,96},{96,128},{128,160},{160,192},{192,224},{224... | collective-permute-start | bytes 1555208 | tf_op jit(solution)/shard_map/ppermute | solution.py:63
  70.3 15.4 %collective-permute-start.14 = (f32[360,360]{1,0:T(8,128)}, f32[360,360]{1,0:T(8,128)}, u32[]{:S(2)}, u32[]{:S(2)}) collective-permute-start(f32[360,360]{1,0:T(8,128)} %collective-permute-done.13), channel_id=1, source_target_pairs={{0,480},{32,0},{64,32},{96,64},{128,96},{160,128},{192,160},{224,1... | collective-permute-start | bytes 1555208 | tf_op jit(solution)/shard_map/ppermute | solution.py:65
  76.4 18.5 %copy-start.4 = (f32[360,360]{1,0:T(8,128)S(1)}, f32[360,360]{1,0:T(8,128)}, u32[]{:S(2)}) copy-start(f32[360,360]{1,0:T(8,128)} %copy-done.3) | copy-start | bytes 1555204
  83.8 18.1 %collective-permute-start.10 = (f32[360,360]{1,0:T(8,128)}, f32[360,360]{1,0:T(8,128)S(1)}, u32[]{:S(2)}, u32[]{:S(2)}) collective-permute-start(f32[360,360]{1,0:T(8,128)} %collective-permute-done.9), channel_id=1, source_target_pairs={{0,32},{32,64},{64,96},{96,128},{128,160},{160,192},{192,224},{224... | collective-permute-start | bytes 1555208 | tf_op jit(solution)/shard_map/ppermute | solution.py:63
  85.7 16.2 %collective-permute-start.15 = (f32[360,360]{1,0:T(8,128)}, f32[360,360]{1,0:T(8,128)S(1)}, u32[]{:S(2)}, u32[]{:S(2)}) collective-permute-start(f32[360,360]{1,0:T(8,128)} %collective-permute-done.14), channel_id=1, source_target_pairs={{0,480},{32,0},{64,32},{96,64},{128,96},{160,128},{192,160},{224,1... | collective-permute-start | bytes 1555208 | tf_op jit(solution)/shard_map/ppermute | solution.py:65
  93.0 8.2 %copy-start.2 = (f32[360,360]{1,0:T(8,128)S(1)}, f32[360,360]{1,0:T(8,128)}, u32[]{:S(2)}) copy-start(f32[360,360]{1,0:T(8,128)} %param.3) | copy-start | bytes 1555204
  93.0 16.8 %copy-start.1 = (f32[360,360]{1,0:T(8,128)S(1)}, f32[360,360]{1,0:T(8,128)}, u32[]{:S(2)}) copy-start(f32[360,360]{1,0:T(8,128)} %copy-done) | copy-start | bytes 1555204
  102.0 13.7 %collective-permute-start.16 = (f32[360,360]{1,0:T(8,128)S(1)}, f32[360,360]{1,0:T(8,128)S(1)}, u32[]{:S(2)}, u32[]{:S(2)}) collective-permute-start(f32[360,360]{1,0:T(8,128)S(1)} %collective-permute-done.10), channel_id=1, source_target_pairs={{0,32},{32,64},{64,96},{96,128},{128,160},{160,192},{192,224},{224... | collective-permute-start | bytes 1555208 | tf_op jit(solution)/shard_map/ppermute | solution.py:63
  103.9 12.9 %collective-permute-start.17 = (f32[360,360]{1,0:T(8,128)S(1)}, f32[360,360]{1,0:T(8,128)S(1)}, u32[]{:S(2)}, u32[]{:S(2)}) collective-permute-start(f32[360,360]{1,0:T(8,128)S(1)} %collective-permute-done.15), channel_id=1, source_target_pairs={{0,480},{32,0},{64,32},{96,64},{128,96},{160,128},{192,160},{224,1... | collective-permute-start | bytes 1555208 | tf_op jit(solution)/shard_map/ppermute | solution.py:65
  116.8 13.2 %collective-permute-start.18 = (f32[360,360]{1,0:T(8,128)S(1)}, f32[360,360]{1,0:T(8,128)S(1)}, u32[]{:S(2)}, u32[]{:S(2)}) collective-permute-start(f32[360,360]{1,0:T(8,128)S(1)} %collective-permute-done.16), channel_id=1, source_target_pairs={{0,32},{32,64},{64,96},{96,128},{128,160},{160,192},{192,224},{224... | collective-permute-start | bytes 1555208 | tf_op jit(solution)/shard_map/ppermute | solution.py:63
  118.7 12.6 %collective-permute-start.19 = (f32[360,360]{1,0:T(8,128)S(1)}, f32[360,360]{1,0:T(8,128)S(1)}, u32[]{:S(2)}, u32[]{:S(2)}) collective-permute-start(f32[360,360]{1,0:T(8,128)S(1)} %collective-permute-done.17), channel_id=1, source_target_pairs={{0,480},{32,0},{64,32},{96,64},{128,96},{160,128},{192,160},{224,1... | collective-permute-start | bytes 1555208 | tf_op jit(solution)/shard_map/ppermute | solution.py:65
  131.4 10.2 %collective-permute-start.20 = (f32[180,360]{1,0:T(8,128)S(1)}, f32[180,360]{1,0:T(8,128)S(1)}, u32[]{:S(2)}, u32[]{:S(2)}) collective-permute-start(f32[180,360]{1,0:T(8,128)S(1)} %slice.26), channel_id=1, source_target_pairs={{0,32},{32,64},{64,96},{96,128},{128,160},{160,192},{192,224},{224... | collective-permute-start | bytes 777608 | tf_op jit(solution)/shard_map/ppermute | solution.py:69
  133.3 9.7 %collective-permute-start.21 = (f32[180,360]{1,0:T(8,128)S(1)}, f32[180,360]{1,0:T(8,128)S(1)}, u32[]{:S(2)}, u32[]{:S(2)}) collective-permute-start(f32[180,360]{1,0:T(8,128)S(1)} %slice.27), channel_id=1, source_target_pairs={{0,480},{32,0},{64,32},{96,64},{128,96},{160,128},{192,160},{224,1... | collective-permute-start | bytes 777608 | tf_op jit(solution)/shard_map/ppermute | solution.py:70
  143.7 8.5 %collective-permute-start.22 = (f32[96,360]{1,0:T(8,128)S(1)}, f32[96,360]{1,0:T(8,128)S(1)}, u32[]{:S(2)}, u32[]{:S(2)}) collective-permute-start(f32[96,360]{1,0:T(8,128)S(1)} %add_add_fusion.1), channel_id=1, source_target_pairs={{0,1},{1,0},{2,3},{3,2},{4,5},{5,4},{6,7},{7,6},{8,9},{9,8},{10,11... | collective-permute-start | bytes 414728 | tf_op jit(solution)/shard_map/ppermute | solution.py:86
